TPU v7x, 128 devices: a whole 4x4x4 slice. The times are simulated.
128 devices in a mesh: clip: 4 (over y_hi, core), frame: 32 (over z, x, y_lo).
Axes of the slice: x: 4, y: 4 (y_hi: 2, y_lo: 2; y = y_hi * 2 + y_lo), z: 4, core: 2. Of those that a mesh axis runs over, the one named last changes fastest.
Arguments:
- clips_in: bfloat16 [4, 64, 32, 32, 320], P('clip', 'frame'), may hold values from -6 to 6
- cotangent: bfloat16 [4, 64, 32, 32, 320], P('clip', 'frame'), may hold values from -0.0234375 to 0.0234375
- spatial_weight: bfloat16 [3, 3, 320, 320], replicated, may hold values from -0.109375 to 0.109375
- temporal_weight: bfloat16 [2, 3, 320, 320], replicated, may hold values from -0.1875 to 0.1875
Outputs:
- block_out: bfloat16 [4, 64, 32, 32, 320], P('clip', 'frame')
- grad_spatial: float32 [320, 3, 3, 320], P('frame', None, None, 'clip')
- grad_temporal: float32 [320, 2, 3, 320], P('frame', None, None, 'clip')
All inputs are finite; a program needn't handle non-finite values.
Results may differ from a plain program's by a relative error of at most 0.0064.
Values may be sent and summed in bfloat16 or wider, within the bound.
No kernel may reach another device: no remote copies, remote signals or barrier semaphores. Data moves between devices by JAX's collectives and lax.ppermute only.
A program may use at most 128 MiB of HBM per device.

v0:
```python
import functools

import jax
import jax.numpy as jnp
from jax import lax
from jax.experimental import pallas as pl
from jax.experimental.pallas import tpu as pltpu
from jax.sharding import PartitionSpec as P


BF = jnp.bfloat16
F32 = jnp.float32
C = 320
COLS = 32
ROWS = 16
PX = ROWS * COLS
TALL = PX + COLS
FULL = 2 * PX
HEAD = 256
TAIL = C - HEAD
LIMIT = 24 * 1024 * 1024
VM = pl.BlockSpec(memory_space=pltpu.VMEM)
SM = pl.BlockSpec(memory_space=pltpu.SMEM)


def dot(a, b):
    return jnp.dot(a, b, preferred_element_type=F32)


def side(*parts):
    return jnp.concatenate(parts, axis=1)


def run(kernel, outs, args, scratch=(), flops=0):
    nbytes = sum(a.size * a.dtype.itemsize for a in args) + sum(
        functools.reduce(lambda m, n: m * n, s, 1) * jnp.dtype(d).itemsize for s, d in outs
    )
    return pl.pallas_call(
        kernel,
        out_shape=[jax.ShapeDtypeStruct(s, d) for s, d in outs],
        in_specs=[SM] + [VM] * (len(args) - 1),
        out_specs=[VM] * len(outs),
        scratch_shapes=list(scratch),
        cost_estimate=pl.CostEstimate(flops=flops, bytes_accessed=nbytes, transcendentals=0),
        compiler_params=pltpu.CompilerParams(vmem_limit_bytes=LIMIT),
    )(*args)


def column_of(rows):
    return lax.broadcasted_iota(jnp.int32, (rows, 1), 0) % COLS


def right_by_one(v):
    return jnp.where(column_of(v.shape[0]) == 0, 0.0, pltpu.roll(v, 1, 0))


def left_by_one(v):
    return jnp.where(column_of(v.shape[0]) == COLS - 1, 0.0, pltpu.roll(v, v.shape[0] - 1, 0))


def sigmoid(v):
    return 1.0 / (1.0 + jnp.exp(-v))


def pad_rows(pad, rows, odd):
    pad[pl.ds(0, COLS), :] = jnp.zeros((COLS, C), BF)
    pad[pl.ds(TALL, COLS), :] = jnp.zeros((COLS, C), BF)
    pad[pl.ds(pl.multiple_of(COLS * (1 - odd), COLS), TALL), :] = rows


def convolve(pad, tails, w, wn, wk, wr, out):
    tails[...] = side(*[pad[pl.ds(COLS * i, PX), pl.ds(HEAD, TAIL)] for i in range(3)])

    def heads(i):
        return pad[pl.ds(COLS * i, PX), pl.ds(0, HEAD)]

    parts = []
    for j in range(3):
        acc = dot(heads(0), w[j, pl.ds(0, HEAD), pl.ds(0, HEAD)])
        acc = acc + dot(heads(1), w[3 + j, pl.ds(0, HEAD), pl.ds(0, HEAD)])
        acc = acc + dot(heads(2), w[6 + j, pl.ds(0, HEAD), pl.ds(0, HEAD)])
        parts.append(acc + dot(tails[...], wk[j]))
    centre = pad[pl.ds(COLS, PX), pl.ds(0, HEAD)].astype(F32)
    total = right_by_one(parts[0]) + parts[1] + left_by_one(parts[2])
    out[:, pl.ds(0, HEAD)] = (centre + total).astype(BF)
    acc = dot(heads(0), wn[0]) + dot(heads(1), wn[1]) + dot(heads(2), wn[2])
    acc = acc + dot(tails[...], wr[...])
    total = right_by_one(acc[:, :TAIL]) + acc[:, TAIL : 2 * TAIL] + left_by_one(acc[:, 2 * TAIL :])
    centre = pad[pl.ds(COLS, PX), pl.ds(HEAD, TAIL)].astype(F32)
    out[:, pl.ds(HEAD, TAIL)] = (centre + total).astype(BF)


def conv_own(at, x, w, out0, out1, pad0, pad1, tails0, tails1, wn, wk, wr):
    odd = at[0]
    for i in range(3):
        wn[i] = side(*[w[3 * i + j, pl.ds(0, HEAD), pl.ds(HEAD, TAIL)] for j in range(3)])
        for j in range(3):
            wk[j, pl.ds(TAIL * i, TAIL), :] = w[3 * i + j, pl.ds(HEAD, TAIL), pl.ds(0, HEAD)]
        wr[pl.ds(TAIL * i, TAIL), :] = side(
            *[w[3 * i + j, pl.ds(HEAD, TAIL), pl.ds(HEAD, TAIL)] for j in range(3)]
        )
    start = pl.multiple_of((TALL - 2 * COLS) * odd, COLS)
    for q, (out, pad, tails) in enumerate(((out0, pad0, tails0), (out1, pad1, tails1))):
        frame = odd + q * (1 - 2 * odd)
        pad_rows(pad, x[frame, pl.ds(start, TALL), :], odd)
        convolve(pad, tails, w, wn, wk, wr, out)


def conv_other(at, x, w, wn, wk, wr, out, pad, tails):
    pad_rows(pad, x[...], at[0])
    convolve(pad, tails, w, wn, wk, wr, out)


def tap(k, odd):
    return k + odd * (2 - 2 * k)


def tail_rows(w, layer, odd, wk):
    for k in range(3):
        wk[pl.ds(TAIL * k, TAIL), :] = w[layer, tap(k, odd), pl.ds(HEAD, TAIL), :]


def three_taps(first, second, third, tails, w, layer, odd, wk):
    total = dot(first[:, pl.ds(0, HEAD)], w[layer, tap(0, odd), pl.ds(0, HEAD), :])
    total = total + dot(second[:, pl.ds(0, HEAD)], w[layer, tap(1, odd), pl.ds(0, HEAD), :])
    total = total + dot(third[:, pl.ds(0, HEAD)], w[layer, tap(2, odd), pl.ds(0, HEAD), :])
    return total + dot(tails, wk[...])


def ends(*refs):
    return side(*[ref[:, pl.ds(HEAD, TAIL)] for ref in refs])


def temporal(states, w, layer, odd, acts, tails, wk):
    tail_rows(w, layer, odd, wk)
    for n, ref in enumerate(states):
        v = ref[...].astype(F32)
        acts[n] = (v * sigmoid(v)).astype(BF)
    for q in range(4):
        three = [acts.at[q + k] for k in range(3)]
        last = ends(*three)
        tails[q] = last
        term = three_taps(*three, last, w, layer, odd, wk)
        yield (states[q + 1][...].astype(F32) + term).astype(BF)


def layer_one(at, left, s0, s1, s2, s3, right, w, acts, tails, nxt, first, last, wk):
    states = (left, s0, s1, s2, s3, right)
    for q, value in enumerate(temporal(states, w, 0, at[0], acts, tails, wk)):
        nxt[q] = value
        if q == 0:
            first[...] = value
        if q == 3:
            last[...] = value


def layer_two(at, left, state, right, w, acts, tails, own, sent, wk):
    states = (left, state.at[0], state.at[1], state.at[2], state.at[3], right)
    for q, value in enumerate(temporal(states, w, 1, at[0], acts, tails, wk)):
        if q < 2:
            own[q] = value
        else:
            sent[3 - q] = value


def descend(six, q, before, w, layer, odd, wk):
    three = (six[q + 2], six[q + 1], six[q])
    carried = three_taps(*three, ends(*three), w, layer, odd, wk)
    v = before.astype(F32)
    s = sigmoid(v)
    return (six[q + 1][...].astype(F32) + carried * (s * (1.0 + v * (1.0 - s)))).astype(BF)


def cotangent_views(cot, c2, c3, odd):
    start = pl.multiple_of(PX * odd, PX)
    own = [cot.at[odd + q * (1 - 2 * odd), pl.ds(start, PX), :] for q in range(2)]
    return own + [c2, c3]


def back_one(at, left, cot, c2, c3, right, state, w, back, first, last, wk):
    odd = at[0]
    tail_rows(w, 1, odd, wk)
    six = [left] + cotangent_views(cot, c2, c3, odd) + [right]
    for q in range(4):
        value = descend(six, q, state[q], w, 1, odd, wk)
        back[q] = value
        if q == 0:
            first[...] = value
        if q == 3:
            last[...] = value


def split_columns(value, blocks, index):
    width = blocks.shape[-1]
    for b in range(4):
        blocks[b, index] = value[:, b * width : (b + 1) * width]


def share(blocks, kept, sent, core):
    for half in range(2):
        kept[half] = blocks[2 * half + core]
        sent[half] = blocks[2 * half + 1 - core]


def temporal_grads(at, cot, c2, c3, acts2, tails2, back, acts1, tails1, kept, sent, flip, blocks):
    odd, core = at[0], at[1]
    views = cotangent_views(cot, c2, c3, odd)
    for layer, acts, tails in ((0, acts1, tails1), (1, acts2, tails2)):
        for q in range(4):
            rows = back[q] if layer == 0 else views[q][...]
            flip[:, pl.ds(q * PX, PX)] = rows.T
        rest = jnp.zeros((C, 3 * TAIL), F32)
        for q in range(4):
            rest = rest + dot(flip[:, pl.ds(q * PX, PX)], tails[q])
        for k in range(3):
            total = jnp.zeros((C, HEAD), F32)
            for q in range(4):
                total = total + dot(flip[:, pl.ds(q * PX, PX)], acts[q + k, :, pl.ds(0, HEAD)])
            value = side(total, rest[:, k * TAIL : (k + 1) * TAIL]).astype(BF)
            split_columns(value, blocks, 3 * layer + tap(k, odd))
    share(blocks, kept, sent, core)


def back_zero(at, left, back, right, s0, s1, s2, s3, w, flip, wk):
    odd = at[0]
    tail_rows(w, 0, odd, wk)
    six = [left] + [back.at[q] for q in range(4)] + [right]
    for q, before in enumerate((s0, s1, s2, s3)):
        value = descend(six, q, before[...], w, 0, odd, wk)
        wide = value.astype(F32)
        flip[pl.ds(0, C), pl.ds(q * PX, PX)] = left_by_one(wide).astype(BF).T
        flip[pl.ds(C, C), pl.ds(q * PX, PX)] = value.T
        flip[pl.ds(2 * C, C), pl.ds(q * PX, PX)] = right_by_one(wide).astype(BF).T


def spatial_grads(at, flip, p0, p1, p2, p3, t0, t1, t2, t3, kept, sent, blocks):
    rest = jnp.zeros((3 * C, 3 * TAIL), F32)
    for q, tails in enumerate((t0, t1, t2, t3)):
        rest = rest + dot(flip[:, pl.ds(q * PX, PX)], tails[...])
    for i in range(3):
        total = jnp.zeros((3 * C, HEAD), F32)
        for q, pad in enumerate((p0, p1, p2, p3)):
            total = total + dot(flip[:, pl.ds(q * PX, PX)], pad[pl.ds(i * COLS, PX), pl.ds(0, HEAD)])
        value = side(total, rest[:, i * TAIL : (i + 1) * TAIL]).astype(BF)
        for j in range(3):
            split_columns(value[j * C : (j + 1) * C], blocks, 3 * i + j)
    share(blocks, kept, sent, at[1])


def pack(at, kept, got, out, wide, rows):
    halves, taps, channels, _ = kept.shape
    owners = out.shape[0] // halves
    count = channels // owners
    for half in range(halves):
        for t in range(taps):
            rows[...] = kept[half, t].astype(F32) + got[half, t].astype(F32)
            for owner in range(owners):
                place = pl.ds(count * t, count)
                wide[halves * owner + half, place, :] = rows[pl.ds(count * owner, count), :]
    for n in range(halves * owners):
        out[n] = wide[n].astype(BF)


def place(at, own, got, out):
    odd = at[0]
    for q in range(2):
        frame = odd + q * (1 - 2 * odd)
        out[frame, pl.ds(pl.multiple_of(PX * odd, PX), PX), :] = own[q]
        out[frame, pl.ds(pl.multiple_of(PX * (1 - odd), PX), PX), :] = got[q]


def after(value, *others):
    return lax.optimization_barrier((value, *others))[0]


def step(clips_in, cotangent, spatial_weight, temporal_weight):
    owners, clips = lax.axis_size("frame"), lax.axis_size("clip")
    odd = lax.axis_index("frame") % 2
    core = lax.axis_index("clip") % 2
    at = jnp.stack([odd, core]).astype(jnp.int32)
    swap = [(n, n ^ 1) for n in range(owners)]
    outer = [(n, n - 2 if n % 2 == 0 else n + 2) for n in range(owners)]
    outer = [(a, b) for a, b in outer if 0 <= b < owners]
    inner = [(n, n + 2 if n % 2 == 0 else n - 2) for n in range(owners)]
    inner = [(a, b) for a, b in inner if 0 <= b < owners]
    cores = [(n, n ^ 1) for n in range(clips)]

    def send(value, perm, axis="frame"):
        return lax.ppermute(value, axis, perm)

    x = clips_in.reshape(2, FULL, C)
    cot = cotangent.reshape(2, FULL, C)
    ws = spatial_weight.reshape(9, C, C)
    flops = 2 * PX * C * C

    def cut(a, frame, start, size):
        return lax.dynamic_slice(a, (frame, start, 0), (1, size, C))[0]

    tall_start = (TALL - 2 * COLS) * (1 - odd)
    one = ((PX, C), BF)
    four = ((4, PX, C), BF)
    six = ((6, PX, C), BF)
    padded = ((PX + 2 * COLS, C), BF)
    tail = ((PX, 3 * TAIL), BF)
    tails = ((4, PX, 3 * TAIL), BF)
    wk = [pltpu.VMEM((3 * TAIL, C), BF)]
    packed = [((3, HEAD, 3 * TAIL), BF), ((3, 3 * TAIL, HEAD), BF), ((3 * TAIL, 3 * TAIL), BF)]

    x3 = send(cut(x, odd, tall_start, TALL), swap)
    s0, s1, p0, p1, t0, t1, *wp = run(
        conv_own, [one, one, padded, padded, tail, tail, *packed], (at, x, ws), (), 8 * flops
    )
    wt = jnp.swapaxes(temporal_weight, 2, 3)
    x2 = send(cut(after(x, s0), 1 - odd, tall_start, TALL), swap)
    right = send(s0, outer)
    cot_right = send(cut(after(cot, s0), odd, PX * odd, PX), outer)

    s3, p3, t3 = run(conv_other, [one, padded, tail], (at, x3, ws, *wp), (), 4 * flops)
    left = send(s3, inner)
    late = after(cot, x3)
    c3 = send(after(cut(late, odd, PX * (1 - odd), PX), x2), swap)
    s2, p2, t2 = run(conv_other, [one, padded, tail], (at, x2, ws, *wp), (), 4 * flops)
    cot_left = send(c3, inner)
    c2 = send(after(cut(late, 1 - odd, PX * (1 - odd), PX), c3), swap)

    acts1, tails1, state1, first, last = run(
        layer_one, [six, tails, four, one, one], (at, left, s0, s1, s2, s3, right, temporal_weight), wk, 8 * flops
    )
    left1 = send(last, inner)
    right1 = send(first, outer)
    back1, first, last = run(
        back_one, [four, one, one], (at, cot_left, cot, c2, c3, cot_right, state1, wt), wk, 8 * flops
    )
    back_left = send(last, inner)
    back_right = send(first, outer)
    two = ((2, PX, C), BF)
    acts2, tails2, own, sent = run(
        layer_two, [six, tails, two, two], (at, left1, state1, right1, temporal_weight), wk, 8 * flops
    )
    returned = send(sent, swap)

    width = C // clips
    kept, sent = run(
        temporal_grads,
        [((2, 6, C, width), BF)] * 2,
        (at, cot, c2, c3, acts2, tails2, back1, acts1, tails1),
        [pltpu.VMEM((C, 4 * PX), BF), pltpu.VMEM((4, 6, C, width), BF)],
        16 * flops,
    )
    temporal_terms = (kept, send(sent, cores, "clip"))
    (flip,) = run(
        back_zero,
        [((3 * C, 4 * PX), BF)],
        (at, back_left, back1, back_right, s0, s1, s2, s3, wt),
        wk,
        8 * flops,
    )

    groups = [[n + half * 2 + c for n in range(0, owners * clips, clips) for half in range(2)] for c in range(2)]

    def exchange(terms):
        kept, got = terms
        _, taps, _, _ = kept.shape
        block = (2 * owners, taps * (C // owners), width)
        scratch = [pltpu.VMEM(block, F32), pltpu.VMEM((C, width), F32)]
        (sent,) = run(pack, [(block, BF)], (at, kept, got), scratch, 1000)
        return lax.all_to_all(
            sent, ("frame", "clip"), split_axis=0, concat_axis=0, axis_index_groups=groups, tiled=True
        )

    def total(parts):
        summed = jnp.sum(parts.astype(F32), axis=0)
        return summed.reshape(-1, C // owners, width).transpose(1, 0, 2)

    temporal_parts = exchange(temporal_terms)
    kept, sent = run(
        spatial_grads,
        [((2, 9, C, width), BF)] * 2,
        (at, flip, p0, p1, p2, p3, t0, t1, t2, t3),
        [pltpu.VMEM((4, 9, C, width), BF)],
        24 * flops,
    )
    spatial_terms = (kept, send(sent, cores, "clip"))
    spatial_parts = exchange(spatial_terms)
    (out,) = run(place, [((2, FULL, C), BF)], (at, own, returned), (), 1000)
    grad_temporal = total(temporal_parts).reshape(C // owners, 2, 3, width)
    grad_spatial = total(spatial_parts).reshape(C // owners, 3, 3, width)
    return (out.reshape(clips_in.shape), grad_spatial, grad_temporal)


def solution(mesh):
    placed = (P("clip", "frame", None, None, None), P("clip", "frame", None, None, None), P(), P())
    return jax.shard_map(
        step,
        mesh=mesh,
        in_specs=placed,
        out_specs=(
            P("clip", "frame", None, None, None),
            P("frame", None, None, "clip"),
            P("frame", None, None, "clip"),
        ),
        check_vma=False,
    )
```

profile of v0, /device:TPU:8, one launch (start us, length us, event | category | flops | bytes accessed | tf_op | source)
XLA Modules:
  0.0 194.0 jit_solution(16428720349275621703)
XLA Ops:
  0.7 1.8 dynamic-slice_bitcast_fusion.1
  2.9 1.6 copy-done
  4.5 1.4 copy-done.11
  5.9 3.1 %shard_map.67 = (bf16[512,320]{1,0:T(8,128)(2,1)S(1)}, bf16[512,320]{1,0:T(8,128)(2,1)S(1)}, bf16[576,320]{1,0:T(8,128)(2,1)S(1)}, bf16[576,320]{1,0:T(8,128)(2,...) custom-call(s32[2]{0:T(128)S(1)} %pad_add_fusion.at, ...), custom_call_target="tpu_custom_call" | custom-call | flops 838860800 | bytes 5603336 | tf_op jit(solution)/shard_map/pallas_call | solution.py:38
  13.6 2.0 %dynamic-slice_bitcast_fusion = bf16[544,320]{1,0:T(8,128)(2,1)} fusion(bf16[2,1024,320]{2,1,0:T(8,128)(2,1)} %bitcast.33, s32[]{:T(128)S(6)} %select_n.35, s32[]{:T(128)S(6)} %select_n.34), kind=kLoop, calls=%fused_computation.2 | loop fusion | bytes 696328 | tf_op jit(solution)/shard_map/squeeze | solution.py:297
  15.6 1.7 collective-permute-start.2
  17.2 2.2 %dynamic-slice_bitcast_fusion.3 = (bf16[512,320]{1,0:T(8,128)(2,1)}, bf16[512,320]{1,0:T(8,128)(2,1)}) fusion(bf16[2,1024,320]{2,1,0:T(8,128)(2,1)} %bitcast.28, s32[]{:T(128)S(6)} %select_n.35, s32[]{:T(128)S(6)} %select_n.36, s32[]{:T(128)S(6)} %select_n.33), kind=kLoop, calls=%fused_computation.5 | loop fusion | bytes 1310732 | tf_op jit(solution)/shard_map/squeeze | solution.py:297
  19.5 7.4 %collective-permute-done.2.x = bf16[544,320]{1,0:T(8,128)(2,1)} collective-permute-done((bf16[544,320]{1,0:T(8,128)(2,1)}, bf16[544,320]{1,0:T(8,128)(2,1)}, u32[]{:S(2)}, u32[]{:S(2)}) %collective-permute-start.2) | collective-permute-done | bytes 348192 | tf_op jit(solution)/shard_map/ppermute | solution.py:289
  26.9 1.7 collective-permute-start.7
  28.7 4.2 %collective-permute-start.3 = (bf16[512,320]{1,0:T(8,128)(2,1)S(1)}, bf16[512,320]{1,0:T(8,128)(2,1)}, u32[]{:S(2)}, u32[]{:S(2)}) collective-permute-start(bf16[512,320]{1,0:T(8,128)(2,1)S(1)} %get-tuple-element.43.s0), channel_id=1, source_target_pairs={{1,3},{2,0},{3,5},{4,2},{5,7},{6,4},{7,9},{8,6},{9,11},{10,8},{11,... | collective-permute-start | bytes 983048 | tf_op jit(solution)/shard_map/ppermute | solution.py:289
  33.8 1.0 copy-done.37
  34.8 1.9 shard_map.68
  38.2 1.3 collective-permute-start.1
  39.5 1.8 dynamic-slice_bitcast_fusion.2
  41.3 5.3 %collective-permute-start.10 = (bf16[512,320]{1,0:T(8,128)(2,1)}, bf16[512,320]{1,0:T(8,128)(2,1)}, u32[]{:S(2)}, u32[]{:S(2)}) collective-permute-start(bf16[512,320]{1,0:T(8,128)(2,1)} %dynamic-slice_bitcast_fusion.2), channel_id=1, source_target_pairs={{1,3},{2,0},{3,5},{4,2},{5,7},{6,4},{7,9},{8,6},{9,11},{10,8},{11,... | collective-permute-start | bytes 983048 | tf_op jit(solution)/shard_map/ppermute | solution.py:289
  46.6 1.4 collective-permute-start.8
  49.0 2.4 %shard_map.69 = (bf16[512,320]{1,0:T(8,128)(2,1)S(1)}, bf16[576,320]{1,0:T(8,128)(2,1)S(1)}, bf16[512,192]{1,0:T(8,128)(2,1)S(1)}) custom-call(s32[2]{0:T(128)S(1)} %pad_add_fusion.at, bf16[544,320]{1,0:T(8,128)(2,1)} %collective-permute-done.2.x, bf16[9,320,320]{2,1,0:T(8,128)(2,1)S(1)} %bitcast.25, bf16[3,256,192]{2,1,0:T(8,128)(2,1)S(1)} %get-tuple-element.39.wn, ...), custom_call_target="tpu_custom_call" | custom-call | flops 419430400 | bytes 3747848 | tf_op jit(solution)/shard_map/pallas_call | solution.py:38
  52.9 1.1 copy-done.18
  54.0 4.9 %shard_map.70 = (bf16[6,512,320]{2,1,0:T(8,128)(2,1)S(1)}, bf16[4,512,192]{2,1,0:T(8,128)(2,1)S(1)}, bf16[4,512,320]{2,1,0:T(8,128)(2,1)S(1)}, bf16[512,320]{1,0:T(8,128)(2,1)}, bf16[512,320]{1,0:T(8,128)(2,1)}) custom-call(s32[2]{0:T(128)S(1)} %pad_add_fusion.at, bf16[512,320]{1,0:T(8,128)(2,1)} %collective-permute-done.1.left, ...), custom_call_target="tpu_custom_call" | custom-call | flops 838860800 | bytes 7913480 | tf_op jit(solution)/shard_map/pallas_call | solution.py:38
  58.9 1.1 copy-done.8
  60.1 1.4 copy-done.12
  61.5 1.0 copy-done.27
  62.5 1.3 collective-permute-start.4
  63.8 5.9 %collective-permute-start.5 = (bf16[512,320]{1,0:T(8,128)(2,1)}, bf16[512,320]{1,0:T(8,128)(2,1)}, u32[]{:S(2)}, u32[]{:S(2)}) collective-permute-start(bf16[512,320]{1,0:T(8,128)(2,1)} %get-tuple-element.49), channel_id=1, source_target_pairs={{1,3},{2,0},{3,5},{4,2},{5,7},{6,4},{7,9},{8,6},{9,11},{10,8},{11,... | collective-permute-start | bytes 983048 | tf_op jit(solution)/shard_map/ppermute | solution.py:289
  70.7 1.4 copy-done.4
  72.1 1.4 copy-done.9
  73.5 5.2 %shard_map.73 = (bf16[4,512,320]{2,1,0:T(8,128)(2,1)S(1)}, bf16[512,320]{1,0:T(8,128)(2,1)}, bf16[512,320]{1,0:T(8,128)(2,1)}) custom-call(s32[2]{0:T(128)S(1)} %pad_add_fusion.at, bf16[512,320]{1,0:T(8,128)(2,1)} %collective-permute-done.8.left, bf16[2,1024,320]{2,1,0:T(8,128)(2,1)S(1)} %bitcast.30, bf16[512,320]{1,0:T(8,128)(2,1)} %collective-permute-done.9.c2, ...), custom_call_target="tpu_custom_call" | custom-call | flops 838860800 | bytes 7127048 | tf_op jit(solution)/shard_map/pallas_call | solution.py:38
  78.7 1.3 collective-permute-start.11
  80.0 5.4 %collective-permute-start.12 = (bf16[512,320]{1,0:T(8,128)(2,1)}, bf16[512,320]{1,0:T(8,128)(2,1)}, u32[]{:S(2)}, u32[]{:S(2)}) collective-permute-start(bf16[512,320]{1,0:T(8,128)(2,1)} %get-tuple-element.58), channel_id=1, source_target_pairs={{1,3},{2,0},{3,5},{4,2},{5,7},{6,4},{7,9},{8,6},{9,11},{10,8},{11,... | collective-permute-start | bytes 983048 | tf_op jit(solution)/shard_map/ppermute | solution.py:289
  85.5 4.0 %shard_map.71 = (bf16[6,512,320]{2,1,0:T(8,128)(2,1)S(1)}, bf16[4,512,192]{2,1,0:T(8,128)(2,1)S(1)}, bf16[2,512,320]{2,1,0:T(8,128)(2,1)S(1)}, bf16[2,512,320]{2,1,0:T(8,128)(2,1)S(1)}) custom-call(s32[2]{0:T(128)S(1)} %pad_add_fusion.at, bf16[512,320]{1,0:T(8,128)(2,1)} %collective-permute-done.4.left, bf16[4,512,320]{2,1,0:T(8,128)(2,1)S(1)} %copy-done.10, ...), custom_call_target="tpu_custom_call" | custom-call | flops 838860800 | bytes 7258120 | tf_op jit(solution)/shard_map/pallas_call | solution.py:38
  91.3 4.8 %shard_map.77 = (bf16[2,6,320,80]{3,2,1,0:T(8,128)(2,1)S(1)}, bf16[2,6,320,80]{3,2,1,0:T(8,128)(2,1)S(1)}) custom-call(s32[2]{0:T(128)S(1)} %pad_add_fusion.at, bf16[2,1024,320]{2,1,0:T(8,128)(2,1)S(1)} %bitcast.31, bf16[512,320]{1,0:T(8,128)(2,1)} %collective-permute-done.9.c2, bf16[512,320]{1,0:T(8,128)(2,1)} %collective-permute-done.7.c3, ...), custom_call_target="tpu_custom_call" | custom-call | flops 1677721600 | bytes 10010632 | tf_op jit(solution)/shard_map/pallas_call | solution.py:38
  97.9 2.4 %copy.30 = bf16[2,6,320,80]{2,3,1,0:T(8,128)(2,1)} copy(bf16[2,6,320,80]{3,2,1,0:T(8,128)(2,1)} %copy-done.31) | data formatting | bytes 1228800 | tf_op jit(solution)/shard_map/pallas_call | solution.py:38
  103.4 4.9 %shard_map.74.flip = bf16[960,2048]{1,0:T(8,128)(2,1)S(1)} custom-call(s32[2]{0:T(128)S(1)} %pad_add_fusion.at, bf16[512,320]{1,0:T(8,128)(2,1)} %collective-permute-done.11.left, bf16[4,512,320]{2,1,0:T(8,128)(2,1)S(1)} %copy-done.7, bf16[512,320]{1,0:T(8,128)(2,1)} %collective-permute-done.12.right, bf16[512,320]{1,0:T(8,128)(2,1)S(1)} %get-tuple-element.43.s0, ...), custom_call_target="tpu_custom_call" | custom-call | flops 838860800 | bytes 8437768 | tf_op jit(solution)/shard_map/pallas_call | solution.py:38
  108.4 5.8 %shard_map.75 = (bf16[2,9,320,80]{3,2,1,0:T(8,128)(2,1)S(1)}, bf16[2,9,320,80]{3,2,1,0:T(8,128)(2,1)S(1)}) custom-call(s32[2]{0:T(128)S(1)} %pad_add_fusion.at, bf16[960,2048]{1,0:T(8,128)(2,1)S(1)} %shard_map.74.flip, bf16[576,320]{1,0:T(8,128)(2,1)S(1)} %copy-done.39, bf16[576,320]{1,0:T(8,128)(2,1)S(1)} %copy-done.41, bf16[576,320]{1,0:T(8,128)(2,1)S(1)} %copy-done.45, ...), custom_call_target="tpu_custom_call" | custom-call | flops 2516582400 | bytes 8036360 | tf_op jit(solution)/shard_map/pallas_call | solution.py:38
  114.2 1.1 copy-done.22
  115.3 1.6 copy.26
  117.4 1.5 copy.31.got
  118.9 2.1 %shard_map.78 = bf16[64,60,80]{2,1,0:T(8,128)(2,1)} custom-call(s32[2]{0:T(128)S(1)} %pad_add_fusion.at, bf16[2,6,320,80]{3,2,1,0:T(8,128)(2,1)S(1)} %copy-done.30, bf16[2,6,320,80]{3,2,1,0:T(8,128)(2,1)S(1)} %copy.31.got), custom_call_target="tpu_custom_call" | custom-call | flops 1000 | bytes 1843208 | tf_op jit(solution)/shard_map/pallas_call | solution.py:38
  121.1 14.7 %all-to-all-start.1 = ((bf16[64,60,80]{2,1,0:T(8,128)(2,1)}), bf16[64,60,80]{2,1,0:T(8,128)(2,1)}, u32[]{:S(2)}, u32[]{:S(2)}) async-start(bf16[64,60,80]{2,1,0:T(8,128)(2,1)} %shard_map.78), calls=%async_computation.1 | async-start | bytes 2097152 | tf_op jit(solution)/shard_map/all_to_all | solution.py:367
  136.7 1.4 copy-done.23
  138.0 1.5 shard_map.76
  139.5 1.6 copy.28
  141.1 12.5 %all-to-all-done.1 = bf16[64,60,80]{2,1,0:T(8,128)(2,1)} async-done(((bf16[64,60,80]{2,1,0:T(8,128)(2,1)}), bf16[64,60,80]{2,1,0:T(8,128)(2,1)}, u32[]{:S(2)}, u32[]{:S(2)}) %all-to-all-start.1) | async-done | bytes 614432 | tf_op jit(solution)/shard_map/all_to_all | solution.py:367
  153.6 6.3 %all-to-all-start = ((bf16[64,90,80]{1,2,0:T(8,128)(2,1)}), bf16[64,90,80]{1,2,0:T(8,128)(2,1)S(1)}, u32[]{:S(2)}, u32[]{:S(2)}) async-start(bf16[64,90,80]{1,2,0:T(8,128)(2,1)} %copy.28), calls=%async_computation | async-start | bytes 2621440 | tf_op jit(solution)/shard_map/all_to_all | solution.py:367
  160.7 26.9 %collective-permute-done.6 = bf16[2,512,320]{1,2,0:T(8,128)(2,1)} collective-permute-done((bf16[2,512,320]{1,2,0:T(8,128)(2,1)S(1)}, bf16[2,512,320]{1,2,0:T(8,128)(2,1)}, u32[]{:S(2)}, u32[]{:S(2)}) %collective-permute-start.6) | collective-permute-done | bytes 655392 | tf_op jit(solution)/shard_map/ppermute | solution.py:289
  187.6 1.4 copy.24.got
  189.1 1.8 shard_map.72
  190.9 1.5 convert_reduce_fusion.1
  (126 shorter events, 21.3 us)
Async XLA Ops:
  2.5 14.8 %collective-permute-start = (bf16[544,320]{1,0:T(8,128)(2,1)}, bf16[544,320]{1,0:T(8,128)(2,1)S(1)}, u32[]{:S(2)}, u32[]{:S(2)}) collective-permute-start(bf16[544,320]{1,0:T(8,128)(2,1)} %dynamic-slice_bitcast_fusion.1), channel_id=1, source_target_pairs={{0,1},{1,0},{2,3},{3,2},{4,5},{5,4},{6,7},{7,6},{8,9},{9,8},{10,11... | collective-permute-start | bytes 1044488 | tf_op jit(solution)/shard_map/ppermute | solution.py:289
  2.9 1.6 copy-start
  4.5 1.4 copy-start.11
  13.6 19.2 %copy-start.1 = (bf16[3,3,320,320]{3,2,1,0:T(8,128)(2,1)S(1)}, bf16[3,3,320,320]{3,2,1,0:T(8,128)(2,1)}, u32[]{:S(2)}) copy-start(bf16[3,3,320,320]{3,2,1,0:T(8,128)(2,1)} %param.6) | copy-start | bytes 5529604
  15.6 11.4 %collective-permute-start.2 = (bf16[544,320]{1,0:T(8,128)(2,1)}, bf16[544,320]{1,0:T(8,128)(2,1)}, u32[]{:S(2)}, u32[]{:S(2)}) collective-permute-start(bf16[544,320]{1,0:T(8,128)(2,1)} %dynamic-slice_bitcast_fusion), channel_id=1, source_target_pairs={{0,1},{1,0},{2,3},{3,2},{4,5},{5,4},{6,7},{7,6},{8,9},{9,8},{10,11... | collective-permute-start | bytes 1044488 | tf_op jit(solution)/shard_map/ppermute | solution.py:289
  17.2 15.6 %copy-start.36 = (bf16[544,320]{1,0:T(8,128)(2,1)}, bf16[544,320]{1,0:T(8,128)(2,1)S(1)}, u32[]{:S(2)}) copy-start(bf16[544,320]{1,0:T(8,128)(2,1)S(1)} %collective-permute-done.x) | copy-start | bytes 1044484
  26.9 19.6 %collective-permute-start.7 = (bf16[512,320]{1,0:T(8,128)(2,1)}, bf16[512,320]{1,0:T(8,128)(2,1)}, u32[]{:S(2)}, u32[]{:S(2)}) collective-permute-start(bf16[512,320]{1,0:T(8,128)(2,1)} %get-tuple-element.53), channel_id=1, source_target_pairs={{0,1},{1,0},{2,3},{3,2},{4,5},{5,4},{6,7},{7,6},{8,9},{9,8},{10,11... | collective-permute-start | bytes 983048 | tf_op jit(solution)/shard_map/ppermute | solution.py:289
  28.7 24.2 %collective-permute-start.3 = (bf16[512,320]{1,0:T(8,128)(2,1)S(1)}, bf16[512,320]{1,0:T(8,128)(2,1)}, u32[]{:S(2)}, u32[]{:S(2)}) collective-permute-start(bf16[512,320]{1,0:T(8,128)(2,1)S(1)} %get-tuple-element.43.s0), channel_id=1, source_target_pairs={{1,3},{2,0},{3,5},{4,2},{5,7},{6,4},{7,9},{8,6},{9,11},{10,8},{11,... | collective-permute-start | bytes 983048 | tf_op jit(solution)/shard_map/ppermute | solution.py:289
  38.2 13.2 %copy-start.17 = (bf16[512,320]{1,0:T(8,128)(2,1)}, bf16[512,320]{1,0:T(8,128)(2,1)S(1)}, u32[]{:S(2)}) copy-start(bf16[512,320]{1,0:T(8,128)(2,1)S(1)} %get-tuple-element.42.s3) | copy-start | bytes 983044
  38.2 14.7 %collective-permute-start.1 = (bf16[512,320]{1,0:T(8,128)(2,1)S(1)}, bf16[512,320]{1,0:T(8,128)(2,1)}, u32[]{:S(2)}, u32[]{:S(2)}) collective-permute-start(bf16[512,320]{1,0:T(8,128)(2,1)S(1)} %get-tuple-element.42.s3), channel_id=1, source_target_pairs={{0,2},{2,4},{3,1},{4,6},{5,3},{6,8},{7,5},{8,10},{9,7},{10,12},{11... | collective-permute-start | bytes 983048 | tf_op jit(solution)/shard_map/ppermute | solution.py:289
  41.3 29.3 %collective-permute-start.10 = (bf16[512,320]{1,0:T(8,128)(2,1)}, bf16[512,320]{1,0:T(8,128)(2,1)}, u32[]{:S(2)}, u32[]{:S(2)}) collective-permute-start(bf16[512,320]{1,0:T(8,128)(2,1)} %dynamic-slice_bitcast_fusion.2), channel_id=1, source_target_pairs={{1,3},{2,0},{3,5},{4,2},{5,7},{6,4},{7,9},{8,6},{9,11},{10,8},{11,... | collective-permute-start | bytes 983048 | tf_op jit(solution)/shard_map/ppermute | solution.py:289
  46.6 6.3 %copy-start.2 = (bf16[2,3,320,320]{3,2,1,0:T(8,128)(2,1)S(1)}, bf16[2,3,320,320]{3,2,1,0:T(8,128)(2,1)}, u32[]{:S(2)}) copy-start(bf16[2,3,320,320]{3,2,1,0:T(8,128)(2,1)} %w.3) | copy-start | bytes 3686404
  46.6 6.3 %copy-start.15 = (bf16[512,320]{1,0:T(8,128)(2,1)S(1)}, bf16[512,320]{1,0:T(8,128)(2,1)}, u32[]{:S(2)}) copy-start(bf16[512,320]{1,0:T(8,128)(2,1)} %copy-done.14) | copy-start | bytes 983044
  46.6 24.1 %collective-permute-start.9 = (bf16[512,320]{1,0:T(8,128)(2,1)}, bf16[512,320]{1,0:T(8,128)(2,1)}, u32[]{:S(2)}, u32[]{:S(2)}) collective-permute-start(bf16[512,320]{1,0:T(8,128)(2,1)} %get-tuple-element.54), channel_id=1, source_target_pairs={{0,1},{1,0},{2,3},{3,2},{4,5},{5,4},{6,7},{7,6},{8,9},{9,8},{10,11... | collective-permute-start | bytes 983048 | tf_op jit(solution)/shard_map/ppermute | solution.py:289
  46.6 24.1 %collective-permute-start.8 = (bf16[512,320]{1,0:T(8,128)(2,1)}, bf16[512,320]{1,0:T(8,128)(2,1)}, u32[]{:S(2)}, u32[]{:S(2)}) collective-permute-start(bf16[512,320]{1,0:T(8,128)(2,1)} %collective-permute-done.7.c3), channel_id=1, source_target_pairs={{0,2},{2,4},{3,1},{4,6},{5,3},{6,8},{7,5},{8,10},{9,7},{10,12},{11... | collective-permute-start | bytes 983048 | tf_op jit(solution)/shard_map/ppermute | solution.py:289
  52.9 6.1 %copy-start.20 = (bf16[512,320]{1,0:T(8,128)(2,1)}, bf16[512,320]{1,0:T(8,128)(2,1)S(1)}, u32[]{:S(2)}) copy-start(bf16[512,320]{1,0:T(8,128)(2,1)S(1)} %get-tuple-element.46.s2) | copy-start | bytes 983044
  54.0 15.7 %copy-start.3 = (bf16[2,3,320,320]{3,2,1,0:T(8,128)(2,1)S(1)}, bf16[2,3,320,320]{3,2,1,0:T(8,128)(2,1)}, u32[]{:S(2)}) copy-start(bf16[2,3,320,320]{3,2,1,0:T(8,128)(2,1)} %w.3) | copy-start | bytes 3686404
  58.9 1.1 copy-start.8
  60.1 1.4 copy-start.12
  62.5 23.0 %collective-permute-start.4 = (bf16[512,320]{1,0:T(8,128)(2,1)}, bf16[512,320]{1,0:T(8,128)(2,1)}, u32[]{:S(2)}, u32[]{:S(2)}) collective-permute-start(bf16[512,320]{1,0:T(8,128)(2,1)} %get-tuple-element.47), channel_id=1, source_target_pairs={{0,2},{2,4},{3,1},{4,6},{5,3},{6,8},{7,5},{8,10},{9,7},{10,12},{11... | collective-permute-start | bytes 983048 | tf_op jit(solution)/shard_map/ppermute | solution.py:289
  63.8 21.7 %collective-permute-start.5 = (bf16[512,320]{1,0:T(8,128)(2,1)}, bf16[512,320]{1,0:T(8,128)(2,1)}, u32[]{:S(2)}, u32[]{:S(2)}) collective-permute-start(bf16[512,320]{1,0:T(8,128)(2,1)} %get-tuple-element.49), channel_id=1, source_target_pairs={{1,3},{2,0},{3,5},{4,2},{5,7},{6,4},{7,9},{8,6},{9,11},{10,8},{11,... | collective-permute-start | bytes 983048 | tf_op jit(solution)/shard_map/ppermute | solution.py:289
  70.7 1.4 copy-start.4
  72.1 1.4 copy-start.9
  73.5 12.0 %copy-start.10 = (bf16[4,512,320]{2,1,0:T(8,128)(2,1)S(1)}, bf16[4,512,320]{2,1,0:T(8,128)(2,1)}, u32[]{:S(2)}) copy-start(bf16[4,512,320]{2,1,0:T(8,128)(2,1)} %copy-done.8) | copy-start | bytes 3932164
  73.5 17.8 %copy-start.13 = (bf16[6,512,320]{2,1,0:T(8,128)(2,1)S(1)}, bf16[6,512,320]{2,1,0:T(8,128)(2,1)}, u32[]{:S(2)}) copy-start(bf16[6,512,320]{2,1,0:T(8,128)(2,1)} %copy-done.12) | copy-start | bytes 5898244
  78.7 12.6 %copy-start.6 = (bf16[4,512,320]{2,1,0:T(8,128)(2,1)}, bf16[4,512,320]{2,1,0:T(8,128)(2,1)S(1)}, u32[]{:S(2)}) copy-start(bf16[4,512,320]{2,1,0:T(8,128)(2,1)S(1)} %get-tuple-element.57.back) | copy-start | bytes 3932164
  78.7 21.6 %collective-permute-start.11 = (bf16[512,320]{1,0:T(8,128)(2,1)}, bf16[512,320]{1,0:T(8,128)(2,1)}, u32[]{:S(2)}, u32[]{:S(2)}) collective-permute-start(bf16[512,320]{1,0:T(8,128)(2,1)} %get-tuple-element.56), channel_id=1, source_target_pairs={{0,2},{2,4},{3,1},{4,6},{5,3},{6,8},{7,5},{8,10},{9,7},{10,12},{11... | collective-permute-start | bytes 983048 | tf_op jit(solution)/shard_map/ppermute | solution.py:289
  80.0 11.3 %copy-start.5 = (bf16[1,2,32,32,320]{4,3,2,1,0:T(8,128)(2,1)S(1)}, bf16[1,2,32,32,320]{4,3,2,1,0:T(8,128)(2,1)}, u32[]{:S(2)}) copy-start(bf16[1,2,32,32,320]{4,3,2,1,0:T(8,128)(2,1)} %param.5) | copy-start | bytes 3932164
  80.0 11.3 %copy-start.28 = (bf16[4,512,192]{2,1,0:T(8,128)(2,1)S(1)}, bf16[4,512,192]{2,1,0:T(8,128)(2,1)}, u32[]{:S(2)}) copy-start(bf16[4,512,192]{2,1,0:T(8,128)(2,1)} %copy-done.27) | copy-start | bytes 2359300
  80.0 20.3 %collective-permute-start.12 = (bf16[512,320]{1,0:T(8,128)(2,1)}, bf16[512,320]{1,0:T(8,128)(2,1)}, u32[]{:S(2)}, u32[]{:S(2)}) collective-permute-start(bf16[512,320]{1,0:T(8,128)(2,1)} %get-tuple-element.58), channel_id=1, source_target_pairs={{1,3},{2,0},{3,5},{4,2},{5,7},{6,4},{7,9},{8,6},{9,11},{10,8},{11,... | collective-permute-start | bytes 983048 | tf_op jit(solution)/shard_map/ppermute | solution.py:289
  97.9 2.4 %copy-start.7 = (bf16[4,512,320]{2,1,0:T(8,128)(2,1)S(1)}, bf16[4,512,320]{2,1,0:T(8,128)(2,1)}, u32[]{:S(2)}) copy-start(bf16[4,512,320]{2,1,0:T(8,128)(2,1)} %copy-done.6) | copy-start | bytes 3932164
  100.3 17.0 %collective-permute-start.14 = (bf16[2,6,320,80]{2,3,1,0:T(8,128)(2,1)}, bf16[2,6,320,80]{2,3,1,0:T(8,128)(2,1)}, u32[]{:S(2)}, u32[]{:S(2)}) collective-permute-start(bf16[2,6,320,80]{2,3,1,0:T(8,128)(2,1)} %copy.30), channel_id=1, source_target_pairs={{0,32},{32,0},{64,96},{96,64},{1,33},{33,1},{65,97},{97,65},{2,34}... | collective-permute-start | bytes 1843208 | tf_op jit(solution)/shard_map/ppermute | solution.py:289
  103.3 4.9 %copy-start.39 = (bf16[576,320]{1,0:T(8,128)(2,1)S(1)}, bf16[576,320]{1,0:T(8,128)(2,1)}, u32[]{:S(2)}) copy-start(bf16[576,320]{1,0:T(8,128)(2,1)} %copy-done.38) | copy-start | bytes 1105924
  103.3 4.9 %copy-start.41 = (bf16[576,320]{1,0:T(8,128)(2,1)S(1)}, bf16[576,320]{1,0:T(8,128)(2,1)}, u32[]{:S(2)}) copy-start(bf16[576,320]{1,0:T(8,128)(2,1)} %copy-done.40) | copy-start | bytes 1105924
  103.3 5.0 %copy-start.43 = (bf16[576,320]{1,0:T(8,128)(2,1)S(1)}, bf16[576,320]{1,0:T(8,128)(2,1)}, u32[]{:S(2)}) copy-start(bf16[576,320]{1,0:T(8,128)(2,1)} %copy-done.42) | copy-start | bytes 1105924
  103.3 5.0 %copy-start.45 = (bf16[576,320]{1,0:T(8,128)(2,1)S(1)}, bf16[576,320]{1,0:T(8,128)(2,1)}, u32[]{:S(2)}) copy-start(bf16[576,320]{1,0:T(8,128)(2,1)} %copy-done.44) | copy-start | bytes 1105924
  103.3 5.0 %copy-start.47 = (bf16[512,192]{1,0:T(8,128)(2,1)S(1)}, bf16[512,192]{1,0:T(8,128)(2,1)}, u32[]{:S(2)}) copy-start(bf16[512,192]{1,0:T(8,128)(2,1)} %copy-done.46) | copy-start | bytes 589828
  103.4 5.0 %copy-start.49 = (bf16[512,192]{1,0:T(8,128)(2,1)S(1)}, bf16[512,192]{1,0:T(8,128)(2,1)}, u32[]{:S(2)}) copy-start(bf16[512,192]{1,0:T(8,128)(2,1)} %copy-done.48) | copy-start | bytes 589828
  103.4 5.0 %copy-start.51 = (bf16[512,192]{1,0:T(8,128)(2,1)S(1)}, bf16[512,192]{1,0:T(8,128)(2,1)}, u32[]{:S(2)}) copy-start(bf16[512,192]{1,0:T(8,128)(2,1)} %copy-done.50) | copy-start | bytes 589828
  103.4 5.0 %copy-start.53 = (bf16[512,192]{1,0:T(8,128)(2,1)S(1)}, bf16[512,192]{1,0:T(8,128)(2,1)}, u32[]{:S(2)}) copy-start(bf16[512,192]{1,0:T(8,128)(2,1)} %copy-done.52) | copy-start | bytes 589828
  115.3 3.6 %copy-start.30 = (bf16[2,6,320,80]{3,2,1,0:T(8,128)(2,1)S(1)}, bf16[2,6,320,80]{3,2,1,0:T(8,128)(2,1)}, u32[]{:S(2)}) copy-start(bf16[2,6,320,80]{3,2,1,0:T(8,128)(2,1)} %copy-done.29) | copy-start | bytes 1843204
  116.9 18.9 %collective-permute-start.13 = (bf16[2,9,320,80]{2,3,1,0:T(8,128)(2,1)}, bf16[2,9,320,80]{2,3,1,0:T(8,128)(2,1)S(1)}, u32[]{:S(2)}, u32[]{:S(2)}) collective-permute-start(bf16[2,9,320,80]{2,3,1,0:T(8,128)(2,1)} %copy.26), channel_id=1, source_target_pairs={{0,32},{32,0},{64,96},{96,64},{1,33},{33,1},{65,97},{97,65},{2,34}... | collective-permute-start | bytes 2764808 | tf_op jit(solution)/shard_map/ppermute | solution.py:289
  121.1 32.5 %all-to-all-start.1 = ((bf16[64,60,80]{2,1,0:T(8,128)(2,1)}), bf16[64,60,80]{2,1,0:T(8,128)(2,1)}, u32[]{:S(2)}, u32[]{:S(2)}) async-start(bf16[64,60,80]{2,1,0:T(8,128)(2,1)} %shard_map.78), calls=%async_computation.1 | async-start | bytes 2097152 | tf_op jit(solution)/shard_map/all_to_all | solution.py:367
  136.7 1.4 copy-start.23
  141.1 18.8 %copy-start.33 = (bf16[2,512,320]{2,1,0:T(8,128)(2,1)S(1)}, bf16[2,512,320]{2,1,0:T(8,128)(2,1)}, u32[]{:S(2)}) copy-start(bf16[2,512,320]{2,1,0:T(8,128)(2,1)} %copy-done.32) | copy-start | bytes 1966084
  153.6 39.4 %all-to-all-start = ((bf16[64,90,80]{1,2,0:T(8,128)(2,1)}), bf16[64,90,80]{1,2,0:T(8,128)(2,1)S(1)}, u32[]{:S(2)}, u32[]{:S(2)}) async-start(bf16[64,90,80]{1,2,0:T(8,128)(2,1)} %copy.28), calls=%async_computation | async-start | bytes 2621440 | tf_op jit(solution)/shard_map/all_to_all | solution.py:367
  159.9 29.2 %copy-start.35 = (bf16[2,512,320]{2,1,0:T(8,128)(2,1)S(1)}, bf16[2,512,320]{2,1,0:T(8,128)(2,1)}, u32[]{:S(2)}) copy-start(bf16[2,512,320]{2,1,0:T(8,128)(2,1)} %copy-done.34) | copy-start | bytes 1966084
  160.2 27.4 %collective-permute-start.6 = (bf16[2,512,320]{1,2,0:T(8,128)(2,1)S(1)}, bf16[2,512,320]{1,2,0:T(8,128)(2,1)}, u32[]{:S(2)}, u32[]{:S(2)}) collective-permute-start(bf16[2,512,320]{1,2,0:T(8,128)(2,1)S(1)} %copy.23), channel_id=1, source_target_pairs={{0,1},{1,0},{2,3},{3,2},{4,5},{5,4},{6,7},{7,6},{8,9},{9,8},{10,11... | collective-permute-start | bytes 1966088 | tf_op jit(solution)/shard_map/ppermute | solution.py:289
  (23 other events, 20.3 us)
where the time goes:
time: 196 us; the launch traced here: 194 us
  starting transfers between devices  51.9 us (26%)
  local copies, waits for them, and re-layouts  49.9 us (25%)
  waiting for transfers between devices  46.8 us (24%)
  Pallas kernels  42.5 us (22%)
    pallas_call x12, Pallas kernels, run(): pl.pallas_call(kernel, out_shape=[jax.ShapeDtypeStruct(s, d) for s, d in...  42.5 us
    ppermute x15, waiting for transfers between devices, send(): return lax.ppermute(value, axis, perm)  34.3 us
    unnamed x111, local copies, waits for them, and re-layouts  32.3 us
    ppermute x15, starting transfers between devices, send(): return lax.ppermute(value, axis, perm)  30.9 us
    all_to_all x2, starting transfers between devices, exchange(): lax.all_to_all(sent, ('frame', 'clip'), split_axis=0, concat_axis=0, axis...  21 us
    all_to_all x2, waiting for transfers between devices, exchange(): lax.all_to_all(sent, ('frame', 'clip'), split_axis=0, concat_axis=0, axis...  12.5 us
    squeeze x4, local copies, waits for them, and re-layouts, cut(): return lax.dynamic_slice(a, (frame, start, 0), (1, size, C))[0]  7.82 us
    pallas_call x4, local copies, waits for them, and re-layouts, run(): pl.pallas_call(kernel, out_shape=[jax.ShapeDtypeStruct(s, d) for s, d in...  5.82 us
  transfers between devices with their start and end apart: 17, of which 3 were waited for; matrix products, arithmetic and copies ran while one was open for 10% of the time, Pallas kernels for 22%

commit v1 on v0

v1 whole, which is shorter than its diff:
```python
import functools

import jax
import jax.numpy as jnp
from jax import lax
from jax.experimental import pallas as pl
from jax.experimental.pallas import tpu as pltpu
from jax.sharding import PartitionSpec as P


BF = jnp.bfloat16
F32 = jnp.float32
C = 320
COLS = 32
ROWS = 16
PX = ROWS * COLS
TALL = PX + COLS
FULL = 2 * PX
HEAD = 256
TAIL = C - HEAD
CLIPS = 4
VMEM_BYTES = 67_043_328
WIDTH = C // CLIPS
HBM = pl.BlockSpec(memory_space=pltpu.HBM)
SM = pl.BlockSpec(memory_space=pltpu.SMEM)


ONE = (PX, C)
TALL_ONE = (TALL, C)
THREE_TAILS = 3 * TAIL
SIDES = (CLIPS, PX, 3 * WIDTH)
KERNELS = (3, C, C)


def dot(a, b):
    return jnp.dot(a, b, preferred_element_type=F32)


def side(*parts):
    return jnp.concatenate(parts, axis=1)


class Mover:
    def __init__(self, sems):
        self.sems, self.count, self.leaving = sems, 0, []

    def copy(self, src, dst):
        c = pltpu.make_async_copy(src, dst, self.sems.at[self.count])
        self.count += 1
        c.start()
        return c

    def fetch(self, src, dst):
        return Arrival(self.copy(src, dst), dst)

    def put(self, src, dst):
        self.leaving.append(self.copy(src, dst))

    def finish(self):
        for c in self.leaving:
            c.wait()


class Arrival:
    def __init__(self, copy, ref):
        self.copy, self.ref = copy, ref

    def get(self):
        if self.copy is not None:
            self.copy.wait()
            self.copy = None
        return self.ref


def nth(ref, n):
    return ref.at[pl.ds(n * PX, PX), :]


def run(kernel, outs, args, scratch, copies, flops=0):
    nbytes = sum(a.size * a.dtype.itemsize for a in args) + sum(
        functools.reduce(lambda m, n: m * n, s, 2) for s in outs
    )
    return pl.pallas_call(
        kernel,
        out_shape=[jax.ShapeDtypeStruct(s, BF) for s in outs],
        in_specs=[SM] + [HBM] * (len(args) - 1),
        out_specs=[HBM] * len(outs),
        scratch_shapes=[s if not isinstance(s, tuple) else pltpu.VMEM(s, BF) for s in scratch]
        + [pltpu.SemaphoreType.DMA((copies,))],
        cost_estimate=pl.CostEstimate(flops=flops, bytes_accessed=nbytes, transcendentals=0),
        compiler_params=pltpu.CompilerParams(vmem_limit_bytes=VMEM_BYTES),
    )(*args)


def column_of(rows):
    return lax.broadcasted_iota(jnp.int32, (rows, 1), 0) % COLS


def right_by_one(v):
    return jnp.where(column_of(v.shape[0]) == 0, 0.0, pltpu.roll(v, 1, 0))


def left_by_one(v):
    return jnp.where(column_of(v.shape[0]) == COLS - 1, 0.0, pltpu.roll(v, v.shape[0] - 1, 0))


def sigmoid(v):
    return 1.0 / (1.0 + jnp.exp(-v))


def padded(pad, odd):
    pad[pl.ds(0, COLS), :] = jnp.zeros((COLS, C), BF)
    pad[pl.ds(TALL, COLS), :] = jnp.zeros((COLS, C), BF)
    return pad.at[pl.ds(pl.multiple_of(COLS * (1 - odd), COLS), TALL), :]


def convolve(pad, w, wn, wk, wr, out, sides):
    tails = side(*[pad[pl.ds(COLS * i, PX), pl.ds(HEAD, TAIL)] for i in range(3)])

    def heads(i):
        return pad[pl.ds(COLS * i, PX), pl.ds(0, HEAD)]

    parts = []
    for j in range(3):
        acc = dot(heads(0), w[j, pl.ds(0, HEAD), pl.ds(0, HEAD)])
        acc = acc + dot(heads(1), w[3 + j, pl.ds(0, HEAD), pl.ds(0, HEAD)])
        acc = acc + dot(heads(2), w[6 + j, pl.ds(0, HEAD), pl.ds(0, HEAD)])
        parts.append(acc + dot(tails, wk[j]))
    centre = pad[pl.ds(COLS, PX), pl.ds(0, HEAD)].astype(F32)
    total = right_by_one(parts[0]) + parts[1] + left_by_one(parts[2])
    out[:, pl.ds(0, HEAD)] = (centre + total).astype(BF)
    acc = dot(heads(0), wn[0]) + dot(heads(1), wn[1]) + dot(heads(2), wn[2])
    acc = acc + dot(tails, wr[...])
    total = right_by_one(acc[:, :TAIL]) + acc[:, TAIL : 2 * TAIL] + left_by_one(acc[:, 2 * TAIL :])
    centre = pad[pl.ds(COLS, PX), pl.ds(HEAD, TAIL)].astype(F32)
    out[:, pl.ds(HEAD, TAIL)] = (centre + total).astype(BF)
    for b in range(CLIPS):
        columns = slice(b * WIDTH, (b + 1) * WIDTH)
        sides[b] = side(*[pad[pl.ds(COLS * i, PX), columns] for i in range(3)])


def conv_own(at, x, cot, w, pair, out1, sides, x2, c3, c2, wn, wk, wr, *rest):
    vw, vwn, vwk, vwr, pads, states, vsides, vx2, vcot, sems = rest
    odd = at[0]
    move = Mover(sems)
    start = pl.multiple_of((TALL - 2 * COLS) * odd, COLS)
    frames = [odd, 1 - odd]
    rows = [
        move.fetch(x.at[frames[q], pl.ds(start, TALL), :], padded(pads.at[q], odd)) for q in range(2)
    ]
    weights = [move.fetch(w.at[n], vw.at[n]) for n in range(9)]
    away = pl.multiple_of((TALL - 2 * COLS) * (1 - odd), COLS)
    parts = [(move.fetch(x.at[1 - odd, pl.ds(away, TALL), :], vx2), x2)]
    here, there = pl.multiple_of(PX * odd, PX), pl.multiple_of(PX * (1 - odd), PX)
    parts += [
        (move.fetch(cot.at[odd, pl.ds(here, PX), :], vcot.at[0]), nth(pair, 1)),
        (move.fetch(cot.at[odd, pl.ds(there, PX), :], vcot.at[1]), c3),
        (move.fetch(cot.at[1 - odd, pl.ds(there, PX), :], vcot.at[2]), c2),
    ]
    for arrival in weights:
        arrival.get()
    for i in range(3):
        vwn[i] = side(*[vw[3 * i + j, pl.ds(0, HEAD), pl.ds(HEAD, TAIL)] for j in range(3)])
        for j in range(3):
            vwk[j, pl.ds(TAIL * i, TAIL), :] = vw[3 * i + j, pl.ds(HEAD, TAIL), pl.ds(0, HEAD)]
        vwr[pl.ds(TAIL * i, TAIL), :] = side(
            *[vw[3 * i + j, pl.ds(HEAD, TAIL), pl.ds(HEAD, TAIL)] for j in range(3)]
        )
    move.put(vwn, wn)
    move.put(vwk, wk)
    move.put(vwr, wr)
    for arrival, out in parts:
        move.put(arrival.get(), out)
    for q, out in enumerate((nth(pair, 0), out1)):
        rows[q].get()
        convolve(pads.at[q], vw, vwn, vwk, vwr, states.at[q], vsides.at[q])
        move.put(states.at[q], out)
        move.put(vsides.at[q], sides.at[q])
    move.finish()


def conv_other(at, x, w, wn, wk, wr, out, sides, *rest):
    vw, vwn, vwk, vwr, pad, state, vsides, sems = rest
    move = Mover(sems)
    needed = [move.fetch(x, padded(pad, at[0]))]
    needed += [move.fetch(w, vw), move.fetch(wn, vwn), move.fetch(wk, vwk), move.fetch(wr, vwr)]
    for arrival in needed:
        arrival.get()
    convolve(pad, vw, vwn, vwk, vwr, state, vsides)
    move.put(state, out)
    move.put(vsides, sides)
    move.finish()


def tap(k, odd):
    return k + odd * (2 - 2 * k)


def taps_of(move, w, layer, odd, vw):
    return [move.fetch(w.at[layer, tap(k, odd)], vw.at[k]) for k in range(3)]


def tail_rows(arrivals, wk):
    for k, arrival in enumerate(arrivals):
        wk[pl.ds(TAIL * k, TAIL), :] = arrival.get()[pl.ds(HEAD, TAIL), :]


def three_taps(three, vw, wk):
    tails = side(*[ref[:, pl.ds(HEAD, TAIL)] for ref in three])
    totals = []
    for columns in (pl.ds(0, HEAD), pl.ds(HEAD, TAIL)):
        total = dot(three[0][:, pl.ds(0, HEAD)], vw[0, pl.ds(0, HEAD), columns])
        total = total + dot(three[1][:, pl.ds(0, HEAD)], vw[1, pl.ds(0, HEAD), columns])
        total = total + dot(three[2][:, pl.ds(0, HEAD)], vw[2, pl.ds(0, HEAD), columns])
        totals.append(total + dot(tails, wk[:, columns]))
    return side(*totals)


def temporal(move, states, w, layer, odd, acts, vw, wk, vacts):
    weights = taps_of(move, w, layer, odd, vw)
    states = [move.fetch(src, dst) for src, dst in states]
    tail_rows(weights, wk)
    done = 0
    for q in range(4):
        while done < q + 3:
            v = states[done].get()[...].astype(F32)
            vacts[done] = (v * sigmoid(v)).astype(BF)
            move.put(vacts.at[done], acts.at[done])
            done += 1
        term = three_taps([vacts.at[q + k] for k in range(3)], vw, wk)
        yield (states[q + 1].get()[...].astype(F32) + term).astype(BF)


def layer_one(at, left, pair, s1, s2, s3, right, c3, w, acts, state, last, first, *rest):
    vs, vc3, vw, wk, vacts, nxt, sems = rest
    move = Mover(sems)
    sources = (left, nth(pair, 0), s1, s2, s3, nth(right, 0))
    states = [(ref, vs.at[n]) for n, ref in enumerate(sources)]
    for q, value in enumerate(temporal(move, states, w, 0, at[0], acts, vw, wk, vacts)):
        nxt[q] = value
        move.put(nxt.at[q], state.at[q])
        if q == 0:
            move.put(nxt.at[0], first)
            passing = move.fetch(c3, vc3)
    move.put(nxt.at[3], nth(last, 0))
    move.put(passing.get(), nth(last, 1))
    move.finish()


def layer_two(at, left, state, right, w, acts, own, sent, *rest):
    vs, vw, wk, vacts, nxt, sems = rest
    move = Mover(sems)
    sources = (nth(left, 0), state.at[0], state.at[1], state.at[2], state.at[3], right)
    states = [(ref, vs.at[n]) for n, ref in enumerate(sources)]
    for q, value in enumerate(temporal(move, states, w, 1, at[0], acts, vw, wk, vacts)):
        nxt[q] = value
        move.put(nxt.at[q], own.at[q] if q < 2 else nth(sent, 3 - q))
    move.finish()


def descend(six, q, before, vw, wk):
    three = [six[q + 2 - k].get() for k in range(3)]
    carried = three_taps(three, vw, wk)
    v = before.get()[...].astype(F32)
    s = sigmoid(v)
    return (three[1][...].astype(F32) + carried * (s * (1.0 + v * (1.0 - s)))).astype(BF)


def cotangent_views(cot, c2, c3, odd):
    start = pl.multiple_of(PX * odd, PX)
    return [cot.at[odd, pl.ds(start, PX), :], cot.at[1 - odd, pl.ds(start, PX), :], c2, c3]


def back_one(at, left, cot, c2, c3, right, state, w, back, first, last, *rest):
    vs, vstate, vw, wk, nxt, sems = rest
    odd = at[0]
    move = Mover(sems)
    weights = taps_of(move, w, 1, odd, vw)
    sources = [nth(left, 1)] + cotangent_views(cot, c2, c3, odd) + [nth(right, 1)]
    six = [move.fetch(ref, vs.at[n]) for n, ref in enumerate(sources)]
    before = [move.fetch(state.at[q], vstate.at[q]) for q in range(4)]
    tail_rows(weights, wk)
    for q in range(4):
        nxt[q] = descend(six, q, before[q], vw, wk)
        move.put(nxt.at[q], back.at[q])
        if q == 0:
            move.put(nxt.at[0], first)
    move.put(nxt.at[3], last)
    move.finish()


def temporal_grads(at, cot, c2, c3, acts2, back, acts1, blocks, *rest):
    vback, vacts, flip, vblocks, sems = rest
    odd = at[0]
    move = Mover(sems)
    views = cotangent_views(cot, c2, c3, odd)
    arrivals = []
    for layer, acts in ((0, acts1), (1, acts2)):
        ups = [back.at[q] for q in range(4)] if layer == 0 else views
        arrivals.append(
            (
                [move.fetch(ref, vback.at[layer, q]) for q, ref in enumerate(ups)],
                [move.fetch(acts.at[n], vacts.at[layer, n]) for n in range(6)],
            )
        )
    for layer, (ups, acts) in enumerate(arrivals):
        for q in range(4):
            flip[:, pl.ds(q * PX, PX)] = ups[q].get()[...].T
        for arrival in acts:
            arrival.get()
        tails = jnp.zeros((C, THREE_TAILS), F32)
        for q in range(4):
            ends = side(*[vacts[layer, q + tap(k, odd), :, pl.ds(HEAD, TAIL)] for k in range(3)])
            tails = tails + dot(flip[:, pl.ds(q * PX, PX)], ends)
        values = []
        for k in range(3):
            total = jnp.zeros((C, HEAD), F32)
            for q in range(4):
                heads = vacts[layer, q + tap(k, odd), :, pl.ds(0, HEAD)]
                total = total + dot(flip[:, pl.ds(q * PX, PX)], heads)
            values.append(side(total, tails[:, k * TAIL : (k + 1) * TAIL]).astype(BF))
        for b in range(CLIPS):
            vblocks[layer, b] = side(*[v[:, b * WIDTH : (b + 1) * WIDTH] for v in values])
            move.put(vblocks.at[layer, b], blocks.at[b, layer])
    move.finish()


def back_zero(at, left, back, right, pair, s1, s2, s3, w, flip, *rest):
    vs, vstate, vw, wk, vflip, sems = rest
    odd = at[0]
    move = Mover(sems)
    weights = taps_of(move, w, 0, odd, vw)
    sources = [left] + [back.at[q] for q in range(4)] + [right]
    six = [move.fetch(ref, vs.at[n]) for n, ref in enumerate(sources)]
    before = [move.fetch(ref, vstate.at[q]) for q, ref in enumerate((nth(pair, 0), s1, s2, s3))]
    tail_rows(weights, wk)
    for q in range(4):
        value = descend(six, q, before[q], vw, wk)
        turned = value.T
        wide = turned.astype(F32)
        column = lax.broadcasted_iota(jnp.int32, (1, PX), 1) % COLS
        ahead = jnp.where(column == COLS - 1, 0.0, pltpu.roll(wide, PX - 1, 1))
        behind = jnp.where(column == 0, 0.0, pltpu.roll(wide, 1, 1))
        vflip[q, pl.ds(0, C), :] = ahead.astype(BF)
        vflip[q, pl.ds(C, C), :] = turned
        vflip[q, pl.ds(2 * C, C), :] = behind.astype(BF)
        move.put(vflip.at[q], flip.at[q])
    move.finish()


def spatial_grads(at, flip, own_sides, sides2, sides3, temporal_blocks, kept, sent, *rest):
    vflip, vsides, blocks, sems = rest
    core = at[1]
    move = Mover(sems)
    sources = (own_sides.at[0], own_sides.at[1], sides2, sides3)
    arrivals = []
    for q in range(4):
        arrivals.append(move.fetch(flip.at[q], vflip.at[q]))
        arrivals.append(move.fetch(sources[q], vsides.at[q]))
    passing = [move.fetch(temporal_blocks.at[b], blocks.at[b, pl.ds(3, 2)]) for b in range(CLIPS)]
    for arrival in arrivals:
        arrival.get()
    for n in range(CLIPS):
        half = n % 2
        b = 2 * half + ((1 - core) if n < 2 else core)
        total = jnp.zeros((3 * C, 3 * WIDTH), F32)
        for q in range(4):
            total = total + dot(vflip[q], vsides[q, b])
        for j in range(3):
            blocks[b, j] = total[j * C : (j + 1) * C].astype(BF)
        if n == 0:
            for arrival in passing:
                arrival.get()
        move.put(blocks.at[b], (sent if n < 2 else kept).at[half])
    move.finish()


def pack(at, kept, got, out, *rest):
    vkept, vgot, wide, rows, vout, sems = rest
    halves, taps, channels, _ = kept.shape
    owners = out.shape[0] // halves
    count = channels // owners
    move = Mover(sems)
    arrivals = [
        (move.fetch(kept.at[h, t], vkept.at[h, t]), move.fetch(got.at[h, t], vgot.at[h, t]))
        for h in range(halves)
        for t in range(taps)
    ]
    for h in range(halves):
        for t in range(taps):
            mine, theirs = arrivals[h * taps + t]
            rows[...] = mine.get()[...].astype(F32) + theirs.get()[...].astype(F32)
            for owner in range(owners):
                wide[owner, pl.ds(count * t, count), :] = rows[pl.ds(count * owner, count), :]
        for owner in range(owners):
            vout[owners * h + owner] = wide[owner].astype(BF)
        move.put(vout.at[pl.ds(owners * h, owners)], out.at[pl.ds(owners * h, owners)])
    move.finish()


def place(at, own, got, out, *rest):
    vown, vgot, sems = rest
    odd = at[0]
    move = Mover(sems)
    here, there = pl.multiple_of(PX * odd, PX), pl.multiple_of(PX * (1 - odd), PX)
    frames = (odd, 1 - odd)
    arrivals = []
    for q in range(2):
        arrivals.append((move.fetch(own.at[q], vown.at[q]), out.at[frames[q], pl.ds(here, PX), :]))
        arrivals.append((move.fetch(nth(got, q), vgot.at[q]), out.at[frames[q], pl.ds(there, PX), :]))
    for arrival, target in arrivals:
        move.put(arrival.get(), target)
    move.finish()


def after(value, *others):
    return lax.optimization_barrier((value, *others))[0]


def step(clips_in, cotangent, spatial_weight, temporal_weight):
    owners, clips = lax.axis_size("frame"), lax.axis_size("clip")
    odd = lax.axis_index("frame") % 2
    core = lax.axis_index("clip") % 2
    at = jnp.stack([odd, core]).astype(jnp.int32)
    swap = [(n, n ^ 1) for n in range(owners)]
    outer = [(n, n - 2 if n % 2 == 0 else n + 2) for n in range(owners)]
    outer = [(a, b) for a, b in outer if 0 <= b < owners]
    inner = [(n, n + 2 if n % 2 == 0 else n - 2) for n in range(owners)]
    inner = [(a, b) for a, b in inner if 0 <= b < owners]
    cores = [(n, n ^ 1) for n in range(clips)]

    def send(value, perm, axis="frame"):
        shape = value.shape
        if axis == "frame":
            value = value.reshape(-1, COLS, C)
        return lax.ppermute(value, axis, perm).reshape(shape)

    x = clips_in.reshape(2, FULL, C)
    cot = cotangent.reshape(2, FULL, C)
    ws = spatial_weight.reshape(9, C, C)
    flops = 2 * PX * C * C

    flat, two, four, six = (2 * PX, C), (2, PX, C), (4, PX, C), (6, PX, C)
    packed = [(3, HEAD, THREE_TAILS), (3, THREE_TAILS, HEAD), (THREE_TAILS, THREE_TAILS)]
    whole = [(9, C, C), *packed]
    pad = (PX + 2 * COLS, C)
    kernels = [KERNELS, (THREE_TAILS, C)]

    tall_start = (TALL - 2 * COLS) * (1 - odd)
    x3 = send(lax.dynamic_slice(x, (odd, tall_start, 0), (1, TALL, C))[0], swap)
    pair, s1, own_sides, x2, c3, c2, *wp = run(
        conv_own,
        [flat, ONE, (2, *SIDES), TALL_ONE, ONE, ONE, *packed],
        (at, x, cot, ws),
        [*whole, (2, *pad), two, (2, *SIDES), TALL_ONE, (3, PX, C)],
        32,
        8 * flops,
    )
    wt = jnp.swapaxes(temporal_weight, 2, 3)
    right = send(pair, outer)
    x2 = send(x2, swap)

    other = [*whole, pad, ONE, SIDES]
    s3, sides3 = run(conv_other, [ONE, SIDES], (at, x3, ws, *wp), other, 8, 4 * flops)
    left = send(s3, inner)
    c3 = send(after(c3, x2), swap)
    s2, sides2 = run(conv_other, [ONE, SIDES], (at, x2, ws, *wp), other, 8, 4 * flops)
    c2 = send(after(c2, c3), swap)

    acts1, state1, last, first = run(
        layer_one,
        [six, four, flat, ONE],
        (at, left, pair, s1, s2, s3, right, c3, temporal_weight),
        [six, ONE, *kernels, six, four],
        32,
        8 * flops,
    )
    left1 = send(last, inner)
    right1 = send(first, outer)
    back1, first, last = run(
        back_one,
        [four, ONE, ONE],
        (at, left1, cot, c2, c3, right, state1, wt),
        [six, four, *kernels, four],
        32,
        8 * flops,
    )
    back_left = send(last, inner)
    back_right = send(first, outer)
    acts2, own, sent = run(
        layer_two,
        [six, two, flat],
        (at, left1, state1, right1, temporal_weight),
        [six, *kernels, six, four],
        32,
        8 * flops,
    )
    returned = send(sent, swap)

    (temporal_blocks,) = run(
        temporal_grads,
        [(CLIPS, 2, C, 3 * WIDTH)],
        (at, cot, c2, c3, acts2, back1, acts1),
        [(2, *four), (2, *six), (C, 4 * PX), (2, CLIPS, C, 3 * WIDTH)],
        32,
        16 * flops,
    )
    (flip,) = run(
        back_zero,
        [(4, 3 * C, PX)],
        (at, back_left, back1, back_right, pair, s1, s2, s3, wt),
        [six, four, *kernels, (4, 3 * C, PX)],
        32,
        8 * flops,
    )
    shares = (2, 5, C, 3 * WIDTH)
    kept, sent = run(
        spatial_grads,
        [shares] * 2,
        (at, flip, own_sides, sides2, sides3, temporal_blocks),
        [(4, 3 * C, PX), (4, *SIDES), (CLIPS, 5, C, 3 * WIDTH)],
        32,
        24 * flops,
    )
    got = send(sent, cores, "clip")

    rows = C // owners
    block = (2 * owners, 5 * rows, 3 * WIDTH)
    (packs,) = run(
        pack,
        [block],
        (at, kept, got),
        [
            shares,
            shares,
            pltpu.VMEM((owners, 5 * rows, 3 * WIDTH), F32),
            pltpu.VMEM((C, 3 * WIDTH), F32),
            block,
        ],
        32,
        1000,
    )
    groups = [[n + half * 2 + c for half in range(2) for n in range(0, owners * clips, clips)] for c in range(2)]
    parts = lax.all_to_all(
        packs, ("frame", "clip"), split_axis=0, concat_axis=0, axis_index_groups=groups, tiled=True
    )
    (out,) = run(place, [(2, FULL, C)], (at, own, returned), [two, two], 16, 1000)
    total = jnp.sum(parts.astype(F32), axis=0).reshape(5, rows, 3, WIDTH)
    grad_spatial = total[:3].transpose(1, 2, 0, 3)
    grad_temporal = total[3:].transpose(1, 0, 2, 3)
    return (out.reshape(clips_in.shape), grad_spatial, grad_temporal)


def solution(mesh):
    placed = (P("clip", "frame", None, None, None), P("clip", "frame", None, None, None), P(), P())
    return jax.shard_map(
        step,
        mesh=mesh,
        in_specs=placed,
        out_specs=(
            P("clip", "frame", None, None, None),
            P("frame", None, None, "clip"),
            P("frame", None, None, "clip"),
        ),
        check_vma=False,
    )
```

time: 196 us -> 190 us (0.969)
  local copies, waits for them, and re-layouts: 49.9 us -> 5.84 us
  Pallas kernels: 42.5 us -> 73.5 us
  waiting for transfers between devices: 46.8 us -> 67.5 us
  starting transfers between devices: 51.9 us -> 38.4 us
    ppermute x15 -> x12, waiting for transfers between devices: 34.3 us -> 67.5 us  [send(): return lax.ppermute(value, axis, perm).reshape(shape)]
    pallas_call x12 -> x11, Pallas kernels: 42.5 us -> 73.5 us  [run(): pl.pallas_call(kernel, out_shape=[jax.ShapeDtypeStruct(s, BF) for s in ou...]
    unnamed x111 -> x9, local copies, waits for them, and re-layouts: 32.3 us -> 4.62 us
    all_to_all x2 -> x1, waiting for transfers between devices: 12.5 us -> 0.01 us  [step(): lax.all_to_all(packs, ('frame', 'clip'), split_axis=0, concat_axis=0, axi...]
    ppermute x15 -> x12, starting transfers between devices: 30.9 us -> 22.6 us  [send(): return lax.ppermute(value, axis, perm).reshape(shape)]
    squeeze x4 -> x0, local copies, waits for them, and re-layouts: 7.82 us -> none  [cut(): return lax.dynamic_slice(a, (frame, start, 0), (1, size, C))[0]]
    pallas_call x4 -> x0, local copies, waits for them, and re-layouts: 5.82 us -> none  [run(): pl.pallas_call(kernel, out_shape=[jax.ShapeDtypeStruct(s, d) for s, d in...]
    all_to_all x2 -> x1, starting transfers between devices: 21 us -> 15.7 us  [step(): lax.all_to_all(packs, ('frame', 'clip'), split_axis=0, concat_axis=0, axi...]
  transfers between devices with their start and end apart: 17 -> 13, of which waited for: 3 -> 7; matrix products, arithmetic and copies ran while one was open for 10% -> 2% of each run, Pallas kernels for 22% -> 19%
where the time goes in v1:
time: 190 us; the launch traced here: 189 us
  Pallas kernels  73.5 us (39%)
  waiting for transfers between devices  67.5 us (36%)
  starting transfers between devices  38.4 us (20%)
  local copies, waits for them, and re-layouts  5.84 us (3%)
  other arithmetic  2.45 us (1%)
    pallas_call x11, Pallas kernels, run(): pl.pallas_call(kernel, out_shape=[jax.ShapeDtypeStruct(s, BF) for s in ou...  73.5 us
    ppermute x12, waiting for transfers between devices, send(): return lax.ppermute(value, axis, perm).reshape(shape)  67.5 us
    ppermute x12, starting transfers between devices, send(): return lax.ppermute(value, axis, perm).reshape(shape)  22.6 us
    all_to_all x1, starting transfers between devices, step(): lax.all_to_all(packs, ('frame', 'clip'), split_axis=0, concat_axis=0, axi...  15.7 us
    unnamed x9, local copies, waits for them, and re-layouts  4.62 us
  transfers between devices with their start and end apart: 13, of which 7 were waited for; matrix products, arithmetic and copies ran while one was open for 2% of the time, Pallas kernels for 19%

profile of v1, /device:TPU:8, one launch (start us, length us, event | category | flops | bytes accessed | tf_op | source)
XLA Modules:
  0.0 188.6 jit_solution(12589390647534107402)
XLA Ops:
  0.6 0.6 pad_add_fusion.at
  1.2 7.0 %shard_map.67 = (bf16[1024,320]{1,0:T(8,128)(2,1)}, bf16[512,320]{1,0:T(8,128)(2,1)}, bf16[2,4,512,240]{3,2,1,0:T(8,128)(2,1)}, bf16[544,320]{1,0:T(8,128)(2,1)}...) custom-call(s32[2]{0:T(128)} %pad_add_fusion.at, ...), custom_call_target="tpu_custom_call" | custom-call | flops 838860800 | bytes 9080840 | tf_op jit(solution)/shard_map/pallas_call | solution.py:83
  8.2 0.4 collective-permute-start.2
  8.6 1.0 constant_dynamic-slice_fusion
  9.7 1.8 collective-permute-start
  11.5 4.3 %collective-permute-start.3 = (bf16[32,32,320]{2,1,0:T(8,128)(2,1)}, bf16[32,32,320]{2,1,0:T(8,128)(2,1)}, u32[]{:S(2)}, u32[]{:S(2)}) collective-permute-start(bf16[32,32,320]{2,1,0:T(8,128)(2,1)} %bitcast.39), channel_id=1, source_target_pairs={{1,3},{2,0},{3,5},{4,2},{5,7},{6,4},{7,9},{8,6},{9,11},{10,8},{11,... | collective-permute-start | bytes 1966088 | tf_op jit(solution)/shard_map/ppermute | solution.py:436
  15.8 5.3 %collective-permute-done.2 = bf16[17,32,320]{2,1,0:T(8,128)(2,1)S(1)} collective-permute-done((bf16[17,32,320]{2,1,0:T(8,128)(2,1)}, bf16[17,32,320]{2,1,0:T(8,128)(2,1)S(1)}, u32[]{:S(2)}, u32[]{:S(2)}) %collective-permute-start.2) | collective-permute-done | bytes 348192 | tf_op jit(solution)/shard_map/ppermute | solution.py:436
  21.0 0.3 collective-permute-start.4
  21.4 8.6 %collective-permute-done = bf16[17,32,320]{2,1,0:T(8,128)(2,1)S(1)} collective-permute-done((bf16[17,32,320]{2,1,0:T(8,128)(2,1)S(1)}, bf16[17,32,320]{2,1,0:T(8,128)(2,1)S(1)}, u32[]{:S(2)}, u32[]{:S(2)}) %collective-permute-start) | collective-permute-done | bytes 348192 | tf_op jit(solution)/shard_map/ppermute | solution.py:436
  30.0 0.0 copy-done
  30.0 0.8 copy-done.1
  30.7 5.1 %shard_map.68 = (bf16[512,320]{1,0:T(8,128)(2,1)}, bf16[4,512,240]{2,1,0:T(8,128)(2,1)}) custom-call(s32[2]{0:T(128)} %pad_add_fusion.at, bf16[544,320]{1,0:T(8,128)(2,1)} %bitcast.46, bf16[9,320,320]{2,1,0:T(8,128)(2,1)} %bitcast.32, bf16[3,256,192]{2,1,0:T(8,128)(2,1)} %get-tuple-element.30.wn, bf16[3,192,256]{2,1,0:T(8,128)(2,1)} %get-tuple-element.31.wk, ...), custom_call_target="tpu_custom_call" | custom-call | flops 419430400 | bytes 4165640 | tf_op jit(solution)/shard_map/pallas_call | solution.py:83
  35.8 1.3 collective-permute-start.1
  37.1 5.1 %shard_map.69 = (bf16[512,320]{1,0:T(8,128)(2,1)}, bf16[4,512,240]{2,1,0:T(8,128)(2,1)}) custom-call(s32[2]{0:T(128)} %pad_add_fusion.at, bf16[544,320]{1,0:T(8,128)(2,1)} %bitcast.45, bf16[9,320,320]{2,1,0:T(8,128)(2,1)} %bitcast.33, bf16[3,256,192]{2,1,0:T(8,128)(2,1)} %get-tuple-element.30.wn, bf16[3,192,256]{2,1,0:T(8,128)(2,1)} %get-tuple-element.31.wk, ...), custom_call_target="tpu_custom_call" | custom-call | flops 419430400 | bytes 4165640 | tf_op jit(solution)/shard_map/pallas_call | solution.py:83
  42.2 0.0 collective-permute-done.3
  42.2 0.0 collective-permute-done.4
  42.2 4.7 %collective-permute-done.1 = bf16[16,32,320]{2,1,0:T(8,128)(2,1)} collective-permute-done((bf16[16,32,320]{2,1,0:T(8,128)(2,1)}, bf16[16,32,320]{2,1,0:T(8,128)(2,1)}, u32[]{:S(2)}, u32[]{:S(2)}) %collective-permute-start.1) | collective-permute-done | bytes 327712 | tf_op jit(solution)/shard_map/ppermute | solution.py:436
  46.9 6.6 %shard_map.70 = (bf16[6,512,320]{2,1,0:T(8,128)(2,1)}, bf16[4,512,320]{2,1,0:T(8,128)(2,1)}, bf16[1024,320]{1,0:T(8,128)(2,1)}, bf16[512,320]{1,0:T(8,128)(2,1)}) custom-call(s32[2]{0:T(128)} %pad_add_fusion.at, bf16[512,320]{1,0:T(8,128)(2,1)} %bitcast.8.left, bf16[1024,320]{1,0:T(8,128)(2,1)} %get-tuple-element.34.pair, ...), custom_call_target="tpu_custom_call" | custom-call | flops 838860800 | bytes 8437768 | tf_op jit(solution)/shard_map/pallas_call | solution.py:83
  53.5 1.3 collective-permute-start.5
  54.8 3.6 %collective-permute-start.8 = (bf16[16,32,320]{2,1,0:T(8,128)(2,1)}, bf16[16,32,320]{2,1,0:T(8,128)(2,1)}, u32[]{:S(2)}, u32[]{:S(2)}) collective-permute-start(bf16[16,32,320]{2,1,0:T(8,128)(2,1)} %bitcast.52), channel_id=1, source_target_pairs={{0,1},{1,0},{2,3},{3,2},{4,5},{5,4},{6,7},{7,6},{8,9},{9,8},{10,11... | collective-permute-start | bytes 983048 | tf_op jit(solution)/shard_map/ppermute | solution.py:436
  58.4 3.3 %collective-permute-start.6 = (bf16[16,32,320]{2,1,0:T(8,128)(2,1)}, bf16[16,32,320]{2,1,0:T(8,128)(2,1)}, u32[]{:S(2)}, u32[]{:S(2)}) collective-permute-start(bf16[16,32,320]{2,1,0:T(8,128)(2,1)} %bitcast.54), channel_id=1, source_target_pairs={{1,3},{2,0},{3,5},{4,2},{5,7},{6,4},{7,9},{8,6},{9,11},{10,8},{11,... | collective-permute-start | bytes 983048 | tf_op jit(solution)/shard_map/ppermute | solution.py:436
  61.7 2.6 %copy.8 = bf16[2,3,320,320]{2,3,1,0:T(8,128)(2,1)} copy(bf16[2,3,320,320]{3,2,1,0:T(8,128)(2,1)} %w.3) | data formatting | bytes 2457600 | tf_op args[3]
  64.3 0.5 collective-permute-done.8
  64.8 7.4 %collective-permute-done.5 = bf16[32,32,320]{2,1,0:T(8,128)(2,1)} collective-permute-done((bf16[32,32,320]{2,1,0:T(8,128)(2,1)}, bf16[32,32,320]{2,1,0:T(8,128)(2,1)}, u32[]{:S(2)}, u32[]{:S(2)}) %collective-permute-start.5) | collective-permute-done | bytes 655392 | tf_op jit(solution)/shard_map/ppermute | solution.py:436
  72.1 7.7 %shard_map.73 = (bf16[4,512,320]{2,1,0:T(8,128)(2,1)}, bf16[512,320]{1,0:T(8,128)(2,1)}, bf16[512,320]{1,0:T(8,128)(2,1)}) custom-call(s32[2]{0:T(128)} %pad_add_fusion.at, bf16[1024,320]{1,0:T(8,128)(2,1)} %bitcast.16.left, bf16[2,1024,320]{2,1,0:T(8,128)(2,1)} %bitcast.35, bf16[512,320]{1,0:T(8,128)(2,1)} %bitcast.23.c2, bf16[512,320]{1,0:T(8,128)(2,1)} %bitcast.14.c3, ...), custom_call_target="tpu_custom_call" | custom-call | flops 838860800 | bytes 7782408 | tf_op jit(solution)/shard_map/pallas_call | solution.py:83
  79.9 4.4 %collective-permute-start.10 = (bf16[16,32,320]{2,1,0:T(8,128)(2,1)}, bf16[16,32,320]{2,1,0:T(8,128)(2,1)}, u32[]{:S(2)}, u32[]{:S(2)}) collective-permute-start(bf16[16,32,320]{2,1,0:T(8,128)(2,1)} %bitcast.56), channel_id=1, source_target_pairs={{1,3},{2,0},{3,5},{4,2},{5,7},{6,4},{7,9},{8,6},{9,11},{10,8},{11,... | collective-permute-start | bytes 983048 | tf_op jit(solution)/shard_map/ppermute | solution.py:436
  84.2 1.3 collective-permute-start.9
  85.5 0.0 collective-permute-done.6
  85.5 6.4 %shard_map.71 = (bf16[6,512,320]{2,1,0:T(8,128)(2,1)}, bf16[2,512,320]{2,1,0:T(8,128)(2,1)}, bf16[1024,320]{1,0:T(8,128)(2,1)}) custom-call(s32[2]{0:T(128)} %pad_add_fusion.at, bf16[1024,320]{1,0:T(8,128)(2,1)} %bitcast.16.left, bf16[4,512,320]{2,1,0:T(8,128)(2,1)} %get-tuple-element.41.state, bf16[512,320]{1,0:T(8,128)(2,1)} %bitcast.18.right, ...), custom_call_target="tpu_custom_call" | custom-call | flops 838860800 | bytes 6799368 | tf_op jit(solution)/shard_map/pallas_call | solution.py:83
  91.9 7.9 %shard_map.75.temporal_blocks = bf16[4,2,320,240]{3,2,1,0:T(8,128)(2,1)} custom-call(s32[2]{0:T(128)} %pad_add_fusion.at, bf16[2,1024,320]{2,1,0:T(8,128)(2,1)} %bitcast.36, bf16[512,320]{1,0:T(8,128)(2,1)} %bitcast.23.c2, bf16[512,320]{1,0:T(8,128)(2,1)} %bitcast.14.c3, bf16[6,512,320]{2,1,0:T(8,128)(2,1)} %get-tuple-element.53.acts2, ...), custom_call_target="tpu_custom_call" | custom-call | flops 1677721600 | bytes 8437768 | tf_op jit(solution)/shard_map/pallas_call | solution.py:83
  99.7 0.0 collective-permute-done.10
  99.8 0.0 collective-permute-done.9
  99.8 9.0 %shard_map.74.flip = bf16[4,960,512]{2,1,0:T(8,128)(2,1)} custom-call(s32[2]{0:T(128)} %pad_add_fusion.at, bf16[512,320]{1,0:T(8,128)(2,1)} %bitcast.26.left, bf16[4,512,320]{2,1,0:T(8,128)(2,1)} %get-tuple-element.48.back, bf16[512,320]{1,0:T(8,128)(2,1)} %bitcast.28.right, bf16[1024,320]{1,0:T(8,128)(2,1)} %get-tuple-element.34.pair, ...), custom_call_target="tpu_custom_call" | custom-call | flops 838860800 | bytes 8765448 | tf_op jit(solution)/shard_map/pallas_call | solution.py:83
  108.7 11.8 %shard_map.76 = (bf16[2,5,320,240]{3,2,1,0:T(8,128)(2,1)}, bf16[2,5,320,240]{3,2,1,0:T(8,128)(2,1)}) custom-call(s32[2]{0:T(128)} %pad_add_fusion.at, bf16[4,960,512]{2,1,0:T(8,128)(2,1)} %shard_map.74.flip, bf16[2,4,512,240]{3,2,1,0:T(8,128)(2,1)} %get-tuple-element.50.own_sides, bf16[4,512,240]{2,1,0:T(8,128)(2,1)} %get-tuple-element.51.sides2, ...), custom_call_target="tpu_custom_call" | custom-call | flops 2516582400 | bytes 12165128 | tf_op jit(solution)/shard_map/pallas_call | solution.py:83
  120.6 0.1 collective-permute-start.11
  120.7 3.8 %collective-permute-done.11.got = bf16[2,5,320,240]{3,2,1,0:T(8,128)(2,1)} collective-permute-done((bf16[2,5,320,240]{3,2,1,0:T(8,128)(2,1)}, bf16[2,5,320,240]{3,2,1,0:T(8,128)(2,1)}, u32[]{:S(2)}, u32[]{:S(2)}) %collective-permute-start.11) | collective-permute-done | bytes 1536032 | tf_op jit(solution)/shard_map/ppermute | solution.py:436
  124.5 4.2 %shard_map.77 = bf16[64,50,240]{2,1,0:T(8,128)(2,1)} custom-call(s32[2]{0:T(128)} %pad_add_fusion.at, bf16[2,5,320,240]{3,2,1,0:T(8,128)(2,1)} %get-tuple-element.55.kept, bf16[2,5,320,240]{3,2,1,0:T(8,128)(2,1)} %collective-permute-done.11.got), custom_call_target="tpu_custom_call" | custom-call | flops 1000 | bytes 4608008 | tf_op jit(solution)/shard_map/pallas_call | solution.py:83
  128.7 15.7 %all-to-all-start = ((bf16[64,50,240]{2,1,0:T(8,128)(2,1)}), bf16[64,50,240]{2,1,0:T(8,128)(2,1)}, u32[]{:S(2)}, u32[]{:S(2)}) async-start(bf16[64,50,240]{2,1,0:T(8,128)(2,1)} %shard_map.77), calls=%async_computation | async-start | bytes 3670016 | tf_op jit(solution)/shard_map/all_to_all | solution.py:544
  144.4 0.0 copy-done.2
  144.4 0.6 collective-permute-start.7
  145.0 37.2 %collective-permute-done.7 = bf16[32,32,320]{2,1,0:T(8,128)(2,1)} collective-permute-done((bf16[32,32,320]{2,1,0:T(8,128)(2,1)S(1)}, bf16[32,32,320]{2,1,0:T(8,128)(2,1)}, u32[]{:S(2)}, u32[]{:S(2)}) %collective-permute-start.7) | collective-permute-done | bytes 655392 | tf_op jit(solution)/shard_map/ppermute | solution.py:436
  182.3 2.9 %shard_map.72 = bf16[2,1024,320]{2,1,0:T(8,128)(2,1)} custom-call(s32[2]{0:T(128)} %pad_add_fusion.at, bf16[2,512,320]{2,1,0:T(8,128)(2,1)} %get-tuple-element.43.own, bf16[1024,320]{1,0:T(8,128)(2,1)} %bitcast.20.got), custom_call_target="tpu_custom_call" | custom-call | flops 1000 | bytes 2621448 | tf_op jit(solution)/shard_map/pallas_call | solution.py:83
  185.2 0.0 all-to-all-done
  185.2 1.8 convert_reduce_fusion
  187.1 0.1 slice.15
  187.2 0.6 copy.10
  187.8 0.1 slice.13
  187.9 0.6 copy.9
  (5 shorter events, 0.0 us)
Async XLA Ops:
  8.2 12.8 %collective-permute-start.2 = (bf16[17,32,320]{2,1,0:T(8,128)(2,1)}, bf16[17,32,320]{2,1,0:T(8,128)(2,1)S(1)}, u32[]{:S(2)}, u32[]{:S(2)}) collective-permute-start(bf16[17,32,320]{2,1,0:T(8,128)(2,1)} %bitcast.51), channel_id=1, source_target_pairs={{0,1},{1,0},{2,3},{3,2},{4,5},{5,4},{6,7},{7,6},{8,9},{9,8},{10,11... | collective-permute-start | bytes 1044488 | tf_op jit(solution)/shard_map/ppermute | solution.py:436
  9.7 20.3 %collective-permute-start = (bf16[17,32,320]{2,1,0:T(8,128)(2,1)S(1)}, bf16[17,32,320]{2,1,0:T(8,128)(2,1)S(1)}, u32[]{:S(2)}, u32[]{:S(2)}) collective-permute-start(bf16[17,32,320]{2,1,0:T(8,128)(2,1)S(1)} %bitcast.44), channel_id=1, source_target_pairs={{0,1},{1,0},{2,3},{3,2},{4,5},{5,4},{6,7},{7,6},{8,9},{9,8},{10,11... | collective-permute-start | bytes 1044488 | tf_op jit(solution)/shard_map/ppermute | solution.py:436
  11.5 30.7 %collective-permute-start.3 = (bf16[32,32,320]{2,1,0:T(8,128)(2,1)}, bf16[32,32,320]{2,1,0:T(8,128)(2,1)}, u32[]{:S(2)}, u32[]{:S(2)}) collective-permute-start(bf16[32,32,320]{2,1,0:T(8,128)(2,1)} %bitcast.39), channel_id=1, source_target_pairs={{1,3},{2,0},{3,5},{4,2},{5,7},{6,4},{7,9},{8,6},{9,11},{10,8},{11,... | collective-permute-start | bytes 1966088 | tf_op jit(solution)/shard_map/ppermute | solution.py:436
  21.0 9.0 %copy-start = (bf16[17,32,320]{2,1,0:T(8,128)(2,1)}, bf16[17,32,320]{2,1,0:T(8,128)(2,1)S(1)}, u32[]{:S(2)}) copy-start(bf16[17,32,320]{2,1,0:T(8,128)(2,1)S(1)} %collective-permute-done.2) | copy-start | bytes 1044484
  21.0 21.2 %collective-permute-start.4 = (bf16[16,32,320]{2,1,0:T(8,128)(2,1)}, bf16[16,32,320]{2,1,0:T(8,128)(2,1)}, u32[]{:S(2)}, u32[]{:S(2)}) collective-permute-start(bf16[16,32,320]{2,1,0:T(8,128)(2,1)} %bitcast.53), channel_id=1, source_target_pairs={{0,1},{1,0},{2,3},{3,2},{4,5},{5,4},{6,7},{7,6},{8,9},{9,8},{10,11... | collective-permute-start | bytes 983048 | tf_op jit(solution)/shard_map/ppermute | solution.py:436
  30.0 0.8 copy-start.1
  35.8 11.1 %collective-permute-start.1 = (bf16[16,32,320]{2,1,0:T(8,128)(2,1)}, bf16[16,32,320]{2,1,0:T(8,128)(2,1)}, u32[]{:S(2)}, u32[]{:S(2)}) collective-permute-start(bf16[16,32,320]{2,1,0:T(8,128)(2,1)} %bitcast.42), channel_id=1, source_target_pairs={{0,2},{2,4},{3,1},{4,6},{5,3},{6,8},{7,5},{8,10},{9,7},{10,12},{11... | collective-permute-start | bytes 983048 | tf_op jit(solution)/shard_map/ppermute | solution.py:436
  53.5 18.7 %collective-permute-start.5 = (bf16[32,32,320]{2,1,0:T(8,128)(2,1)}, bf16[32,32,320]{2,1,0:T(8,128)(2,1)}, u32[]{:S(2)}, u32[]{:S(2)}) collective-permute-start(bf16[32,32,320]{2,1,0:T(8,128)(2,1)} %bitcast.50), channel_id=1, source_target_pairs={{0,2},{2,4},{3,1},{4,6},{5,3},{6,8},{7,5},{8,10},{9,7},{10,12},{11... | collective-permute-start | bytes 1966088 | tf_op jit(solution)/shard_map/ppermute | solution.py:436
  54.8 10.0 %collective-permute-start.8 = (bf16[16,32,320]{2,1,0:T(8,128)(2,1)}, bf16[16,32,320]{2,1,0:T(8,128)(2,1)}, u32[]{:S(2)}, u32[]{:S(2)}) collective-permute-start(bf16[16,32,320]{2,1,0:T(8,128)(2,1)} %bitcast.52), channel_id=1, source_target_pairs={{0,1},{1,0},{2,3},{3,2},{4,5},{5,4},{6,7},{7,6},{8,9},{9,8},{10,11... | collective-permute-start | bytes 983048 | tf_op jit(solution)/shard_map/ppermute | solution.py:436
  58.4 27.2 %collective-permute-start.6 = (bf16[16,32,320]{2,1,0:T(8,128)(2,1)}, bf16[16,32,320]{2,1,0:T(8,128)(2,1)}, u32[]{:S(2)}, u32[]{:S(2)}) collective-permute-start(bf16[16,32,320]{2,1,0:T(8,128)(2,1)} %bitcast.54), channel_id=1, source_target_pairs={{1,3},{2,0},{3,5},{4,2},{5,7},{6,4},{7,9},{8,6},{9,11},{10,8},{11,... | collective-permute-start | bytes 983048 | tf_op jit(solution)/shard_map/ppermute | solution.py:436
  79.9 19.9 %collective-permute-start.10 = (bf16[16,32,320]{2,1,0:T(8,128)(2,1)}, bf16[16,32,320]{2,1,0:T(8,128)(2,1)}, u32[]{:S(2)}, u32[]{:S(2)}) collective-permute-start(bf16[16,32,320]{2,1,0:T(8,128)(2,1)} %bitcast.56), channel_id=1, source_target_pairs={{1,3},{2,0},{3,5},{4,2},{5,7},{6,4},{7,9},{8,6},{9,11},{10,8},{11,... | collective-permute-start | bytes 983048 | tf_op jit(solution)/shard_map/ppermute | solution.py:436
  84.2 15.5 %collective-permute-start.9 = (bf16[16,32,320]{2,1,0:T(8,128)(2,1)}, bf16[16,32,320]{2,1,0:T(8,128)(2,1)}, u32[]{:S(2)}, u32[]{:S(2)}) collective-permute-start(bf16[16,32,320]{2,1,0:T(8,128)(2,1)} %bitcast.55), channel_id=1, source_target_pairs={{0,2},{2,4},{3,1},{4,6},{5,3},{6,8},{7,5},{8,10},{9,7},{10,12},{11... | collective-permute-start | bytes 983048 | tf_op jit(solution)/shard_map/ppermute | solution.py:436
  120.6 3.9 %collective-permute-start.11 = (bf16[2,5,320,240]{3,2,1,0:T(8,128)(2,1)}, bf16[2,5,320,240]{3,2,1,0:T(8,128)(2,1)}, u32[]{:S(2)}, u32[]{:S(2)}) collective-permute-start(bf16[2,5,320,240]{3,2,1,0:T(8,128)(2,1)} %get-tuple-element.56), channel_id=1, source_target_pairs={{0,32},{32,0},{64,96},{96,64},{1,33},{33,1},{65,97},{97,65},{2,34}... | collective-permute-start | bytes 4608008 | tf_op jit(solution)/shard_map/ppermute | solution.py:436
  128.7 15.8 %copy-start.2 = (bf16[1024,320]{1,0:T(8,128)(2,1)S(1)}, bf16[1024,320]{1,0:T(8,128)(2,1)}, u32[]{:S(2)}) copy-start(bf16[1024,320]{1,0:T(8,128)(2,1)} %get-tuple-element.44) | copy-start | bytes 1966084
  128.7 56.5 %all-to-all-start = ((bf16[64,50,240]{2,1,0:T(8,128)(2,1)}), bf16[64,50,240]{2,1,0:T(8,128)(2,1)}, u32[]{:S(2)}, u32[]{:S(2)}) async-start(bf16[64,50,240]{2,1,0:T(8,128)(2,1)} %shard_map.77), calls=%async_computation | async-start | bytes 3670016 | tf_op jit(solution)/shard_map/all_to_all | solution.py:544
  144.4 37.8 %collective-permute-start.7 = (bf16[32,32,320]{2,1,0:T(8,128)(2,1)S(1)}, bf16[32,32,320]{2,1,0:T(8,128)(2,1)}, u32[]{:S(2)}, u32[]{:S(2)}) collective-permute-start(bf16[32,32,320]{2,1,0:T(8,128)(2,1)S(1)} %bitcast.49), channel_id=1, source_target_pairs={{0,1},{1,0},{2,3},{3,2},{4,5},{5,4},{6,7},{7,6},{8,9},{9,8},{10,11... | collective-permute-start | bytes 1966088 | tf_op jit(solution)/shard_map/ppermute | solution.py:436

commit v2 on v1

v2 whole, which is shorter than its diff:
```python
import functools

import jax
import jax.numpy as jnp
from jax import lax
from jax.experimental import pallas as pl
from jax.experimental.pallas import tpu as pltpu
from jax.sharding import PartitionSpec as P


BF = jnp.bfloat16
F32 = jnp.float32
C = 320
COLS = 32
ROWS = 16
PX = ROWS * COLS
TALL = PX + COLS
FULL = 2 * PX
HEAD = 256
TAIL = C - HEAD
CLIPS = 4
VMEM_BYTES = 24 * 1024 * 1024
WIDTH = C // CLIPS
HBM = pl.BlockSpec(memory_space=pltpu.HBM)
VM = pl.BlockSpec(memory_space=pltpu.VMEM)
SM = pl.BlockSpec(memory_space=pltpu.SMEM)


ONE = (PX, C)
TALL_ONE = (TALL, C)
THREE_TAILS = 3 * TAIL
SIDES = (CLIPS, PX, 3 * WIDTH)
KERNELS = (3, C, C)


def dot(a, b):
    return jnp.dot(a, b, preferred_element_type=F32)


def side(*parts):
    return jnp.concatenate(parts, axis=1)


class Mover:
    def __init__(self, sems):
        self.sems, self.count, self.leaving = sems, 0, []

    def copy(self, src, dst):
        c = pltpu.make_async_copy(src, dst, self.sems.at[self.count])
        self.count += 1
        c.start()
        return c

    def fetch(self, src, dst):
        return Arrival(self.copy(src, dst), dst)

    def put(self, src, dst):
        self.leaving.append(self.copy(src, dst))

    def finish(self):
        for c in self.leaving:
            c.wait()


class Arrival:
    def __init__(self, copy, ref):
        self.copy, self.ref = copy, ref

    def get(self):
        if self.copy is not None:
            self.copy.wait()
            self.copy = None
        return self.ref


def nth(ref, n):
    return ref.at[pl.ds(n * PX, PX), :]


def run(kernel, outs, args, scratch=(), copies=0, flops=0, far=(), far_outs=False, limit=VMEM_BYTES):
    nbytes = sum(a.size * a.dtype.itemsize for a in args) + sum(
        functools.reduce(lambda m, n: m * n, s, 2) for s in outs
    )
    return pl.pallas_call(
        kernel,
        out_shape=[jax.ShapeDtypeStruct(s, BF) for s in outs],
        in_specs=[SM] + [HBM if n in far else VM for n in range(1, len(args))],
        out_specs=[HBM if far_outs else VM] * len(outs),
        scratch_shapes=[s if not isinstance(s, tuple) else pltpu.VMEM(s, BF) for s in scratch]
        + ([pltpu.SemaphoreType.DMA((copies,))] if copies else []),
        cost_estimate=pl.CostEstimate(flops=flops, bytes_accessed=nbytes, transcendentals=0),
        compiler_params=pltpu.CompilerParams(vmem_limit_bytes=limit),
    )(*args)


def column_of(rows):
    return lax.broadcasted_iota(jnp.int32, (rows, 1), 0) % COLS


def right_by_one(v):
    return jnp.where(column_of(v.shape[0]) == 0, 0.0, pltpu.roll(v, 1, 0))


def left_by_one(v):
    return jnp.where(column_of(v.shape[0]) == COLS - 1, 0.0, pltpu.roll(v, v.shape[0] - 1, 0))


def sigmoid(v):
    return 1.0 / (1.0 + jnp.exp(-v))


def padded(pad, odd):
    pad[pl.ds(0, COLS), :] = jnp.zeros((COLS, C), BF)
    pad[pl.ds(TALL, COLS), :] = jnp.zeros((COLS, C), BF)
    return pad.at[pl.ds(pl.multiple_of(COLS * (1 - odd), COLS), TALL), :]


def convolve(pad, w, wn, wk, wr, out, sides):
    tails = side(*[pad[pl.ds(COLS * i, PX), pl.ds(HEAD, TAIL)] for i in range(3)])

    def heads(i):
        return pad[pl.ds(COLS * i, PX), pl.ds(0, HEAD)]

    parts = []
    for j in range(3):
        acc = dot(heads(0), w[j, pl.ds(0, HEAD), pl.ds(0, HEAD)])
        acc = acc + dot(heads(1), w[3 + j, pl.ds(0, HEAD), pl.ds(0, HEAD)])
        acc = acc + dot(heads(2), w[6 + j, pl.ds(0, HEAD), pl.ds(0, HEAD)])
        parts.append(acc + dot(tails, wk[j]))
    centre = pad[pl.ds(COLS, PX), pl.ds(0, HEAD)].astype(F32)
    total = right_by_one(parts[0]) + parts[1] + left_by_one(parts[2])
    out[:, pl.ds(0, HEAD)] = (centre + total).astype(BF)
    acc = dot(heads(0), wn[0]) + dot(heads(1), wn[1]) + dot(heads(2), wn[2])
    acc = acc + dot(tails, wr[...])
    total = right_by_one(acc[:, :TAIL]) + acc[:, TAIL : 2 * TAIL] + left_by_one(acc[:, 2 * TAIL :])
    centre = pad[pl.ds(COLS, PX), pl.ds(HEAD, TAIL)].astype(F32)
    out[:, pl.ds(HEAD, TAIL)] = (centre + total).astype(BF)
    for b in range(CLIPS):
        columns = slice(b * WIDTH, (b + 1) * WIDTH)
        sides[b] = side(*[pad[pl.ds(COLS * i, PX), columns] for i in range(3)])


def conv_own(at, x, cot, w, tw, out0, out1, sides, x2, c3, c2, cot0, cot1, vw, wn, wk, wr, vt, vtk, vb, vbk, pads, sems):
    odd = at[0]
    move = Mover(sems)
    start = pl.multiple_of((TALL - 2 * COLS) * odd, COLS)
    frames = [odd, 1 - odd]
    rows = [
        move.fetch(x.at[frames[q], pl.ds(start, TALL), :], padded(pads.at[q], odd)) for q in range(2)
    ]
    weights = [move.fetch(w.at[n], vw.at[n]) for n in range(9)]
    away = pl.multiple_of((TALL - 2 * COLS) * (1 - odd), COLS)
    here, there = pl.multiple_of(PX * odd, PX), pl.multiple_of(PX * (1 - odd), PX)
    later = [
        move.fetch(x.at[1 - odd, pl.ds(away, TALL), :], x2),
        move.fetch(cot.at[odd, pl.ds(here, PX), :], cot0),
        move.fetch(cot.at[1 - odd, pl.ds(here, PX), :], cot1),
        move.fetch(cot.at[odd, pl.ds(there, PX), :], c3),
        move.fetch(cot.at[1 - odd, pl.ds(there, PX), :], c2),
    ]
    taps = [(l, k, move.fetch(tw.at[l, tap(k, odd)], vt.at[l, k])) for l in range(2) for k in range(3)]
    for arrival in weights:
        arrival.get()
    for i in range(3):
        wn[i] = side(*[vw[3 * i + j, pl.ds(0, HEAD), pl.ds(HEAD, TAIL)] for j in range(3)])
        for j in range(3):
            wk[j, pl.ds(TAIL * i, TAIL), :] = vw[3 * i + j, pl.ds(HEAD, TAIL), pl.ds(0, HEAD)]
        wr[pl.ds(TAIL * i, TAIL), :] = side(
            *[vw[3 * i + j, pl.ds(HEAD, TAIL), pl.ds(HEAD, TAIL)] for j in range(3)]
        )
    for arrival in rows:
        arrival.get()
    for l, k, arrival in taps:
        arrival.get()
        turned = vt[l, k].T
        vb[l, k] = turned
        vtk[l, pl.ds(TAIL * k, TAIL), :] = vt[l, k, pl.ds(HEAD, TAIL), :]
        vbk[l, pl.ds(TAIL * k, TAIL), :] = turned[HEAD:, :]
    for q, out in enumerate((out0, out1)):
        convolve(pads.at[q], vw, wn, wk, wr, out, sides.at[q])
    for arrival in later:
        arrival.get()


def conv_other(at, x, w, wn, wk, wr, out, sides, pad):
    padded(pad, at[0])[...] = x[...]
    convolve(pad, w, wn, wk, wr, out, sides)


def tap(k, odd):
    return k + odd * (2 - 2 * k)


def three_taps(three, vw, layer, wk):
    tails = side(*[ref[:, pl.ds(HEAD, TAIL)] for ref in three])
    totals = []
    for columns in (pl.ds(0, HEAD), pl.ds(HEAD, TAIL)):
        total = dot(three[0][:, pl.ds(0, HEAD)], vw[layer, 0, pl.ds(0, HEAD), columns])
        total = total + dot(three[1][:, pl.ds(0, HEAD)], vw[layer, 1, pl.ds(0, HEAD), columns])
        total = total + dot(three[2][:, pl.ds(0, HEAD)], vw[layer, 2, pl.ds(0, HEAD), columns])
        totals.append(total + dot(tails, wk[layer, :, columns]))
    return side(*totals)


def temporal(states, vw, layer, wk, acts):
    done = 0
    for q in range(4):
        while done < q + 3:
            v = states[done][...].astype(F32)
            acts[done] = (v * sigmoid(v)).astype(BF)
            done += 1
        term = three_taps([acts.at[q + k] for k in range(3)], vw, layer, wk)
        yield (states[q + 1][...].astype(F32) + term).astype(BF)


def layer_one(at, left, s0, s1, s2, s3, right, vw, wk, acts, state, last, first):
    states = (left, s0, s1, s2, s3, right)
    for q, value in enumerate(temporal(states, vw, 0, wk, acts)):
        state[q] = value
        if q == 0:
            first[...] = value
        if q == 3:
            last[...] = value


def layer_two(at, left, state, right, vw, wk, acts, own, sent):
    states = (left, state.at[0], state.at[1], state.at[2], state.at[3], right)
    for q, value in enumerate(temporal(states, vw, 1, wk, acts)):
        if q < 2:
            own[q] = value
        else:
            sent[pl.ds((3 - q) * PX, PX), :] = value


def descend(six, q, before, vw, layer, wk):
    three = [six[q + 2 - k] for k in range(3)]
    carried = three_taps(three, vw, layer, wk)
    v = before[...].astype(F32)
    s = sigmoid(v)
    return (three[1][...].astype(F32) + carried * (s * (1.0 + v * (1.0 - s)))).astype(BF)


def back_one(at, left, cot0, cot1, c2, c3, right, state, vw, wk, back, first, last):
    six = (left, cot0, cot1, c2, c3, right)
    for q in range(4):
        value = descend(six, q, state.at[q], vw, 1, wk)
        back[q] = value
        if q == 0:
            first[...] = value
        if q == 3:
            last[...] = value


def temporal_grads(at, cot0, cot1, c2, c3, acts2, back, acts1, blocks, flip):
    odd = at[0]
    views = (cot0, cot1, c2, c3)
    for layer, acts in ((0, acts1), (1, acts2)):
        for q in range(4):
            up = back.at[q] if layer == 0 else views[q]
            flip[:, pl.ds(q * PX, PX)] = up[...].T
        tails = jnp.zeros((C, THREE_TAILS), F32)
        for q in range(4):
            ends = side(*[acts[q + tap(k, odd), :, pl.ds(HEAD, TAIL)] for k in range(3)])
            tails = tails + dot(flip[:, pl.ds(q * PX, PX)], ends)
        values = []
        for k in range(3):
            total = jnp.zeros((C, HEAD), F32)
            for q in range(4):
                heads = acts[q + tap(k, odd), :, pl.ds(0, HEAD)]
                total = total + dot(flip[:, pl.ds(q * PX, PX)], heads)
            values.append(side(total, tails[:, k * TAIL : (k + 1) * TAIL]).astype(BF))
        for b in range(CLIPS):
            blocks[b, layer] = side(*[v[:, b * WIDTH : (b + 1) * WIDTH] for v in values])


def back_zero(at, left, back, right, s0, s1, s2, s3, vw, wk, own_sides, sides2, sides3, passing, kept, sent, flip):
    core = at[1]
    six = [left] + [back.at[q] for q in range(4)] + [right]
    column = lax.broadcasted_iota(jnp.int32, (1, PX), 1) % COLS
    for q, before in enumerate((s0, s1, s2, s3)):
        turned = descend(six, q, before, vw, 0, wk).T
        wide = turned.astype(F32)
        ahead = jnp.where(column == COLS - 1, 0.0, pltpu.roll(wide, PX - 1, 1))
        behind = jnp.where(column == 0, 0.0, pltpu.roll(wide, 1, 1))
        flip[q, pl.ds(0, C), :] = ahead.astype(BF)
        flip[q, pl.ds(C, C), :] = turned
        flip[q, pl.ds(2 * C, C), :] = behind.astype(BF)
    sides = (own_sides.at[0], own_sides.at[1], sides2, sides3)
    for half in range(2):
        for out, b in ((kept, 2 * half + core), (sent, 2 * half + 1 - core)):
            total = jnp.zeros((3 * C, 3 * WIDTH), F32)
            for q in range(4):
                total = total + dot(flip[q], sides[q][b])
            for j in range(3):
                out[half, j] = total[j * C : (j + 1) * C].astype(BF)
            for layer in range(2):
                out[half, 3 + layer] = passing[b, layer]


def pack(at, kept, got, out, wide, rows, vout, sems):
    halves, taps, channels, _ = kept.shape
    owners = out.shape[0] // halves
    count = channels // owners
    move = Mover(sems)
    for h in range(halves):
        for t in range(taps):
            rows[...] = kept[h, t].astype(F32) + got[h, t].astype(F32)
            for owner in range(owners):
                wide[owner, pl.ds(count * t, count), :] = rows[pl.ds(count * owner, count), :]
        for owner in range(owners):
            vout[owners * h + owner] = wide[owner].astype(BF)
        move.put(vout.at[pl.ds(owners * h, owners)], out.at[pl.ds(owners * h, owners)])
    move.finish()


def place(at, own, got, out, sems):
    odd = at[0]
    move = Mover(sems)
    here, there = pl.multiple_of(PX * odd, PX), pl.multiple_of(PX * (1 - odd), PX)
    for q, frame in enumerate((odd, 1 - odd)):
        move.put(own.at[q], out.at[frame, pl.ds(here, PX), :])
        move.put(nth(got, q), out.at[frame, pl.ds(there, PX), :])
    move.finish()


def after(value, *others):
    return lax.optimization_barrier((value, *others))[0]


def step(clips_in, cotangent, spatial_weight, temporal_weight):
    owners, clips = lax.axis_size("frame"), lax.axis_size("clip")
    odd = lax.axis_index("frame") % 2
    core = lax.axis_index("clip") % 2
    at = jnp.stack([odd, core]).astype(jnp.int32)
    swap = [(n, n ^ 1) for n in range(owners)]
    outer = [(n, n - 2 if n % 2 == 0 else n + 2) for n in range(owners)]
    outer = [(a, b) for a, b in outer if 0 <= b < owners]
    inner = [(n, n + 2 if n % 2 == 0 else n - 2) for n in range(owners)]
    inner = [(a, b) for a, b in inner if 0 <= b < owners]
    cores = [(n, n ^ 1) for n in range(clips)]

    def send(value, perm, axis="frame"):
        shape = value.shape
        if axis == "frame":
            value = value.reshape(-1, COLS, C)
        return lax.ppermute(value, axis, perm).reshape(shape)

    x = clips_in.reshape(2, FULL, C)
    cot = cotangent.reshape(2, FULL, C)
    ws = spatial_weight.reshape(9, C, C)
    flops = 2 * PX * C * C

    flat, two, four, six = (2 * PX, C), (2, PX, C), (4, PX, C), (6, PX, C)
    packed = [(9, C, C), (3, HEAD, THREE_TAILS), (3, THREE_TAILS, HEAD), (THREE_TAILS, THREE_TAILS)]
    taps = [(2, *KERNELS), (2, THREE_TAILS, C)]
    pad = (PX + 2 * COLS, C)

    tall_start = (TALL - 2 * COLS) * (1 - odd)
    x3 = send(lax.dynamic_slice(x, (odd, tall_start, 0), (1, TALL, C))[0], swap)
    s0, s1, own_sides, x2, c3, c2, cot0, cot1, w, wn, wk, wr, vt, vtk, vb, vbk = run(
        conv_own,
        [ONE, ONE, (2, *SIDES), TALL_ONE, ONE, ONE, ONE, ONE, *packed, *taps, *taps],
        (at, x, cot, ws, temporal_weight),
        [(2, *pad)],
        32,
        8 * flops,
        far=(1, 2, 3, 4),
    )
    wp = (w, wn, wk, wr)
    right = send(s0, outer)
    x2 = send(x2, swap)

    s3, sides3 = run(conv_other, [ONE, SIDES], (at, x3, *wp), [pad], 0, 4 * flops)
    left = send(s3, inner)
    c3 = send(after(c3, x2), swap)
    s2, sides2 = run(conv_other, [ONE, SIDES], (at, x2, *wp), [pad], 0, 4 * flops)
    c2 = send(after(c2, c3), swap)
    cot_right = send(after(cot0, right), outer)
    cot_left = send(c3, inner)

    acts1, state1, last, first = run(
        layer_one,
        [six, four, ONE, ONE],
        (at, left, s0, s1, s2, s3, right, vt, vtk),
        flops=8 * flops,
    )
    left1 = send(last, inner)
    right1 = send(first, outer)
    back1, first, last = run(
        back_one,
        [four, ONE, ONE],
        (at, cot_left, cot0, cot1, c2, c3, cot_right, state1, vb, vbk),
        flops=8 * flops,
    )
    back_left = send(last, inner)
    back_right = send(first, outer)
    acts2, own, sent = run(
        layer_two, [six, two, flat], (at, left1, state1, right1, vt, vtk), flops=8 * flops
    )
    returned = send(sent, swap)

    (temporal_blocks,) = run(
        temporal_grads,
        [(CLIPS, 2, C, 3 * WIDTH)],
        (at, cot0, cot1, c2, c3, acts2, back1, acts1),
        [(C, 4 * PX)],
        flops=16 * flops,
    )
    shares = (2, 5, C, 3 * WIDTH)
    kept, sent = run(
        back_zero,
        [shares] * 2,
        (at, back_left, back1, back_right, s0, s1, s2, s3, vb, vbk, own_sides, sides2, sides3, temporal_blocks),
        [(4, 3 * C, PX)],
        flops=32 * flops,
    )
    got = send(sent, cores, "clip")
    (out,) = run(place, [(2, FULL, C)], (at, own, returned), (), 4, 1000, far_outs=True)

    rows = C // owners
    block = (2 * owners, 5 * rows, 3 * WIDTH)
    (packs,) = run(
        pack,
        [block],
        (at, kept, got),
        [pltpu.VMEM((owners, 5 * rows, 3 * WIDTH), F32), pltpu.VMEM((C, 3 * WIDTH), F32), block],
        4,
        1000,
        far_outs=True,
    )
    groups = [[n + half * 2 + c for half in range(2) for n in range(0, owners * clips, clips)] for c in range(2)]
    parts = lax.all_to_all(packs, ("frame", "clip"), split_axis=0, concat_axis=0, axis_index_groups=groups, tiled=True)
    total = jnp.sum(parts.astype(F32), axis=0).reshape(5, rows, 3, WIDTH)
    grad_spatial = total[:3].transpose(1, 2, 0, 3)
    grad_temporal = total[3:].transpose(1, 0, 2, 3)
    return (out.reshape(clips_in.shape), grad_spatial, grad_temporal)


def solution(mesh):
    placed = (P("clip", "frame", None, None, None), P("clip", "frame", None, None, None), P(), P())
    return jax.shard_map(
        step,
        mesh=mesh,
        in_specs=placed,
        out_specs=(
            P("clip", "frame", None, None, None),
            P("frame", None, None, "clip"),
            P("frame", None, None, "clip"),
        ),
        check_vma=False,
    )
```

time: 190 us -> 166 us (0.87)
  Pallas kernels: 73.5 us -> 41.4 us
  local copies, waits for them, and re-layouts: 5.84 us -> 18.1 us
  waiting for transfers between devices: 67.5 us -> 60.4 us
  starting transfers between devices: 38.4 us -> 41.7 us
    pallas_call x11 -> x10, Pallas kernels: 73.5 us -> 41.4 us  [run(): pl.pallas_call(kernel, out_shape=[jax.ShapeDtypeStruct(s, BF) for s in ou...]
    unnamed x9 -> x50, local copies, waits for them, and re-layouts: 4.62 us -> 16.9 us
    ppermute x12 -> x14, waiting for transfers between devices: 67.5 us -> 60.4 us  [send(): return lax.ppermute(value, axis, perm).reshape(shape)]
    ppermute x12 -> x14, starting transfers between devices: 22.6 us -> 24.6 us  [send(): return lax.ppermute(value, axis, perm).reshape(shape)]
  transfers between devices with their start and end apart: 13 -> 15, of which waited for: 7 -> 6; matrix products, arithmetic and copies ran while one was open for 2% -> 1% of each run, Pallas kernels for 19% -> 12%
where the time goes in v2:
time: 166 us; the launch traced here: 164 us
  waiting for transfers between devices  60.4 us (36%)
  starting transfers between devices  41.7 us (25%)
  Pallas kernels  41.4 us (25%)
  local copies, waits for them, and re-layouts  18.1 us (11%)
  other arithmetic  1.92 us (1%)
    ppermute x14, waiting for transfers between devices, send(): return lax.ppermute(value, axis, perm).reshape(shape)  60.4 us
    pallas_call x10, Pallas kernels, run(): pl.pallas_call(kernel, out_shape=[jax.ShapeDtypeStruct(s, BF) for s in ou...  41.4 us
    ppermute x14, starting transfers between devices, send(): return lax.ppermute(value, axis, perm).reshape(shape)  24.6 us
    all_to_all x1, starting transfers between devices, step(): lax.all_to_all(packs, ('frame', 'clip'), split_axis=0, concat_axis=0, axi...  17.1 us
    unnamed x50, local copies, waits for them, and re-layouts  16.9 us
  transfers between devices with their start and end apart: 15, of which 6 were waited for; matrix products, arithmetic and copies ran while one was open for 1% of the time, Pallas kernels for 12%

profile of v2, /device:TPU:8, one launch (start us, length us, event | category | flops | bytes accessed | tf_op | source)
XLA Modules:
  0.0 164.5 jit_solution(18374796269075397356)
XLA Ops:
  0.7 1.4 copy-done.2
  2.1 1.6 copy-done.3
  3.8 1.4 copy-done.4
  5.2 1.4 copy-done.5
  6.5 11.9 %shard_map.67 = (bf16[512,320]{1,0:T(8,128)(2,1)S(1)}, bf16[512,320]{1,0:T(8,128)(2,1)S(1)}, bf16[2,4,512,240]{3,2,1,0:T(8,128)(2,1)S(1)}, bf16[544,320]{1,0:T(8...) custom-call(s32[2]{0:T(128)S(1)} %pad_add_fusion.at, ...), custom_call_target="tpu_custom_call" | custom-call | flops 838860800 | bytes 15429640 | tf_op jit(solution)/shard_map/pallas_call | solution.py:84
  18.5 1.1 copy-done
  19.6 1.1 copy-done.6
  20.7 0.7 copy-done.8
  21.4 0.7 copy-done.10
  22.2 0.8 copy-done.13
  22.9 0.8 copy-done.15
  23.7 0.7 copy-done.17
  24.4 1.4 copy-done.19
  25.8 0.7 copy-done.21
  26.5 0.7 copy-done.23
  27.3 0.3 collective-permute-start.2
  27.6 1.0 constant_dynamic-slice_fusion
  28.7 1.8 %collective-permute-start = (bf16[17,32,320]{2,1,0:T(8,128)(2,1)S(1)}, bf16[17,32,320]{2,1,0:T(8,128)(2,1)S(1)}, u32[]{:S(2)}, u32[]{:S(2)}) collective-permute-start(bf16[17,32,320]{2,1,0:T(8,128)(2,1)S(1)} %bitcast.62), channel_id=1, source_target_pairs={{0,1},{1,0},{2,3},{3,2},{4,5},{5,4},{6,7},{7,6},{8,9},{9,8},{10,11... | collective-permute-start | bytes 1044488 | tf_op jit(solution)/shard_map/ppermute | solution.py:346
  30.4 3.4 %collective-permute-start.3 = (bf16[16,32,320]{2,1,0:T(8,128)(2,1)}, bf16[16,32,320]{2,1,0:T(8,128)(2,1)S(1)}, u32[]{:S(2)}, u32[]{:S(2)}) collective-permute-start(bf16[16,32,320]{2,1,0:T(8,128)(2,1)} %bitcast.44), channel_id=1, source_target_pairs={{1,3},{2,0},{3,5},{4,2},{5,7},{6,4},{7,9},{8,6},{9,11},{10,8},{11,... | collective-permute-start | bytes 983048 | tf_op jit(solution)/shard_map/ppermute | solution.py:346
  33.9 6.3 %collective-permute-done.2 = bf16[17,32,320]{2,1,0:T(8,128)(2,1)} collective-permute-done((bf16[17,32,320]{2,1,0:T(8,128)(2,1)}, bf16[17,32,320]{2,1,0:T(8,128)(2,1)}, u32[]{:S(2)}, u32[]{:S(2)}) %collective-permute-start.2) | collective-permute-done | bytes 348192 | tf_op jit(solution)/shard_map/ppermute | solution.py:346
  40.1 0.3 collective-permute-start.7
  40.5 8.5 %collective-permute-done = bf16[17,32,320]{2,1,0:T(8,128)(2,1)S(1)} collective-permute-done((bf16[17,32,320]{2,1,0:T(8,128)(2,1)S(1)}, bf16[17,32,320]{2,1,0:T(8,128)(2,1)S(1)}, u32[]{:S(2)}, u32[]{:S(2)}) %collective-permute-start) | collective-permute-done | bytes 348192 | tf_op jit(solution)/shard_map/ppermute | solution.py:346
  49.0 1.0 copy-done.11
  49.9 1.9 %shard_map.68 = (bf16[512,320]{1,0:T(8,128)(2,1)S(1)}, bf16[4,512,240]{2,1,0:T(8,128)(2,1)S(1)}) custom-call(s32[2]{0:T(128)S(1)} %pad_add_fusion.at, bf16[544,320]{1,0:T(8,128)(2,1)S(1)} %bitcast.43, bf16[9,320,320]{2,1,0:T(8,128)(2,1)S(1)} %get-tuple-element.38.w, bf16[3,256,192]{2,1,0:T(8,128)(2,1)S(1)} %get-tuple-element.39.wn, ...), custom_call_target="tpu_custom_call" | custom-call | flops 419430400 | bytes 4165640 | tf_op jit(solution)/shard_map/pallas_call | solution.py:84
  51.9 1.3 collective-permute-start.1
  53.2 4.6 %collective-permute-start.10 = (bf16[16,32,320]{2,1,0:T(8,128)(2,1)S(1)}, bf16[16,32,320]{2,1,0:T(8,128)(2,1)S(1)}, u32[]{:S(2)}, u32[]{:S(2)}) collective-permute-start(bf16[16,32,320]{2,1,0:T(8,128)(2,1)S(1)} %bitcast.36), channel_id=1, source_target_pairs={{1,3},{2,0},{3,5},{4,2},{5,7},{6,4},{7,9},{8,6},{9,11},{10,8},{11,... | collective-permute-start | bytes 983048 | tf_op jit(solution)/shard_map/ppermute | solution.py:346
  57.9 1.4 collective-permute-start.8
  59.3 2.4 %shard_map.69 = (bf16[512,320]{1,0:T(8,128)(2,1)S(1)}, bf16[4,512,240]{2,1,0:T(8,128)(2,1)S(1)}) custom-call(s32[2]{0:T(128)S(1)} %pad_add_fusion.at, bf16[544,320]{1,0:T(8,128)(2,1)} %bitcast.10.x, bf16[9,320,320]{2,1,0:T(8,128)(2,1)S(1)} %get-tuple-element.38.w, bf16[3,256,192]{2,1,0:T(8,128)(2,1)S(1)} %get-tuple-element.39.wn, ...), custom_call_target="tpu_custom_call" | custom-call | flops 419430400 | bytes 4165640 | tf_op jit(solution)/shard_map/pallas_call | solution.py:84
  61.7 3.5 %collective-permute-done.1 = bf16[16,32,320]{2,1,0:T(8,128)(2,1)S(1)} collective-permute-done((bf16[16,32,320]{2,1,0:T(8,128)(2,1)S(1)}, bf16[16,32,320]{2,1,0:T(8,128)(2,1)S(1)}, u32[]{:S(2)}, u32[]{:S(2)}) %collective-permute-start.1) | collective-permute-done | bytes 327712 | tf_op jit(solution)/shard_map/ppermute | solution.py:346
  65.3 3.2 %shard_map.70 = (bf16[6,512,320]{2,1,0:T(8,128)(2,1)S(1)}, bf16[4,512,320]{2,1,0:T(8,128)(2,1)S(1)}, bf16[512,320]{1,0:T(8,128)(2,1)S(1)}, bf16[512,320]{1,0:T(8,128)(2,1)S(1)}) custom-call(s32[2]{0:T(128)S(1)} %pad_add_fusion.at, bf16[512,320]{1,0:T(8,128)(2,1)S(1)} %bitcast.51, bf16[512,320]{1,0:T(8,128)(2,1)S(1)} %copy-done.14, ...), custom_call_target="tpu_custom_call" | custom-call | flops 838860800 | bytes 7372808 | tf_op jit(solution)/shard_map/pallas_call | solution.py:84
  68.5 3.3 %collective-permute-start.5 = (bf16[16,32,320]{2,1,0:T(8,128)(2,1)S(1)}, bf16[16,32,320]{2,1,0:T(8,128)(2,1)S(1)}, u32[]{:S(2)}, u32[]{:S(2)}) collective-permute-start(bf16[16,32,320]{2,1,0:T(8,128)(2,1)S(1)} %bitcast.59), channel_id=1, source_target_pairs={{1,3},{2,0},{3,5},{4,2},{5,7},{6,4},{7,9},{8,6},{9,11},{10,8},{11,... | collective-permute-start | bytes 983048 | tf_op jit(solution)/shard_map/ppermute | solution.py:346
  71.9 1.5 collective-permute-start.4
  73.4 3.5 %shard_map.73 = (bf16[4,512,320]{2,1,0:T(8,128)(2,1)S(1)}, bf16[512,320]{1,0:T(8,128)(2,1)S(1)}, bf16[512,320]{1,0:T(8,128)(2,1)S(1)}) custom-call(s32[2]{0:T(128)S(1)} %pad_add_fusion.at, bf16[512,320]{1,0:T(8,128)(2,1)S(1)} %bitcast.49, bf16[512,320]{1,0:T(8,128)(2,1)S(1)} %get-tuple-element.60.cot0, bf16[512,320]{1,0:T(8,128)(2,1)S(1)} %get-tuple-element.57.cot1, ...), custom_call_target="tpu_custom_call" | custom-call | flops 838860800 | bytes 6717448 | tf_op jit(solution)/shard_map/pallas_call | solution.py:84
  76.9 4.6 %collective-permute-start.12 = (bf16[16,32,320]{2,1,0:T(8,128)(2,1)S(1)}, bf16[16,32,320]{2,1,0:T(8,128)(2,1)S(1)}, u32[]{:S(2)}, u32[]{:S(2)}) collective-permute-start(bf16[16,32,320]{2,1,0:T(8,128)(2,1)S(1)} %bitcast.60), channel_id=1, source_target_pairs={{1,3},{2,0},{3,5},{4,2},{5,7},{6,4},{7,9},{8,6},{9,11},{10,8},{11,... | collective-permute-start | bytes 983048 | tf_op jit(solution)/shard_map/ppermute | solution.py:346
  81.4 1.3 collective-permute-start.11
  82.8 3.2 %shard_map.71 = (bf16[6,512,320]{2,1,0:T(8,128)(2,1)S(1)}, bf16[2,512,320]{2,1,0:T(8,128)(2,1)S(1)}, bf16[1024,320]{1,0:T(8,128)(2,1)S(1)}) custom-call(s32[2]{0:T(128)S(1)} %pad_add_fusion.at, bf16[512,320]{1,0:T(8,128)(2,1)S(1)} %bitcast.50, bf16[4,512,320]{2,1,0:T(8,128)(2,1)S(1)} %get-tuple-element.50.state, bf16[512,320]{1,0:T(8,128)(2,1)S(1)} %bitcast.48, ...), custom_call_target="tpu_custom_call" | custom-call | flops 838860800 | bytes 6717448 | tf_op jit(solution)/shard_map/pallas_call | solution.py:84
  86.0 3.7 %shard_map.74.passing = bf16[4,2,320,240]{3,2,1,0:T(8,128)(2,1)S(1)} custom-call(s32[2]{0:T(128)S(1)} %pad_add_fusion.at, bf16[512,320]{1,0:T(8,128)(2,1)S(1)} %get-tuple-element.60.cot0, bf16[512,320]{1,0:T(8,128)(2,1)S(1)} %get-tuple-element.57.cot1, bf16[512,320]{1,0:T(8,128)(2,1)S(1)} %bitcast.40, bf16[512,320]{1,0:T(8,128)(2,1)S(1)} %bitcast.38, ...), custom_call_target="tpu_custom_call" | custom-call | flops 1677721600 | bytes 7782408 | tf_op jit(solution)/shard_map/pallas_call | solution.py:84
  89.7 1.4 collective-permute-done.11
  91.1 7.3 %shard_map.75 = (bf16[2,5,320,240]{3,2,1,0:T(8,128)(2,1)S(1)}, bf16[2,5,320,240]{3,2,1,0:T(8,128)(2,1)S(1)}) custom-call(s32[2]{0:T(128)S(1)} %pad_add_fusion.at, bf16[512,320]{1,0:T(8,128)(2,1)S(1)} %bitcast.56, bf16[4,512,320]{2,1,0:T(8,128)(2,1)S(1)} %get-tuple-element.64.back, bf16[512,320]{1,0:T(8,128)(2,1)S(1)} %bitcast.55, ...), custom_call_target="tpu_custom_call" | custom-call | flops 3355443200 | bytes 12984328 | tf_op jit(solution)/shard_map/pallas_call | solution.py:84
  98.5 3.5 %collective-permute-done.13.got = bf16[2,5,320,240]{3,2,1,0:T(8,128)(2,1)S(1)} collective-permute-done((bf16[2,5,320,240]{3,2,1,0:T(8,128)(2,1)S(1)}, bf16[2,5,320,240]{3,2,1,0:T(8,128)(2,1)S(1)}, u32[]{:S(2)}, u32[]{:S(2)}) %collective-permute-start.13) | collective-permute-done | bytes 1536032 | tf_op jit(solution)/shard_map/ppermute | solution.py:346
  102.0 2.5 %shard_map.76 = bf16[64,50,240]{2,1,0:T(8,128)(2,1)} custom-call(s32[2]{0:T(128)S(1)} %pad_add_fusion.at, bf16[2,5,320,240]{3,2,1,0:T(8,128)(2,1)S(1)} %get-tuple-element.71.kept, bf16[2,5,320,240]{3,2,1,0:T(8,128)(2,1)S(1)} %collective-permute-done.13.got), custom_call_target="tpu_custom_call" | custom-call | flops 1000 | bytes 4608008 | tf_op jit(solution)/shard_map/pallas_call | solution.py:84
  104.5 17.1 %all-to-all-start = ((bf16[64,50,240]{2,1,0:T(8,128)(2,1)}), bf16[64,50,240]{2,1,0:T(8,128)(2,1)}, u32[]{:S(2)}, u32[]{:S(2)}) async-start(bf16[64,50,240]{2,1,0:T(8,128)(2,1)} %shard_map.76), calls=%async_computation | async-start | bytes 3670016 | tf_op jit(solution)/shard_map/all_to_all | solution.py:432
  121.7 0.6 collective-permute-start.6
  122.3 37.2 %collective-permute-done.6 = bf16[32,32,320]{2,1,0:T(8,128)(2,1)S(1)} collective-permute-done((bf16[32,32,320]{2,1,0:T(8,128)(2,1)S(1)}, bf16[32,32,320]{2,1,0:T(8,128)(2,1)S(1)}, u32[]{:S(2)}, u32[]{:S(2)}) %collective-permute-start.6) | collective-permute-done | bytes 655392 | tf_op jit(solution)/shard_map/ppermute | solution.py:346
  159.4 1.7 %shard_map.72 = bf16[2,1024,320]{2,1,0:T(8,128)(2,1)} custom-call(s32[2]{0:T(128)S(1)} %pad_add_fusion.at, bf16[2,512,320]{2,1,0:T(8,128)(2,1)S(1)} %get-tuple-element.52.own, bf16[1024,320]{1,0:T(8,128)(2,1)S(1)} %bitcast.42), custom_call_target="tpu_custom_call" | custom-call | flops 1000 | bytes 2621448 | tf_op jit(solution)/shard_map/pallas_call | solution.py:84
  161.2 1.8 %convert_reduce_fusion = f32[50,240]{1,0:T(8,128)S(1)} fusion(bf16[64,50,240]{2,1,0:T(8,128)(2,1)} %all-to-all-done), kind=kLoop, calls=%fused_computation | loop fusion | flops 1524000 | bytes 1584000 | tf_op jit(solution)/shard_map/reduce_sum | solution.py:433
  163.1 0.6 copy.8
  163.8 0.6 copy.7
  (49 shorter events, 0.5 us)
Async XLA Ops:
  0.7 1.4 copy-start.2
  2.1 1.6 copy-start.3
  3.8 1.4 copy-start.4
  5.2 1.4 copy-start.5
  18.5 1.1 copy-start
  19.6 1.1 copy-start.6
  20.7 0.7 copy-start.8
  21.4 0.7 copy-start.10
  22.1 0.8 copy-start.13
  22.9 0.8 copy-start.15
  23.7 0.7 copy-start.17
  24.4 1.4 copy-start.19
  25.8 0.8 copy-start.21
  26.5 0.7 copy-start.23
  27.3 12.8 %collective-permute-start.2 = (bf16[17,32,320]{2,1,0:T(8,128)(2,1)}, bf16[17,32,320]{2,1,0:T(8,128)(2,1)}, u32[]{:S(2)}, u32[]{:S(2)}) collective-permute-start(bf16[17,32,320]{2,1,0:T(8,128)(2,1)} %bitcast.9), channel_id=1, source_target_pairs={{0,1},{1,0},{2,3},{3,2},{4,5},{5,4},{6,7},{7,6},{8,9},{9,8},{10,11... | collective-permute-start | bytes 1044488 | tf_op jit(solution)/shard_map/ppermute | solution.py:346
  28.7 20.3 %collective-permute-start = (bf16[17,32,320]{2,1,0:T(8,128)(2,1)S(1)}, bf16[17,32,320]{2,1,0:T(8,128)(2,1)S(1)}, u32[]{:S(2)}, u32[]{:S(2)}) collective-permute-start(bf16[17,32,320]{2,1,0:T(8,128)(2,1)S(1)} %bitcast.62), channel_id=1, source_target_pairs={{0,1},{1,0},{2,3},{3,2},{4,5},{5,4},{6,7},{7,6},{8,9},{9,8},{10,11... | collective-permute-start | bytes 1044488 | tf_op jit(solution)/shard_map/ppermute | solution.py:346
  30.4 22.7 %collective-permute-start.3 = (bf16[16,32,320]{2,1,0:T(8,128)(2,1)}, bf16[16,32,320]{2,1,0:T(8,128)(2,1)S(1)}, u32[]{:S(2)}, u32[]{:S(2)}) collective-permute-start(bf16[16,32,320]{2,1,0:T(8,128)(2,1)} %bitcast.44), channel_id=1, source_target_pairs={{1,3},{2,0},{3,5},{4,2},{5,7},{6,4},{7,9},{8,6},{9,11},{10,8},{11,... | collective-permute-start | bytes 983048 | tf_op jit(solution)/shard_map/ppermute | solution.py:346
  40.1 17.6 %collective-permute-start.7 = (bf16[16,32,320]{2,1,0:T(8,128)(2,1)}, bf16[16,32,320]{2,1,0:T(8,128)(2,1)S(1)}, u32[]{:S(2)}, u32[]{:S(2)}) collective-permute-start(bf16[16,32,320]{2,1,0:T(8,128)(2,1)} %bitcast.54), channel_id=1, source_target_pairs={{0,1},{1,0},{2,3},{3,2},{4,5},{5,4},{6,7},{7,6},{8,9},{9,8},{10,11... | collective-permute-start | bytes 983048 | tf_op jit(solution)/shard_map/ppermute | solution.py:346
  49.0 1.0 copy-start.11
  49.9 7.8 %copy-start.22 = (bf16[512,320]{1,0:T(8,128)(2,1)S(1)}, bf16[512,320]{1,0:T(8,128)(2,1)}, u32[]{:S(2)}) copy-start(bf16[512,320]{1,0:T(8,128)(2,1)} %copy-done.21) | copy-start | bytes 983044
  49.9 9.4 %copy-start.12 = (bf16[3,192,256]{2,1,0:T(8,128)(2,1)S(1)}, bf16[3,192,256]{2,1,0:T(8,128)(2,1)}, u32[]{:S(2)}) copy-start(bf16[3,192,256]{2,1,0:T(8,128)(2,1)} %copy-done.10) | copy-start | bytes 884740
  51.9 13.4 %collective-permute-start.1 = (bf16[16,32,320]{2,1,0:T(8,128)(2,1)S(1)}, bf16[16,32,320]{2,1,0:T(8,128)(2,1)S(1)}, u32[]{:S(2)}, u32[]{:S(2)}) collective-permute-start(bf16[16,32,320]{2,1,0:T(8,128)(2,1)S(1)} %bitcast.45), channel_id=1, source_target_pairs={{0,2},{2,4},{3,1},{4,6},{5,3},{6,8},{7,5},{8,10},{9,7},{10,12},{11... | collective-permute-start | bytes 983048 | tf_op jit(solution)/shard_map/ppermute | solution.py:346
  53.2 20.2 %collective-permute-start.10 = (bf16[16,32,320]{2,1,0:T(8,128)(2,1)S(1)}, bf16[16,32,320]{2,1,0:T(8,128)(2,1)S(1)}, u32[]{:S(2)}, u32[]{:S(2)}) collective-permute-start(bf16[16,32,320]{2,1,0:T(8,128)(2,1)S(1)} %bitcast.36), channel_id=1, source_target_pairs={{1,3},{2,0},{3,5},{4,2},{5,7},{6,4},{7,9},{8,6},{9,11},{10,8},{11,... | collective-permute-start | bytes 983048 | tf_op jit(solution)/shard_map/ppermute | solution.py:346
  57.8 7.5 %copy-start.1 = (bf16[2,3,320,320]{3,2,1,0:T(8,128)(2,1)S(1)}, bf16[2,3,320,320]{3,2,1,0:T(8,128)(2,1)}, u32[]{:S(2)}) copy-start(bf16[2,3,320,320]{3,2,1,0:T(8,128)(2,1)} %copy-done) | copy-start | bytes 3686404
  57.8 7.5 %copy-start.9 = (bf16[2,192,320]{2,1,0:T(8,128)(2,1)S(1)}, bf16[2,192,320]{2,1,0:T(8,128)(2,1)}, u32[]{:S(2)}) copy-start(bf16[2,192,320]{2,1,0:T(8,128)(2,1)} %copy-done.8) | copy-start | bytes 737284
  57.8 7.5 %copy-start.14 = (bf16[512,320]{1,0:T(8,128)(2,1)S(1)}, bf16[512,320]{1,0:T(8,128)(2,1)}, u32[]{:S(2)}) copy-start(bf16[512,320]{1,0:T(8,128)(2,1)} %copy-done.13) | copy-start | bytes 983044
  57.8 7.5 %copy-start.16 = (bf16[512,320]{1,0:T(8,128)(2,1)S(1)}, bf16[512,320]{1,0:T(8,128)(2,1)}, u32[]{:S(2)}) copy-start(bf16[512,320]{1,0:T(8,128)(2,1)} %copy-done.15) | copy-start | bytes 983044
  57.8 15.6 %collective-permute-start.9 = (bf16[16,32,320]{2,1,0:T(8,128)(2,1)S(1)}, bf16[16,32,320]{2,1,0:T(8,128)(2,1)S(1)}, u32[]{:S(2)}, u32[]{:S(2)}) collective-permute-start(bf16[16,32,320]{2,1,0:T(8,128)(2,1)S(1)} %bitcast.53), channel_id=1, source_target_pairs={{0,1},{1,0},{2,3},{3,2},{4,5},{5,4},{6,7},{7,6},{8,9},{9,8},{10,11... | collective-permute-start | bytes 983048 | tf_op jit(solution)/shard_map/ppermute | solution.py:346
  57.9 15.5 %collective-permute-start.8 = (bf16[16,32,320]{2,1,0:T(8,128)(2,1)S(1)}, bf16[16,32,320]{2,1,0:T(8,128)(2,1)S(1)}, u32[]{:S(2)}, u32[]{:S(2)}) collective-permute-start(bf16[16,32,320]{2,1,0:T(8,128)(2,1)S(1)} %collective-permute-done.7), channel_id=1, source_target_pairs={{0,2},{2,4},{3,1},{4,6},{5,3},{6,8},{7,5},{8,10},{9,7},{10,12},{11... | collective-permute-start | bytes 983048 | tf_op jit(solution)/shard_map/ppermute | solution.py:346
  65.3 8.1 %copy-start.7 = (bf16[2,3,320,320]{3,2,1,0:T(8,128)(2,1)S(1)}, bf16[2,3,320,320]{3,2,1,0:T(8,128)(2,1)}, u32[]{:S(2)}) copy-start(bf16[2,3,320,320]{3,2,1,0:T(8,128)(2,1)} %copy-done.6) | copy-start | bytes 3686404
  65.3 8.1 %copy-start.18 = (bf16[2,192,320]{2,1,0:T(8,128)(2,1)S(1)}, bf16[2,192,320]{2,1,0:T(8,128)(2,1)}, u32[]{:S(2)}) copy-start(bf16[2,192,320]{2,1,0:T(8,128)(2,1)} %copy-done.17) | copy-start | bytes 737284
  68.5 14.2 %collective-permute-start.5 = (bf16[16,32,320]{2,1,0:T(8,128)(2,1)S(1)}, bf16[16,32,320]{2,1,0:T(8,128)(2,1)S(1)}, u32[]{:S(2)}, u32[]{:S(2)}) collective-permute-start(bf16[16,32,320]{2,1,0:T(8,128)(2,1)S(1)} %bitcast.59), channel_id=1, source_target_pairs={{1,3},{2,0},{3,5},{4,2},{5,7},{6,4},{7,9},{8,6},{9,11},{10,8},{11,... | collective-permute-start | bytes 983048 | tf_op jit(solution)/shard_map/ppermute | solution.py:346
  71.9 10.9 %collective-permute-start.4 = (bf16[16,32,320]{2,1,0:T(8,128)(2,1)S(1)}, bf16[16,32,320]{2,1,0:T(8,128)(2,1)S(1)}, u32[]{:S(2)}, u32[]{:S(2)}) collective-permute-start(bf16[16,32,320]{2,1,0:T(8,128)(2,1)S(1)} %bitcast.57), channel_id=1, source_target_pairs={{0,2},{2,4},{3,1},{4,6},{5,3},{6,8},{7,5},{8,10},{9,7},{10,12},{11... | collective-permute-start | bytes 983048 | tf_op jit(solution)/shard_map/ppermute | solution.py:346
  76.9 12.8 %collective-permute-start.12 = (bf16[16,32,320]{2,1,0:T(8,128)(2,1)S(1)}, bf16[16,32,320]{2,1,0:T(8,128)(2,1)S(1)}, u32[]{:S(2)}, u32[]{:S(2)}) collective-permute-start(bf16[16,32,320]{2,1,0:T(8,128)(2,1)S(1)} %bitcast.60), channel_id=1, source_target_pairs={{1,3},{2,0},{3,5},{4,2},{5,7},{6,4},{7,9},{8,6},{9,11},{10,8},{11,... | collective-permute-start | bytes 983048 | tf_op jit(solution)/shard_map/ppermute | solution.py:346
  81.4 9.7 %collective-permute-start.11 = (bf16[16,32,320]{2,1,0:T(8,128)(2,1)S(1)}, bf16[16,32,320]{2,1,0:T(8,128)(2,1)S(1)}, u32[]{:S(2)}, u32[]{:S(2)}) collective-permute-start(bf16[16,32,320]{2,1,0:T(8,128)(2,1)S(1)} %bitcast.58), channel_id=1, source_target_pairs={{0,2},{2,4},{3,1},{4,6},{5,3},{6,8},{7,5},{8,10},{9,7},{10,12},{11... | collective-permute-start | bytes 983048 | tf_op jit(solution)/shard_map/ppermute | solution.py:346
  86.0 5.1 %copy-start.20 = (bf16[2,4,512,240]{3,2,1,0:T(8,128)(2,1)S(1)}, bf16[2,4,512,240]{3,2,1,0:T(8,128)(2,1)}, u32[]{:S(2)}) copy-start(bf16[2,4,512,240]{3,2,1,0:T(8,128)(2,1)} %copy-done.19) | copy-start | bytes 5898244
  98.4 3.6 %collective-permute-start.13 = (bf16[2,5,320,240]{3,2,1,0:T(8,128)(2,1)S(1)}, bf16[2,5,320,240]{3,2,1,0:T(8,128)(2,1)S(1)}, u32[]{:S(2)}, u32[]{:S(2)}) collective-permute-start(bf16[2,5,320,240]{3,2,1,0:T(8,128)(2,1)S(1)} %get-tuple-element.72), channel_id=1, source_target_pairs={{0,32},{32,0},{64,96},{96,64},{1,33},{33,1},{65,97},{97,65},{2,34}... | collective-permute-start | bytes 4608008 | tf_op jit(solution)/shard_map/ppermute | solution.py:346
  104.5 56.6 %all-to-all-start = ((bf16[64,50,240]{2,1,0:T(8,128)(2,1)}), bf16[64,50,240]{2,1,0:T(8,128)(2,1)}, u32[]{:S(2)}, u32[]{:S(2)}) async-start(bf16[64,50,240]{2,1,0:T(8,128)(2,1)} %shard_map.76), calls=%async_computation | async-start | bytes 3670016 | tf_op jit(solution)/shard_map/all_to_all | solution.py:432
  121.7 37.8 %collective-permute-start.6 = (bf16[32,32,320]{2,1,0:T(8,128)(2,1)S(1)}, bf16[32,32,320]{2,1,0:T(8,128)(2,1)S(1)}, u32[]{:S(2)}, u32[]{:S(2)}) collective-permute-start(bf16[32,32,320]{2,1,0:T(8,128)(2,1)S(1)} %bitcast.52), channel_id=1, source_target_pairs={{0,1},{1,0},{2,3},{3,2},{4,5},{5,4},{6,7},{7,6},{8,9},{9,8},{10,11... | collective-permute-start | bytes 1966088 | tf_op jit(solution)/shard_map/ppermute | solution.py:346

commit v3 on v2

--- a/solution.py
+++ b/solution.py
@@ -140,46 +140,38 @@
         sides[b] = side(*[pad[pl.ds(COLS * i, PX), columns] for i in range(3)])
 
 
-def conv_own(at, x, cot, w, tw, out0, out1, sides, x2, c3, c2, cot0, cot1, vw, wn, wk, wr, vt, vtk, vb, vbk, pads, sems):
+def conv_own(at, x, w, out0, out1, sides, x2, wn, wk, wr, pads):
     odd = at[0]
-    move = Mover(sems)
+    for i in range(3):
+        wn[i] = side(*[w[3 * i + j, pl.ds(0, HEAD), pl.ds(HEAD, TAIL)] for j in range(3)])
+        for j in range(3):
+            wk[j, pl.ds(TAIL * i, TAIL), :] = w[3 * i + j, pl.ds(HEAD, TAIL), pl.ds(0, HEAD)]
+        wr[pl.ds(TAIL * i, TAIL), :] = side(
+            *[w[3 * i + j, pl.ds(HEAD, TAIL), pl.ds(HEAD, TAIL)] for j in range(3)]
+        )
     start = pl.multiple_of((TALL - 2 * COLS) * odd, COLS)
-    frames = [odd, 1 - odd]
-    rows = [
-        move.fetch(x.at[frames[q], pl.ds(start, TALL), :], padded(pads.at[q], odd)) for q in range(2)
-    ]
-    weights = [move.fetch(w.at[n], vw.at[n]) for n in range(9)]
+    for q, out in enumerate((out0, out1)):
+        padded(pads.at[q], odd)[...] = x[odd + q * (1 - 2 * odd), pl.ds(start, TALL), :]
+        convolve(pads.at[q], w, wn, wk, wr, out, sides.at[q])
     away = pl.multiple_of((TALL - 2 * COLS) * (1 - odd), COLS)
+    x2[...] = x[1 - odd, pl.ds(away, TALL), :]
+
+
+def prepare(at, cot, tw, c3, c2, cot0, cot1, vt, vtk, vb, vbk):
+    odd = at[0]
     here, there = pl.multiple_of(PX * odd, PX), pl.multiple_of(PX * (1 - odd), PX)
-    later = [
-        move.fetch(x.at[1 - odd, pl.ds(away, TALL), :], x2),
-        move.fetch(cot.at[odd, pl.ds(here, PX), :], cot0),
-        move.fetch(cot.at[1 - odd, pl.ds(here, PX), :], cot1),
-        move.fetch(cot.at[odd, pl.ds(there, PX), :], c3),
-        move.fetch(cot.at[1 - odd, pl.ds(there, PX), :], c2),
-    ]
-    taps = [(l, k, move.fetch(tw.at[l, tap(k, odd)], vt.at[l, k])) for l in range(2) for k in range(3)]
-    for arrival in weights:
-        arrival.get()
-    for i in range(3):
-        wn[i] = side(*[vw[3 * i + j, pl.ds(0, HEAD), pl.ds(HEAD, TAIL)] for j in range(3)])
-        for j in range(3):
-            wk[j, pl.ds(TAIL * i, TAIL), :] = vw[3 * i + j, pl.ds(HEAD, TAIL), pl.ds(0, HEAD)]
-        wr[pl.ds(TAIL * i, TAIL), :] = side(
-            *[vw[3 * i + j, pl.ds(HEAD, TAIL), pl.ds(HEAD, TAIL)] for j in range(3)]
-        )
-    for arrival in rows:
-        arrival.get()
-    for l, k, arrival in taps:
-        arrival.get()
-        turned = vt[l, k].T
-        vb[l, k] = turned
-        vtk[l, pl.ds(TAIL * k, TAIL), :] = vt[l, k, pl.ds(HEAD, TAIL), :]
-        vbk[l, pl.ds(TAIL * k, TAIL), :] = turned[HEAD:, :]
-    for q, out in enumerate((out0, out1)):
-        convolve(pads.at[q], vw, wn, wk, wr, out, sides.at[q])
-    for arrival in later:
-        arrival.get()
+    c3[...] = cot[odd, pl.ds(there, PX), :]
+    c2[...] = cot[1 - odd, pl.ds(there, PX), :]
+    cot0[...] = cot[odd, pl.ds(here, PX), :]
+    cot1[...] = cot[1 - odd, pl.ds(here, PX), :]
+    for l in range(2):
+        for k in range(3):
+            value = tw[l, tap(k, odd)]
+            turned = value.T
+            vt[l, k] = value
+            vb[l, k] = turned
+            vtk[l, pl.ds(TAIL * k, TAIL), :] = value[HEAD:, :]
+            vbk[l, pl.ds(TAIL * k, TAIL), :] = turned[HEAD:, :]
 
 
 def conv_other(at, x, w, wn, wk, wr, out, sides, pad):
@@ -351,24 +343,25 @@
     flops = 2 * PX * C * C
 
     flat, two, four, six = (2 * PX, C), (2, PX, C), (4, PX, C), (6, PX, C)
-    packed = [(9, C, C), (3, HEAD, THREE_TAILS), (3, THREE_TAILS, HEAD), (THREE_TAILS, THREE_TAILS)]
+    packed = [(3, HEAD, THREE_TAILS), (3, THREE_TAILS, HEAD), (THREE_TAILS, THREE_TAILS)]
     taps = [(2, *KERNELS), (2, THREE_TAILS, C)]
     pad = (PX + 2 * COLS, C)
 
     tall_start = (TALL - 2 * COLS) * (1 - odd)
     x3 = send(lax.dynamic_slice(x, (odd, tall_start, 0), (1, TALL, C))[0], swap)
-    s0, s1, own_sides, x2, c3, c2, cot0, cot1, w, wn, wk, wr, vt, vtk, vb, vbk = run(
+    s0, s1, own_sides, x2, wn, wk, wr = run(
         conv_own,
-        [ONE, ONE, (2, *SIDES), TALL_ONE, ONE, ONE, ONE, ONE, *packed, *taps, *taps],
-        (at, x, cot, ws, temporal_weight),
+        [ONE, ONE, (2, *SIDES), TALL_ONE, *packed],
+        (at, x, ws),
         [(2, *pad)],
-        32,
-        8 * flops,
-        far=(1, 2, 3, 4),
-    )
-    wp = (w, wn, wk, wr)
+        flops=8 * flops,
+    )
+    wp = (ws, wn, wk, wr)
     right = send(s0, outer)
     x2 = send(x2, swap)
+    c3, c2, cot0, cot1, vt, vtk, vb, vbk = run(
+        prepare, [ONE] * 4 + taps * 2, (at, after(cot, s0), after(temporal_weight, s0)), flops=flops
+    )
 
     s3, sides3 = run(conv_other, [ONE, SIDES], (at, x3, *wp), [pad], 0, 4 * flops)
     left = send(s3, inner)
@@ -429,7 +422,9 @@
         far_outs=True,
     )
     groups = [[n + half * 2 + c for half in range(2) for n in range(0, owners * clips, clips)] for c in range(2)]
-    parts = lax.all_to_all(packs, ("frame", "clip"), split_axis=0, concat_axis=0, axis_index_groups=groups, tiled=True)
+    parts = lax.all_to_all(
+        packs, ("frame", "clip"), split_axis=0, concat_axis=0, axis_index_groups=groups, tiled=True
+    )
     total = jnp.sum(parts.astype(F32), axis=0).reshape(5, rows, 3, WIDTH)
     grad_spatial = total[:3].transpose(1, 2, 0, 3)
     grad_temporal = total[3:].transpose(1, 0, 2, 3)

time: 166 us -> 147 us (0.89)
  local copies, waits for them, and re-layouts: 18.1 us -> 9.13 us
  Pallas kernels: 41.4 us -> 34.4 us
  waiting for transfers between devices: 60.4 us -> 58.4 us
    unnamed x50 -> x32, local copies, waits for them, and re-layouts: 16.9 us -> 7.91 us
    pallas_call x10 -> x11, Pallas kernels: 41.4 us -> 34.4 us  [run(): pl.pallas_call(kernel, out_shape=[jax.ShapeDtypeStruct(s, BF) for s in ou...]
    ppermute x14, waiting for transfers between devices: 60.4 us -> 58.4 us  [send(): return lax.ppermute(value, axis, perm).reshape(shape)]
  transfers between devices with their start and end apart: 15 -> 15, of which waited for: 6 -> 6; matrix products, arithmetic and copies ran while one was open for 1% -> 1% of each run, Pallas kernels for 12% -> 14%
where the time goes in v3:
time: 147 us; the launch traced here: 146 us
  waiting for transfers between devices  58.4 us (40%)
  starting transfers between devices  42.4 us (29%)
  Pallas kernels  34.4 us (23%)
  local copies, waits for them, and re-layouts  9.13 us (6%)
    ppermute x14, waiting for transfers between devices, send(): return lax.ppermute(value, axis, perm).reshape(shape)  58.4 us
    pallas_call x11, Pallas kernels, run(): pl.pallas_call(kernel, out_shape=[jax.ShapeDtypeStruct(s, BF) for s in ou...  34.4 us
    ppermute x14, starting transfers between devices, send(): return lax.ppermute(value, axis, perm).reshape(shape)  24.4 us
    all_to_all x1, starting transfers between devices, step(): lax.all_to_all(packs, ('frame', 'clip'), split_axis=0, concat_axis=0, axi...  18 us
    unnamed x32, local copies, waits for them, and re-layouts  7.91 us
  transfers between devices with their start and end apart: 15, of which 6 were waited for; matrix products, arithmetic and copies ran while one was open for 1% of the time, Pallas kernels for 14%

profile of v3, /device:TPU:8, one launch (start us, length us, event | category | flops | bytes accessed | tf_op | source)
XLA Modules:
  0.0 145.8 jit_solution(11431328499537757146)
XLA Ops:
  0.6 0.1 pad_add_fusion.at
  0.7 1.6 %copy-done = bf16[3,3,320,320]{3,2,1,0:T(8,128)(2,1)S(1)} copy-done((bf16[3,3,320,320]{3,2,1,0:T(8,128)(2,1)S(1)}, bf16[3,3,320,320]{3,2,1,0:T(8,128)(2,1)}, u32[]{:S(2)}) %copy-start) | copy-done | bytes 1843224
  2.4 1.4 copy-done.2
  3.8 3.9 %shard_map.67 = (bf16[512,320]{1,0:T(8,128)(2,1)S(1)}, bf16[512,320]{1,0:T(8,128)(2,1)S(1)}, bf16[2,4,512,240]{3,2,1,0:T(8,128)(2,1)S(1)}, bf16[544,320]{1,0:T(8...) custom-call(s32[2]{0:T(128)S(1)} %pad_add_fusion.at, ...), custom_call_target="tpu_custom_call" | custom-call | flops 838860800 | bytes 6787080 | tf_op jit(solution)/shard_map/pallas_call | solution.py:84
  7.6 0.7 copy-done.5
  8.3 0.8 copy-done.7
  9.1 0.8 copy-done.9
  9.9 1.3 copy-done.11
  11.2 0.3 collective-permute-start.2
  11.5 1.0 constant_dynamic-slice_fusion
  12.6 0.0 copy-start.1
  12.6 1.8 %collective-permute-start = (bf16[17,32,320]{2,1,0:T(8,128)(2,1)S(1)}, bf16[17,32,320]{2,1,0:T(8,128)(2,1)S(1)}, u32[]{:S(2)}, u32[]{:S(2)}) collective-permute-start(bf16[17,32,320]{2,1,0:T(8,128)(2,1)S(1)} %bitcast.64), channel_id=1, source_target_pairs={{0,1},{1,0},{2,3},{3,2},{4,5},{5,4},{6,7},{7,6},{8,9},{9,8},{10,11... | collective-permute-start | bytes 1044488 | tf_op jit(solution)/shard_map/ppermute | solution.py:338
  14.4 3.4 %collective-permute-start.3 = (bf16[16,32,320]{2,1,0:T(8,128)(2,1)}, bf16[16,32,320]{2,1,0:T(8,128)(2,1)S(1)}, u32[]{:S(2)}, u32[]{:S(2)}) collective-permute-start(bf16[16,32,320]{2,1,0:T(8,128)(2,1)} %bitcast.46), channel_id=1, source_target_pairs={{1,3},{2,0},{3,5},{4,2},{5,7},{6,4},{7,9},{8,6},{9,11},{10,8},{11,... | collective-permute-start | bytes 983048 | tf_op jit(solution)/shard_map/ppermute | solution.py:338
  17.8 1.2 shard_map.70
  19.0 5.0 %collective-permute-done.2 = bf16[17,32,320]{2,1,0:T(8,128)(2,1)} collective-permute-done((bf16[17,32,320]{2,1,0:T(8,128)(2,1)}, bf16[17,32,320]{2,1,0:T(8,128)(2,1)}, u32[]{:S(2)}, u32[]{:S(2)}) %collective-permute-start.2) | collective-permute-done | bytes 348192 | tf_op jit(solution)/shard_map/ppermute | solution.py:338
  24.0 0.3 collective-permute-start.7
  24.4 8.5 %collective-permute-done = bf16[17,32,320]{2,1,0:T(8,128)(2,1)S(1)} collective-permute-done((bf16[17,32,320]{2,1,0:T(8,128)(2,1)S(1)}, bf16[17,32,320]{2,1,0:T(8,128)(2,1)S(1)}, u32[]{:S(2)}, u32[]{:S(2)}) %collective-permute-start) | collective-permute-done | bytes 348192 | tf_op jit(solution)/shard_map/ppermute | solution.py:338
  32.9 1.9 %shard_map.68 = (bf16[512,320]{1,0:T(8,128)(2,1)S(1)}, bf16[4,512,240]{2,1,0:T(8,128)(2,1)S(1)}) custom-call(s32[2]{0:T(128)S(1)} %pad_add_fusion.at, bf16[544,320]{1,0:T(8,128)(2,1)S(1)} %bitcast.45, bf16[9,320,320]{2,1,0:T(8,128)(2,1)S(1)} %bitcast.34, bf16[3,256,192]{2,1,0:T(8,128)(2,1)S(1)} %get-tuple-element.39.wn, bf16[3,192,256]{2,1,0:T(8,128)(2,1)S(1)} %copy-done.6, ...), custom_call_target="tpu_custom_call" | custom-call | flops 419430400 | bytes 4165640 | tf_op jit(solution)/shard_map/pallas_call | solution.py:84
  34.8 1.3 collective-permute-start.1
  36.1 4.6 %collective-permute-start.10 = (bf16[16,32,320]{2,1,0:T(8,128)(2,1)S(1)}, bf16[16,32,320]{2,1,0:T(8,128)(2,1)S(1)}, u32[]{:S(2)}, u32[]{:S(2)}) collective-permute-start(bf16[16,32,320]{2,1,0:T(8,128)(2,1)S(1)} %bitcast.38), channel_id=1, source_target_pairs={{1,3},{2,0},{3,5},{4,2},{5,7},{6,4},{7,9},{8,6},{9,11},{10,8},{11,... | collective-permute-start | bytes 983048 | tf_op jit(solution)/shard_map/ppermute | solution.py:338
  40.7 0.1 collective-permute-start.9
  40.8 1.4 collective-permute-start.8
  42.2 2.4 %shard_map.69 = (bf16[512,320]{1,0:T(8,128)(2,1)S(1)}, bf16[4,512,240]{2,1,0:T(8,128)(2,1)S(1)}) custom-call(s32[2]{0:T(128)S(1)} %pad_add_fusion.at, bf16[544,320]{1,0:T(8,128)(2,1)} %bitcast.9.x, bf16[9,320,320]{2,1,0:T(8,128)(2,1)S(1)} %bitcast.35, bf16[3,256,192]{2,1,0:T(8,128)(2,1)S(1)} %get-tuple-element.39.wn, bf16[3,192,256]{2,1,0:T(8,128)(2,1)S(1)} %copy-done.6, ...), custom_call_target="tpu_custom_call" | custom-call | flops 419430400 | bytes 4165640 | tf_op jit(solution)/shard_map/pallas_call | solution.py:84
  44.6 2.7 %collective-permute-done.1 = bf16[16,32,320]{2,1,0:T(8,128)(2,1)S(1)} collective-permute-done((bf16[16,32,320]{2,1,0:T(8,128)(2,1)S(1)}, bf16[16,32,320]{2,1,0:T(8,128)(2,1)S(1)}, u32[]{:S(2)}, u32[]{:S(2)}) %collective-permute-start.1) | collective-permute-done | bytes 327712 | tf_op jit(solution)/shard_map/ppermute | solution.py:338
  47.3 3.2 %shard_map.71 = (bf16[6,512,320]{2,1,0:T(8,128)(2,1)S(1)}, bf16[4,512,320]{2,1,0:T(8,128)(2,1)S(1)}, bf16[512,320]{1,0:T(8,128)(2,1)S(1)}, bf16[512,320]{1,0:T(8,128)(2,1)S(1)}) custom-call(s32[2]{0:T(128)S(1)} %pad_add_fusion.at, bf16[512,320]{1,0:T(8,128)(2,1)S(1)} %bitcast.53, bf16[512,320]{1,0:T(8,128)(2,1)S(1)} %copy-done.8, ...), custom_call_target="tpu_custom_call" | custom-call | flops 838860800 | bytes 7372808 | tf_op jit(solution)/shard_map/pallas_call | solution.py:84
  50.5 3.3 %collective-permute-start.5 = (bf16[16,32,320]{2,1,0:T(8,128)(2,1)S(1)}, bf16[16,32,320]{2,1,0:T(8,128)(2,1)S(1)}, u32[]{:S(2)}, u32[]{:S(2)}) collective-permute-start(bf16[16,32,320]{2,1,0:T(8,128)(2,1)S(1)} %bitcast.60), channel_id=1, source_target_pairs={{1,3},{2,0},{3,5},{4,2},{5,7},{6,4},{7,9},{8,6},{9,11},{10,8},{11,... | collective-permute-start | bytes 983048 | tf_op jit(solution)/shard_map/ppermute | solution.py:338
  53.8 1.5 %collective-permute-start.4 = (bf16[16,32,320]{2,1,0:T(8,128)(2,1)S(1)}, bf16[16,32,320]{2,1,0:T(8,128)(2,1)S(1)}, u32[]{:S(2)}, u32[]{:S(2)}) collective-permute-start(bf16[16,32,320]{2,1,0:T(8,128)(2,1)S(1)} %bitcast.58), channel_id=1, source_target_pairs={{0,2},{2,4},{3,1},{4,6},{5,3},{6,8},{7,5},{8,10},{9,7},{10,12},{11... | collective-permute-start | bytes 983048 | tf_op jit(solution)/shard_map/ppermute | solution.py:338
  55.3 3.4 %shard_map.74 = (bf16[4,512,320]{2,1,0:T(8,128)(2,1)S(1)}, bf16[512,320]{1,0:T(8,128)(2,1)S(1)}, bf16[512,320]{1,0:T(8,128)(2,1)S(1)}) custom-call(s32[2]{0:T(128)S(1)} %pad_add_fusion.at, bf16[512,320]{1,0:T(8,128)(2,1)S(1)} %bitcast.51, bf16[512,320]{1,0:T(8,128)(2,1)S(1)} %get-tuple-element.62.cot0, bf16[512,320]{1,0:T(8,128)(2,1)S(1)} %get-tuple-element.59.cot1, ...), custom_call_target="tpu_custom_call" | custom-call | flops 838860800 | bytes 6717448 | tf_op jit(solution)/shard_map/pallas_call | solution.py:84
  58.7 4.6 %collective-permute-start.12 = (bf16[16,32,320]{2,1,0:T(8,128)(2,1)S(1)}, bf16[16,32,320]{2,1,0:T(8,128)(2,1)S(1)}, u32[]{:S(2)}, u32[]{:S(2)}) collective-permute-start(bf16[16,32,320]{2,1,0:T(8,128)(2,1)S(1)} %bitcast.61), channel_id=1, source_target_pairs={{1,3},{2,0},{3,5},{4,2},{5,7},{6,4},{7,9},{8,6},{9,11},{10,8},{11,... | collective-permute-start | bytes 983048 | tf_op jit(solution)/shard_map/ppermute | solution.py:338
  63.3 1.3 collective-permute-start.11
  64.6 3.2 %shard_map.72 = (bf16[6,512,320]{2,1,0:T(8,128)(2,1)S(1)}, bf16[2,512,320]{2,1,0:T(8,128)(2,1)S(1)}, bf16[1024,320]{1,0:T(8,128)(2,1)S(1)}) custom-call(s32[2]{0:T(128)S(1)} %pad_add_fusion.at, bf16[512,320]{1,0:T(8,128)(2,1)S(1)} %bitcast.52, bf16[4,512,320]{2,1,0:T(8,128)(2,1)S(1)} %get-tuple-element.52.state, bf16[512,320]{1,0:T(8,128)(2,1)S(1)} %bitcast.50, ...), custom_call_target="tpu_custom_call" | custom-call | flops 838860800 | bytes 6717448 | tf_op jit(solution)/shard_map/pallas_call | solution.py:84
  67.9 0.0 copy-start.13
  67.9 3.7 %shard_map.75.passing = bf16[4,2,320,240]{3,2,1,0:T(8,128)(2,1)S(1)} custom-call(s32[2]{0:T(128)S(1)} %pad_add_fusion.at, bf16[512,320]{1,0:T(8,128)(2,1)S(1)} %get-tuple-element.62.cot0, bf16[512,320]{1,0:T(8,128)(2,1)S(1)} %get-tuple-element.59.cot1, bf16[512,320]{1,0:T(8,128)(2,1)S(1)} %bitcast.42, bf16[512,320]{1,0:T(8,128)(2,1)S(1)} %bitcast.40, ...), custom_call_target="tpu_custom_call" | custom-call | flops 1677721600 | bytes 7782408 | tf_op jit(solution)/shard_map/pallas_call | solution.py:84
  71.6 1.4 collective-permute-done.11
  73.0 7.3 %shard_map.76 = (bf16[2,5,320,240]{3,2,1,0:T(8,128)(2,1)S(1)}, bf16[2,5,320,240]{3,2,1,0:T(8,128)(2,1)S(1)}) custom-call(s32[2]{0:T(128)S(1)} %pad_add_fusion.at, bf16[512,320]{1,0:T(8,128)(2,1)S(1)} %bitcast.57, bf16[4,512,320]{2,1,0:T(8,128)(2,1)S(1)} %get-tuple-element.66.back, bf16[512,320]{1,0:T(8,128)(2,1)S(1)} %bitcast.56, ...), custom_call_target="tpu_custom_call" | custom-call | flops 3355443200 | bytes 12984328 | tf_op jit(solution)/shard_map/pallas_call | solution.py:84
  80.3 0.1 collective-permute-start.13
  80.4 3.5 %collective-permute-done.13.got = bf16[2,5,320,240]{3,2,1,0:T(8,128)(2,1)S(1)} collective-permute-done((bf16[2,5,320,240]{3,2,1,0:T(8,128)(2,1)S(1)}, bf16[2,5,320,240]{3,2,1,0:T(8,128)(2,1)S(1)}, u32[]{:S(2)}, u32[]{:S(2)}) %collective-permute-start.13) | collective-permute-done | bytes 1536032 | tf_op jit(solution)/shard_map/ppermute | solution.py:338
  83.9 2.5 %shard_map.77 = bf16[64,50,240]{2,1,0:T(8,128)(2,1)} custom-call(s32[2]{0:T(128)S(1)} %pad_add_fusion.at, bf16[2,5,320,240]{3,2,1,0:T(8,128)(2,1)S(1)} %get-tuple-element.73.kept, bf16[2,5,320,240]{3,2,1,0:T(8,128)(2,1)S(1)} %collective-permute-done.13.got), custom_call_target="tpu_custom_call" | custom-call | flops 1000 | bytes 4608008 | tf_op jit(solution)/shard_map/pallas_call | solution.py:84
  86.4 0.0 copy-start.14
  86.4 18.0 %all-to-all-start = ((bf16[64,50,240]{2,1,0:T(8,128)(2,1)}), bf16[64,50,240]{2,1,0:T(8,128)(2,1)S(1)}, u32[]{:S(2)}, u32[]{:S(2)}) async-start(bf16[64,50,240]{2,1,0:T(8,128)(2,1)} %shard_map.77), calls=%async_computation | async-start | bytes 3670016 | tf_op jit(solution)/shard_map/all_to_all | solution.py:425
  104.4 0.5 collective-permute-start.6
  104.9 37.3 %collective-permute-done.6 = bf16[32,32,320]{2,1,0:T(8,128)(2,1)S(1)} collective-permute-done((bf16[32,32,320]{2,1,0:T(8,128)(2,1)S(1)}, bf16[32,32,320]{2,1,0:T(8,128)(2,1)S(1)}, u32[]{:S(2)}, u32[]{:S(2)}) %collective-permute-start.6) | collective-permute-done | bytes 655392 | tf_op jit(solution)/shard_map/ppermute | solution.py:338
  142.2 1.7 %shard_map.73 = bf16[2,1024,320]{2,1,0:T(8,128)(2,1)} custom-call(s32[2]{0:T(128)S(1)} %pad_add_fusion.at, bf16[2,512,320]{2,1,0:T(8,128)(2,1)S(1)} %get-tuple-element.54.own, bf16[1024,320]{1,0:T(8,128)(2,1)S(1)} %bitcast.44), custom_call_target="tpu_custom_call" | custom-call | flops 1000 | bytes 2621448 | tf_op jit(solution)/shard_map/pallas_call | solution.py:84
  144.0 0.3 convert_reduce_fusion
  144.3 0.1 slice.15
  144.4 0.6 copy.8
  145.1 0.1 slice.13
  145.2 0.6 copy.7
  (32 shorter events, 0.1 us)
Async XLA Ops:
  0.7 1.6 %copy-start = (bf16[3,3,320,320]{3,2,1,0:T(8,128)(2,1)S(1)}, bf16[3,3,320,320]{3,2,1,0:T(8,128)(2,1)}, u32[]{:S(2)}) copy-start(bf16[3,3,320,320]{3,2,1,0:T(8,128)(2,1)} %param.6) | copy-start | bytes 5529604
  2.3 1.4 copy-start.2
  3.8 14.0 %copy-start.3 = (bf16[1,2,32,32,320]{4,3,2,1,0:T(8,128)(2,1)S(1)}, bf16[1,2,32,32,320]{4,3,2,1,0:T(8,128)(2,1)}, u32[]{:S(2)}) copy-start(bf16[1,2,32,32,320]{4,3,2,1,0:T(8,128)(2,1)} %param.5) | copy-start | bytes 3932164
  3.8 14.0 %copy-start.4 = (bf16[2,3,320,320]{3,2,1,0:T(8,128)(2,1)S(1)}, bf16[2,3,320,320]{3,2,1,0:T(8,128)(2,1)}, u32[]{:S(2)}) copy-start(bf16[2,3,320,320]{3,2,1,0:T(8,128)(2,1)} %tw) | copy-start | bytes 3686404
  7.6 0.7 copy-start.5
  8.3 0.8 copy-start.7
  9.1 0.8 copy-start.9
  9.9 1.3 copy-start.11
  11.2 12.8 %collective-permute-start.2 = (bf16[17,32,320]{2,1,0:T(8,128)(2,1)}, bf16[17,32,320]{2,1,0:T(8,128)(2,1)}, u32[]{:S(2)}, u32[]{:S(2)}) collective-permute-start(bf16[17,32,320]{2,1,0:T(8,128)(2,1)} %bitcast.8), channel_id=1, source_target_pairs={{0,1},{1,0},{2,3},{3,2},{4,5},{5,4},{6,7},{7,6},{8,9},{9,8},{10,11... | collective-permute-start | bytes 1044488 | tf_op jit(solution)/shard_map/ppermute | solution.py:338
  12.6 20.3 %copy-start.1 = (bf16[3,3,320,320]{3,2,1,0:T(8,128)(2,1)S(1)}, bf16[3,3,320,320]{3,2,1,0:T(8,128)(2,1)}, u32[]{:S(2)}) copy-start(bf16[3,3,320,320]{3,2,1,0:T(8,128)(2,1)} %param.6) | copy-start | bytes 5529604
  12.6 20.3 %copy-start.6 = (bf16[3,192,256]{2,1,0:T(8,128)(2,1)S(1)}, bf16[3,192,256]{2,1,0:T(8,128)(2,1)}, u32[]{:S(2)}) copy-start(bf16[3,192,256]{2,1,0:T(8,128)(2,1)} %copy-done.5) | copy-start | bytes 884740
  12.6 20.3 %collective-permute-start = (bf16[17,32,320]{2,1,0:T(8,128)(2,1)S(1)}, bf16[17,32,320]{2,1,0:T(8,128)(2,1)S(1)}, u32[]{:S(2)}, u32[]{:S(2)}) collective-permute-start(bf16[17,32,320]{2,1,0:T(8,128)(2,1)S(1)} %bitcast.64), channel_id=1, source_target_pairs={{0,1},{1,0},{2,3},{3,2},{4,5},{5,4},{6,7},{7,6},{8,9},{9,8},{10,11... | collective-permute-start | bytes 1044488 | tf_op jit(solution)/shard_map/ppermute | solution.py:338
  14.4 21.7 %collective-permute-start.3 = (bf16[16,32,320]{2,1,0:T(8,128)(2,1)}, bf16[16,32,320]{2,1,0:T(8,128)(2,1)S(1)}, u32[]{:S(2)}, u32[]{:S(2)}) collective-permute-start(bf16[16,32,320]{2,1,0:T(8,128)(2,1)} %bitcast.46), channel_id=1, source_target_pairs={{1,3},{2,0},{3,5},{4,2},{5,7},{6,4},{7,9},{8,6},{9,11},{10,8},{11,... | collective-permute-start | bytes 983048 | tf_op jit(solution)/shard_map/ppermute | solution.py:338
  24.0 16.6 %collective-permute-start.7 = (bf16[16,32,320]{2,1,0:T(8,128)(2,1)S(1)}, bf16[16,32,320]{2,1,0:T(8,128)(2,1)S(1)}, u32[]{:S(2)}, u32[]{:S(2)}) collective-permute-start(bf16[16,32,320]{2,1,0:T(8,128)(2,1)S(1)} %bitcast.62), channel_id=1, source_target_pairs={{0,1},{1,0},{2,3},{3,2},{4,5},{5,4},{6,7},{7,6},{8,9},{9,8},{10,11... | collective-permute-start | bytes 983048 | tf_op jit(solution)/shard_map/ppermute | solution.py:338
  34.8 12.5 %collective-permute-start.1 = (bf16[16,32,320]{2,1,0:T(8,128)(2,1)S(1)}, bf16[16,32,320]{2,1,0:T(8,128)(2,1)S(1)}, u32[]{:S(2)}, u32[]{:S(2)}) collective-permute-start(bf16[16,32,320]{2,1,0:T(8,128)(2,1)S(1)} %bitcast.47), channel_id=1, source_target_pairs={{0,2},{2,4},{3,1},{4,6},{5,3},{6,8},{7,5},{8,10},{9,7},{10,12},{11... | collective-permute-start | bytes 983048 | tf_op jit(solution)/shard_map/ppermute | solution.py:338
  36.1 19.2 %collective-permute-start.10 = (bf16[16,32,320]{2,1,0:T(8,128)(2,1)S(1)}, bf16[16,32,320]{2,1,0:T(8,128)(2,1)S(1)}, u32[]{:S(2)}, u32[]{:S(2)}) collective-permute-start(bf16[16,32,320]{2,1,0:T(8,128)(2,1)S(1)} %bitcast.38), channel_id=1, source_target_pairs={{1,3},{2,0},{3,5},{4,2},{5,7},{6,4},{7,9},{8,6},{9,11},{10,8},{11,... | collective-permute-start | bytes 983048 | tf_op jit(solution)/shard_map/ppermute | solution.py:338
  40.7 6.6 %copy-start.8 = (bf16[512,320]{1,0:T(8,128)(2,1)S(1)}, bf16[512,320]{1,0:T(8,128)(2,1)}, u32[]{:S(2)}) copy-start(bf16[512,320]{1,0:T(8,128)(2,1)} %copy-done.7) | copy-start | bytes 983044
  40.7 6.6 %copy-start.10 = (bf16[512,320]{1,0:T(8,128)(2,1)S(1)}, bf16[512,320]{1,0:T(8,128)(2,1)}, u32[]{:S(2)}) copy-start(bf16[512,320]{1,0:T(8,128)(2,1)} %copy-done.9) | copy-start | bytes 983044
  40.7 14.6 %collective-permute-start.9 = (bf16[16,32,320]{2,1,0:T(8,128)(2,1)S(1)}, bf16[16,32,320]{2,1,0:T(8,128)(2,1)S(1)}, u32[]{:S(2)}, u32[]{:S(2)}) collective-permute-start(bf16[16,32,320]{2,1,0:T(8,128)(2,1)S(1)} %bitcast.55), channel_id=1, source_target_pairs={{0,1},{1,0},{2,3},{3,2},{4,5},{5,4},{6,7},{7,6},{8,9},{9,8},{10,11... | collective-permute-start | bytes 983048 | tf_op jit(solution)/shard_map/ppermute | solution.py:338
  40.8 14.5 %collective-permute-start.8 = (bf16[16,32,320]{2,1,0:T(8,128)(2,1)S(1)}, bf16[16,32,320]{2,1,0:T(8,128)(2,1)S(1)}, u32[]{:S(2)}, u32[]{:S(2)}) collective-permute-start(bf16[16,32,320]{2,1,0:T(8,128)(2,1)S(1)} %collective-permute-done.7), channel_id=1, source_target_pairs={{0,2},{2,4},{3,1},{4,6},{5,3},{6,8},{7,5},{8,10},{9,7},{10,12},{11... | collective-permute-start | bytes 983048 | tf_op jit(solution)/shard_map/ppermute | solution.py:338
  50.5 14.1 %collective-permute-start.5 = (bf16[16,32,320]{2,1,0:T(8,128)(2,1)S(1)}, bf16[16,32,320]{2,1,0:T(8,128)(2,1)S(1)}, u32[]{:S(2)}, u32[]{:S(2)}) collective-permute-start(bf16[16,32,320]{2,1,0:T(8,128)(2,1)S(1)} %bitcast.60), channel_id=1, source_target_pairs={{1,3},{2,0},{3,5},{4,2},{5,7},{6,4},{7,9},{8,6},{9,11},{10,8},{11,... | collective-permute-start | bytes 983048 | tf_op jit(solution)/shard_map/ppermute | solution.py:338
  53.8 10.8 %collective-permute-start.4 = (bf16[16,32,320]{2,1,0:T(8,128)(2,1)S(1)}, bf16[16,32,320]{2,1,0:T(8,128)(2,1)S(1)}, u32[]{:S(2)}, u32[]{:S(2)}) collective-permute-start(bf16[16,32,320]{2,1,0:T(8,128)(2,1)S(1)} %bitcast.58), channel_id=1, source_target_pairs={{0,2},{2,4},{3,1},{4,6},{5,3},{6,8},{7,5},{8,10},{9,7},{10,12},{11... | collective-permute-start | bytes 983048 | tf_op jit(solution)/shard_map/ppermute | solution.py:338
  58.7 12.9 %collective-permute-start.12 = (bf16[16,32,320]{2,1,0:T(8,128)(2,1)S(1)}, bf16[16,32,320]{2,1,0:T(8,128)(2,1)S(1)}, u32[]{:S(2)}, u32[]{:S(2)}) collective-permute-start(bf16[16,32,320]{2,1,0:T(8,128)(2,1)S(1)} %bitcast.61), channel_id=1, source_target_pairs={{1,3},{2,0},{3,5},{4,2},{5,7},{6,4},{7,9},{8,6},{9,11},{10,8},{11,... | collective-permute-start | bytes 983048 | tf_op jit(solution)/shard_map/ppermute | solution.py:338
  63.3 9.7 %collective-permute-start.11 = (bf16[16,32,320]{2,1,0:T(8,128)(2,1)S(1)}, bf16[16,32,320]{2,1,0:T(8,128)(2,1)S(1)}, u32[]{:S(2)}, u32[]{:S(2)}) collective-permute-start(bf16[16,32,320]{2,1,0:T(8,128)(2,1)S(1)} %bitcast.59), channel_id=1, source_target_pairs={{0,2},{2,4},{3,1},{4,6},{5,3},{6,8},{7,5},{8,10},{9,7},{10,12},{11... | collective-permute-start | bytes 983048 | tf_op jit(solution)/shard_map/ppermute | solution.py:338
  67.9 3.7 %copy-start.13 = (bf16[1024,320]{1,0:T(8,128)(2,1)}, bf16[1024,320]{1,0:T(8,128)(2,1)S(1)}, u32[]{:S(2)}) copy-start(bf16[1024,320]{1,0:T(8,128)(2,1)S(1)} %get-tuple-element.55) | copy-start | bytes 1966084
  67.9 5.1 %copy-start.12 = (bf16[2,4,512,240]{3,2,1,0:T(8,128)(2,1)S(1)}, bf16[2,4,512,240]{3,2,1,0:T(8,128)(2,1)}, u32[]{:S(2)}) copy-start(bf16[2,4,512,240]{3,2,1,0:T(8,128)(2,1)} %copy-done.11) | copy-start | bytes 5898244
  80.3 3.6 %collective-permute-start.13 = (bf16[2,5,320,240]{3,2,1,0:T(8,128)(2,1)S(1)}, bf16[2,5,320,240]{3,2,1,0:T(8,128)(2,1)S(1)}, u32[]{:S(2)}, u32[]{:S(2)}) collective-permute-start(bf16[2,5,320,240]{3,2,1,0:T(8,128)(2,1)S(1)} %get-tuple-element.74), channel_id=1, source_target_pairs={{0,32},{32,0},{64,96},{96,64},{1,33},{33,1},{65,97},{97,65},{2,34}... | collective-permute-start | bytes 4608008 | tf_op jit(solution)/shard_map/ppermute | solution.py:338
  86.4 18.0 %copy-start.14 = (bf16[1024,320]{1,0:T(8,128)(2,1)S(1)}, bf16[1024,320]{1,0:T(8,128)(2,1)}, u32[]{:S(2)}) copy-start(bf16[1024,320]{1,0:T(8,128)(2,1)} %copy-done.13) | copy-start | bytes 1966084
  86.4 57.6 %all-to-all-start = ((bf16[64,50,240]{2,1,0:T(8,128)(2,1)}), bf16[64,50,240]{2,1,0:T(8,128)(2,1)S(1)}, u32[]{:S(2)}, u32[]{:S(2)}) async-start(bf16[64,50,240]{2,1,0:T(8,128)(2,1)} %shard_map.77), calls=%async_computation | async-start | bytes 3670016 | tf_op jit(solution)/shard_map/all_to_all | solution.py:425
  104.4 37.9 %collective-permute-start.6 = (bf16[32,32,320]{2,1,0:T(8,128)(2,1)S(1)}, bf16[32,32,320]{2,1,0:T(8,128)(2,1)S(1)}, u32[]{:S(2)}, u32[]{:S(2)}) collective-permute-start(bf16[32,32,320]{2,1,0:T(8,128)(2,1)S(1)} %bitcast.54), channel_id=1, source_target_pairs={{0,1},{1,0},{2,3},{3,2},{4,5},{5,4},{6,7},{7,6},{8,9},{9,8},{10,11... | collective-permute-start | bytes 1966088 | tf_op jit(solution)/shard_map/ppermute | solution.py:338

commit v4 on v3

--- a/solution.py
+++ b/solution.py
@@ -77,19 +77,20 @@
     return ref.at[pl.ds(n * PX, PX), :]
 
 
-def run(kernel, outs, args, scratch=(), copies=0, flops=0, far=(), far_outs=False, limit=VMEM_BYTES):
+def run(kernel, outs, args, scratch=(), copies=0, flops=0, far=(), far_outs=False, out_kind=None):
     nbytes = sum(a.size * a.dtype.itemsize for a in args) + sum(
         functools.reduce(lambda m, n: m * n, s, 2) for s in outs
     )
+    kind = BF if out_kind is None else out_kind
     return pl.pallas_call(
         kernel,
-        out_shape=[jax.ShapeDtypeStruct(s, BF) for s in outs],
+        out_shape=[jax.ShapeDtypeStruct(s, kind) for s in outs],
         in_specs=[SM] + [HBM if n in far else VM for n in range(1, len(args))],
         out_specs=[HBM if far_outs else VM] * len(outs),
         scratch_shapes=[s if not isinstance(s, tuple) else pltpu.VMEM(s, BF) for s in scratch]
         + ([pltpu.SemaphoreType.DMA((copies,))] if copies else []),
         cost_estimate=pl.CostEstimate(flops=flops, bytes_accessed=nbytes, transcendentals=0),
-        compiler_params=pltpu.CompilerParams(vmem_limit_bytes=limit),
+        compiler_params=pltpu.CompilerParams(vmem_limit_bytes=VMEM_BYTES),
     )(*args)
 
 
@@ -289,20 +290,28 @@
                 out[half, 3 + layer] = passing[b, layer]
 
 
-def pack(at, kept, got, out, wide, rows, vout, sems):
+def pack(at, kept, got, out, wide, rows):
     halves, taps, channels, _ = kept.shape
-    owners = out.shape[0] // halves
+    owners = out.shape[0]
     count = channels // owners
-    move = Mover(sems)
     for h in range(halves):
         for t in range(taps):
             rows[...] = kept[h, t].astype(F32) + got[h, t].astype(F32)
             for owner in range(owners):
-                wide[owner, pl.ds(count * t, count), :] = rows[pl.ds(count * owner, count), :]
-        for owner in range(owners):
-            vout[owners * h + owner] = wide[owner].astype(BF)
-        move.put(vout.at[pl.ds(owners * h, owners)], out.at[pl.ds(owners * h, owners)])
-    move.finish()
+                block = pl.ds(count * (taps * h + t), count)
+                wide[owner, block, :] = rows[pl.ds(count * owner, count), :]
+    for owner in range(owners):
+        out[owner] = wide[owner].astype(BF)
+
+
+def gather_parts(at, parts, mine, theirs):
+    total = parts[0].astype(F32)
+    for n in range(1, parts.shape[0]):
+        total = total + parts[n].astype(F32)
+    count = mine.shape[0]
+    upper = at[2] == 1
+    mine[...] = jnp.where(upper, total[count:], total[:count])
+    theirs[...] = jnp.where(upper, total[:count], total[count:])
 
 
 def place(at, own, got, out, sems):
@@ -323,7 +332,7 @@
     owners, clips = lax.axis_size("frame"), lax.axis_size("clip")
     odd = lax.axis_index("frame") % 2
     core = lax.axis_index("clip") % 2
-    at = jnp.stack([odd, core]).astype(jnp.int32)
+    at = jnp.stack([odd, core, lax.axis_index("clip") // 2]).astype(jnp.int32)
     swap = [(n, n ^ 1) for n in range(owners)]
     outer = [(n, n - 2 if n % 2 == 0 else n + 2) for n in range(owners)]
     outer = [(a, b) for a, b in outer if 0 <= b < owners]
@@ -411,21 +420,14 @@
     (out,) = run(place, [(2, FULL, C)], (at, own, returned), (), 4, 1000, far_outs=True)
 
     rows = C // owners
-    block = (2 * owners, 5 * rows, 3 * WIDTH)
+    block = (owners, 10 * rows, 3 * WIDTH)
     (packs,) = run(
-        pack,
-        [block],
-        (at, kept, got),
-        [pltpu.VMEM((owners, 5 * rows, 3 * WIDTH), F32), pltpu.VMEM((C, 3 * WIDTH), F32), block],
-        4,
-        1000,
-        far_outs=True,
-    )
-    groups = [[n + half * 2 + c for half in range(2) for n in range(0, owners * clips, clips)] for c in range(2)]
-    parts = lax.all_to_all(
-        packs, ("frame", "clip"), split_axis=0, concat_axis=0, axis_index_groups=groups, tiled=True
-    )
-    total = jnp.sum(parts.astype(F32), axis=0).reshape(5, rows, 3, WIDTH)
+        pack, [block], (at, kept, got), [pltpu.VMEM(block, F32), pltpu.VMEM((C, 3 * WIDTH), F32)], flops=1000
+    )
+    parts = lax.all_to_all(packs, "frame", split_axis=0, concat_axis=0, tiled=True)
+    mine, theirs = run(gather_parts, [(5 * rows, 3 * WIDTH)] * 2, (at, parts), flops=1000, out_kind=F32)
+    halves = [(n, n ^ 2) for n in range(clips)]
+    total = (mine + send(theirs, halves, "clip")).reshape(5, rows, 3, WIDTH)
     grad_spatial = total[:3].transpose(1, 2, 0, 3)
     grad_temporal = total[3:].transpose(1, 0, 2, 3)
     return (out.reshape(clips_in.shape), grad_spatial, grad_temporal)

time: 147 us -> 146 us (level)
  waiting for transfers between devices: 58.4 us -> 55.1 us
    ppermute x14 -> x15, waiting for transfers between devices: 58.4 us -> 31.7 us  [send(): return lax.ppermute(value, axis, perm).reshape(shape)]
    all_to_all x1, waiting for transfers between devices: 0.01 us -> 23.4 us  [step(): lax.all_to_all(packs, 'frame', split_axis=0, concat_axis=0, tiled=True)]
    ppermute x14 -> x15, starting transfers between devices: 24.4 us -> 26.6 us  [send(): return lax.ppermute(value, axis, perm).reshape(shape)]
    all_to_all x1, starting transfers between devices: 18 us -> 16 us  [step(): lax.all_to_all(packs, 'frame', split_axis=0, concat_axis=0, tiled=True)]
    pallas_call x11 -> x12, Pallas kernels: 34.4 us -> 35.5 us  [run(): pl.pallas_call(kernel, out_shape=[jax.ShapeDtypeStruct(s, kind) for s in...]
    unnamed x32 -> x29, local copies, waits for them, and re-layouts: 7.91 us -> 7.25 us
  transfers between devices with their start and end apart: 15 -> 16, of which waited for: 6 -> 8; matrix products, arithmetic and copies ran while one was open for 1% -> 1% of each run, Pallas kernels for 14% -> 15%
where the time goes in v4:
time: 146 us; the launch traced here: 143 us
  waiting for transfers between devices  55.1 us (38%)
  starting transfers between devices  42.6 us (29%)
  Pallas kernels  35.5 us (24%)
  local copies, waits for them, and re-layouts  9.12 us (6%)
    pallas_call x12, Pallas kernels, run(): pl.pallas_call(kernel, out_shape=[jax.ShapeDtypeStruct(s, kind) for s in...  35.5 us
    ppermute x15, waiting for transfers between devices, send(): return lax.ppermute(value, axis, perm).reshape(shape)  31.7 us
    ppermute x15, starting transfers between devices, send(): return lax.ppermute(value, axis, perm).reshape(shape)  26.6 us
    all_to_all x1, waiting for transfers between devices, step(): lax.all_to_all(packs, 'frame', split_axis=0, concat_axis=0, tiled=True)  23.4 us
    all_to_all x1, starting transfers between devices, step(): lax.all_to_all(packs, 'frame', split_axis=0, concat_axis=0, tiled=True)  16 us
    unnamed x29, local copies, waits for them, and re-layouts  7.25 us
  transfers between devices with their start and end apart: 16, of which 8 were waited for; matrix products, arithmetic and copies ran while one was open for 1% of the time, Pallas kernels for 15%

profile of v4, /device:TPU:8, one launch (start us, length us, event | category | flops | bytes accessed | tf_op | source)
XLA Modules:
  0.0 143.3 jit_solution(15007263617880241652)
XLA Ops:
  0.7 0.1 pad_add_fusion.at
  0.7 1.6 %copy-done = bf16[3,3,320,320]{3,2,1,0:T(8,128)(2,1)S(1)} copy-done((bf16[3,3,320,320]{3,2,1,0:T(8,128)(2,1)S(1)}, bf16[3,3,320,320]{3,2,1,0:T(8,128)(2,1)}, u32[]{:S(2)}) %copy-start) | copy-done | bytes 1843224
  2.4 1.4 copy-done.2
  3.8 3.9 %shard_map.67 = (bf16[512,320]{1,0:T(8,128)(2,1)S(1)}, bf16[512,320]{1,0:T(8,128)(2,1)S(1)}, bf16[2,4,512,240]{3,2,1,0:T(8,128)(2,1)S(1)}, bf16[544,320]{1,0:T(8...) custom-call(s32[3]{0:T(128)S(1)} %pad_add_fusion.at, ...), custom_call_target="tpu_custom_call" | custom-call | flops 838860800 | bytes 6787084 | tf_op jit(solution)/shard_map/pallas_call | solution.py:85
  7.7 0.7 copy-done.5
  8.4 0.7 copy-done.7
  9.1 0.7 copy-done.9
  9.9 1.4 copy-done.11
  11.2 0.3 collective-permute-start.2
  11.6 1.0 constant_dynamic-slice_fusion
  12.6 1.8 %collective-permute-start = (bf16[17,32,320]{2,1,0:T(8,128)(2,1)S(1)}, bf16[17,32,320]{2,1,0:T(8,128)(2,1)S(1)}, u32[]{:S(2)}, u32[]{:S(2)}) collective-permute-start(bf16[17,32,320]{2,1,0:T(8,128)(2,1)S(1)} %bitcast.67), channel_id=1, source_target_pairs={{0,1},{1,0},{2,3},{3,2},{4,5},{5,4},{6,7},{7,6},{8,9},{9,8},{10,11... | collective-permute-start | bytes 1044488 | tf_op jit(solution)/shard_map/ppermute | solution.py:347
  14.4 3.4 %collective-permute-start.3 = (bf16[16,32,320]{2,1,0:T(8,128)(2,1)}, bf16[16,32,320]{2,1,0:T(8,128)(2,1)S(1)}, u32[]{:S(2)}, u32[]{:S(2)}) collective-permute-start(bf16[16,32,320]{2,1,0:T(8,128)(2,1)} %bitcast.49), channel_id=1, source_target_pairs={{1,3},{2,0},{3,5},{4,2},{5,7},{6,4},{7,9},{8,6},{9,11},{10,8},{11,... | collective-permute-start | bytes 983048 | tf_op jit(solution)/shard_map/ppermute | solution.py:347
  17.8 1.2 shard_map.70
  19.0 5.0 %collective-permute-done.2 = bf16[17,32,320]{2,1,0:T(8,128)(2,1)} collective-permute-done((bf16[17,32,320]{2,1,0:T(8,128)(2,1)}, bf16[17,32,320]{2,1,0:T(8,128)(2,1)}, u32[]{:S(2)}, u32[]{:S(2)}) %collective-permute-start.2) | collective-permute-done | bytes 348192 | tf_op jit(solution)/shard_map/ppermute | solution.py:347
  24.0 0.3 collective-permute-start.7
  24.4 8.5 %collective-permute-done = bf16[17,32,320]{2,1,0:T(8,128)(2,1)S(1)} collective-permute-done((bf16[17,32,320]{2,1,0:T(8,128)(2,1)S(1)}, bf16[17,32,320]{2,1,0:T(8,128)(2,1)S(1)}, u32[]{:S(2)}, u32[]{:S(2)}) %collective-permute-start) | collective-permute-done | bytes 348192 | tf_op jit(solution)/shard_map/ppermute | solution.py:347
  32.9 1.9 %shard_map.68 = (bf16[512,320]{1,0:T(8,128)(2,1)S(1)}, bf16[4,512,240]{2,1,0:T(8,128)(2,1)S(1)}) custom-call(s32[3]{0:T(128)S(1)} %pad_add_fusion.at, bf16[544,320]{1,0:T(8,128)(2,1)S(1)} %bitcast.48, bf16[9,320,320]{2,1,0:T(8,128)(2,1)S(1)} %bitcast.37, bf16[3,256,192]{2,1,0:T(8,128)(2,1)S(1)} %get-tuple-element.41.wn, bf16[3,192,256]{2,1,0:T(8,128)(2,1)S(1)} %copy-done.6, ...), custom_call_target="tpu_custom_call" | custom-call | flops 419430400 | bytes 4165644 | tf_op jit(solution)/shard_map/pallas_call | solution.py:85
  34.8 1.3 collective-permute-start.1
  36.1 4.6 %collective-permute-start.10 = (bf16[16,32,320]{2,1,0:T(8,128)(2,1)S(1)}, bf16[16,32,320]{2,1,0:T(8,128)(2,1)S(1)}, u32[]{:S(2)}, u32[]{:S(2)}) collective-permute-start(bf16[16,32,320]{2,1,0:T(8,128)(2,1)S(1)} %bitcast.41), channel_id=1, source_target_pairs={{1,3},{2,0},{3,5},{4,2},{5,7},{6,4},{7,9},{8,6},{9,11},{10,8},{11,... | collective-permute-start | bytes 983048 | tf_op jit(solution)/shard_map/ppermute | solution.py:347
  40.7 0.1 collective-permute-start.9
  40.8 1.4 collective-permute-start.8
  42.2 2.4 %shard_map.69 = (bf16[512,320]{1,0:T(8,128)(2,1)S(1)}, bf16[4,512,240]{2,1,0:T(8,128)(2,1)S(1)}) custom-call(s32[3]{0:T(128)S(1)} %pad_add_fusion.at, bf16[544,320]{1,0:T(8,128)(2,1)} %bitcast.10.x, bf16[9,320,320]{2,1,0:T(8,128)(2,1)S(1)} %bitcast.38, bf16[3,256,192]{2,1,0:T(8,128)(2,1)S(1)} %get-tuple-element.41.wn, bf16[3,192,256]{2,1,0:T(8,128)(2,1)S(1)} %copy-done.6, ...), custom_call_target="tpu_custom_call" | custom-call | flops 419430400 | bytes 4165644 | tf_op jit(solution)/shard_map/pallas_call | solution.py:85
  44.6 2.7 %collective-permute-done.1 = bf16[16,32,320]{2,1,0:T(8,128)(2,1)S(1)} collective-permute-done((bf16[16,32,320]{2,1,0:T(8,128)(2,1)S(1)}, bf16[16,32,320]{2,1,0:T(8,128)(2,1)S(1)}, u32[]{:S(2)}, u32[]{:S(2)}) %collective-permute-start.1) | collective-permute-done | bytes 327712 | tf_op jit(solution)/shard_map/ppermute | solution.py:347
  47.3 3.2 %shard_map.71 = (bf16[6,512,320]{2,1,0:T(8,128)(2,1)S(1)}, bf16[4,512,320]{2,1,0:T(8,128)(2,1)S(1)}, bf16[512,320]{1,0:T(8,128)(2,1)S(1)}, bf16[512,320]{1,0:T(8,128)(2,1)S(1)}) custom-call(s32[3]{0:T(128)S(1)} %pad_add_fusion.at, bf16[512,320]{1,0:T(8,128)(2,1)S(1)} %bitcast.56, bf16[512,320]{1,0:T(8,128)(2,1)S(1)} %copy-done.8, ...), custom_call_target="tpu_custom_call" | custom-call | flops 838860800 | bytes 7372812 | tf_op jit(solution)/shard_map/pallas_call | solution.py:85
  50.6 3.2 %collective-permute-start.5 = (bf16[16,32,320]{2,1,0:T(8,128)(2,1)S(1)}, bf16[16,32,320]{2,1,0:T(8,128)(2,1)S(1)}, u32[]{:S(2)}, u32[]{:S(2)}) collective-permute-start(bf16[16,32,320]{2,1,0:T(8,128)(2,1)S(1)} %bitcast.63), channel_id=1, source_target_pairs={{1,3},{2,0},{3,5},{4,2},{5,7},{6,4},{7,9},{8,6},{9,11},{10,8},{11,... | collective-permute-start | bytes 983048 | tf_op jit(solution)/shard_map/ppermute | solution.py:347
  53.8 1.5 %collective-permute-start.4 = (bf16[16,32,320]{2,1,0:T(8,128)(2,1)S(1)}, bf16[16,32,320]{2,1,0:T(8,128)(2,1)S(1)}, u32[]{:S(2)}, u32[]{:S(2)}) collective-permute-start(bf16[16,32,320]{2,1,0:T(8,128)(2,1)S(1)} %bitcast.61), channel_id=1, source_target_pairs={{0,2},{2,4},{3,1},{4,6},{5,3},{6,8},{7,5},{8,10},{9,7},{10,12},{11... | collective-permute-start | bytes 983048 | tf_op jit(solution)/shard_map/ppermute | solution.py:347
  55.3 3.4 %shard_map.74 = (bf16[4,512,320]{2,1,0:T(8,128)(2,1)S(1)}, bf16[512,320]{1,0:T(8,128)(2,1)S(1)}, bf16[512,320]{1,0:T(8,128)(2,1)S(1)}) custom-call(s32[3]{0:T(128)S(1)} %pad_add_fusion.at, bf16[512,320]{1,0:T(8,128)(2,1)S(1)} %bitcast.54, bf16[512,320]{1,0:T(8,128)(2,1)S(1)} %get-tuple-element.64.cot0, bf16[512,320]{1,0:T(8,128)(2,1)S(1)} %get-tuple-element.61.cot1, ...), custom_call_target="tpu_custom_call" | custom-call | flops 838860800 | bytes 6717452 | tf_op jit(solution)/shard_map/pallas_call | solution.py:85
  58.8 4.6 %collective-permute-start.12 = (bf16[16,32,320]{2,1,0:T(8,128)(2,1)S(1)}, bf16[16,32,320]{2,1,0:T(8,128)(2,1)S(1)}, u32[]{:S(2)}, u32[]{:S(2)}) collective-permute-start(bf16[16,32,320]{2,1,0:T(8,128)(2,1)S(1)} %bitcast.64), channel_id=1, source_target_pairs={{1,3},{2,0},{3,5},{4,2},{5,7},{6,4},{7,9},{8,6},{9,11},{10,8},{11,... | collective-permute-start | bytes 983048 | tf_op jit(solution)/shard_map/ppermute | solution.py:347
  63.3 1.3 collective-permute-start.11
  64.7 3.2 %shard_map.72 = (bf16[6,512,320]{2,1,0:T(8,128)(2,1)S(1)}, bf16[2,512,320]{2,1,0:T(8,128)(2,1)S(1)}, bf16[1024,320]{1,0:T(8,128)(2,1)S(1)}) custom-call(s32[3]{0:T(128)S(1)} %pad_add_fusion.at, bf16[512,320]{1,0:T(8,128)(2,1)S(1)} %bitcast.55, bf16[4,512,320]{2,1,0:T(8,128)(2,1)S(1)} %get-tuple-element.54.state, bf16[512,320]{1,0:T(8,128)(2,1)S(1)} %bitcast.53, ...), custom_call_target="tpu_custom_call" | custom-call | flops 838860800 | bytes 6717452 | tf_op jit(solution)/shard_map/pallas_call | solution.py:85
  67.9 3.7 %shard_map.75.passing = bf16[4,2,320,240]{3,2,1,0:T(8,128)(2,1)S(1)} custom-call(s32[3]{0:T(128)S(1)} %pad_add_fusion.at, bf16[512,320]{1,0:T(8,128)(2,1)S(1)} %get-tuple-element.64.cot0, bf16[512,320]{1,0:T(8,128)(2,1)S(1)} %get-tuple-element.61.cot1, bf16[512,320]{1,0:T(8,128)(2,1)S(1)} %bitcast.45, bf16[512,320]{1,0:T(8,128)(2,1)S(1)} %bitcast.43, ...), custom_call_target="tpu_custom_call" | custom-call | flops 1677721600 | bytes 7782412 | tf_op jit(solution)/shard_map/pallas_call | solution.py:85
  71.6 1.4 collective-permute-done.11
  73.0 7.3 %shard_map.76 = (bf16[2,5,320,240]{3,2,1,0:T(8,128)(2,1)S(1)}, bf16[2,5,320,240]{3,2,1,0:T(8,128)(2,1)S(1)}) custom-call(s32[3]{0:T(128)S(1)} %pad_add_fusion.at, bf16[512,320]{1,0:T(8,128)(2,1)S(1)} %bitcast.60, bf16[4,512,320]{2,1,0:T(8,128)(2,1)S(1)} %get-tuple-element.68.back, bf16[512,320]{1,0:T(8,128)(2,1)S(1)} %bitcast.59, ...), custom_call_target="tpu_custom_call" | custom-call | flops 3355443200 | bytes 12984332 | tf_op jit(solution)/shard_map/pallas_call | solution.py:85
  80.3 0.1 collective-permute-start.13
  80.4 3.5 %collective-permute-done.13.got = bf16[2,5,320,240]{3,2,1,0:T(8,128)(2,1)S(1)} collective-permute-done((bf16[2,5,320,240]{3,2,1,0:T(8,128)(2,1)S(1)}, bf16[2,5,320,240]{3,2,1,0:T(8,128)(2,1)S(1)}, u32[]{:S(2)}, u32[]{:S(2)}) %collective-permute-start.13) | collective-permute-done | bytes 1536032 | tf_op jit(solution)/shard_map/ppermute | solution.py:347
  83.9 2.8 %shard_map.77 = bf16[32,100,240]{2,1,0:T(8,128)(2,1)} custom-call(s32[3]{0:T(128)S(1)} %pad_add_fusion.at, bf16[2,5,320,240]{3,2,1,0:T(8,128)(2,1)S(1)} %get-tuple-element.75.kept, bf16[2,5,320,240]{3,2,1,0:T(8,128)(2,1)S(1)} %collective-permute-done.13.got), custom_call_target="tpu_custom_call" | custom-call | flops 1000 | bytes 4608012 | tf_op jit(solution)/shard_map/pallas_call | solution.py:85
  86.7 16.0 %all-to-all-start = ((bf16[32,100,240]{2,1,0:T(8,128)(2,1)}), bf16[32,100,240]{2,1,0:T(8,128)(2,1)S(1)}, u32[]{:S(2)}, u32[]{:S(2)}) async-start(bf16[32,100,240]{2,1,0:T(8,128)(2,1)} %shard_map.77), calls=%async_computation | async-start | bytes 3407872 | tf_op jit(solution)/shard_map/all_to_all | solution.py:427
  102.7 0.3 collective-permute-start.6
  103.0 23.4 %all-to-all-done.parts = bf16[32,100,240]{2,1,0:T(8,128)(2,1)S(1)} async-done(((bf16[32,100,240]{2,1,0:T(8,128)(2,1)}), bf16[32,100,240]{2,1,0:T(8,128)(2,1)S(1)}, u32[]{:S(2)}, u32[]{:S(2)}) %all-to-all-start) | async-done | bytes 1536032 | tf_op jit(solution)/shard_map/all_to_all | solution.py:427
  126.3 0.8 shard_map.78
  127.1 2.4 %collective-permute-start.14 = (f32[50,240]{1,0:T(8,128)S(1)}, f32[50,240]{1,0:T(8,128)S(1)}, u32[]{:S(2)}, u32[]{:S(2)}) collective-permute-start(f32[50,240]{1,0:T(8,128)S(1)} %get-tuple-element.78), channel_id=1, source_target_pairs={{0,64},{32,96},{64,0},{96,32},{1,65},{33,97},{65,1},{97,33},{2,66}... | collective-permute-start | bytes 144008 | tf_op jit(solution)/shard_map/ppermute | solution.py:347
  129.5 9.8 %collective-permute-done.6 = bf16[32,32,320]{2,1,0:T(8,128)(2,1)S(1)} collective-permute-done((bf16[32,32,320]{2,1,0:T(8,128)(2,1)}, bf16[32,32,320]{2,1,0:T(8,128)(2,1)S(1)}, u32[]{:S(2)}, u32[]{:S(2)}) %collective-permute-start.6) | collective-permute-done | bytes 655392 | tf_op jit(solution)/shard_map/ppermute | solution.py:347
  139.3 1.7 %shard_map.73 = bf16[2,1024,320]{2,1,0:T(8,128)(2,1)} custom-call(s32[3]{0:T(128)S(1)} %pad_add_fusion.at, bf16[2,512,320]{2,1,0:T(8,128)(2,1)S(1)} %get-tuple-element.56.own, bf16[1024,320]{1,0:T(8,128)(2,1)S(1)} %bitcast.47), custom_call_target="tpu_custom_call" | custom-call | flops 1000 | bytes 2621452 | tf_op jit(solution)/shard_map/pallas_call | solution.py:85
  141.0 0.8 collective-permute-done.14
  141.9 0.1 slice.15
  142.0 0.6 copy.10
  142.6 0.1 slice.13
  142.7 0.6 copy.12
  (33 shorter events, 0.1 us)
Async XLA Ops:
  0.7 1.6 %copy-start = (bf16[3,3,320,320]{3,2,1,0:T(8,128)(2,1)S(1)}, bf16[3,3,320,320]{3,2,1,0:T(8,128)(2,1)}, u32[]{:S(2)}) copy-start(bf16[3,3,320,320]{3,2,1,0:T(8,128)(2,1)} %param.6) | copy-start | bytes 5529604
  2.4 1.4 copy-start.2
  3.8 14.0 %copy-start.3 = (bf16[1,2,32,32,320]{4,3,2,1,0:T(8,128)(2,1)S(1)}, bf16[1,2,32,32,320]{4,3,2,1,0:T(8,128)(2,1)}, u32[]{:S(2)}) copy-start(bf16[1,2,32,32,320]{4,3,2,1,0:T(8,128)(2,1)} %param.5) | copy-start | bytes 3932164
  3.8 14.1 %copy-start.4 = (bf16[2,3,320,320]{3,2,1,0:T(8,128)(2,1)S(1)}, bf16[2,3,320,320]{3,2,1,0:T(8,128)(2,1)}, u32[]{:S(2)}) copy-start(bf16[2,3,320,320]{3,2,1,0:T(8,128)(2,1)} %tw) | copy-start | bytes 3686404
  7.7 0.7 copy-start.5
  8.4 0.8 copy-start.7
  9.1 0.7 copy-start.9
  9.9 1.4 copy-start.11
  11.2 12.8 %collective-permute-start.2 = (bf16[17,32,320]{2,1,0:T(8,128)(2,1)}, bf16[17,32,320]{2,1,0:T(8,128)(2,1)}, u32[]{:S(2)}, u32[]{:S(2)}) collective-permute-start(bf16[17,32,320]{2,1,0:T(8,128)(2,1)} %bitcast.9), channel_id=1, source_target_pairs={{0,1},{1,0},{2,3},{3,2},{4,5},{5,4},{6,7},{7,6},{8,9},{9,8},{10,11... | collective-permute-start | bytes 1044488 | tf_op jit(solution)/shard_map/ppermute | solution.py:347
  12.6 20.3 %copy-start.1 = (bf16[3,3,320,320]{3,2,1,0:T(8,128)(2,1)S(1)}, bf16[3,3,320,320]{3,2,1,0:T(8,128)(2,1)}, u32[]{:S(2)}) copy-start(bf16[3,3,320,320]{3,2,1,0:T(8,128)(2,1)} %param.6) | copy-start | bytes 5529604
  12.6 20.3 %copy-start.6 = (bf16[3,192,256]{2,1,0:T(8,128)(2,1)S(1)}, bf16[3,192,256]{2,1,0:T(8,128)(2,1)}, u32[]{:S(2)}) copy-start(bf16[3,192,256]{2,1,0:T(8,128)(2,1)} %copy-done.5) | copy-start | bytes 884740
  12.6 20.3 %collective-permute-start = (bf16[17,32,320]{2,1,0:T(8,128)(2,1)S(1)}, bf16[17,32,320]{2,1,0:T(8,128)(2,1)S(1)}, u32[]{:S(2)}, u32[]{:S(2)}) collective-permute-start(bf16[17,32,320]{2,1,0:T(8,128)(2,1)S(1)} %bitcast.67), channel_id=1, source_target_pairs={{0,1},{1,0},{2,3},{3,2},{4,5},{5,4},{6,7},{7,6},{8,9},{9,8},{10,11... | collective-permute-start | bytes 1044488 | tf_op jit(solution)/shard_map/ppermute | solution.py:347
  14.4 21.7 %collective-permute-start.3 = (bf16[16,32,320]{2,1,0:T(8,128)(2,1)}, bf16[16,32,320]{2,1,0:T(8,128)(2,1)S(1)}, u32[]{:S(2)}, u32[]{:S(2)}) collective-permute-start(bf16[16,32,320]{2,1,0:T(8,128)(2,1)} %bitcast.49), channel_id=1, source_target_pairs={{1,3},{2,0},{3,5},{4,2},{5,7},{6,4},{7,9},{8,6},{9,11},{10,8},{11,... | collective-permute-start | bytes 983048 | tf_op jit(solution)/shard_map/ppermute | solution.py:347
  24.0 16.6 %collective-permute-start.7 = (bf16[16,32,320]{2,1,0:T(8,128)(2,1)S(1)}, bf16[16,32,320]{2,1,0:T(8,128)(2,1)S(1)}, u32[]{:S(2)}, u32[]{:S(2)}) collective-permute-start(bf16[16,32,320]{2,1,0:T(8,128)(2,1)S(1)} %bitcast.65), channel_id=1, source_target_pairs={{0,1},{1,0},{2,3},{3,2},{4,5},{5,4},{6,7},{7,6},{8,9},{9,8},{10,11... | collective-permute-start | bytes 983048 | tf_op jit(solution)/shard_map/ppermute | solution.py:347
  34.8 12.5 %collective-permute-start.1 = (bf16[16,32,320]{2,1,0:T(8,128)(2,1)S(1)}, bf16[16,32,320]{2,1,0:T(8,128)(2,1)S(1)}, u32[]{:S(2)}, u32[]{:S(2)}) collective-permute-start(bf16[16,32,320]{2,1,0:T(8,128)(2,1)S(1)} %bitcast.50), channel_id=1, source_target_pairs={{0,2},{2,4},{3,1},{4,6},{5,3},{6,8},{7,5},{8,10},{9,7},{10,12},{11... | collective-permute-start | bytes 983048 | tf_op jit(solution)/shard_map/ppermute | solution.py:347
  36.1 19.2 %collective-permute-start.10 = (bf16[16,32,320]{2,1,0:T(8,128)(2,1)S(1)}, bf16[16,32,320]{2,1,0:T(8,128)(2,1)S(1)}, u32[]{:S(2)}, u32[]{:S(2)}) collective-permute-start(bf16[16,32,320]{2,1,0:T(8,128)(2,1)S(1)} %bitcast.41), channel_id=1, source_target_pairs={{1,3},{2,0},{3,5},{4,2},{5,7},{6,4},{7,9},{8,6},{9,11},{10,8},{11,... | collective-permute-start | bytes 983048 | tf_op jit(solution)/shard_map/ppermute | solution.py:347
  40.7 6.6 %copy-start.8 = (bf16[512,320]{1,0:T(8,128)(2,1)S(1)}, bf16[512,320]{1,0:T(8,128)(2,1)}, u32[]{:S(2)}) copy-start(bf16[512,320]{1,0:T(8,128)(2,1)} %copy-done.7) | copy-start | bytes 983044
  40.7 6.6 %copy-start.10 = (bf16[512,320]{1,0:T(8,128)(2,1)S(1)}, bf16[512,320]{1,0:T(8,128)(2,1)}, u32[]{:S(2)}) copy-start(bf16[512,320]{1,0:T(8,128)(2,1)} %copy-done.9) | copy-start | bytes 983044
  40.7 14.6 %collective-permute-start.9 = (bf16[16,32,320]{2,1,0:T(8,128)(2,1)S(1)}, bf16[16,32,320]{2,1,0:T(8,128)(2,1)S(1)}, u32[]{:S(2)}, u32[]{:S(2)}) collective-permute-start(bf16[16,32,320]{2,1,0:T(8,128)(2,1)S(1)} %bitcast.58), channel_id=1, source_target_pairs={{0,1},{1,0},{2,3},{3,2},{4,5},{5,4},{6,7},{7,6},{8,9},{9,8},{10,11... | collective-permute-start | bytes 983048 | tf_op jit(solution)/shard_map/ppermute | solution.py:347
  40.8 14.5 %collective-permute-start.8 = (bf16[16,32,320]{2,1,0:T(8,128)(2,1)S(1)}, bf16[16,32,320]{2,1,0:T(8,128)(2,1)S(1)}, u32[]{:S(2)}, u32[]{:S(2)}) collective-permute-start(bf16[16,32,320]{2,1,0:T(8,128)(2,1)S(1)} %collective-permute-done.7), channel_id=1, source_target_pairs={{0,2},{2,4},{3,1},{4,6},{5,3},{6,8},{7,5},{8,10},{9,7},{10,12},{11... | collective-permute-start | bytes 983048 | tf_op jit(solution)/shard_map/ppermute | solution.py:347
  50.6 14.1 %collective-permute-start.5 = (bf16[16,32,320]{2,1,0:T(8,128)(2,1)S(1)}, bf16[16,32,320]{2,1,0:T(8,128)(2,1)S(1)}, u32[]{:S(2)}, u32[]{:S(2)}) collective-permute-start(bf16[16,32,320]{2,1,0:T(8,128)(2,1)S(1)} %bitcast.63), channel_id=1, source_target_pairs={{1,3},{2,0},{3,5},{4,2},{5,7},{6,4},{7,9},{8,6},{9,11},{10,8},{11,... | collective-permute-start | bytes 983048 | tf_op jit(solution)/shard_map/ppermute | solution.py:347
  53.8 10.8 %collective-permute-start.4 = (bf16[16,32,320]{2,1,0:T(8,128)(2,1)S(1)}, bf16[16,32,320]{2,1,0:T(8,128)(2,1)S(1)}, u32[]{:S(2)}, u32[]{:S(2)}) collective-permute-start(bf16[16,32,320]{2,1,0:T(8,128)(2,1)S(1)} %bitcast.61), channel_id=1, source_target_pairs={{0,2},{2,4},{3,1},{4,6},{5,3},{6,8},{7,5},{8,10},{9,7},{10,12},{11... | collective-permute-start | bytes 983048 | tf_op jit(solution)/shard_map/ppermute | solution.py:347
  58.8 12.9 %collective-permute-start.12 = (bf16[16,32,320]{2,1,0:T(8,128)(2,1)S(1)}, bf16[16,32,320]{2,1,0:T(8,128)(2,1)S(1)}, u32[]{:S(2)}, u32[]{:S(2)}) collective-permute-start(bf16[16,32,320]{2,1,0:T(8,128)(2,1)S(1)} %bitcast.64), channel_id=1, source_target_pairs={{1,3},{2,0},{3,5},{4,2},{5,7},{6,4},{7,9},{8,6},{9,11},{10,8},{11,... | collective-permute-start | bytes 983048 | tf_op jit(solution)/shard_map/ppermute | solution.py:347
  63.3 9.7 %collective-permute-start.11 = (bf16[16,32,320]{2,1,0:T(8,128)(2,1)S(1)}, bf16[16,32,320]{2,1,0:T(8,128)(2,1)S(1)}, u32[]{:S(2)}, u32[]{:S(2)}) collective-permute-start(bf16[16,32,320]{2,1,0:T(8,128)(2,1)S(1)} %bitcast.62), channel_id=1, source_target_pairs={{0,2},{2,4},{3,1},{4,6},{5,3},{6,8},{7,5},{8,10},{9,7},{10,12},{11... | collective-permute-start | bytes 983048 | tf_op jit(solution)/shard_map/ppermute | solution.py:347
  67.9 3.7 %copy-start.13 = (bf16[1024,320]{1,0:T(8,128)(2,1)}, bf16[1024,320]{1,0:T(8,128)(2,1)S(1)}, u32[]{:S(2)}) copy-start(bf16[1024,320]{1,0:T(8,128)(2,1)S(1)} %get-tuple-element.57) | copy-start | bytes 1966084
  67.9 5.1 %copy-start.12 = (bf16[2,4,512,240]{3,2,1,0:T(8,128)(2,1)S(1)}, bf16[2,4,512,240]{3,2,1,0:T(8,128)(2,1)}, u32[]{:S(2)}) copy-start(bf16[2,4,512,240]{3,2,1,0:T(8,128)(2,1)} %copy-done.11) | copy-start | bytes 5898244
  80.3 3.6 %collective-permute-start.13 = (bf16[2,5,320,240]{3,2,1,0:T(8,128)(2,1)S(1)}, bf16[2,5,320,240]{3,2,1,0:T(8,128)(2,1)S(1)}, u32[]{:S(2)}, u32[]{:S(2)}) collective-permute-start(bf16[2,5,320,240]{3,2,1,0:T(8,128)(2,1)S(1)} %get-tuple-element.76), channel_id=1, source_target_pairs={{0,32},{32,0},{64,96},{96,64},{1,33},{33,1},{65,97},{97,65},{2,34}... | collective-permute-start | bytes 4608008 | tf_op jit(solution)/shard_map/ppermute | solution.py:347
  86.7 39.7 %all-to-all-start = ((bf16[32,100,240]{2,1,0:T(8,128)(2,1)}), bf16[32,100,240]{2,1,0:T(8,128)(2,1)S(1)}, u32[]{:S(2)}, u32[]{:S(2)}) async-start(bf16[32,100,240]{2,1,0:T(8,128)(2,1)} %shard_map.77), calls=%async_computation | async-start | bytes 3407872 | tf_op jit(solution)/shard_map/all_to_all | solution.py:427
  102.7 36.7 %collective-permute-start.6 = (bf16[32,32,320]{2,1,0:T(8,128)(2,1)}, bf16[32,32,320]{2,1,0:T(8,128)(2,1)S(1)}, u32[]{:S(2)}, u32[]{:S(2)}) collective-permute-start(bf16[32,32,320]{2,1,0:T(8,128)(2,1)} %bitcast.57), channel_id=1, source_target_pairs={{0,1},{1,0},{2,3},{3,2},{4,5},{5,4},{6,7},{7,6},{8,9},{9,8},{10,11... | collective-permute-start | bytes 1966088 | tf_op jit(solution)/shard_map/ppermute | solution.py:347
  127.1 14.7 %collective-permute-start.14 = (f32[50,240]{1,0:T(8,128)S(1)}, f32[50,240]{1,0:T(8,128)S(1)}, u32[]{:S(2)}, u32[]{:S(2)}) collective-permute-start(f32[50,240]{1,0:T(8,128)S(1)} %get-tuple-element.78), channel_id=1, source_target_pairs={{0,64},{32,96},{64,0},{96,32},{1,65},{33,97},{65,1},{97,33},{2,66}... | collective-permute-start | bytes 144008 | tf_op jit(solution)/shard_map/ppermute | solution.py:347

commit v5 on v3

--- a/solution.py
+++ b/solution.py
@@ -19,6 +19,7 @@
 HEAD = 256
 TAIL = C - HEAD
 CLIPS = 4
+LANES = 128
 VMEM_BYTES = 24 * 1024 * 1024
 WIDTH = C // CLIPS
 HBM = pl.BlockSpec(memory_space=pltpu.HBM)
@@ -27,7 +28,6 @@
 
 
 ONE = (PX, C)
-TALL_ONE = (TALL, C)
 THREE_TAILS = 3 * TAIL
 SIDES = (CLIPS, PX, 3 * WIDTH)
 KERNELS = (3, C, C)
@@ -77,7 +77,7 @@
     return ref.at[pl.ds(n * PX, PX), :]
 
 
-def run(kernel, outs, args, scratch=(), copies=0, flops=0, far=(), far_outs=False, limit=VMEM_BYTES):
+def run(kernel, outs, args, scratch=(), copies=0, flops=0, far=(), far_outs=False):
     nbytes = sum(a.size * a.dtype.itemsize for a in args) + sum(
         functools.reduce(lambda m, n: m * n, s, 2) for s in outs
     )
@@ -89,7 +89,7 @@
         scratch_shapes=[s if not isinstance(s, tuple) else pltpu.VMEM(s, BF) for s in scratch]
         + ([pltpu.SemaphoreType.DMA((copies,))] if copies else []),
         cost_estimate=pl.CostEstimate(flops=flops, bytes_accessed=nbytes, transcendentals=0),
-        compiler_params=pltpu.CompilerParams(vmem_limit_bytes=limit),
+        compiler_params=pltpu.CompilerParams(vmem_limit_bytes=VMEM_BYTES),
     )(*args)
 
 
@@ -113,6 +113,23 @@
     pad[pl.ds(0, COLS), :] = jnp.zeros((COLS, C), BF)
     pad[pl.ds(TALL, COLS), :] = jnp.zeros((COLS, C), BF)
     return pad.at[pl.ds(pl.multiple_of(COLS * (1 - odd), COLS), TALL), :]
+
+
+def fold(rows, dst):
+    count = rows.shape[0]
+    for n in range(2):
+        dst[pl.ds(n * count, count), :] = rows[:, n * LANES : (n + 1) * LANES]
+    half = count // 2
+    dst[pl.ds(2 * count, half), :] = side(rows[:half, HEAD:], rows[half:, HEAD:])
+
+
+def unfold(src, dst):
+    count = dst.shape[0]
+    for n in range(2):
+        dst[:, pl.ds(n * LANES, LANES)] = src[pl.ds(n * count, count), :]
+    half = count // 2
+    for n in range(2):
+        dst[pl.ds(n * half, half), pl.ds(HEAD, TAIL)] = src[pl.ds(2 * count, half), pl.ds(n * TAIL, TAIL)]
 
 
 def convolve(pad, w, wn, wk, wr, out, sides):
@@ -154,14 +171,14 @@
         padded(pads.at[q], odd)[...] = x[odd + q * (1 - 2 * odd), pl.ds(start, TALL), :]
         convolve(pads.at[q], w, wn, wk, wr, out, sides.at[q])
     away = pl.multiple_of((TALL - 2 * COLS) * (1 - odd), COLS)
-    x2[...] = x[1 - odd, pl.ds(away, TALL), :]
+    fold(x[1 - odd, pl.ds(away, TALL), :], x2)
 
 
 def prepare(at, cot, tw, c3, c2, cot0, cot1, vt, vtk, vb, vbk):
     odd = at[0]
     here, there = pl.multiple_of(PX * odd, PX), pl.multiple_of(PX * (1 - odd), PX)
-    c3[...] = cot[odd, pl.ds(there, PX), :]
-    c2[...] = cot[1 - odd, pl.ds(there, PX), :]
+    fold(cot[odd, pl.ds(there, PX), :], c3)
+    fold(cot[1 - odd, pl.ds(there, PX), :], c2)
     cot0[...] = cot[odd, pl.ds(here, PX), :]
     cot1[...] = cot[1 - odd, pl.ds(here, PX), :]
     for l in range(2):
@@ -179,6 +196,11 @@
     convolve(pad, w, wn, wk, wr, out, sides)
 
 
+def conv_folded(at, x, w, wn, wk, wr, out, sides, pad):
+    unfold(x, padded(pad, at[0]))
+    convolve(pad, w, wn, wk, wr, out, sides)
+
+
 def tap(k, odd):
     return k + odd * (2 - 2 * k)
 
@@ -232,7 +254,10 @@
     return (three[1][...].astype(F32) + carried * (s * (1.0 + v * (1.0 - s)))).astype(BF)
 
 
-def back_one(at, left, cot0, cot1, c2, c3, right, state, vw, wk, back, first, last):
+def back_one(at, folded, cot0, cot1, folded2, folded3, right, state, vw, wk, back, first, last, c2, c3, left):
+    unfold(folded, left)
+    unfold(folded2, c2)
+    unfold(folded3, c3)
     six = (left, cot0, cot1, c2, c3, right)
     for q in range(4):
         value = descend(six, q, state.at[q], vw, 1, wk)
@@ -333,7 +358,7 @@
 
     def send(value, perm, axis="frame"):
         shape = value.shape
-        if axis == "frame":
+        if axis == "frame" and shape[-1] == C:
             value = value.reshape(-1, COLS, C)
         return lax.ppermute(value, axis, perm).reshape(shape)
 
@@ -351,7 +376,7 @@
     x3 = send(lax.dynamic_slice(x, (odd, tall_start, 0), (1, TALL, C))[0], swap)
     s0, s1, own_sides, x2, wn, wk, wr = run(
         conv_own,
-        [ONE, ONE, (2, *SIDES), TALL_ONE, *packed],
+        [ONE, ONE, (2, *SIDES), (TALL * C // LANES, LANES), *packed],
         (at, x, ws),
         [(2, *pad)],
         flops=8 * flops,
@@ -360,13 +385,13 @@
     right = send(s0, outer)
     x2 = send(x2, swap)
     c3, c2, cot0, cot1, vt, vtk, vb, vbk = run(
-        prepare, [ONE] * 4 + taps * 2, (at, after(cot, s0), after(temporal_weight, s0)), flops=flops
+        prepare, [(PX * C // LANES, LANES)] * 2 + [ONE] * 2 + taps * 2, (at, after(cot, s0), after(temporal_weight, s0)), flops=flops
     )
 
     s3, sides3 = run(conv_other, [ONE, SIDES], (at, x3, *wp), [pad], 0, 4 * flops)
     left = send(s3, inner)
     c3 = send(after(c3, x2), swap)
-    s2, sides2 = run(conv_other, [ONE, SIDES], (at, x2, *wp), [pad], 0, 4 * flops)
+    s2, sides2 = run(conv_folded, [ONE, SIDES], (at, x2, *wp), [pad], 0, 4 * flops)
     c2 = send(after(c2, c3), swap)
     cot_right = send(after(cot0, right), outer)
     cot_left = send(c3, inner)
@@ -379,10 +404,11 @@
     )
     left1 = send(last, inner)
     right1 = send(first, outer)
-    back1, first, last = run(
+    back1, first, last, u2, u3 = run(
         back_one,
-        [four, ONE, ONE],
+        [four, ONE, ONE, ONE, ONE],
         (at, cot_left, cot0, cot1, c2, c3, cot_right, state1, vb, vbk),
+        [ONE],
         flops=8 * flops,
     )
     back_left = send(last, inner)
@@ -395,7 +421,7 @@
     (temporal_blocks,) = run(
         temporal_grads,
         [(CLIPS, 2, C, 3 * WIDTH)],
-        (at, cot0, cot1, c2, c3, acts2, back1, acts1),
+        (at, cot0, cot1, u2, u3, acts2, back1, acts1),
         [(C, 4 * PX)],
         flops=16 * flops,
     )
@@ -422,9 +448,7 @@
         far_outs=True,
     )
     groups = [[n + half * 2 + c for half in range(2) for n in range(0, owners * clips, clips)] for c in range(2)]
-    parts = lax.all_to_all(
-        packs, ("frame", "clip"), split_axis=0, concat_axis=0, axis_index_groups=groups, tiled=True
-    )
+    parts = lax.all_to_all(packs, ("frame", "clip"), split_axis=0, concat_axis=0, axis_index_groups=groups, tiled=True)
     total = jnp.sum(parts.astype(F32), axis=0).reshape(5, rows, 3, WIDTH)
     grad_spatial = total[:3].transpose(1, 2, 0, 3)
     grad_temporal = total[3:].transpose(1, 0, 2, 3)

time: 147 us -> 146 us (level)
  no operation moved by 1% of the time
where the time goes in v5:
time: 146 us; the launch traced here: 144 us
  waiting for transfers between devices  58 us (40%)
  starting transfers between devices  41.3 us (28%)
  Pallas kernels  34.5 us (24%)
  local copies, waits for them, and re-layouts  9.14 us (6%)
    ppermute x14, waiting for transfers between devices, send(): return lax.ppermute(value, axis, perm).reshape(shape)  58 us
    pallas_call x11, Pallas kernels, run(): pl.pallas_call(kernel, out_shape=[jax.ShapeDtypeStruct(s, BF) for s in ou...  34.5 us
    ppermute x14, starting transfers between devices, send(): return lax.ppermute(value, axis, perm).reshape(shape)  24.6 us
    all_to_all x1, starting transfers between devices, step(): lax.all_to_all(packs, ('frame', 'clip'), split_axis=0, concat_axis=0, axi...  16.8 us
    unnamed x32, local copies, waits for them, and re-layouts  7.91 us
  transfers between devices with their start and end apart: 15, of which 6 were waited for; matrix products, arithmetic and copies ran while one was open for 1% of the time, Pallas kernels for 14%

profile of v5, /device:TPU:8, one launch (start us, length us, event | category | flops | bytes accessed | tf_op | source)
XLA Modules:
  0.0 144.4 jit_solution(8446648040723052627)
XLA Ops:
  0.6 0.1 pad_add_fusion.at
  0.7 1.6 %copy-done = bf16[3,3,320,320]{3,2,1,0:T(8,128)(2,1)S(1)} copy-done((bf16[3,3,320,320]{3,2,1,0:T(8,128)(2,1)S(1)}, bf16[3,3,320,320]{3,2,1,0:T(8,128)(2,1)}, u32[]{:S(2)}) %copy-start) | copy-done | bytes 1843224
  2.4 1.4 copy-done.2
  3.8 3.9 %shard_map.67 = (bf16[512,320]{1,0:T(8,128)(2,1)S(1)}, bf16[512,320]{1,0:T(8,128)(2,1)S(1)}, bf16[2,4,512,240]{3,2,1,0:T(8,128)(2,1)S(1)}, bf16[1360,128]{1,0:T(...) custom-call(s32[2]{0:T(128)S(1)} %pad_add_fusion.at, ...), custom_call_target="tpu_custom_call" | custom-call | flops 838860800 | bytes 6787080 | tf_op jit(solution)/shard_map/pallas_call | solution.py:84
  7.7 0.7 copy-done.5
  8.4 0.7 copy-done.7
  9.1 0.8 copy-done.9
  9.9 1.3 copy-done.11
  11.3 0.3 collective-permute-start.2
  11.6 1.0 constant_dynamic-slice_fusion
  12.6 0.0 copy-start.1
  12.7 1.8 %collective-permute-start = (bf16[17,32,320]{2,1,0:T(8,128)(2,1)S(1)}, bf16[17,32,320]{2,1,0:T(8,128)(2,1)S(1)}, u32[]{:S(2)}, u32[]{:S(2)}) collective-permute-start(bf16[17,32,320]{2,1,0:T(8,128)(2,1)S(1)} %bitcast.50), channel_id=1, source_target_pairs={{0,1},{1,0},{2,3},{3,2},{4,5},{5,4},{6,7},{7,6},{8,9},{9,8},{10,11... | collective-permute-start | bytes 1044488 | tf_op jit(solution)/shard_map/ppermute | solution.py:363
  14.4 3.4 %collective-permute-start.3 = (bf16[16,32,320]{2,1,0:T(8,128)(2,1)}, bf16[16,32,320]{2,1,0:T(8,128)(2,1)S(1)}, u32[]{:S(2)}, u32[]{:S(2)}) collective-permute-start(bf16[16,32,320]{2,1,0:T(8,128)(2,1)} %bitcast.35), channel_id=1, source_target_pairs={{1,3},{2,0},{3,5},{4,2},{5,7},{6,4},{7,9},{8,6},{9,11},{10,8},{11,... | collective-permute-start | bytes 983048 | tf_op jit(solution)/shard_map/ppermute | solution.py:363
  17.8 1.2 shard_map.70
  19.0 3.6 %collective-permute-done.2.x = bf16[1360,128]{1,0:T(8,128)(2,1)} collective-permute-done((bf16[1360,128]{1,0:T(8,128)(2,1)}, bf16[1360,128]{1,0:T(8,128)(2,1)}, u32[]{:S(2)}, u32[]{:S(2)}) %collective-permute-start.2) | collective-permute-done | bytes 348192 | tf_op jit(solution)/shard_map/ppermute | solution.py:363
  22.6 0.3 collective-permute-start.7
  22.9 8.5 %collective-permute-done = bf16[17,32,320]{2,1,0:T(8,128)(2,1)S(1)} collective-permute-done((bf16[17,32,320]{2,1,0:T(8,128)(2,1)S(1)}, bf16[17,32,320]{2,1,0:T(8,128)(2,1)S(1)}, u32[]{:S(2)}, u32[]{:S(2)}) %collective-permute-start) | collective-permute-done | bytes 348192 | tf_op jit(solution)/shard_map/ppermute | solution.py:363
  31.4 1.9 %shard_map.68 = (bf16[512,320]{1,0:T(8,128)(2,1)S(1)}, bf16[4,512,240]{2,1,0:T(8,128)(2,1)S(1)}) custom-call(s32[2]{0:T(128)S(1)} %pad_add_fusion.at, bf16[544,320]{1,0:T(8,128)(2,1)S(1)} %bitcast.34, bf16[9,320,320]{2,1,0:T(8,128)(2,1)S(1)} %bitcast.27, bf16[3,256,192]{2,1,0:T(8,128)(2,1)S(1)} %get-tuple-element.41.wn, bf16[3,192,256]{2,1,0:T(8,128)(2,1)S(1)} %copy-done.6, ...), custom_call_target="tpu_custom_call" | custom-call | flops 419430400 | bytes 4165640 | tf_op jit(solution)/shard_map/pallas_call | solution.py:84
  33.3 1.3 collective-permute-start.1
  34.6 4.6 %collective-permute-start.10 = (bf16[16,32,320]{2,1,0:T(8,128)(2,1)S(1)}, bf16[16,32,320]{2,1,0:T(8,128)(2,1)S(1)}, u32[]{:S(2)}, u32[]{:S(2)}) collective-permute-start(bf16[16,32,320]{2,1,0:T(8,128)(2,1)S(1)} %bitcast.31), channel_id=1, source_target_pairs={{1,3},{2,0},{3,5},{4,2},{5,7},{6,4},{7,9},{8,6},{9,11},{10,8},{11,... | collective-permute-start | bytes 983048 | tf_op jit(solution)/shard_map/ppermute | solution.py:363
  39.2 0.0 copy-start.8
  39.3 0.1 collective-permute-start.9
  39.4 1.4 collective-permute-start.8
  40.8 2.4 %shard_map.69 = (bf16[512,320]{1,0:T(8,128)(2,1)S(1)}, bf16[4,512,240]{2,1,0:T(8,128)(2,1)S(1)}) custom-call(s32[2]{0:T(128)S(1)} %pad_add_fusion.at, bf16[1360,128]{1,0:T(8,128)(2,1)} %collective-permute-done.2.x, bf16[9,320,320]{2,1,0:T(8,128)(2,1)S(1)} %bitcast.28, bf16[3,256,192]{2,1,0:T(8,128)(2,1)S(1)} %get-tuple-element.41.wn, ...), custom_call_target="tpu_custom_call" | custom-call | flops 419430400 | bytes 4165640 | tf_op jit(solution)/shard_map/pallas_call | solution.py:84
  43.2 3.7 %collective-permute-done.1 = bf16[16,32,320]{2,1,0:T(8,128)(2,1)S(1)} collective-permute-done((bf16[16,32,320]{2,1,0:T(8,128)(2,1)S(1)}, bf16[16,32,320]{2,1,0:T(8,128)(2,1)S(1)}, u32[]{:S(2)}, u32[]{:S(2)}) %collective-permute-start.1) | collective-permute-done | bytes 327712 | tf_op jit(solution)/shard_map/ppermute | solution.py:363
  46.9 3.2 %shard_map.71 = (bf16[6,512,320]{2,1,0:T(8,128)(2,1)S(1)}, bf16[4,512,320]{2,1,0:T(8,128)(2,1)S(1)}, bf16[512,320]{1,0:T(8,128)(2,1)S(1)}, bf16[512,320]{1,0:T(8,128)(2,1)S(1)}) custom-call(s32[2]{0:T(128)S(1)} %pad_add_fusion.at, bf16[512,320]{1,0:T(8,128)(2,1)S(1)} %bitcast.41, bf16[512,320]{1,0:T(8,128)(2,1)S(1)} %copy-done.8, ...), custom_call_target="tpu_custom_call" | custom-call | flops 838860800 | bytes 7372808 | tf_op jit(solution)/shard_map/pallas_call | solution.py:84
  50.1 3.4 %collective-permute-start.5 = (bf16[16,32,320]{2,1,0:T(8,128)(2,1)S(1)}, bf16[16,32,320]{2,1,0:T(8,128)(2,1)S(1)}, u32[]{:S(2)}, u32[]{:S(2)}) collective-permute-start(bf16[16,32,320]{2,1,0:T(8,128)(2,1)S(1)} %bitcast.46), channel_id=1, source_target_pairs={{1,3},{2,0},{3,5},{4,2},{5,7},{6,4},{7,9},{8,6},{9,11},{10,8},{11,... | collective-permute-start | bytes 983048 | tf_op jit(solution)/shard_map/ppermute | solution.py:363
  53.6 1.5 %collective-permute-start.4 = (bf16[16,32,320]{2,1,0:T(8,128)(2,1)S(1)}, bf16[16,32,320]{2,1,0:T(8,128)(2,1)S(1)}, u32[]{:S(2)}, u32[]{:S(2)}) collective-permute-start(bf16[16,32,320]{2,1,0:T(8,128)(2,1)S(1)} %bitcast.45), channel_id=1, source_target_pairs={{0,2},{2,4},{3,1},{4,6},{5,3},{6,8},{7,5},{8,10},{9,7},{10,12},{11... | collective-permute-start | bytes 983048 | tf_op jit(solution)/shard_map/ppermute | solution.py:363
  55.1 3.5 %shard_map.74 = (bf16[4,512,320]{2,1,0:T(8,128)(2,1)S(1)}, bf16[512,320]{1,0:T(8,128)(2,1)S(1)}, bf16[512,320]{1,0:T(8,128)(2,1)S(1)}, bf16[512,320]{1,0:T(8,128)(2,1)S(1)}, bf16[512,320]{1,0:T(8,128)(2,1)S(1)}) custom-call(s32[2]{0:T(128)S(1)} %pad_add_fusion.at, bf16[1280,128]{1,0:T(8,128)(2,1)S(1)} %collective-permute-done.8.folded, ...), custom_call_target="tpu_custom_call" | custom-call | flops 838860800 | bytes 7372808 | tf_op jit(solution)/shard_map/pallas_call | solution.py:84
  58.6 4.6 %collective-permute-start.12 = (bf16[16,32,320]{2,1,0:T(8,128)(2,1)S(1)}, bf16[16,32,320]{2,1,0:T(8,128)(2,1)S(1)}, u32[]{:S(2)}, u32[]{:S(2)}) collective-permute-start(bf16[16,32,320]{2,1,0:T(8,128)(2,1)S(1)} %bitcast.48), channel_id=1, source_target_pairs={{1,3},{2,0},{3,5},{4,2},{5,7},{6,4},{7,9},{8,6},{9,11},{10,8},{11,... | collective-permute-start | bytes 983048 | tf_op jit(solution)/shard_map/ppermute | solution.py:363
  63.2 1.3 collective-permute-start.11
  64.5 3.2 %shard_map.72 = (bf16[6,512,320]{2,1,0:T(8,128)(2,1)S(1)}, bf16[2,512,320]{2,1,0:T(8,128)(2,1)S(1)}, bf16[1024,320]{1,0:T(8,128)(2,1)S(1)}) custom-call(s32[2]{0:T(128)S(1)} %pad_add_fusion.at, bf16[512,320]{1,0:T(8,128)(2,1)S(1)} %bitcast.40, bf16[4,512,320]{2,1,0:T(8,128)(2,1)S(1)} %get-tuple-element.54.state, bf16[512,320]{1,0:T(8,128)(2,1)S(1)} %bitcast.39, ...), custom_call_target="tpu_custom_call" | custom-call | flops 838860800 | bytes 6717448 | tf_op jit(solution)/shard_map/pallas_call | solution.py:84
  67.7 0.0 copy-start.13
  67.7 3.7 %shard_map.75.passing = bf16[4,2,320,240]{3,2,1,0:T(8,128)(2,1)S(1)} custom-call(s32[2]{0:T(128)S(1)} %pad_add_fusion.at, bf16[512,320]{1,0:T(8,128)(2,1)S(1)} %get-tuple-element.64.cot0, bf16[512,320]{1,0:T(8,128)(2,1)S(1)} %get-tuple-element.61.cot1, bf16[512,320]{1,0:T(8,128)(2,1)S(1)} %get-tuple-element.73.c2, ...), custom_call_target="tpu_custom_call" | custom-call | flops 1677721600 | bytes 7782408 | tf_op jit(solution)/shard_map/pallas_call | solution.py:84
  71.4 1.4 collective-permute-done.11
  72.8 7.3 %shard_map.76 = (bf16[2,5,320,240]{3,2,1,0:T(8,128)(2,1)S(1)}, bf16[2,5,320,240]{3,2,1,0:T(8,128)(2,1)S(1)}) custom-call(s32[2]{0:T(128)S(1)} %pad_add_fusion.at, bf16[512,320]{1,0:T(8,128)(2,1)S(1)} %bitcast.44, bf16[4,512,320]{2,1,0:T(8,128)(2,1)S(1)} %get-tuple-element.68.back, bf16[512,320]{1,0:T(8,128)(2,1)S(1)} %bitcast.43, ...), custom_call_target="tpu_custom_call" | custom-call | flops 3355443200 | bytes 12984328 | tf_op jit(solution)/shard_map/pallas_call | solution.py:84
  80.1 0.1 collective-permute-start.13
  80.2 3.5 %collective-permute-done.13.got = bf16[2,5,320,240]{3,2,1,0:T(8,128)(2,1)S(1)} collective-permute-done((bf16[2,5,320,240]{3,2,1,0:T(8,128)(2,1)S(1)}, bf16[2,5,320,240]{3,2,1,0:T(8,128)(2,1)S(1)}, u32[]{:S(2)}, u32[]{:S(2)}) %collective-permute-start.13) | collective-permute-done | bytes 1536032 | tf_op jit(solution)/shard_map/ppermute | solution.py:363
  83.7 2.5 %shard_map.77 = bf16[64,50,240]{2,1,0:T(8,128)(2,1)} custom-call(s32[2]{0:T(128)S(1)} %pad_add_fusion.at, bf16[2,5,320,240]{3,2,1,0:T(8,128)(2,1)S(1)} %get-tuple-element.77.kept, bf16[2,5,320,240]{3,2,1,0:T(8,128)(2,1)S(1)} %collective-permute-done.13.got), custom_call_target="tpu_custom_call" | custom-call | flops 1000 | bytes 4608008 | tf_op jit(solution)/shard_map/pallas_call | solution.py:84
  86.3 16.8 %all-to-all-start = ((bf16[64,50,240]{2,1,0:T(8,128)(2,1)}), bf16[64,50,240]{2,1,0:T(8,128)(2,1)S(1)}, u32[]{:S(2)}, u32[]{:S(2)}) async-start(bf16[64,50,240]{2,1,0:T(8,128)(2,1)} %shard_map.77), calls=%async_computation | async-start | bytes 3670016 | tf_op jit(solution)/shard_map/all_to_all | solution.py:451
  103.0 0.5 collective-permute-start.6
  103.6 37.3 %collective-permute-done.6 = bf16[32,32,320]{2,1,0:T(8,128)(2,1)S(1)} collective-permute-done((bf16[32,32,320]{2,1,0:T(8,128)(2,1)S(1)}, bf16[32,32,320]{2,1,0:T(8,128)(2,1)S(1)}, u32[]{:S(2)}, u32[]{:S(2)}) %collective-permute-start.6) | collective-permute-done | bytes 655392 | tf_op jit(solution)/shard_map/ppermute | solution.py:363
  140.9 1.7 %shard_map.73 = bf16[2,1024,320]{2,1,0:T(8,128)(2,1)} custom-call(s32[2]{0:T(128)S(1)} %pad_add_fusion.at, bf16[2,512,320]{2,1,0:T(8,128)(2,1)S(1)} %get-tuple-element.56.own, bf16[1024,320]{1,0:T(8,128)(2,1)S(1)} %bitcast.33), custom_call_target="tpu_custom_call" | custom-call | flops 1000 | bytes 2621448 | tf_op jit(solution)/shard_map/pallas_call | solution.py:84
  142.6 0.3 convert_reduce_fusion
  143.0 0.1 slice.15
  143.1 0.6 copy.8
  143.7 0.1 slice.13
  143.8 0.6 copy.7
  (32 shorter events, 0.1 us)
Async XLA Ops:
  0.7 1.6 %copy-start = (bf16[3,3,320,320]{3,2,1,0:T(8,128)(2,1)S(1)}, bf16[3,3,320,320]{3,2,1,0:T(8,128)(2,1)}, u32[]{:S(2)}) copy-start(bf16[3,3,320,320]{3,2,1,0:T(8,128)(2,1)} %param.6) | copy-start | bytes 5529604
  2.3 1.4 copy-start.2
  3.8 14.1 %copy-start.3 = (bf16[1,2,32,32,320]{4,3,2,1,0:T(8,128)(2,1)S(1)}, bf16[1,2,32,32,320]{4,3,2,1,0:T(8,128)(2,1)}, u32[]{:S(2)}) copy-start(bf16[1,2,32,32,320]{4,3,2,1,0:T(8,128)(2,1)} %param.5) | copy-start | bytes 3932164
  3.8 14.1 %copy-start.4 = (bf16[2,3,320,320]{3,2,1,0:T(8,128)(2,1)S(1)}, bf16[2,3,320,320]{3,2,1,0:T(8,128)(2,1)}, u32[]{:S(2)}) copy-start(bf16[2,3,320,320]{3,2,1,0:T(8,128)(2,1)} %tw) | copy-start | bytes 3686404
  7.7 0.7 copy-start.5
  8.4 0.7 copy-start.7
  9.1 0.8 copy-start.9
  9.9 1.3 copy-start.11
  11.3 11.3 %collective-permute-start.2 = (bf16[1360,128]{1,0:T(8,128)(2,1)}, bf16[1360,128]{1,0:T(8,128)(2,1)}, u32[]{:S(2)}, u32[]{:S(2)}) collective-permute-start(bf16[1360,128]{1,0:T(8,128)(2,1)} %get-tuple-element.47), channel_id=1, source_target_pairs={{0,1},{1,0},{2,3},{3,2},{4,5},{5,4},{6,7},{7,6},{8,9},{9,8},{10,11... | collective-permute-start | bytes 1044488 | tf_op jit(solution)/shard_map/ppermute | solution.py:363
  12.6 18.8 %copy-start.1 = (bf16[3,3,320,320]{3,2,1,0:T(8,128)(2,1)S(1)}, bf16[3,3,320,320]{3,2,1,0:T(8,128)(2,1)}, u32[]{:S(2)}) copy-start(bf16[3,3,320,320]{3,2,1,0:T(8,128)(2,1)} %param.6) | copy-start | bytes 5529604
  12.7 18.8 %copy-start.6 = (bf16[3,192,256]{2,1,0:T(8,128)(2,1)S(1)}, bf16[3,192,256]{2,1,0:T(8,128)(2,1)}, u32[]{:S(2)}) copy-start(bf16[3,192,256]{2,1,0:T(8,128)(2,1)} %copy-done.5) | copy-start | bytes 884740
  12.7 18.8 %collective-permute-start = (bf16[17,32,320]{2,1,0:T(8,128)(2,1)S(1)}, bf16[17,32,320]{2,1,0:T(8,128)(2,1)S(1)}, u32[]{:S(2)}, u32[]{:S(2)}) collective-permute-start(bf16[17,32,320]{2,1,0:T(8,128)(2,1)S(1)} %bitcast.50), channel_id=1, source_target_pairs={{0,1},{1,0},{2,3},{3,2},{4,5},{5,4},{6,7},{7,6},{8,9},{9,8},{10,11... | collective-permute-start | bytes 1044488 | tf_op jit(solution)/shard_map/ppermute | solution.py:363
  14.4 20.2 %collective-permute-start.3 = (bf16[16,32,320]{2,1,0:T(8,128)(2,1)}, bf16[16,32,320]{2,1,0:T(8,128)(2,1)S(1)}, u32[]{:S(2)}, u32[]{:S(2)}) collective-permute-start(bf16[16,32,320]{2,1,0:T(8,128)(2,1)} %bitcast.35), channel_id=1, source_target_pairs={{1,3},{2,0},{3,5},{4,2},{5,7},{6,4},{7,9},{8,6},{9,11},{10,8},{11,... | collective-permute-start | bytes 983048 | tf_op jit(solution)/shard_map/ppermute | solution.py:363
  22.6 16.6 %collective-permute-start.7 = (bf16[1280,128]{1,0:T(8,128)(2,1)S(1)}, bf16[1280,128]{1,0:T(8,128)(2,1)S(1)}, u32[]{:S(2)}, u32[]{:S(2)}) collective-permute-start(bf16[1280,128]{1,0:T(8,128)(2,1)S(1)} %get-tuple-element.59), channel_id=1, source_target_pairs={{0,1},{1,0},{2,3},{3,2},{4,5},{5,4},{6,7},{7,6},{8,9},{9,8},{10,11... | collective-permute-start | bytes 983048 | tf_op jit(solution)/shard_map/ppermute | solution.py:363
  33.3 13.6 %collective-permute-start.1 = (bf16[16,32,320]{2,1,0:T(8,128)(2,1)S(1)}, bf16[16,32,320]{2,1,0:T(8,128)(2,1)S(1)}, u32[]{:S(2)}, u32[]{:S(2)}) collective-permute-start(bf16[16,32,320]{2,1,0:T(8,128)(2,1)S(1)} %bitcast.36), channel_id=1, source_target_pairs={{0,2},{2,4},{3,1},{4,6},{5,3},{6,8},{7,5},{8,10},{9,7},{10,12},{11... | collective-permute-start | bytes 983048 | tf_op jit(solution)/shard_map/ppermute | solution.py:363
  34.6 20.4 %collective-permute-start.10 = (bf16[16,32,320]{2,1,0:T(8,128)(2,1)S(1)}, bf16[16,32,320]{2,1,0:T(8,128)(2,1)S(1)}, u32[]{:S(2)}, u32[]{:S(2)}) collective-permute-start(bf16[16,32,320]{2,1,0:T(8,128)(2,1)S(1)} %bitcast.31), channel_id=1, source_target_pairs={{1,3},{2,0},{3,5},{4,2},{5,7},{6,4},{7,9},{8,6},{9,11},{10,8},{11,... | collective-permute-start | bytes 983048 | tf_op jit(solution)/shard_map/ppermute | solution.py:363
  39.2 7.7 %copy-start.8 = (bf16[512,320]{1,0:T(8,128)(2,1)S(1)}, bf16[512,320]{1,0:T(8,128)(2,1)}, u32[]{:S(2)}) copy-start(bf16[512,320]{1,0:T(8,128)(2,1)} %copy-done.7) | copy-start | bytes 983044
  39.2 7.7 %copy-start.10 = (bf16[512,320]{1,0:T(8,128)(2,1)S(1)}, bf16[512,320]{1,0:T(8,128)(2,1)}, u32[]{:S(2)}) copy-start(bf16[512,320]{1,0:T(8,128)(2,1)} %copy-done.9) | copy-start | bytes 983044
  39.3 15.8 %collective-permute-start.9 = (bf16[1280,128]{1,0:T(8,128)(2,1)S(1)}, bf16[1280,128]{1,0:T(8,128)(2,1)S(1)}, u32[]{:S(2)}, u32[]{:S(2)}) collective-permute-start(bf16[1280,128]{1,0:T(8,128)(2,1)S(1)} %get-tuple-element.63), channel_id=1, source_target_pairs={{0,1},{1,0},{2,3},{3,2},{4,5},{5,4},{6,7},{7,6},{8,9},{9,8},{10,11... | collective-permute-start | bytes 983048 | tf_op jit(solution)/shard_map/ppermute | solution.py:363
  39.4 15.7 %collective-permute-start.8 = (bf16[1280,128]{1,0:T(8,128)(2,1)S(1)}, bf16[1280,128]{1,0:T(8,128)(2,1)S(1)}, u32[]{:S(2)}, u32[]{:S(2)}) collective-permute-start(bf16[1280,128]{1,0:T(8,128)(2,1)S(1)} %collective-permute-done.7.folded3), channel_id=1, source_target_pairs={{0,2},{2,4},{3,1},{4,6},{5,3},{6,8},{7,5},{8,10},{9,7},{10,12},{11... | collective-permute-start | bytes 983048 | tf_op jit(solution)/shard_map/ppermute | solution.py:363
  50.1 14.3 %collective-permute-start.5 = (bf16[16,32,320]{2,1,0:T(8,128)(2,1)S(1)}, bf16[16,32,320]{2,1,0:T(8,128)(2,1)S(1)}, u32[]{:S(2)}, u32[]{:S(2)}) collective-permute-start(bf16[16,32,320]{2,1,0:T(8,128)(2,1)S(1)} %bitcast.46), channel_id=1, source_target_pairs={{1,3},{2,0},{3,5},{4,2},{5,7},{6,4},{7,9},{8,6},{9,11},{10,8},{11,... | collective-permute-start | bytes 983048 | tf_op jit(solution)/shard_map/ppermute | solution.py:363
  53.6 10.9 %collective-permute-start.4 = (bf16[16,32,320]{2,1,0:T(8,128)(2,1)S(1)}, bf16[16,32,320]{2,1,0:T(8,128)(2,1)S(1)}, u32[]{:S(2)}, u32[]{:S(2)}) collective-permute-start(bf16[16,32,320]{2,1,0:T(8,128)(2,1)S(1)} %bitcast.45), channel_id=1, source_target_pairs={{0,2},{2,4},{3,1},{4,6},{5,3},{6,8},{7,5},{8,10},{9,7},{10,12},{11... | collective-permute-start | bytes 983048 | tf_op jit(solution)/shard_map/ppermute | solution.py:363
  58.6 12.9 %collective-permute-start.12 = (bf16[16,32,320]{2,1,0:T(8,128)(2,1)S(1)}, bf16[16,32,320]{2,1,0:T(8,128)(2,1)S(1)}, u32[]{:S(2)}, u32[]{:S(2)}) collective-permute-start(bf16[16,32,320]{2,1,0:T(8,128)(2,1)S(1)} %bitcast.48), channel_id=1, source_target_pairs={{1,3},{2,0},{3,5},{4,2},{5,7},{6,4},{7,9},{8,6},{9,11},{10,8},{11,... | collective-permute-start | bytes 983048 | tf_op jit(solution)/shard_map/ppermute | solution.py:363
  63.2 9.7 %collective-permute-start.11 = (bf16[16,32,320]{2,1,0:T(8,128)(2,1)S(1)}, bf16[16,32,320]{2,1,0:T(8,128)(2,1)S(1)}, u32[]{:S(2)}, u32[]{:S(2)}) collective-permute-start(bf16[16,32,320]{2,1,0:T(8,128)(2,1)S(1)} %bitcast.47), channel_id=1, source_target_pairs={{0,2},{2,4},{3,1},{4,6},{5,3},{6,8},{7,5},{8,10},{9,7},{10,12},{11... | collective-permute-start | bytes 983048 | tf_op jit(solution)/shard_map/ppermute | solution.py:363
  67.7 3.7 %copy-start.13 = (bf16[1024,320]{1,0:T(8,128)(2,1)}, bf16[1024,320]{1,0:T(8,128)(2,1)S(1)}, u32[]{:S(2)}) copy-start(bf16[1024,320]{1,0:T(8,128)(2,1)S(1)} %get-tuple-element.57) | copy-start | bytes 1966084
  67.7 5.1 %copy-start.12 = (bf16[2,4,512,240]{3,2,1,0:T(8,128)(2,1)S(1)}, bf16[2,4,512,240]{3,2,1,0:T(8,128)(2,1)}, u32[]{:S(2)}) copy-start(bf16[2,4,512,240]{3,2,1,0:T(8,128)(2,1)} %copy-done.11) | copy-start | bytes 5898244
  80.1 3.6 %collective-permute-start.13 = (bf16[2,5,320,240]{3,2,1,0:T(8,128)(2,1)S(1)}, bf16[2,5,320,240]{3,2,1,0:T(8,128)(2,1)S(1)}, u32[]{:S(2)}, u32[]{:S(2)}) collective-permute-start(bf16[2,5,320,240]{3,2,1,0:T(8,128)(2,1)S(1)} %get-tuple-element.78), channel_id=1, source_target_pairs={{0,32},{32,0},{64,96},{96,64},{1,33},{33,1},{65,97},{97,65},{2,34}... | collective-permute-start | bytes 4608008 | tf_op jit(solution)/shard_map/ppermute | solution.py:363
  86.2 16.8 %copy-start.14 = (bf16[1024,320]{1,0:T(8,128)(2,1)S(1)}, bf16[1024,320]{1,0:T(8,128)(2,1)}, u32[]{:S(2)}) copy-start(bf16[1024,320]{1,0:T(8,128)(2,1)} %copy-done.13) | copy-start | bytes 1966084
  86.3 56.4 %all-to-all-start = ((bf16[64,50,240]{2,1,0:T(8,128)(2,1)}), bf16[64,50,240]{2,1,0:T(8,128)(2,1)S(1)}, u32[]{:S(2)}, u32[]{:S(2)}) async-start(bf16[64,50,240]{2,1,0:T(8,128)(2,1)} %shard_map.77), calls=%async_computation | async-start | bytes 3670016 | tf_op jit(solution)/shard_map/all_to_all | solution.py:451
  103.0 37.9 %collective-permute-start.6 = (bf16[32,32,320]{2,1,0:T(8,128)(2,1)S(1)}, bf16[32,32,320]{2,1,0:T(8,128)(2,1)S(1)}, u32[]{:S(2)}, u32[]{:S(2)}) collective-permute-start(bf16[32,32,320]{2,1,0:T(8,128)(2,1)S(1)} %bitcast.42), channel_id=1, source_target_pairs={{0,1},{1,0},{2,3},{3,2},{4,5},{5,4},{6,7},{7,6},{8,9},{9,8},{10,11... | collective-permute-start | bytes 1966088 | tf_op jit(solution)/shard_map/ppermute | solution.py:363

commit v6 on v5

--- a/solution.py
+++ b/solution.py
@@ -29,6 +29,7 @@
 
 ONE = (PX, C)
 THREE_TAILS = 3 * TAIL
+FOLDED = PX * C // LANES
 SIDES = (CLIPS, PX, 3 * WIDTH)
 KERNELS = (3, C, C)
 
@@ -71,10 +72,6 @@
             self.copy.wait()
             self.copy = None
         return self.ref
-
-
-def nth(ref, n):
-    return ref.at[pl.ds(n * PX, PX), :]
 
 
 def run(kernel, outs, args, scratch=(), copies=0, flops=0, far=(), far_outs=False):
@@ -113,6 +110,10 @@
     pad[pl.ds(0, COLS), :] = jnp.zeros((COLS, C), BF)
     pad[pl.ds(TALL, COLS), :] = jnp.zeros((COLS, C), BF)
     return pad.at[pl.ds(pl.multiple_of(COLS * (1 - odd), COLS), TALL), :]
+
+
+def part(ref, n):
+    return ref.at[pl.ds(n * FOLDED, FOLDED), :]
 
 
 def fold(rows, dst):
@@ -174,11 +175,13 @@
     fold(x[1 - odd, pl.ds(away, TALL), :], x2)
 
 
-def prepare(at, cot, tw, c3, c2, cot0, cot1, vt, vtk, vb, vbk):
+def prepare(at, cot, tw, s0, c3, c2, pair, cot0, cot1, vt, vtk, vb, vbk):
     odd = at[0]
     here, there = pl.multiple_of(PX * odd, PX), pl.multiple_of(PX * (1 - odd), PX)
     fold(cot[odd, pl.ds(there, PX), :], c3)
     fold(cot[1 - odd, pl.ds(there, PX), :], c2)
+    fold(s0[...], part(pair, 0))
+    fold(cot[odd, pl.ds(here, PX), :], part(pair, 1))
     cot0[...] = cot[odd, pl.ds(here, PX), :]
     cot1[...] = cot[1 - odd, pl.ds(here, PX), :]
     for l in range(2):
@@ -227,7 +230,8 @@
         yield (states[q + 1][...].astype(F32) + term).astype(BF)
 
 
-def layer_one(at, left, s0, s1, s2, s3, right, vw, wk, acts, state, last, first):
+def layer_one(at, left, s0, s1, s2, s3, pair, vw, wk, acts, state, last, first, right):
+    unfold(part(pair, 0), right)
     states = (left, s0, s1, s2, s3, right)
     for q, value in enumerate(temporal(states, vw, 0, wk, acts)):
         state[q] = value
@@ -243,7 +247,7 @@
         if q < 2:
             own[q] = value
         else:
-            sent[pl.ds((3 - q) * PX, PX), :] = value
+            fold(value, part(sent, 3 - q))
 
 
 def descend(six, q, before, vw, layer, wk):
@@ -254,7 +258,8 @@
     return (three[1][...].astype(F32) + carried * (s * (1.0 + v * (1.0 - s)))).astype(BF)
 
 
-def back_one(at, folded, cot0, cot1, folded2, folded3, right, state, vw, wk, back, first, last, c2, c3, left):
+def back_one(at, folded, cot0, cot1, folded2, folded3, pair, state, vw, wk, back, first, last, c2, c3, left, right):
+    unfold(part(pair, 1), right)
     unfold(folded, left)
     unfold(folded2, c2)
     unfold(folded3, c3)
@@ -330,13 +335,14 @@
     move.finish()
 
 
-def place(at, own, got, out, sems):
+def place(at, own, got, out, vgot, sems):
     odd = at[0]
     move = Mover(sems)
     here, there = pl.multiple_of(PX * odd, PX), pl.multiple_of(PX * (1 - odd), PX)
     for q, frame in enumerate((odd, 1 - odd)):
         move.put(own.at[q], out.at[frame, pl.ds(here, PX), :])
-        move.put(nth(got, q), out.at[frame, pl.ds(there, PX), :])
+        unfold(part(got, q), vgot.at[q])
+        move.put(vgot.at[q], out.at[frame, pl.ds(there, PX), :])
     move.finish()
 
 
@@ -367,7 +373,7 @@
     ws = spatial_weight.reshape(9, C, C)
     flops = 2 * PX * C * C
 
-    flat, two, four, six = (2 * PX, C), (2, PX, C), (4, PX, C), (6, PX, C)
+    two, four, six = (2, PX, C), (4, PX, C), (6, PX, C)
     packed = [(3, HEAD, THREE_TAILS), (3, THREE_TAILS, HEAD), (THREE_TAILS, THREE_TAILS)]
     taps = [(2, *KERNELS), (2, THREE_TAILS, C)]
     pad = (PX + 2 * COLS, C)
@@ -382,24 +388,27 @@
         flops=8 * flops,
     )
     wp = (ws, wn, wk, wr)
-    right = send(s0, outer)
     x2 = send(x2, swap)
-    c3, c2, cot0, cot1, vt, vtk, vb, vbk = run(
-        prepare, [(PX * C // LANES, LANES)] * 2 + [ONE] * 2 + taps * 2, (at, after(cot, s0), after(temporal_weight, s0)), flops=flops
-    )
+    c3, c2, pair, cot0, cot1, vt, vtk, vb, vbk = run(
+        prepare,
+        [(FOLDED, LANES), (FOLDED, LANES), (2 * FOLDED, LANES), ONE, ONE, *taps, *taps],
+        (at, after(cot, s0), after(temporal_weight, s0), s0),
+        flops=flops,
+    )
+    right = send(pair, outer)
 
     s3, sides3 = run(conv_other, [ONE, SIDES], (at, x3, *wp), [pad], 0, 4 * flops)
     left = send(s3, inner)
     c3 = send(after(c3, x2), swap)
     s2, sides2 = run(conv_folded, [ONE, SIDES], (at, x2, *wp), [pad], 0, 4 * flops)
     c2 = send(after(c2, c3), swap)
-    cot_right = send(after(cot0, right), outer)
     cot_left = send(c3, inner)
 
     acts1, state1, last, first = run(
         layer_one,
         [six, four, ONE, ONE],
         (at, left, s0, s1, s2, s3, right, vt, vtk),
+        [ONE],
         flops=8 * flops,
     )
     left1 = send(last, inner)
@@ -407,14 +416,14 @@
     back1, first, last, u2, u3 = run(
         back_one,
         [four, ONE, ONE, ONE, ONE],
-        (at, cot_left, cot0, cot1, c2, c3, cot_right, state1, vb, vbk),
-        [ONE],
+        (at, cot_left, cot0, cot1, c2, c3, right, state1, vb, vbk),
+        [ONE, ONE],
         flops=8 * flops,
     )
     back_left = send(last, inner)
     back_right = send(first, outer)
     acts2, own, sent = run(
-        layer_two, [six, two, flat], (at, left1, state1, right1, vt, vtk), flops=8 * flops
+        layer_two, [six, two, (2 * FOLDED, LANES)], (at, left1, state1, right1, vt, vtk), flops=8 * flops
     )
     returned = send(sent, swap)
 
@@ -434,7 +443,7 @@
         flops=32 * flops,
     )
     got = send(sent, cores, "clip")
-    (out,) = run(place, [(2, FULL, C)], (at, own, returned), (), 4, 1000, far_outs=True)
+    (out,) = run(place, [(2, FULL, C)], (at, own, returned), [two], 4, 1000, far_outs=True)
 
     rows = C // owners
     block = (2 * owners, 5 * rows, 3 * WIDTH)

time: 146 us -> 142 us (0.973)
  starting transfers between devices: 41.3 us -> 34.9 us
  other arithmetic: 0.42 us -> 1.92 us
    ppermute x14 -> x13, starting transfers between devices: 24.6 us -> 20.2 us  [send(): return lax.ppermute(value, axis, perm).reshape(shape)]
    all_to_all x1, starting transfers between devices: 16.8 us -> 14.8 us  [step(): lax.all_to_all(packs, ('frame', 'clip'), split_axis=0, concat_axis=0, axi...]
    reduce_sum x1, other arithmetic: 0.34 us -> 1.85 us  [step(): total = jnp.sum(parts.astype(F32), axis=0).reshape(5, rows, 3, WIDTH)]
    ppermute x14 -> x13, waiting for transfers between devices: 58 us -> 59.4 us  [send(): return lax.ppermute(value, axis, perm).reshape(shape)]
    unnamed x32 -> x16, local copies, waits for them, and re-layouts: 7.91 us -> 7.01 us
  transfers between devices with their start and end apart: 15 -> 14, of which waited for: 6 -> 7; matrix products, arithmetic and copies ran while one was open for 1% -> 1% of each run, Pallas kernels for 14% -> 15%
where the time goes in v6:
time: 142 us; the launch traced here: 140 us
  waiting for transfers between devices  59.4 us (42%)
  starting transfers between devices  34.9 us (25%)
  Pallas kernels  34.8 us (25%)
  local copies, waits for them, and re-layouts  8.24 us (6%)
  other arithmetic  1.92 us (1%)
    ppermute x13, waiting for transfers between devices, send(): return lax.ppermute(value, axis, perm).reshape(shape)  59.4 us
    pallas_call x11, Pallas kernels, run(): pl.pallas_call(kernel, out_shape=[jax.ShapeDtypeStruct(s, BF) for s in ou...  34.8 us
    ppermute x13, starting transfers between devices, send(): return lax.ppermute(value, axis, perm).reshape(shape)  20.2 us
    all_to_all x1, starting transfers between devices, step(): lax.all_to_all(packs, ('frame', 'clip'), split_axis=0, concat_axis=0, axi...  14.8 us
    unnamed x16, local copies, waits for them, and re-layouts  7.01 us
  transfers between devices with their start and end apart: 14, of which 7 were waited for; matrix products, arithmetic and copies ran while one was open for 1% of the time, Pallas kernels for 15%

profile of v6, /device:TPU:8, one launch (start us, length us, event | category | flops | bytes accessed | tf_op | source)
XLA Modules:
  0.0 140.2 jit_solution(7396839092293755838)
XLA Ops:
  0.6 0.1 pad_add_fusion.at
  0.7 1.6 %copy-done = bf16[3,3,320,320]{3,2,1,0:T(8,128)(2,1)S(1)} copy-done((bf16[3,3,320,320]{3,2,1,0:T(8,128)(2,1)S(1)}, bf16[3,3,320,320]{3,2,1,0:T(8,128)(2,1)}, u32[]{:S(2)}) %copy-start) | copy-done | bytes 1843224
  2.4 1.4 %copy-done.2 = bf16[1,2,32,32,320]{4,3,2,1,0:T(8,128)(2,1)S(1)} copy-done((bf16[1,2,32,32,320]{4,3,2,1,0:T(8,128)(2,1)S(1)}, bf16[1,2,32,32,320]{4,3,2,1,0:T(8,128)(2,1)}, u32[]{:S(2)}) %copy-start.2) | copy-done | bytes 1310744
  3.8 4.0 %shard_map.67 = (bf16[512,320]{1,0:T(8,128)(2,1)S(1)}, bf16[512,320]{1,0:T(8,128)(2,1)S(1)}, bf16[2,4,512,240]{3,2,1,0:T(8,128)(2,1)S(1)}, bf16[1360,128]{1,0:T(...) custom-call(s32[2]{0:T(128)S(1)} %pad_add_fusion.at, ...), custom_call_target="tpu_custom_call" | custom-call | flops 838860800 | bytes 6787080 | tf_op jit(solution)/shard_map/pallas_call | solution.py:81
  7.7 1.3 copy-done.5
  9.1 0.3 collective-permute-start.2
  9.4 1.0 constant_dynamic-slice_fusion
  10.5 1.8 %collective-permute-start = (bf16[17,32,320]{2,1,0:T(8,128)(2,1)S(1)}, bf16[17,32,320]{2,1,0:T(8,128)(2,1)S(1)}, u32[]{:S(2)}, u32[]{:S(2)}) collective-permute-start(bf16[17,32,320]{2,1,0:T(8,128)(2,1)S(1)} %bitcast.38), channel_id=1, source_target_pairs={{0,1},{1,0},{2,3},{3,2},{4,5},{5,4},{6,7},{7,6},{8,9},{9,8},{10,11... | collective-permute-start | bytes 1044488 | tf_op jit(solution)/shard_map/ppermute | solution.py:369
  12.2 1.4 copy-done.4
  13.6 1.3 shard_map.70
  14.9 3.4 %collective-permute-start.3 = (bf16[2560,128]{1,0:T(8,128)(2,1)S(1)}, bf16[2560,128]{1,0:T(8,128)(2,1)S(1)}, u32[]{:S(2)}, u32[]{:S(2)}) collective-permute-start(bf16[2560,128]{1,0:T(8,128)(2,1)S(1)} %get-tuple-element.51), channel_id=1, source_target_pairs={{1,3},{2,0},{3,5},{4,2},{5,7},{6,4},{7,9},{8,6},{9,11},{10,8},{11,... | collective-permute-start | bytes 1966088 | tf_op jit(solution)/shard_map/ppermute | solution.py:369
  18.3 2.0 %collective-permute-done.2.x = bf16[1360,128]{1,0:T(8,128)(2,1)S(1)} collective-permute-done((bf16[1360,128]{1,0:T(8,128)(2,1)}, bf16[1360,128]{1,0:T(8,128)(2,1)S(1)}, u32[]{:S(2)}, u32[]{:S(2)}) %collective-permute-start.2) | collective-permute-done | bytes 348192 | tf_op jit(solution)/shard_map/ppermute | solution.py:369
  20.3 0.3 collective-permute-start.7
  20.6 8.6 %collective-permute-done = bf16[17,32,320]{2,1,0:T(8,128)(2,1)S(1)} collective-permute-done((bf16[17,32,320]{2,1,0:T(8,128)(2,1)S(1)}, bf16[17,32,320]{2,1,0:T(8,128)(2,1)S(1)}, u32[]{:S(2)}, u32[]{:S(2)}) %collective-permute-start) | collective-permute-done | bytes 348192 | tf_op jit(solution)/shard_map/ppermute | solution.py:369
  29.3 1.9 %shard_map.68 = (bf16[512,320]{1,0:T(8,128)(2,1)S(1)}, bf16[4,512,240]{2,1,0:T(8,128)(2,1)S(1)}) custom-call(s32[2]{0:T(128)S(1)} %pad_add_fusion.at, bf16[544,320]{1,0:T(8,128)(2,1)S(1)} %bitcast.26, bf16[9,320,320]{2,1,0:T(8,128)(2,1)S(1)} %bitcast.21, bf16[3,256,192]{2,1,0:T(8,128)(2,1)S(1)} %get-tuple-element.41.wn, ...), custom_call_target="tpu_custom_call" | custom-call | flops 419430400 | bytes 4165640 | tf_op jit(solution)/shard_map/pallas_call | solution.py:81
  31.2 1.3 collective-permute-start.1
  32.5 2.7 %collective-permute-done.7.folded3 = bf16[1280,128]{1,0:T(8,128)(2,1)S(1)} collective-permute-done((bf16[1280,128]{1,0:T(8,128)(2,1)S(1)}, bf16[1280,128]{1,0:T(8,128)(2,1)S(1)}, u32[]{:S(2)}, u32[]{:S(2)}) %collective-permute-start.7) | collective-permute-done | bytes 327712 | tf_op jit(solution)/shard_map/ppermute | solution.py:369
  35.1 0.3 collective-permute-start.9
  35.4 1.3 collective-permute-start.8
  36.7 2.0 %shard_map.69 = (bf16[512,320]{1,0:T(8,128)(2,1)S(1)}, bf16[4,512,240]{2,1,0:T(8,128)(2,1)S(1)}) custom-call(s32[2]{0:T(128)S(1)} %pad_add_fusion.at, bf16[1360,128]{1,0:T(8,128)(2,1)S(1)} %collective-permute-done.2.x, bf16[9,320,320]{2,1,0:T(8,128)(2,1)S(1)} %bitcast.22, bf16[3,256,192]{2,1,0:T(8,128)(2,1)S(1)} %get-tuple-element.41.wn, ...), custom_call_target="tpu_custom_call" | custom-call | flops 419430400 | bytes 4165640 | tf_op jit(solution)/shard_map/pallas_call | solution.py:81
  38.7 0.0 collective-permute-done.3.pair
  38.7 6.3 %collective-permute-done.1 = bf16[16,32,320]{2,1,0:T(8,128)(2,1)S(1)} collective-permute-done((bf16[16,32,320]{2,1,0:T(8,128)(2,1)S(1)}, bf16[16,32,320]{2,1,0:T(8,128)(2,1)S(1)}, u32[]{:S(2)}, u32[]{:S(2)}) %collective-permute-start.1) | collective-permute-done | bytes 327712 | tf_op jit(solution)/shard_map/ppermute | solution.py:369
  45.0 3.3 %shard_map.71 = (bf16[6,512,320]{2,1,0:T(8,128)(2,1)S(1)}, bf16[4,512,320]{2,1,0:T(8,128)(2,1)S(1)}, bf16[512,320]{1,0:T(8,128)(2,1)S(1)}, bf16[512,320]{1,0:T(8,128)(2,1)S(1)}) custom-call(s32[2]{0:T(128)S(1)} %pad_add_fusion.at, bf16[512,320]{1,0:T(8,128)(2,1)S(1)} %bitcast.30, bf16[512,320]{1,0:T(8,128)(2,1)S(1)} %get-tuple-element.45.s0, ...), custom_call_target="tpu_custom_call" | custom-call | flops 838860800 | bytes 7700488 | tf_op jit(solution)/shard_map/pallas_call | solution.py:81
  48.4 3.4 %collective-permute-start.5 = (bf16[16,32,320]{2,1,0:T(8,128)(2,1)S(1)}, bf16[16,32,320]{2,1,0:T(8,128)(2,1)S(1)}, u32[]{:S(2)}, u32[]{:S(2)}) collective-permute-start(bf16[16,32,320]{2,1,0:T(8,128)(2,1)S(1)} %bitcast.36), channel_id=1, source_target_pairs={{1,3},{2,0},{3,5},{4,2},{5,7},{6,4},{7,9},{8,6},{9,11},{10,8},{11,... | collective-permute-start | bytes 983048 | tf_op jit(solution)/shard_map/ppermute | solution.py:369
  51.8 1.5 %collective-permute-start.4 = (bf16[16,32,320]{2,1,0:T(8,128)(2,1)S(1)}, bf16[16,32,320]{2,1,0:T(8,128)(2,1)S(1)}, u32[]{:S(2)}, u32[]{:S(2)}) collective-permute-start(bf16[16,32,320]{2,1,0:T(8,128)(2,1)S(1)} %bitcast.34), channel_id=1, source_target_pairs={{0,2},{2,4},{3,1},{4,6},{5,3},{6,8},{7,5},{8,10},{9,7},{10,12},{11... | collective-permute-start | bytes 983048 | tf_op jit(solution)/shard_map/ppermute | solution.py:369
  53.3 0.0 collective-permute-done.9.folded2
  53.3 3.5 %shard_map.74 = (bf16[4,512,320]{2,1,0:T(8,128)(2,1)S(1)}, bf16[512,320]{1,0:T(8,128)(2,1)S(1)}, bf16[512,320]{1,0:T(8,128)(2,1)S(1)}, bf16[512,320]{1,0:T(8,128)(2,1)S(1)}, bf16[512,320]{1,0:T(8,128)(2,1)S(1)}) custom-call(s32[2]{0:T(128)S(1)} %pad_add_fusion.at, bf16[1280,128]{1,0:T(8,128)(2,1)S(1)} %collective-permute-done.8.folded, ...), custom_call_target="tpu_custom_call" | custom-call | flops 838860800 | bytes 7700488 | tf_op jit(solution)/shard_map/pallas_call | solution.py:81
  56.8 4.6 %collective-permute-start.11 = (bf16[16,32,320]{2,1,0:T(8,128)(2,1)S(1)}, bf16[16,32,320]{2,1,0:T(8,128)(2,1)S(1)}, u32[]{:S(2)}, u32[]{:S(2)}) collective-permute-start(bf16[16,32,320]{2,1,0:T(8,128)(2,1)S(1)} %bitcast.35), channel_id=1, source_target_pairs={{1,3},{2,0},{3,5},{4,2},{5,7},{6,4},{7,9},{8,6},{9,11},{10,8},{11,... | collective-permute-start | bytes 983048 | tf_op jit(solution)/shard_map/ppermute | solution.py:369
  61.4 1.3 collective-permute-start.10
  62.7 0.0 collective-permute-done.5
  62.7 3.4 %shard_map.72 = (bf16[6,512,320]{2,1,0:T(8,128)(2,1)S(1)}, bf16[2,512,320]{2,1,0:T(8,128)(2,1)S(1)}, bf16[2560,128]{1,0:T(8,128)(2,1)S(1)}) custom-call(s32[2]{0:T(128)S(1)} %pad_add_fusion.at, bf16[512,320]{1,0:T(8,128)(2,1)S(1)} %bitcast.29, bf16[4,512,320]{2,1,0:T(8,128)(2,1)S(1)} %get-tuple-element.55.state, bf16[512,320]{1,0:T(8,128)(2,1)S(1)} %bitcast.28, ...), custom_call_target="tpu_custom_call" | custom-call | flops 838860800 | bytes 6717448 | tf_op jit(solution)/shard_map/pallas_call | solution.py:81
  66.1 3.8 %shard_map.75.passing = bf16[4,2,320,240]{3,2,1,0:T(8,128)(2,1)S(1)} custom-call(s32[2]{0:T(128)S(1)} %pad_add_fusion.at, bf16[512,320]{1,0:T(8,128)(2,1)S(1)} %get-tuple-element.61.cot0, bf16[512,320]{1,0:T(8,128)(2,1)S(1)} %get-tuple-element.62.cot1, bf16[512,320]{1,0:T(8,128)(2,1)S(1)} %get-tuple-element.73.c2, ...), custom_call_target="tpu_custom_call" | custom-call | flops 1677721600 | bytes 7782408 | tf_op jit(solution)/shard_map/pallas_call | solution.py:81
  69.9 0.0 collective-permute-done.11
  69.9 1.9 %collective-permute-done.10 = bf16[16,32,320]{2,1,0:T(8,128)(2,1)S(1)} collective-permute-done((bf16[16,32,320]{2,1,0:T(8,128)(2,1)S(1)}, bf16[16,32,320]{2,1,0:T(8,128)(2,1)S(1)}, u32[]{:S(2)}, u32[]{:S(2)}) %collective-permute-start.10) | collective-permute-done | bytes 327712 | tf_op jit(solution)/shard_map/ppermute | solution.py:369
  71.8 7.4 %shard_map.76 = (bf16[2,5,320,240]{3,2,1,0:T(8,128)(2,1)S(1)}, bf16[2,5,320,240]{3,2,1,0:T(8,128)(2,1)S(1)}) custom-call(s32[2]{0:T(128)S(1)} %pad_add_fusion.at, bf16[512,320]{1,0:T(8,128)(2,1)S(1)} %bitcast.32, bf16[4,512,320]{2,1,0:T(8,128)(2,1)S(1)} %get-tuple-element.68.back, bf16[512,320]{1,0:T(8,128)(2,1)S(1)} %bitcast.31, ...), custom_call_target="tpu_custom_call" | custom-call | flops 3355443200 | bytes 12984328 | tf_op jit(solution)/shard_map/pallas_call | solution.py:81
  79.3 0.1 collective-permute-start.12
  79.3 3.5 %collective-permute-done.12.got = bf16[2,5,320,240]{3,2,1,0:T(8,128)(2,1)S(1)} collective-permute-done((bf16[2,5,320,240]{3,2,1,0:T(8,128)(2,1)S(1)}, bf16[2,5,320,240]{3,2,1,0:T(8,128)(2,1)S(1)}, u32[]{:S(2)}, u32[]{:S(2)}) %collective-permute-start.12) | collective-permute-done | bytes 1536032 | tf_op jit(solution)/shard_map/ppermute | solution.py:369
  82.8 2.5 %shard_map.77 = bf16[64,50,240]{2,1,0:T(8,128)(2,1)} custom-call(s32[2]{0:T(128)S(1)} %pad_add_fusion.at, bf16[2,5,320,240]{3,2,1,0:T(8,128)(2,1)S(1)} %get-tuple-element.77.kept, bf16[2,5,320,240]{3,2,1,0:T(8,128)(2,1)S(1)} %collective-permute-done.12.got), custom_call_target="tpu_custom_call" | custom-call | flops 1000 | bytes 4608008 | tf_op jit(solution)/shard_map/pallas_call | solution.py:81
  85.4 14.8 %all-to-all-start = ((bf16[64,50,240]{2,1,0:T(8,128)(2,1)}), bf16[64,50,240]{2,1,0:T(8,128)(2,1)}, u32[]{:S(2)}, u32[]{:S(2)}) async-start(bf16[64,50,240]{2,1,0:T(8,128)(2,1)} %shard_map.77), calls=%async_computation | async-start | bytes 3670016 | tf_op jit(solution)/shard_map/all_to_all | solution.py:460
  100.2 0.6 collective-permute-start.6
  100.8 34.3 %collective-permute-done.6.got = bf16[2560,128]{1,0:T(8,128)(2,1)S(1)} collective-permute-done((bf16[2560,128]{1,0:T(8,128)(2,1)S(1)}, bf16[2560,128]{1,0:T(8,128)(2,1)S(1)}, u32[]{:S(2)}, u32[]{:S(2)}) %collective-permute-start.6) | collective-permute-done | bytes 655392 | tf_op jit(solution)/shard_map/ppermute | solution.py:369
  135.1 1.7 %shard_map.73 = bf16[2,1024,320]{2,1,0:T(8,128)(2,1)} custom-call(s32[2]{0:T(128)S(1)} %pad_add_fusion.at, bf16[2,512,320]{2,1,0:T(8,128)(2,1)S(1)} %get-tuple-element.57.own, bf16[2560,128]{1,0:T(8,128)(2,1)S(1)} %collective-permute-done.6.got), custom_call_target="tpu_custom_call" | custom-call | flops 1000 | bytes 2621448 | tf_op jit(solution)/shard_map/pallas_call | solution.py:81
  136.8 0.0 all-to-all-done
  136.8 1.8 %convert_reduce_fusion = f32[50,240]{1,0:T(8,128)S(1)} fusion(bf16[64,50,240]{2,1,0:T(8,128)(2,1)} %all-to-all-done), kind=kLoop, calls=%fused_computation | loop fusion | flops 1524000 | bytes 1584000 | tf_op jit(solution)/shard_map/reduce_sum | solution.py:461
  138.7 0.1 slice.15
  138.8 0.6 copy.8
  139.4 0.1 slice.13
  139.5 0.6 copy.7
  (14 shorter events, 0.0 us)
Async XLA Ops:
  0.7 1.6 %copy-start = (bf16[3,3,320,320]{3,2,1,0:T(8,128)(2,1)S(1)}, bf16[3,3,320,320]{3,2,1,0:T(8,128)(2,1)}, u32[]{:S(2)}) copy-start(bf16[3,3,320,320]{3,2,1,0:T(8,128)(2,1)} %param.6) | copy-start | bytes 5529604
  2.3 1.4 %copy-start.2 = (bf16[1,2,32,32,320]{4,3,2,1,0:T(8,128)(2,1)S(1)}, bf16[1,2,32,32,320]{4,3,2,1,0:T(8,128)(2,1)}, u32[]{:S(2)}) copy-start(bf16[1,2,32,32,320]{4,3,2,1,0:T(8,128)(2,1)} %param.4) | copy-start | bytes 3932164
  3.8 8.5 %copy-start.3 = (bf16[1,2,32,32,320]{4,3,2,1,0:T(8,128)(2,1)S(1)}, bf16[1,2,32,32,320]{4,3,2,1,0:T(8,128)(2,1)}, u32[]{:S(2)}) copy-start(bf16[1,2,32,32,320]{4,3,2,1,0:T(8,128)(2,1)} %param.5) | copy-start | bytes 3932164
  7.7 1.3 copy-start.5
  9.1 11.2 %collective-permute-start.2 = (bf16[1360,128]{1,0:T(8,128)(2,1)}, bf16[1360,128]{1,0:T(8,128)(2,1)S(1)}, u32[]{:S(2)}, u32[]{:S(2)}) collective-permute-start(bf16[1360,128]{1,0:T(8,128)(2,1)} %get-tuple-element.47), channel_id=1, source_target_pairs={{0,1},{1,0},{2,3},{3,2},{4,5},{5,4},{6,7},{7,6},{8,9},{9,8},{10,11... | collective-permute-start | bytes 1044488 | tf_op jit(solution)/shard_map/ppermute | solution.py:369
  10.5 18.8 %collective-permute-start = (bf16[17,32,320]{2,1,0:T(8,128)(2,1)S(1)}, bf16[17,32,320]{2,1,0:T(8,128)(2,1)S(1)}, u32[]{:S(2)}, u32[]{:S(2)}) collective-permute-start(bf16[17,32,320]{2,1,0:T(8,128)(2,1)S(1)} %bitcast.38), channel_id=1, source_target_pairs={{0,1},{1,0},{2,3},{3,2},{4,5},{5,4},{6,7},{7,6},{8,9},{9,8},{10,11... | collective-permute-start | bytes 1044488 | tf_op jit(solution)/shard_map/ppermute | solution.py:369
  12.2 1.4 copy-start.4
  13.6 15.7 %copy-start.1 = (bf16[3,3,320,320]{3,2,1,0:T(8,128)(2,1)S(1)}, bf16[3,3,320,320]{3,2,1,0:T(8,128)(2,1)}, u32[]{:S(2)}) copy-start(bf16[3,3,320,320]{3,2,1,0:T(8,128)(2,1)} %param.6) | copy-start | bytes 5529604
  14.9 23.8 %collective-permute-start.3 = (bf16[2560,128]{1,0:T(8,128)(2,1)S(1)}, bf16[2560,128]{1,0:T(8,128)(2,1)S(1)}, u32[]{:S(2)}, u32[]{:S(2)}) collective-permute-start(bf16[2560,128]{1,0:T(8,128)(2,1)S(1)} %get-tuple-element.51), channel_id=1, source_target_pairs={{1,3},{2,0},{3,5},{4,2},{5,7},{6,4},{7,9},{8,6},{9,11},{10,8},{11,... | collective-permute-start | bytes 1966088 | tf_op jit(solution)/shard_map/ppermute | solution.py:369
  20.3 14.8 %collective-permute-start.7 = (bf16[1280,128]{1,0:T(8,128)(2,1)S(1)}, bf16[1280,128]{1,0:T(8,128)(2,1)S(1)}, u32[]{:S(2)}, u32[]{:S(2)}) collective-permute-start(bf16[1280,128]{1,0:T(8,128)(2,1)S(1)} %get-tuple-element.60), channel_id=1, source_target_pairs={{0,1},{1,0},{2,3},{3,2},{4,5},{5,4},{6,7},{7,6},{8,9},{9,8},{10,11... | collective-permute-start | bytes 983048 | tf_op jit(solution)/shard_map/ppermute | solution.py:369
  31.2 13.9 %collective-permute-start.1 = (bf16[16,32,320]{2,1,0:T(8,128)(2,1)S(1)}, bf16[16,32,320]{2,1,0:T(8,128)(2,1)S(1)}, u32[]{:S(2)}, u32[]{:S(2)}) collective-permute-start(bf16[16,32,320]{2,1,0:T(8,128)(2,1)S(1)} %bitcast.27), channel_id=1, source_target_pairs={{0,2},{2,4},{3,1},{4,6},{5,3},{6,8},{7,5},{8,10},{9,7},{10,12},{11... | collective-permute-start | bytes 983048 | tf_op jit(solution)/shard_map/ppermute | solution.py:369
  35.1 18.1 %collective-permute-start.9 = (bf16[1280,128]{1,0:T(8,128)(2,1)S(1)}, bf16[1280,128]{1,0:T(8,128)(2,1)S(1)}, u32[]{:S(2)}, u32[]{:S(2)}) collective-permute-start(bf16[1280,128]{1,0:T(8,128)(2,1)S(1)} %get-tuple-element.64), channel_id=1, source_target_pairs={{0,1},{1,0},{2,3},{3,2},{4,5},{5,4},{6,7},{7,6},{8,9},{9,8},{10,11... | collective-permute-start | bytes 983048 | tf_op jit(solution)/shard_map/ppermute | solution.py:369
  35.4 17.9 %collective-permute-start.8 = (bf16[1280,128]{1,0:T(8,128)(2,1)S(1)}, bf16[1280,128]{1,0:T(8,128)(2,1)S(1)}, u32[]{:S(2)}, u32[]{:S(2)}) collective-permute-start(bf16[1280,128]{1,0:T(8,128)(2,1)S(1)} %collective-permute-done.7.folded3), channel_id=1, source_target_pairs={{0,2},{2,4},{3,1},{4,6},{5,3},{6,8},{7,5},{8,10},{9,7},{10,12},{11... | collective-permute-start | bytes 983048 | tf_op jit(solution)/shard_map/ppermute | solution.py:369
  48.4 14.3 %collective-permute-start.5 = (bf16[16,32,320]{2,1,0:T(8,128)(2,1)S(1)}, bf16[16,32,320]{2,1,0:T(8,128)(2,1)S(1)}, u32[]{:S(2)}, u32[]{:S(2)}) collective-permute-start(bf16[16,32,320]{2,1,0:T(8,128)(2,1)S(1)} %bitcast.36), channel_id=1, source_target_pairs={{1,3},{2,0},{3,5},{4,2},{5,7},{6,4},{7,9},{8,6},{9,11},{10,8},{11,... | collective-permute-start | bytes 983048 | tf_op jit(solution)/shard_map/ppermute | solution.py:369
  51.8 10.9 %collective-permute-start.4 = (bf16[16,32,320]{2,1,0:T(8,128)(2,1)S(1)}, bf16[16,32,320]{2,1,0:T(8,128)(2,1)S(1)}, u32[]{:S(2)}, u32[]{:S(2)}) collective-permute-start(bf16[16,32,320]{2,1,0:T(8,128)(2,1)S(1)} %bitcast.34), channel_id=1, source_target_pairs={{0,2},{2,4},{3,1},{4,6},{5,3},{6,8},{7,5},{8,10},{9,7},{10,12},{11... | collective-permute-start | bytes 983048 | tf_op jit(solution)/shard_map/ppermute | solution.py:369
  56.8 13.0 %collective-permute-start.11 = (bf16[16,32,320]{2,1,0:T(8,128)(2,1)S(1)}, bf16[16,32,320]{2,1,0:T(8,128)(2,1)S(1)}, u32[]{:S(2)}, u32[]{:S(2)}) collective-permute-start(bf16[16,32,320]{2,1,0:T(8,128)(2,1)S(1)} %bitcast.35), channel_id=1, source_target_pairs={{1,3},{2,0},{3,5},{4,2},{5,7},{6,4},{7,9},{8,6},{9,11},{10,8},{11,... | collective-permute-start | bytes 983048 | tf_op jit(solution)/shard_map/ppermute | solution.py:369
  61.4 10.4 %collective-permute-start.10 = (bf16[16,32,320]{2,1,0:T(8,128)(2,1)S(1)}, bf16[16,32,320]{2,1,0:T(8,128)(2,1)S(1)}, u32[]{:S(2)}, u32[]{:S(2)}) collective-permute-start(bf16[16,32,320]{2,1,0:T(8,128)(2,1)S(1)} %bitcast.33), channel_id=1, source_target_pairs={{0,2},{2,4},{3,1},{4,6},{5,3},{6,8},{7,5},{8,10},{9,7},{10,12},{11... | collective-permute-start | bytes 983048 | tf_op jit(solution)/shard_map/ppermute | solution.py:369
  66.1 5.7 %copy-start.6 = (bf16[2,4,512,240]{3,2,1,0:T(8,128)(2,1)S(1)}, bf16[2,4,512,240]{3,2,1,0:T(8,128)(2,1)}, u32[]{:S(2)}) copy-start(bf16[2,4,512,240]{3,2,1,0:T(8,128)(2,1)} %copy-done.5) | copy-start | bytes 5898244
  79.3 3.6 %collective-permute-start.12 = (bf16[2,5,320,240]{3,2,1,0:T(8,128)(2,1)S(1)}, bf16[2,5,320,240]{3,2,1,0:T(8,128)(2,1)S(1)}, u32[]{:S(2)}, u32[]{:S(2)}) collective-permute-start(bf16[2,5,320,240]{3,2,1,0:T(8,128)(2,1)S(1)} %get-tuple-element.78), channel_id=1, source_target_pairs={{0,32},{32,0},{64,96},{96,64},{1,33},{33,1},{65,97},{97,65},{2,34}... | collective-permute-start | bytes 4608008 | tf_op jit(solution)/shard_map/ppermute | solution.py:369
  85.4 51.5 %all-to-all-start = ((bf16[64,50,240]{2,1,0:T(8,128)(2,1)}), bf16[64,50,240]{2,1,0:T(8,128)(2,1)}, u32[]{:S(2)}, u32[]{:S(2)}) async-start(bf16[64,50,240]{2,1,0:T(8,128)(2,1)} %shard_map.77), calls=%async_computation | async-start | bytes 3670016 | tf_op jit(solution)/shard_map/all_to_all | solution.py:460
  100.2 34.9 %collective-permute-start.6 = (bf16[2560,128]{1,0:T(8,128)(2,1)S(1)}, bf16[2560,128]{1,0:T(8,128)(2,1)S(1)}, u32[]{:S(2)}, u32[]{:S(2)}) collective-permute-start(bf16[2560,128]{1,0:T(8,128)(2,1)S(1)} %get-tuple-element.58), channel_id=1, source_target_pairs={{0,1},{1,0},{2,3},{3,2},{4,5},{5,4},{6,7},{7,6},{8,9},{9,8},{10,11... | collective-permute-start | bytes 1966088 | tf_op jit(solution)/shard_map/ppermute | solution.py:369

commit v7 on v5

--- a/solution.py
+++ b/solution.py
@@ -29,6 +29,7 @@
 
 ONE = (PX, C)
 THREE_TAILS = 3 * TAIL
+FOLDED = PX * C // LANES
 SIDES = (CLIPS, PX, 3 * WIDTH)
 KERNELS = (3, C, C)
 
@@ -71,10 +72,6 @@
             self.copy.wait()
             self.copy = None
         return self.ref
-
-
-def nth(ref, n):
-    return ref.at[pl.ds(n * PX, PX), :]
 
 
 def run(kernel, outs, args, scratch=(), copies=0, flops=0, far=(), far_outs=False):
@@ -113,6 +110,10 @@
     pad[pl.ds(0, COLS), :] = jnp.zeros((COLS, C), BF)
     pad[pl.ds(TALL, COLS), :] = jnp.zeros((COLS, C), BF)
     return pad.at[pl.ds(pl.multiple_of(COLS * (1 - odd), COLS), TALL), :]
+
+
+def part(ref, n):
+    return ref.at[pl.ds(n * FOLDED, FOLDED), :]
 
 
 def fold(rows, dst):
@@ -243,7 +244,7 @@
         if q < 2:
             own[q] = value
         else:
-            sent[pl.ds((3 - q) * PX, PX), :] = value
+            fold(value, part(sent, 3 - q))
 
 
 def descend(six, q, before, vw, layer, wk):
@@ -330,13 +331,14 @@
     move.finish()
 
 
-def place(at, own, got, out, sems):
+def place(at, own, got, out, vgot, sems):
     odd = at[0]
     move = Mover(sems)
     here, there = pl.multiple_of(PX * odd, PX), pl.multiple_of(PX * (1 - odd), PX)
     for q, frame in enumerate((odd, 1 - odd)):
         move.put(own.at[q], out.at[frame, pl.ds(here, PX), :])
-        move.put(nth(got, q), out.at[frame, pl.ds(there, PX), :])
+        unfold(part(got, q), vgot.at[q])
+        move.put(vgot.at[q], out.at[frame, pl.ds(there, PX), :])
     move.finish()
 
 
@@ -367,7 +369,7 @@
     ws = spatial_weight.reshape(9, C, C)
     flops = 2 * PX * C * C
 
-    flat, two, four, six = (2 * PX, C), (2, PX, C), (4, PX, C), (6, PX, C)
+    two, four, six = (2, PX, C), (4, PX, C), (6, PX, C)
     packed = [(3, HEAD, THREE_TAILS), (3, THREE_TAILS, HEAD), (THREE_TAILS, THREE_TAILS)]
     taps = [(2, *KERNELS), (2, THREE_TAILS, C)]
     pad = (PX + 2 * COLS, C)
@@ -393,7 +395,7 @@
     c3 = send(after(c3, x2), swap)
     s2, sides2 = run(conv_folded, [ONE, SIDES], (at, x2, *wp), [pad], 0, 4 * flops)
     c2 = send(after(c2, c3), swap)
-    cot_right = send(after(cot0, right), outer)
+    cot_right = send(after(cot0, s3), outer)
     cot_left = send(c3, inner)
 
     acts1, state1, last, first = run(
@@ -414,7 +416,7 @@
     back_left = send(last, inner)
     back_right = send(first, outer)
     acts2, own, sent = run(
-        layer_two, [six, two, flat], (at, left1, state1, right1, vt, vtk), flops=8 * flops
+        layer_two, [six, two, (2 * FOLDED, LANES)], (at, left1, state1, right1, vt, vtk), flops=8 * flops
     )
     returned = send(sent, swap)
 
@@ -434,7 +436,7 @@
         flops=32 * flops,
     )
     got = send(sent, cores, "clip")
-    (out,) = run(place, [(2, FULL, C)], (at, own, returned), (), 4, 1000, far_outs=True)
+    (out,) = run(place, [(2, FULL, C)], (at, own, returned), [two], 4, 1000, far_outs=True)
 
     rows = C // owners
     block = (2 * owners, 5 * rows, 3 * WIDTH)

time: 146 us -> 143 us (0.979)
  waiting for transfers between devices: 58 us -> 54.9 us
    ppermute x14, waiting for transfers between devices: 58 us -> 54.9 us  [send(): return lax.ppermute(value, axis, perm).reshape(shape)]
  transfers between devices with their start and end apart: 15 -> 15, of which waited for: 6 -> 6; matrix products, arithmetic and copies ran while one was open for 1% -> 1% of each run, Pallas kernels for 14% -> 15%
where the time goes in v7:
time: 143 us; the launch traced here: 142 us
  waiting for transfers between devices  54.9 us (38%)
  starting transfers between devices  41.5 us (29%)
  Pallas kernels  35.1 us (25%)
  local copies, waits for them, and re-layouts  9.14 us (6%)
    ppermute x14, waiting for transfers between devices, send(): return lax.ppermute(value, axis, perm).reshape(shape)  54.9 us
    pallas_call x11, Pallas kernels, run(): pl.pallas_call(kernel, out_shape=[jax.ShapeDtypeStruct(s, BF) for s in ou...  35.1 us
    ppermute x14, starting transfers between devices, send(): return lax.ppermute(value, axis, perm).reshape(shape)  24.7 us
    all_to_all x1, starting transfers between devices, step(): lax.all_to_all(packs, ('frame', 'clip'), split_axis=0, concat_axis=0, axi...  16.8 us
    unnamed x32, local copies, waits for them, and re-layouts  7.91 us
  transfers between devices with their start and end apart: 15, of which 6 were waited for; matrix products, arithmetic and copies ran while one was open for 1% of the time, Pallas kernels for 15%

profile of v7, /device:TPU:8, one launch (start us, length us, event | category | flops | bytes accessed | tf_op | source)
XLA Modules:
  0.0 142.0 jit_solution(7558743482314615072)
XLA Ops:
  0.6 0.1 pad_add_fusion.at
  0.7 1.6 %copy-done = bf16[3,3,320,320]{3,2,1,0:T(8,128)(2,1)S(1)} copy-done((bf16[3,3,320,320]{3,2,1,0:T(8,128)(2,1)S(1)}, bf16[3,3,320,320]{3,2,1,0:T(8,128)(2,1)}, u32[]{:S(2)}) %copy-start) | copy-done | bytes 1843224
  2.4 1.4 copy-done.2
  3.8 4.0 %shard_map.67 = (bf16[512,320]{1,0:T(8,128)(2,1)S(1)}, bf16[512,320]{1,0:T(8,128)(2,1)S(1)}, bf16[2,4,512,240]{3,2,1,0:T(8,128)(2,1)S(1)}, bf16[1360,128]{1,0:T(...) custom-call(s32[2]{0:T(128)S(1)} %pad_add_fusion.at, ...), custom_call_target="tpu_custom_call" | custom-call | flops 838860800 | bytes 6787080 | tf_op jit(solution)/shard_map/pallas_call | solution.py:81
  7.8 0.7 copy-done.5
  8.5 0.7 copy-done.7
  9.2 0.8 copy-done.9
  10.0 1.3 copy-done.11
  11.3 0.3 collective-permute-start.2
  11.7 1.0 constant_dynamic-slice_fusion
  12.7 0.0 copy-start.8
  12.7 0.0 copy-start.1
  12.8 1.8 %collective-permute-start = (bf16[17,32,320]{2,1,0:T(8,128)(2,1)S(1)}, bf16[17,32,320]{2,1,0:T(8,128)(2,1)S(1)}, u32[]{:S(2)}, u32[]{:S(2)}) collective-permute-start(bf16[17,32,320]{2,1,0:T(8,128)(2,1)S(1)} %bitcast.46), channel_id=1, source_target_pairs={{0,1},{1,0},{2,3},{3,2},{4,5},{5,4},{6,7},{7,6},{8,9},{9,8},{10,11... | collective-permute-start | bytes 1044488 | tf_op jit(solution)/shard_map/ppermute | solution.py:365
  14.5 1.2 shard_map.70
  15.7 7.0 %collective-permute-done.2.x = bf16[1360,128]{1,0:T(8,128)(2,1)} collective-permute-done((bf16[1360,128]{1,0:T(8,128)(2,1)}, bf16[1360,128]{1,0:T(8,128)(2,1)}, u32[]{:S(2)}, u32[]{:S(2)}) %collective-permute-start.2) | collective-permute-done | bytes 348192 | tf_op jit(solution)/shard_map/ppermute | solution.py:365
  22.7 0.3 collective-permute-start.7
  23.0 3.5 %collective-permute-start.3 = (bf16[16,32,320]{2,1,0:T(8,128)(2,1)S(1)}, bf16[16,32,320]{2,1,0:T(8,128)(2,1)S(1)}, u32[]{:S(2)}, u32[]{:S(2)}) collective-permute-start(bf16[16,32,320]{2,1,0:T(8,128)(2,1)S(1)} %bitcast.32), channel_id=1, source_target_pairs={{1,3},{2,0},{3,5},{4,2},{5,7},{6,4},{7,9},{8,6},{9,11},{10,8},{11,... | collective-permute-start | bytes 983048 | tf_op jit(solution)/shard_map/ppermute | solution.py:365
  26.5 5.0 %collective-permute-done = bf16[17,32,320]{2,1,0:T(8,128)(2,1)S(1)} collective-permute-done((bf16[17,32,320]{2,1,0:T(8,128)(2,1)S(1)}, bf16[17,32,320]{2,1,0:T(8,128)(2,1)S(1)}, u32[]{:S(2)}, u32[]{:S(2)}) %collective-permute-start) | collective-permute-done | bytes 348192 | tf_op jit(solution)/shard_map/ppermute | solution.py:365
  31.5 1.9 %shard_map.68 = (bf16[512,320]{1,0:T(8,128)(2,1)S(1)}, bf16[4,512,240]{2,1,0:T(8,128)(2,1)S(1)}) custom-call(s32[2]{0:T(128)S(1)} %pad_add_fusion.at, bf16[544,320]{1,0:T(8,128)(2,1)S(1)} %bitcast.31, bf16[9,320,320]{2,1,0:T(8,128)(2,1)S(1)} %bitcast.25, bf16[3,256,192]{2,1,0:T(8,128)(2,1)S(1)} %get-tuple-element.41.wn, bf16[3,192,256]{2,1,0:T(8,128)(2,1)S(1)} %copy-done.6, ...), custom_call_target="tpu_custom_call" | custom-call | flops 419430400 | bytes 4165640 | tf_op jit(solution)/shard_map/pallas_call | solution.py:81
  33.4 1.3 collective-permute-start.1
  34.7 4.6 %collective-permute-start.10 = (bf16[16,32,320]{2,1,0:T(8,128)(2,1)S(1)}, bf16[16,32,320]{2,1,0:T(8,128)(2,1)S(1)}, u32[]{:S(2)}, u32[]{:S(2)}) collective-permute-start(bf16[16,32,320]{2,1,0:T(8,128)(2,1)S(1)} %bitcast.29), channel_id=1, source_target_pairs={{1,3},{2,0},{3,5},{4,2},{5,7},{6,4},{7,9},{8,6},{9,11},{10,8},{11,... | collective-permute-start | bytes 983048 | tf_op jit(solution)/shard_map/ppermute | solution.py:365
  39.3 0.1 collective-permute-start.9
  39.4 1.4 %collective-permute-start.8 = (bf16[1280,128]{1,0:T(8,128)(2,1)S(1)}, bf16[1280,128]{1,0:T(8,128)(2,1)S(1)}, u32[]{:S(2)}, u32[]{:S(2)}) collective-permute-start(bf16[1280,128]{1,0:T(8,128)(2,1)S(1)} %collective-permute-done.7.folded3), channel_id=1, source_target_pairs={{0,2},{2,4},{3,1},{4,6},{5,3},{6,8},{7,5},{8,10},{9,7},{10,12},{11... | collective-permute-start | bytes 983048 | tf_op jit(solution)/shard_map/ppermute | solution.py:365
  40.9 2.4 %shard_map.69 = (bf16[512,320]{1,0:T(8,128)(2,1)S(1)}, bf16[4,512,240]{2,1,0:T(8,128)(2,1)S(1)}) custom-call(s32[2]{0:T(128)S(1)} %pad_add_fusion.at, bf16[1360,128]{1,0:T(8,128)(2,1)} %collective-permute-done.2.x, bf16[9,320,320]{2,1,0:T(8,128)(2,1)S(1)} %bitcast.26, bf16[3,256,192]{2,1,0:T(8,128)(2,1)S(1)} %get-tuple-element.41.wn, ...), custom_call_target="tpu_custom_call" | custom-call | flops 419430400 | bytes 4165640 | tf_op jit(solution)/shard_map/pallas_call | solution.py:81
  43.3 3.7 %collective-permute-done.1 = bf16[16,32,320]{2,1,0:T(8,128)(2,1)S(1)} collective-permute-done((bf16[16,32,320]{2,1,0:T(8,128)(2,1)S(1)}, bf16[16,32,320]{2,1,0:T(8,128)(2,1)S(1)}, u32[]{:S(2)}, u32[]{:S(2)}) %collective-permute-start.1) | collective-permute-done | bytes 327712 | tf_op jit(solution)/shard_map/ppermute | solution.py:365
  47.1 3.3 %shard_map.71 = (bf16[6,512,320]{2,1,0:T(8,128)(2,1)S(1)}, bf16[4,512,320]{2,1,0:T(8,128)(2,1)S(1)}, bf16[512,320]{1,0:T(8,128)(2,1)S(1)}, bf16[512,320]{1,0:T(8,128)(2,1)S(1)}) custom-call(s32[2]{0:T(128)S(1)} %pad_add_fusion.at, bf16[512,320]{1,0:T(8,128)(2,1)S(1)} %bitcast.38, bf16[512,320]{1,0:T(8,128)(2,1)S(1)} %copy-done.8, ...), custom_call_target="tpu_custom_call" | custom-call | flops 838860800 | bytes 7372808 | tf_op jit(solution)/shard_map/pallas_call | solution.py:81
  50.3 3.4 %collective-permute-start.5 = (bf16[16,32,320]{2,1,0:T(8,128)(2,1)S(1)}, bf16[16,32,320]{2,1,0:T(8,128)(2,1)S(1)}, u32[]{:S(2)}, u32[]{:S(2)}) collective-permute-start(bf16[16,32,320]{2,1,0:T(8,128)(2,1)S(1)} %bitcast.42), channel_id=1, source_target_pairs={{1,3},{2,0},{3,5},{4,2},{5,7},{6,4},{7,9},{8,6},{9,11},{10,8},{11,... | collective-permute-start | bytes 983048 | tf_op jit(solution)/shard_map/ppermute | solution.py:365
  53.7 1.5 %collective-permute-start.4 = (bf16[16,32,320]{2,1,0:T(8,128)(2,1)S(1)}, bf16[16,32,320]{2,1,0:T(8,128)(2,1)S(1)}, u32[]{:S(2)}, u32[]{:S(2)}) collective-permute-start(bf16[16,32,320]{2,1,0:T(8,128)(2,1)S(1)} %bitcast.41), channel_id=1, source_target_pairs={{0,2},{2,4},{3,1},{4,6},{5,3},{6,8},{7,5},{8,10},{9,7},{10,12},{11... | collective-permute-start | bytes 983048 | tf_op jit(solution)/shard_map/ppermute | solution.py:365
  55.2 3.5 %shard_map.74 = (bf16[4,512,320]{2,1,0:T(8,128)(2,1)S(1)}, bf16[512,320]{1,0:T(8,128)(2,1)S(1)}, bf16[512,320]{1,0:T(8,128)(2,1)S(1)}, bf16[512,320]{1,0:T(8,128)(2,1)S(1)}, bf16[512,320]{1,0:T(8,128)(2,1)S(1)}) custom-call(s32[2]{0:T(128)S(1)} %pad_add_fusion.at, bf16[1280,128]{1,0:T(8,128)(2,1)S(1)} %collective-permute-done.8.folded, ...), custom_call_target="tpu_custom_call" | custom-call | flops 838860800 | bytes 7372808 | tf_op jit(solution)/shard_map/pallas_call | solution.py:81
  58.8 4.6 %collective-permute-start.12 = (bf16[16,32,320]{2,1,0:T(8,128)(2,1)S(1)}, bf16[16,32,320]{2,1,0:T(8,128)(2,1)S(1)}, u32[]{:S(2)}, u32[]{:S(2)}) collective-permute-start(bf16[16,32,320]{2,1,0:T(8,128)(2,1)S(1)} %bitcast.44), channel_id=1, source_target_pairs={{1,3},{2,0},{3,5},{4,2},{5,7},{6,4},{7,9},{8,6},{9,11},{10,8},{11,... | collective-permute-start | bytes 983048 | tf_op jit(solution)/shard_map/ppermute | solution.py:365
  63.4 1.3 collective-permute-start.11
  64.7 3.4 %shard_map.72 = (bf16[6,512,320]{2,1,0:T(8,128)(2,1)S(1)}, bf16[2,512,320]{2,1,0:T(8,128)(2,1)S(1)}, bf16[2560,128]{1,0:T(8,128)(2,1)S(1)}) custom-call(s32[2]{0:T(128)S(1)} %pad_add_fusion.at, bf16[512,320]{1,0:T(8,128)(2,1)S(1)} %bitcast.37, bf16[4,512,320]{2,1,0:T(8,128)(2,1)S(1)} %get-tuple-element.54.state, bf16[512,320]{1,0:T(8,128)(2,1)S(1)} %bitcast.35, ...), custom_call_target="tpu_custom_call" | custom-call | flops 838860800 | bytes 6717448 | tf_op jit(solution)/shard_map/pallas_call | solution.py:81
  68.1 3.8 %shard_map.75.passing = bf16[4,2,320,240]{3,2,1,0:T(8,128)(2,1)S(1)} custom-call(s32[2]{0:T(128)S(1)} %pad_add_fusion.at, bf16[512,320]{1,0:T(8,128)(2,1)S(1)} %get-tuple-element.64.cot0, bf16[512,320]{1,0:T(8,128)(2,1)S(1)} %get-tuple-element.61.cot1, bf16[512,320]{1,0:T(8,128)(2,1)S(1)} %get-tuple-element.73.c2, ...), custom_call_target="tpu_custom_call" | custom-call | flops 1677721600 | bytes 7782408 | tf_op jit(solution)/shard_map/pallas_call | solution.py:81
  71.9 1.2 collective-permute-done.11
  73.1 7.4 %shard_map.76 = (bf16[2,5,320,240]{3,2,1,0:T(8,128)(2,1)S(1)}, bf16[2,5,320,240]{3,2,1,0:T(8,128)(2,1)S(1)}) custom-call(s32[2]{0:T(128)S(1)} %pad_add_fusion.at, bf16[512,320]{1,0:T(8,128)(2,1)S(1)} %bitcast.40, bf16[4,512,320]{2,1,0:T(8,128)(2,1)S(1)} %get-tuple-element.68.back, bf16[512,320]{1,0:T(8,128)(2,1)S(1)} %bitcast.39, ...), custom_call_target="tpu_custom_call" | custom-call | flops 3355443200 | bytes 12984328 | tf_op jit(solution)/shard_map/pallas_call | solution.py:81
  80.4 0.1 collective-permute-start.13
  80.5 3.5 %collective-permute-done.13.got = bf16[2,5,320,240]{3,2,1,0:T(8,128)(2,1)S(1)} collective-permute-done((bf16[2,5,320,240]{3,2,1,0:T(8,128)(2,1)S(1)}, bf16[2,5,320,240]{3,2,1,0:T(8,128)(2,1)S(1)}, u32[]{:S(2)}, u32[]{:S(2)}) %collective-permute-start.13) | collective-permute-done | bytes 1536032 | tf_op jit(solution)/shard_map/ppermute | solution.py:365
  84.0 2.5 %shard_map.77 = bf16[64,50,240]{2,1,0:T(8,128)(2,1)} custom-call(s32[2]{0:T(128)S(1)} %pad_add_fusion.at, bf16[2,5,320,240]{3,2,1,0:T(8,128)(2,1)S(1)} %get-tuple-element.77.kept, bf16[2,5,320,240]{3,2,1,0:T(8,128)(2,1)S(1)} %collective-permute-done.13.got), custom_call_target="tpu_custom_call" | custom-call | flops 1000 | bytes 4608008 | tf_op jit(solution)/shard_map/pallas_call | solution.py:81
  86.6 0.0 copy-start.14
  86.6 16.8 %all-to-all-start = ((bf16[64,50,240]{2,1,0:T(8,128)(2,1)}), bf16[64,50,240]{2,1,0:T(8,128)(2,1)S(1)}, u32[]{:S(2)}, u32[]{:S(2)}) async-start(bf16[64,50,240]{2,1,0:T(8,128)(2,1)} %shard_map.77), calls=%async_computation | async-start | bytes 3670016 | tf_op jit(solution)/shard_map/all_to_all | solution.py:453
  103.4 0.5 collective-permute-start.6
  103.9 34.5 %collective-permute-done.6.got = bf16[2560,128]{1,0:T(8,128)(2,1)S(1)} collective-permute-done((bf16[2560,128]{1,0:T(8,128)(2,1)S(1)}, bf16[2560,128]{1,0:T(8,128)(2,1)S(1)}, u32[]{:S(2)}, u32[]{:S(2)}) %collective-permute-start.6) | collective-permute-done | bytes 655392 | tf_op jit(solution)/shard_map/ppermute | solution.py:365
  138.4 1.7 %shard_map.73 = bf16[2,1024,320]{2,1,0:T(8,128)(2,1)} custom-call(s32[2]{0:T(128)S(1)} %pad_add_fusion.at, bf16[2,512,320]{2,1,0:T(8,128)(2,1)S(1)} %get-tuple-element.56.own, bf16[2560,128]{1,0:T(8,128)(2,1)S(1)} %collective-permute-done.6.got), custom_call_target="tpu_custom_call" | custom-call | flops 1000 | bytes 2621448 | tf_op jit(solution)/shard_map/pallas_call | solution.py:81
  140.2 0.3 convert_reduce_fusion
  140.5 0.1 slice.15
  140.6 0.6 copy.8
  141.3 0.1 slice.13
  141.3 0.6 copy.7
  (32 shorter events, 0.1 us)
Async XLA Ops:
  0.7 1.6 %copy-start = (bf16[3,3,320,320]{3,2,1,0:T(8,128)(2,1)S(1)}, bf16[3,3,320,320]{3,2,1,0:T(8,128)(2,1)}, u32[]{:S(2)}) copy-start(bf16[3,3,320,320]{3,2,1,0:T(8,128)(2,1)} %param.6) | copy-start | bytes 5529604
  2.3 1.4 copy-start.2
  3.8 10.8 %copy-start.3 = (bf16[1,2,32,32,320]{4,3,2,1,0:T(8,128)(2,1)S(1)}, bf16[1,2,32,32,320]{4,3,2,1,0:T(8,128)(2,1)}, u32[]{:S(2)}) copy-start(bf16[1,2,32,32,320]{4,3,2,1,0:T(8,128)(2,1)} %param.5) | copy-start | bytes 3932164
  3.8 10.8 %copy-start.4 = (bf16[2,3,320,320]{3,2,1,0:T(8,128)(2,1)S(1)}, bf16[2,3,320,320]{3,2,1,0:T(8,128)(2,1)}, u32[]{:S(2)}) copy-start(bf16[2,3,320,320]{3,2,1,0:T(8,128)(2,1)} %tw) | copy-start | bytes 3686404
  7.8 0.7 copy-start.5
  8.5 0.7 copy-start.7
  9.2 0.8 copy-start.9
  10.0 1.3 copy-start.11
  11.3 11.3 %collective-permute-start.2 = (bf16[1360,128]{1,0:T(8,128)(2,1)}, bf16[1360,128]{1,0:T(8,128)(2,1)}, u32[]{:S(2)}, u32[]{:S(2)}) collective-permute-start(bf16[1360,128]{1,0:T(8,128)(2,1)} %get-tuple-element.47), channel_id=1, source_target_pairs={{0,1},{1,0},{2,3},{3,2},{4,5},{5,4},{6,7},{7,6},{8,9},{9,8},{10,11... | collective-permute-start | bytes 1044488 | tf_op jit(solution)/shard_map/ppermute | solution.py:365
  12.7 10.3 %copy-start.8 = (bf16[512,320]{1,0:T(8,128)(2,1)S(1)}, bf16[512,320]{1,0:T(8,128)(2,1)}, u32[]{:S(2)}) copy-start(bf16[512,320]{1,0:T(8,128)(2,1)} %copy-done.7) | copy-start | bytes 983044
  12.7 18.8 %copy-start.1 = (bf16[3,3,320,320]{3,2,1,0:T(8,128)(2,1)S(1)}, bf16[3,3,320,320]{3,2,1,0:T(8,128)(2,1)}, u32[]{:S(2)}) copy-start(bf16[3,3,320,320]{3,2,1,0:T(8,128)(2,1)} %param.6) | copy-start | bytes 5529604
  12.8 18.8 %copy-start.6 = (bf16[3,192,256]{2,1,0:T(8,128)(2,1)S(1)}, bf16[3,192,256]{2,1,0:T(8,128)(2,1)}, u32[]{:S(2)}) copy-start(bf16[3,192,256]{2,1,0:T(8,128)(2,1)} %copy-done.5) | copy-start | bytes 884740
  12.8 18.8 %collective-permute-start = (bf16[17,32,320]{2,1,0:T(8,128)(2,1)S(1)}, bf16[17,32,320]{2,1,0:T(8,128)(2,1)S(1)}, u32[]{:S(2)}, u32[]{:S(2)}) collective-permute-start(bf16[17,32,320]{2,1,0:T(8,128)(2,1)S(1)} %bitcast.46), channel_id=1, source_target_pairs={{0,1},{1,0},{2,3},{3,2},{4,5},{5,4},{6,7},{7,6},{8,9},{9,8},{10,11... | collective-permute-start | bytes 1044488 | tf_op jit(solution)/shard_map/ppermute | solution.py:365
  22.7 16.6 %collective-permute-start.7 = (bf16[1280,128]{1,0:T(8,128)(2,1)S(1)}, bf16[1280,128]{1,0:T(8,128)(2,1)S(1)}, u32[]{:S(2)}, u32[]{:S(2)}) collective-permute-start(bf16[1280,128]{1,0:T(8,128)(2,1)S(1)} %get-tuple-element.59), channel_id=1, source_target_pairs={{0,1},{1,0},{2,3},{3,2},{4,5},{5,4},{6,7},{7,6},{8,9},{9,8},{10,11... | collective-permute-start | bytes 983048 | tf_op jit(solution)/shard_map/ppermute | solution.py:365
  23.0 20.3 %collective-permute-start.3 = (bf16[16,32,320]{2,1,0:T(8,128)(2,1)S(1)}, bf16[16,32,320]{2,1,0:T(8,128)(2,1)S(1)}, u32[]{:S(2)}, u32[]{:S(2)}) collective-permute-start(bf16[16,32,320]{2,1,0:T(8,128)(2,1)S(1)} %bitcast.32), channel_id=1, source_target_pairs={{1,3},{2,0},{3,5},{4,2},{5,7},{6,4},{7,9},{8,6},{9,11},{10,8},{11,... | collective-permute-start | bytes 983048 | tf_op jit(solution)/shard_map/ppermute | solution.py:365
  33.4 13.6 %collective-permute-start.1 = (bf16[16,32,320]{2,1,0:T(8,128)(2,1)S(1)}, bf16[16,32,320]{2,1,0:T(8,128)(2,1)S(1)}, u32[]{:S(2)}, u32[]{:S(2)}) collective-permute-start(bf16[16,32,320]{2,1,0:T(8,128)(2,1)S(1)} %bitcast.33), channel_id=1, source_target_pairs={{0,2},{2,4},{3,1},{4,6},{5,3},{6,8},{7,5},{8,10},{9,7},{10,12},{11... | collective-permute-start | bytes 983048 | tf_op jit(solution)/shard_map/ppermute | solution.py:365
  34.7 20.5 %collective-permute-start.10 = (bf16[16,32,320]{2,1,0:T(8,128)(2,1)S(1)}, bf16[16,32,320]{2,1,0:T(8,128)(2,1)S(1)}, u32[]{:S(2)}, u32[]{:S(2)}) collective-permute-start(bf16[16,32,320]{2,1,0:T(8,128)(2,1)S(1)} %bitcast.29), channel_id=1, source_target_pairs={{1,3},{2,0},{3,5},{4,2},{5,7},{6,4},{7,9},{8,6},{9,11},{10,8},{11,... | collective-permute-start | bytes 983048 | tf_op jit(solution)/shard_map/ppermute | solution.py:365
  39.3 7.7 %copy-start.10 = (bf16[512,320]{1,0:T(8,128)(2,1)S(1)}, bf16[512,320]{1,0:T(8,128)(2,1)}, u32[]{:S(2)}) copy-start(bf16[512,320]{1,0:T(8,128)(2,1)} %copy-done.9) | copy-start | bytes 983044
  39.3 15.9 %collective-permute-start.9 = (bf16[1280,128]{1,0:T(8,128)(2,1)S(1)}, bf16[1280,128]{1,0:T(8,128)(2,1)S(1)}, u32[]{:S(2)}, u32[]{:S(2)}) collective-permute-start(bf16[1280,128]{1,0:T(8,128)(2,1)S(1)} %get-tuple-element.63), channel_id=1, source_target_pairs={{0,1},{1,0},{2,3},{3,2},{4,5},{5,4},{6,7},{7,6},{8,9},{9,8},{10,11... | collective-permute-start | bytes 983048 | tf_op jit(solution)/shard_map/ppermute | solution.py:365
  39.4 15.8 %collective-permute-start.8 = (bf16[1280,128]{1,0:T(8,128)(2,1)S(1)}, bf16[1280,128]{1,0:T(8,128)(2,1)S(1)}, u32[]{:S(2)}, u32[]{:S(2)}) collective-permute-start(bf16[1280,128]{1,0:T(8,128)(2,1)S(1)} %collective-permute-done.7.folded3), channel_id=1, source_target_pairs={{0,2},{2,4},{3,1},{4,6},{5,3},{6,8},{7,5},{8,10},{9,7},{10,12},{11... | collective-permute-start | bytes 983048 | tf_op jit(solution)/shard_map/ppermute | solution.py:365
  50.3 14.3 %collective-permute-start.5 = (bf16[16,32,320]{2,1,0:T(8,128)(2,1)S(1)}, bf16[16,32,320]{2,1,0:T(8,128)(2,1)S(1)}, u32[]{:S(2)}, u32[]{:S(2)}) collective-permute-start(bf16[16,32,320]{2,1,0:T(8,128)(2,1)S(1)} %bitcast.42), channel_id=1, source_target_pairs={{1,3},{2,0},{3,5},{4,2},{5,7},{6,4},{7,9},{8,6},{9,11},{10,8},{11,... | collective-permute-start | bytes 983048 | tf_op jit(solution)/shard_map/ppermute | solution.py:365
  53.7 11.0 %collective-permute-start.4 = (bf16[16,32,320]{2,1,0:T(8,128)(2,1)S(1)}, bf16[16,32,320]{2,1,0:T(8,128)(2,1)S(1)}, u32[]{:S(2)}, u32[]{:S(2)}) collective-permute-start(bf16[16,32,320]{2,1,0:T(8,128)(2,1)S(1)} %bitcast.41), channel_id=1, source_target_pairs={{0,2},{2,4},{3,1},{4,6},{5,3},{6,8},{7,5},{8,10},{9,7},{10,12},{11... | collective-permute-start | bytes 983048 | tf_op jit(solution)/shard_map/ppermute | solution.py:365
  58.8 13.1 %collective-permute-start.12 = (bf16[16,32,320]{2,1,0:T(8,128)(2,1)S(1)}, bf16[16,32,320]{2,1,0:T(8,128)(2,1)S(1)}, u32[]{:S(2)}, u32[]{:S(2)}) collective-permute-start(bf16[16,32,320]{2,1,0:T(8,128)(2,1)S(1)} %bitcast.44), channel_id=1, source_target_pairs={{1,3},{2,0},{3,5},{4,2},{5,7},{6,4},{7,9},{8,6},{9,11},{10,8},{11,... | collective-permute-start | bytes 983048 | tf_op jit(solution)/shard_map/ppermute | solution.py:365
  63.4 9.7 %collective-permute-start.11 = (bf16[16,32,320]{2,1,0:T(8,128)(2,1)S(1)}, bf16[16,32,320]{2,1,0:T(8,128)(2,1)S(1)}, u32[]{:S(2)}, u32[]{:S(2)}) collective-permute-start(bf16[16,32,320]{2,1,0:T(8,128)(2,1)S(1)} %bitcast.43), channel_id=1, source_target_pairs={{0,2},{2,4},{3,1},{4,6},{5,3},{6,8},{7,5},{8,10},{9,7},{10,12},{11... | collective-permute-start | bytes 983048 | tf_op jit(solution)/shard_map/ppermute | solution.py:365
  68.1 3.8 %copy-start.13 = (bf16[2560,128]{1,0:T(8,128)(2,1)}, bf16[2560,128]{1,0:T(8,128)(2,1)S(1)}, u32[]{:S(2)}) copy-start(bf16[2560,128]{1,0:T(8,128)(2,1)S(1)} %get-tuple-element.57) | copy-start | bytes 1966084
  68.1 5.0 %copy-start.12 = (bf16[2,4,512,240]{3,2,1,0:T(8,128)(2,1)S(1)}, bf16[2,4,512,240]{3,2,1,0:T(8,128)(2,1)}, u32[]{:S(2)}) copy-start(bf16[2,4,512,240]{3,2,1,0:T(8,128)(2,1)} %copy-done.11) | copy-start | bytes 5898244
  80.4 3.6 %collective-permute-start.13 = (bf16[2,5,320,240]{3,2,1,0:T(8,128)(2,1)S(1)}, bf16[2,5,320,240]{3,2,1,0:T(8,128)(2,1)S(1)}, u32[]{:S(2)}, u32[]{:S(2)}) collective-permute-start(bf16[2,5,320,240]{3,2,1,0:T(8,128)(2,1)S(1)} %get-tuple-element.78), channel_id=1, source_target_pairs={{0,32},{32,0},{64,96},{96,64},{1,33},{33,1},{65,97},{97,65},{2,34}... | collective-permute-start | bytes 4608008 | tf_op jit(solution)/shard_map/ppermute | solution.py:365
  86.6 16.8 %copy-start.14 = (bf16[2560,128]{1,0:T(8,128)(2,1)S(1)}, bf16[2560,128]{1,0:T(8,128)(2,1)}, u32[]{:S(2)}) copy-start(bf16[2560,128]{1,0:T(8,128)(2,1)} %copy-done.13) | copy-start | bytes 1966084
  86.6 53.6 %all-to-all-start = ((bf16[64,50,240]{2,1,0:T(8,128)(2,1)}), bf16[64,50,240]{2,1,0:T(8,128)(2,1)S(1)}, u32[]{:S(2)}, u32[]{:S(2)}) async-start(bf16[64,50,240]{2,1,0:T(8,128)(2,1)} %shard_map.77), calls=%async_computation | async-start | bytes 3670016 | tf_op jit(solution)/shard_map/all_to_all | solution.py:453
  103.4 35.0 %collective-permute-start.6 = (bf16[2560,128]{1,0:T(8,128)(2,1)S(1)}, bf16[2560,128]{1,0:T(8,128)(2,1)S(1)}, u32[]{:S(2)}, u32[]{:S(2)}) collective-permute-start(bf16[2560,128]{1,0:T(8,128)(2,1)S(1)} %copy-done.14), channel_id=1, source_target_pairs={{0,1},{1,0},{2,3},{3,2},{4,5},{5,4},{6,7},{7,6},{8,9},{9,8},{10,11... | collective-permute-start | bytes 1966088 | tf_op jit(solution)/shard_map/ppermute | solution.py:365

commit v8 on v7

--- a/solution.py
+++ b/solution.py
@@ -74,13 +74,13 @@
         return self.ref
 
 
-def run(kernel, outs, args, scratch=(), copies=0, flops=0, far=(), far_outs=False):
+def run(kernel, outs, args, scratch=(), copies=0, flops=0, far=(), far_outs=False, kind=BF):
     nbytes = sum(a.size * a.dtype.itemsize for a in args) + sum(
         functools.reduce(lambda m, n: m * n, s, 2) for s in outs
     )
     return pl.pallas_call(
         kernel,
-        out_shape=[jax.ShapeDtypeStruct(s, BF) for s in outs],
+        out_shape=[jax.ShapeDtypeStruct(s, kind) for s in outs],
         in_specs=[SM] + [HBM if n in far else VM for n in range(1, len(args))],
         out_specs=[HBM if far_outs else VM] * len(outs),
         scratch_shapes=[s if not isinstance(s, tuple) else pltpu.VMEM(s, BF) for s in scratch]
@@ -315,20 +315,38 @@
                 out[half, 3 + layer] = passing[b, layer]
 
 
-def pack(at, kept, got, out, wide, rows, vout, sems):
-    halves, taps, channels, _ = kept.shape
+def pack(at, kept, got, out, wide, rows):
+    halves, taps, channels, width = kept.shape
     owners = out.shape[0] // halves
     count = channels // owners
-    move = Mover(sems)
+    rows[:, pl.ds(width, 2 * LANES - width)] = jnp.zeros((channels, 2 * LANES - width), F32)
     for h in range(halves):
         for t in range(taps):
-            rows[...] = kept[h, t].astype(F32) + got[h, t].astype(F32)
+            rows[:, pl.ds(0, width)] = kept[h, t].astype(F32) + got[h, t].astype(F32)
             for owner in range(owners):
-                wide[owner, pl.ds(count * t, count), :] = rows[pl.ds(count * owner, count), :]
+                for n in range(2):
+                    block = pl.ds(count * (2 * t + n), count)
+                    wide[owner, block, :] = rows[pl.ds(count * owner, count), pl.ds(n * LANES, LANES)]
         for owner in range(owners):
-            vout[owners * h + owner] = wide[owner].astype(BF)
-        move.put(vout.at[pl.ds(owners * h, owners)], out.at[pl.ds(owners * h, owners)])
-    move.finish()
+            out[owners * h + owner] = wide[owner].astype(BF)
+
+
+def finish(at, parts, spatial, temporal):
+    total = parts[0].astype(F32)
+    for n in range(1, parts.shape[0]):
+        total = total + parts[n].astype(F32)
+    count = spatial.shape[0]
+    for t in range(5):
+        low = total[2 * t * count : (2 * t + 1) * count]
+        high = total[(2 * t + 1) * count : (2 * t + 2) * count]
+        row = side(low, high[:, : 3 * WIDTH - LANES])
+        for i in range(3):
+            piece = row[:, i * WIDTH : (i + 1) * WIDTH]
+            for r in range(count):
+                if t < 3:
+                    spatial[r, i, pl.ds(t, 1), :] = piece[r : r + 1]
+                else:
+                    temporal[r, i, pl.ds(t - 3, 1), :] = piece[r : r + 1]
 
 
 def place(at, own, got, out, vgot, sems):
@@ -386,12 +404,11 @@
     wp = (ws, wn, wk, wr)
     right = send(s0, outer)
     x2 = send(x2, swap)
-    c3, c2, cot0, cot1, vt, vtk, vb, vbk = run(
-        prepare, [(PX * C // LANES, LANES)] * 2 + [ONE] * 2 + taps * 2, (at, after(cot, s0), after(temporal_weight, s0)), flops=flops
-    )
-
     s3, sides3 = run(conv_other, [ONE, SIDES], (at, x3, *wp), [pad], 0, 4 * flops)
     left = send(s3, inner)
+    c3, c2, cot0, cot1, vt, vtk, vb, vbk = run(
+        prepare, [(PX * C // LANES, LANES)] * 2 + [ONE] * 2 + taps * 2, (at, after(cot, s3), after(temporal_weight, s3)), flops=flops
+    )
     c3 = send(after(c3, x2), swap)
     s2, sides2 = run(conv_folded, [ONE, SIDES], (at, x2, *wp), [pad], 0, 4 * flops)
     c2 = send(after(c2, c3), swap)
@@ -439,21 +456,20 @@
     (out,) = run(place, [(2, FULL, C)], (at, own, returned), [two], 4, 1000, far_outs=True)
 
     rows = C // owners
-    block = (2 * owners, 5 * rows, 3 * WIDTH)
+    block = (2 * owners, 10 * rows, LANES)
     (packs,) = run(
         pack,
         [block],
         (at, kept, got),
-        [pltpu.VMEM((owners, 5 * rows, 3 * WIDTH), F32), pltpu.VMEM((C, 3 * WIDTH), F32), block],
-        4,
-        1000,
-        far_outs=True,
+        [pltpu.VMEM((owners, 10 * rows, LANES), F32), pltpu.VMEM((C, 2 * LANES), F32)],
+        flops=1000,
     )
     groups = [[n + half * 2 + c for half in range(2) for n in range(0, owners * clips, clips)] for c in range(2)]
     parts = lax.all_to_all(packs, ("frame", "clip"), split_axis=0, concat_axis=0, axis_index_groups=groups, tiled=True)
-    total = jnp.sum(parts.astype(F32), axis=0).reshape(5, rows, 3, WIDTH)
-    grad_spatial = total[:3].transpose(1, 2, 0, 3)
-    grad_temporal = total[3:].transpose(1, 0, 2, 3)
+    grad_spatial, grad_temporal = run(
+        finish, [(rows, 3, 3, WIDTH), (rows, 3, 2, WIDTH)], (at, parts), flops=1000, kind=F32
+    )
+    grad_temporal = grad_temporal.transpose(0, 2, 1, 3)
     return (out.reshape(clips_in.shape), grad_spatial, grad_temporal)
 
 

time: 143 us -> 133 us (0.930)
  waiting for transfers between devices: 54.9 us -> 49.6 us
  local copies, waits for them, and re-layouts: 9.14 us -> 4.1 us
    ppermute x14, waiting for transfers between devices: 54.9 us -> 49.6 us  [send(): return lax.ppermute(value, axis, perm).reshape(shape)]
    unnamed x32 -> x10, local copies, waits for them, and re-layouts: 7.91 us -> 3.04 us
    pallas_call x11 -> x12, Pallas kernels: 35.1 us -> 35.6 us  [run(): pl.pallas_call(kernel, out_shape=[jax.ShapeDtypeStruct(s, kind) for s in...]
  transfers between devices with their start and end apart: 15 -> 15, of which waited for: 6 -> 7; matrix products, arithmetic and copies ran while one was open for 1% -> 0% of each run, Pallas kernels for 15% -> 18%
where the time goes in v8:
time: 133 us; the launch traced here: 132 us
  waiting for transfers between devices  49.6 us (37%)
  starting transfers between devices  41.4 us (31%)
  Pallas kernels  35.6 us (27%)
  local copies, waits for them, and re-layouts  4.1 us (3%)
    ppermute x14, waiting for transfers between devices, send(): return lax.ppermute(value, axis, perm).reshape(shape)  49.6 us
    pallas_call x12, Pallas kernels, run(): pl.pallas_call(kernel, out_shape=[jax.ShapeDtypeStruct(s, kind) for s in...  35.6 us
    ppermute x14, starting transfers between devices, send(): return lax.ppermute(value, axis, perm).reshape(shape)  24.6 us
    all_to_all x1, starting transfers between devices, step(): lax.all_to_all(packs, ('frame', 'clip'), split_axis=0, concat_axis=0, axi...  16.7 us
    unnamed x10, local copies, waits for them, and re-layouts  3.04 us
  transfers between devices with their start and end apart: 15, of which 7 were waited for; matrix products, arithmetic and copies ran while one was open for 0% of the time, Pallas kernels for 18%

profile of v8, /device:TPU:8, one launch (start us, length us, event | category | flops | bytes accessed | tf_op | source)
XLA Modules:
  0.0 131.6 jit_solution(11034420630854706530)
XLA Ops:
  0.7 1.1 constant_dynamic-slice_fusion
  1.7 0.4 collective-permute-start
  2.1 0.1 pad_add_fusion.at
  2.2 1.6 %copy-done = bf16[3,3,320,320]{3,2,1,0:T(8,128)(2,1)S(1)} copy-done((bf16[3,3,320,320]{3,2,1,0:T(8,128)(2,1)S(1)}, bf16[3,3,320,320]{3,2,1,0:T(8,128)(2,1)}, u32[]{:S(2)}) %copy-start) | copy-done | bytes 1843224
  3.8 1.4 %copy-done.2 = bf16[1,2,32,32,320]{4,3,2,1,0:T(8,128)(2,1)S(1)} copy-done((bf16[1,2,32,32,320]{4,3,2,1,0:T(8,128)(2,1)S(1)}, bf16[1,2,32,32,320]{4,3,2,1,0:T(8,128)(2,1)}, u32[]{:S(2)}) %copy-start.2) | copy-done | bytes 1310744
  5.2 3.3 %shard_map.67 = (bf16[512,320]{1,0:T(8,128)(2,1)S(1)}, bf16[512,320]{1,0:T(8,128)(2,1)S(1)}, bf16[2,4,512,240]{3,2,1,0:T(8,128)(2,1)S(1)}, bf16[1360,128]{1,0:T(...) custom-call(s32[2]{0:T(128)S(1)} %pad_add_fusion.at, ...), custom_call_target="tpu_custom_call" | custom-call | flops 838860800 | bytes 6787080 | tf_op jit(solution)/shard_map/pallas_call | solution.py:81
  8.5 1.8 %collective-permute-start.2 = (bf16[1360,128]{1,0:T(8,128)(2,1)S(1)}, bf16[1360,128]{1,0:T(8,128)(2,1)S(1)}, u32[]{:S(2)}, u32[]{:S(2)}) collective-permute-start(bf16[1360,128]{1,0:T(8,128)(2,1)S(1)} %get-tuple-element.49), channel_id=1, source_target_pairs={{0,1},{1,0},{2,3},{3,2},{4,5},{5,4},{6,7},{7,6},{8,9},{9,8},{10,11... | collective-permute-start | bytes 1044488 | tf_op jit(solution)/shard_map/ppermute | solution.py:383
  10.3 4.0 %collective-permute-done = bf16[17,32,320]{2,1,0:T(8,128)(2,1)S(1)} collective-permute-done((bf16[17,32,320]{2,1,0:T(8,128)(2,1)S(1)}, bf16[17,32,320]{2,1,0:T(8,128)(2,1)S(1)}, u32[]{:S(2)}, u32[]{:S(2)}) %collective-permute-start) | collective-permute-done | bytes 348192 | tf_op jit(solution)/shard_map/ppermute | solution.py:383
  14.3 0.0 copy-done.1
  14.3 1.9 %shard_map.68 = (bf16[512,320]{1,0:T(8,128)(2,1)S(1)}, bf16[4,512,240]{2,1,0:T(8,128)(2,1)S(1)}) custom-call(s32[2]{0:T(128)S(1)} %pad_add_fusion.at, bf16[544,320]{1,0:T(8,128)(2,1)S(1)} %bitcast.30, bf16[9,320,320]{2,1,0:T(8,128)(2,1)S(1)} %bitcast.24, bf16[3,256,192]{2,1,0:T(8,128)(2,1)S(1)} %get-tuple-element.43.wn, ...), custom_call_target="tpu_custom_call" | custom-call | flops 419430400 | bytes 4165640 | tf_op jit(solution)/shard_map/pallas_call | solution.py:81
  16.2 0.0 copy-done.3
  16.3 1.2 shard_map.70
  17.4 3.2 %collective-permute-done.2.x = bf16[1360,128]{1,0:T(8,128)(2,1)S(1)} collective-permute-done((bf16[1360,128]{1,0:T(8,128)(2,1)S(1)}, bf16[1360,128]{1,0:T(8,128)(2,1)S(1)}, u32[]{:S(2)}, u32[]{:S(2)}) %collective-permute-start.2) | collective-permute-done | bytes 348192 | tf_op jit(solution)/shard_map/ppermute | solution.py:383
  20.6 0.3 collective-permute-start.7
  20.9 3.6 %collective-permute-start.3 = (bf16[16,32,320]{2,1,0:T(8,128)(2,1)S(1)}, bf16[16,32,320]{2,1,0:T(8,128)(2,1)S(1)}, u32[]{:S(2)}, u32[]{:S(2)}) collective-permute-start(bf16[16,32,320]{2,1,0:T(8,128)(2,1)S(1)} %bitcast.31), channel_id=1, source_target_pairs={{1,3},{2,0},{3,5},{4,2},{5,7},{6,4},{7,9},{8,6},{9,11},{10,8},{11,... | collective-permute-start | bytes 983048 | tf_op jit(solution)/shard_map/ppermute | solution.py:383
  24.5 1.3 collective-permute-start.1
  25.8 4.6 %collective-permute-start.10 = (bf16[16,32,320]{2,1,0:T(8,128)(2,1)S(1)}, bf16[16,32,320]{2,1,0:T(8,128)(2,1)S(1)}, u32[]{:S(2)}, u32[]{:S(2)}) collective-permute-start(bf16[16,32,320]{2,1,0:T(8,128)(2,1)S(1)} %bitcast.28), channel_id=1, source_target_pairs={{1,3},{2,0},{3,5},{4,2},{5,7},{6,4},{7,9},{8,6},{9,11},{10,8},{11,... | collective-permute-start | bytes 983048 | tf_op jit(solution)/shard_map/ppermute | solution.py:383
  30.4 0.0 collective-permute-done.7.folded3
  30.4 0.1 collective-permute-start.9
  30.5 1.3 collective-permute-start.8
  31.8 2.0 %shard_map.69 = (bf16[512,320]{1,0:T(8,128)(2,1)S(1)}, bf16[4,512,240]{2,1,0:T(8,128)(2,1)S(1)}) custom-call(s32[2]{0:T(128)S(1)} %pad_add_fusion.at, bf16[1360,128]{1,0:T(8,128)(2,1)S(1)} %collective-permute-done.2.x, bf16[9,320,320]{2,1,0:T(8,128)(2,1)S(1)} %bitcast.25, bf16[3,256,192]{2,1,0:T(8,128)(2,1)S(1)} %get-tuple-element.43.wn, ...), custom_call_target="tpu_custom_call" | custom-call | flops 419430400 | bytes 4165640 | tf_op jit(solution)/shard_map/pallas_call | solution.py:81
  33.8 0.2 collective-permute-done.3
  34.0 4.4 %collective-permute-done.1 = bf16[16,32,320]{2,1,0:T(8,128)(2,1)S(1)} collective-permute-done((bf16[16,32,320]{2,1,0:T(8,128)(2,1)S(1)}, bf16[16,32,320]{2,1,0:T(8,128)(2,1)S(1)}, u32[]{:S(2)}, u32[]{:S(2)}) %collective-permute-start.1) | collective-permute-done | bytes 327712 | tf_op jit(solution)/shard_map/ppermute | solution.py:383
  38.4 3.3 %shard_map.71 = (bf16[6,512,320]{2,1,0:T(8,128)(2,1)S(1)}, bf16[4,512,320]{2,1,0:T(8,128)(2,1)S(1)}, bf16[512,320]{1,0:T(8,128)(2,1)S(1)}, bf16[512,320]{1,0:T(8,128)(2,1)S(1)}) custom-call(s32[2]{0:T(128)S(1)} %pad_add_fusion.at, bf16[512,320]{1,0:T(8,128)(2,1)S(1)} %bitcast.37, bf16[512,320]{1,0:T(8,128)(2,1)S(1)} %get-tuple-element.47.s0, ...), custom_call_target="tpu_custom_call" | custom-call | flops 838860800 | bytes 7372808 | tf_op jit(solution)/shard_map/pallas_call | solution.py:81
  41.7 3.4 %collective-permute-start.5 = (bf16[16,32,320]{2,1,0:T(8,128)(2,1)S(1)}, bf16[16,32,320]{2,1,0:T(8,128)(2,1)S(1)}, u32[]{:S(2)}, u32[]{:S(2)}) collective-permute-start(bf16[16,32,320]{2,1,0:T(8,128)(2,1)S(1)} %bitcast.41), channel_id=1, source_target_pairs={{1,3},{2,0},{3,5},{4,2},{5,7},{6,4},{7,9},{8,6},{9,11},{10,8},{11,... | collective-permute-start | bytes 983048 | tf_op jit(solution)/shard_map/ppermute | solution.py:383
  45.1 1.5 %collective-permute-start.4 = (bf16[16,32,320]{2,1,0:T(8,128)(2,1)S(1)}, bf16[16,32,320]{2,1,0:T(8,128)(2,1)S(1)}, u32[]{:S(2)}, u32[]{:S(2)}) collective-permute-start(bf16[16,32,320]{2,1,0:T(8,128)(2,1)S(1)} %bitcast.40), channel_id=1, source_target_pairs={{0,2},{2,4},{3,1},{4,6},{5,3},{6,8},{7,5},{8,10},{9,7},{10,12},{11... | collective-permute-start | bytes 983048 | tf_op jit(solution)/shard_map/ppermute | solution.py:383
  46.5 0.0 collective-permute-done.10
  46.6 0.0 collective-permute-done.9.folded2
  46.6 0.0 collective-permute-done.8.folded
  46.6 3.5 %shard_map.74 = (bf16[4,512,320]{2,1,0:T(8,128)(2,1)S(1)}, bf16[512,320]{1,0:T(8,128)(2,1)S(1)}, bf16[512,320]{1,0:T(8,128)(2,1)S(1)}, bf16[512,320]{1,0:T(8,128)(2,1)S(1)}, bf16[512,320]{1,0:T(8,128)(2,1)S(1)}) custom-call(s32[2]{0:T(128)S(1)} %pad_add_fusion.at, bf16[1280,128]{1,0:T(8,128)(2,1)S(1)} %collective-permute-done.8.folded, ...), custom_call_target="tpu_custom_call" | custom-call | flops 838860800 | bytes 7372808 | tf_op jit(solution)/shard_map/pallas_call | solution.py:81
  50.1 4.6 %collective-permute-start.12 = (bf16[16,32,320]{2,1,0:T(8,128)(2,1)S(1)}, bf16[16,32,320]{2,1,0:T(8,128)(2,1)S(1)}, u32[]{:S(2)}, u32[]{:S(2)}) collective-permute-start(bf16[16,32,320]{2,1,0:T(8,128)(2,1)S(1)} %bitcast.43), channel_id=1, source_target_pairs={{1,3},{2,0},{3,5},{4,2},{5,7},{6,4},{7,9},{8,6},{9,11},{10,8},{11,... | collective-permute-start | bytes 983048 | tf_op jit(solution)/shard_map/ppermute | solution.py:383
  54.7 1.3 collective-permute-start.11
  56.0 0.0 collective-permute-done.5
  56.0 0.0 collective-permute-done.4
  56.0 3.4 %shard_map.72 = (bf16[6,512,320]{2,1,0:T(8,128)(2,1)S(1)}, bf16[2,512,320]{2,1,0:T(8,128)(2,1)S(1)}, bf16[2560,128]{1,0:T(8,128)(2,1)S(1)}) custom-call(s32[2]{0:T(128)S(1)} %pad_add_fusion.at, bf16[512,320]{1,0:T(8,128)(2,1)S(1)} %bitcast.35, bf16[4,512,320]{2,1,0:T(8,128)(2,1)S(1)} %get-tuple-element.56.state, bf16[512,320]{1,0:T(8,128)(2,1)S(1)} %bitcast.34, ...), custom_call_target="tpu_custom_call" | custom-call | flops 838860800 | bytes 6717448 | tf_op jit(solution)/shard_map/pallas_call | solution.py:81
  59.4 3.8 %shard_map.75.passing = bf16[4,2,320,240]{3,2,1,0:T(8,128)(2,1)S(1)} custom-call(s32[2]{0:T(128)S(1)} %pad_add_fusion.at, bf16[512,320]{1,0:T(8,128)(2,1)S(1)} %get-tuple-element.66.cot0, bf16[512,320]{1,0:T(8,128)(2,1)S(1)} %get-tuple-element.63.cot1, bf16[512,320]{1,0:T(8,128)(2,1)S(1)} %get-tuple-element.75.c2, ...), custom_call_target="tpu_custom_call" | custom-call | flops 1677721600 | bytes 7782408 | tf_op jit(solution)/shard_map/pallas_call | solution.py:81
  63.1 0.0 collective-permute-done.12
  63.1 1.2 collective-permute-done.11
  64.4 7.4 %shard_map.76 = (bf16[2,5,320,240]{3,2,1,0:T(8,128)(2,1)S(1)}, bf16[2,5,320,240]{3,2,1,0:T(8,128)(2,1)S(1)}) custom-call(s32[2]{0:T(128)S(1)} %pad_add_fusion.at, bf16[512,320]{1,0:T(8,128)(2,1)S(1)} %bitcast.39, bf16[4,512,320]{2,1,0:T(8,128)(2,1)S(1)} %get-tuple-element.70.back, bf16[512,320]{1,0:T(8,128)(2,1)S(1)} %bitcast.38, ...), custom_call_target="tpu_custom_call" | custom-call | flops 3355443200 | bytes 12984328 | tf_op jit(solution)/shard_map/pallas_call | solution.py:81
  71.8 0.1 collective-permute-start.13
  71.9 3.5 %collective-permute-done.13.got = bf16[2,5,320,240]{3,2,1,0:T(8,128)(2,1)S(1)} collective-permute-done((bf16[2,5,320,240]{3,2,1,0:T(8,128)(2,1)S(1)}, bf16[2,5,320,240]{3,2,1,0:T(8,128)(2,1)S(1)}, u32[]{:S(2)}, u32[]{:S(2)}) %collective-permute-start.13) | collective-permute-done | bytes 1536032 | tf_op jit(solution)/shard_map/ppermute | solution.py:383
  75.4 2.7 %shard_map.77 = bf16[64,100,128]{2,1,0:T(8,128)(2,1)} custom-call(s32[2]{0:T(128)S(1)} %pad_add_fusion.at, bf16[2,5,320,240]{3,2,1,0:T(8,128)(2,1)S(1)} %get-tuple-element.79.kept, bf16[2,5,320,240]{3,2,1,0:T(8,128)(2,1)S(1)} %collective-permute-done.13.got), custom_call_target="tpu_custom_call" | custom-call | flops 1000 | bytes 4710408 | tf_op jit(solution)/shard_map/pallas_call | solution.py:81
  78.0 16.7 %all-to-all-start = ((bf16[64,100,128]{2,1,0:T(8,128)(2,1)}), bf16[64,100,128]{2,1,0:T(8,128)(2,1)S(1)}, u32[]{:S(2)}, u32[]{:S(2)}) async-start(bf16[64,100,128]{2,1,0:T(8,128)(2,1)} %shard_map.77), calls=%async_computation | async-start | bytes 3407872 | tf_op jit(solution)/shard_map/all_to_all | solution.py:468
  94.7 0.5 collective-permute-start.6
  95.3 33.1 %collective-permute-done.6.got = bf16[2560,128]{1,0:T(8,128)(2,1)S(1)} collective-permute-done((bf16[2560,128]{1,0:T(8,128)(2,1)S(1)}, bf16[2560,128]{1,0:T(8,128)(2,1)S(1)}, u32[]{:S(2)}, u32[]{:S(2)}) %collective-permute-start.6) | collective-permute-done | bytes 655392 | tf_op jit(solution)/shard_map/ppermute | solution.py:383
  128.4 1.7 %shard_map.73 = bf16[2,1024,320]{2,1,0:T(8,128)(2,1)} custom-call(s32[2]{0:T(128)S(1)} %pad_add_fusion.at, bf16[2,512,320]{2,1,0:T(8,128)(2,1)S(1)} %get-tuple-element.58.own, bf16[2560,128]{1,0:T(8,128)(2,1)S(1)} %collective-permute-done.6.got), custom_call_target="tpu_custom_call" | custom-call | flops 1000 | bytes 2621448 | tf_op jit(solution)/shard_map/pallas_call | solution.py:81
  130.1 0.0 all-to-all-done.parts
  130.1 1.5 %shard_map.78 = (f32[10,3,3,80]{3,2,1,0:T(4,128)}, f32[10,3,2,80]{3,2,1,0:T(2,128)}) custom-call(s32[2]{0:T(128)S(1)} %pad_add_fusion.at, bf16[64,100,128]{2,1,0:T(8,128)(2,1)S(1)} %all-to-all-done.parts), custom_call_target="tpu_custom_call" | custom-call | flops 1000 | bytes 1662408 | tf_op jit(solution)/shard_map/pallas_call | solution.py:81
  (6 shorter events, 0.0 us)
Async XLA Ops:
  1.7 12.6 %collective-permute-start = (bf16[17,32,320]{2,1,0:T(8,128)(2,1)S(1)}, bf16[17,32,320]{2,1,0:T(8,128)(2,1)S(1)}, u32[]{:S(2)}, u32[]{:S(2)}) collective-permute-start(bf16[17,32,320]{2,1,0:T(8,128)(2,1)S(1)} %bitcast.45), channel_id=1, source_target_pairs={{0,1},{1,0},{2,3},{3,2},{4,5},{5,4},{6,7},{7,6},{8,9},{9,8},{10,11... | collective-permute-start | bytes 1044488 | tf_op jit(solution)/shard_map/ppermute | solution.py:383
  2.2 1.6 %copy-start = (bf16[3,3,320,320]{3,2,1,0:T(8,128)(2,1)S(1)}, bf16[3,3,320,320]{3,2,1,0:T(8,128)(2,1)}, u32[]{:S(2)}) copy-start(bf16[3,3,320,320]{3,2,1,0:T(8,128)(2,1)} %param.6) | copy-start | bytes 5529604
  3.8 1.4 %copy-start.2 = (bf16[1,2,32,32,320]{4,3,2,1,0:T(8,128)(2,1)S(1)}, bf16[1,2,32,32,320]{4,3,2,1,0:T(8,128)(2,1)}, u32[]{:S(2)}) copy-start(bf16[1,2,32,32,320]{4,3,2,1,0:T(8,128)(2,1)} %param.4) | copy-start | bytes 3932164
  5.2 9.1 %copy-start.1 = (bf16[3,3,320,320]{3,2,1,0:T(8,128)(2,1)S(1)}, bf16[3,3,320,320]{3,2,1,0:T(8,128)(2,1)}, u32[]{:S(2)}) copy-start(bf16[3,3,320,320]{3,2,1,0:T(8,128)(2,1)} %param.6) | copy-start | bytes 5529604
  8.5 12.1 %collective-permute-start.2 = (bf16[1360,128]{1,0:T(8,128)(2,1)S(1)}, bf16[1360,128]{1,0:T(8,128)(2,1)S(1)}, u32[]{:S(2)}, u32[]{:S(2)}) collective-permute-start(bf16[1360,128]{1,0:T(8,128)(2,1)S(1)} %get-tuple-element.49), channel_id=1, source_target_pairs={{0,1},{1,0},{2,3},{3,2},{4,5},{5,4},{6,7},{7,6},{8,9},{9,8},{10,11... | collective-permute-start | bytes 1044488 | tf_op jit(solution)/shard_map/ppermute | solution.py:383
  14.3 1.9 %copy-start.3 = (bf16[1,2,32,32,320]{4,3,2,1,0:T(8,128)(2,1)S(1)}, bf16[1,2,32,32,320]{4,3,2,1,0:T(8,128)(2,1)}, u32[]{:S(2)}) copy-start(bf16[1,2,32,32,320]{4,3,2,1,0:T(8,128)(2,1)} %param.5) | copy-start | bytes 3932164
  14.3 1.9 %copy-start.4 = (bf16[2,3,320,320]{3,2,1,0:T(8,128)(2,1)S(1)}, bf16[2,3,320,320]{3,2,1,0:T(8,128)(2,1)}, u32[]{:S(2)}) copy-start(bf16[2,3,320,320]{3,2,1,0:T(8,128)(2,1)} %tw) | copy-start | bytes 3686404
  20.6 9.7 %collective-permute-start.7 = (bf16[1280,128]{1,0:T(8,128)(2,1)S(1)}, bf16[1280,128]{1,0:T(8,128)(2,1)S(1)}, u32[]{:S(2)}, u32[]{:S(2)}) collective-permute-start(bf16[1280,128]{1,0:T(8,128)(2,1)S(1)} %get-tuple-element.61), channel_id=1, source_target_pairs={{0,1},{1,0},{2,3},{3,2},{4,5},{5,4},{6,7},{7,6},{8,9},{9,8},{10,11... | collective-permute-start | bytes 983048 | tf_op jit(solution)/shard_map/ppermute | solution.py:383
  20.9 13.0 %collective-permute-start.3 = (bf16[16,32,320]{2,1,0:T(8,128)(2,1)S(1)}, bf16[16,32,320]{2,1,0:T(8,128)(2,1)S(1)}, u32[]{:S(2)}, u32[]{:S(2)}) collective-permute-start(bf16[16,32,320]{2,1,0:T(8,128)(2,1)S(1)} %bitcast.31), channel_id=1, source_target_pairs={{1,3},{2,0},{3,5},{4,2},{5,7},{6,4},{7,9},{8,6},{9,11},{10,8},{11,... | collective-permute-start | bytes 983048 | tf_op jit(solution)/shard_map/ppermute | solution.py:383
  24.5 13.9 %collective-permute-start.1 = (bf16[16,32,320]{2,1,0:T(8,128)(2,1)S(1)}, bf16[16,32,320]{2,1,0:T(8,128)(2,1)S(1)}, u32[]{:S(2)}, u32[]{:S(2)}) collective-permute-start(bf16[16,32,320]{2,1,0:T(8,128)(2,1)S(1)} %bitcast.32), channel_id=1, source_target_pairs={{0,2},{2,4},{3,1},{4,6},{5,3},{6,8},{7,5},{8,10},{9,7},{10,12},{11... | collective-permute-start | bytes 983048 | tf_op jit(solution)/shard_map/ppermute | solution.py:383
  25.8 20.8 %collective-permute-start.10 = (bf16[16,32,320]{2,1,0:T(8,128)(2,1)S(1)}, bf16[16,32,320]{2,1,0:T(8,128)(2,1)S(1)}, u32[]{:S(2)}, u32[]{:S(2)}) collective-permute-start(bf16[16,32,320]{2,1,0:T(8,128)(2,1)S(1)} %bitcast.28), channel_id=1, source_target_pairs={{1,3},{2,0},{3,5},{4,2},{5,7},{6,4},{7,9},{8,6},{9,11},{10,8},{11,... | collective-permute-start | bytes 983048 | tf_op jit(solution)/shard_map/ppermute | solution.py:383
  30.4 16.2 %collective-permute-start.9 = (bf16[1280,128]{1,0:T(8,128)(2,1)S(1)}, bf16[1280,128]{1,0:T(8,128)(2,1)S(1)}, u32[]{:S(2)}, u32[]{:S(2)}) collective-permute-start(bf16[1280,128]{1,0:T(8,128)(2,1)S(1)} %get-tuple-element.65), channel_id=1, source_target_pairs={{0,1},{1,0},{2,3},{3,2},{4,5},{5,4},{6,7},{7,6},{8,9},{9,8},{10,11... | collective-permute-start | bytes 983048 | tf_op jit(solution)/shard_map/ppermute | solution.py:383
  30.5 16.1 %collective-permute-start.8 = (bf16[1280,128]{1,0:T(8,128)(2,1)S(1)}, bf16[1280,128]{1,0:T(8,128)(2,1)S(1)}, u32[]{:S(2)}, u32[]{:S(2)}) collective-permute-start(bf16[1280,128]{1,0:T(8,128)(2,1)S(1)} %collective-permute-done.7.folded3), channel_id=1, source_target_pairs={{0,2},{2,4},{3,1},{4,6},{5,3},{6,8},{7,5},{8,10},{9,7},{10,12},{11... | collective-permute-start | bytes 983048 | tf_op jit(solution)/shard_map/ppermute | solution.py:383
  41.7 14.3 %collective-permute-start.5 = (bf16[16,32,320]{2,1,0:T(8,128)(2,1)S(1)}, bf16[16,32,320]{2,1,0:T(8,128)(2,1)S(1)}, u32[]{:S(2)}, u32[]{:S(2)}) collective-permute-start(bf16[16,32,320]{2,1,0:T(8,128)(2,1)S(1)} %bitcast.41), channel_id=1, source_target_pairs={{1,3},{2,0},{3,5},{4,2},{5,7},{6,4},{7,9},{8,6},{9,11},{10,8},{11,... | collective-permute-start | bytes 983048 | tf_op jit(solution)/shard_map/ppermute | solution.py:383
  45.1 10.9 %collective-permute-start.4 = (bf16[16,32,320]{2,1,0:T(8,128)(2,1)S(1)}, bf16[16,32,320]{2,1,0:T(8,128)(2,1)S(1)}, u32[]{:S(2)}, u32[]{:S(2)}) collective-permute-start(bf16[16,32,320]{2,1,0:T(8,128)(2,1)S(1)} %bitcast.40), channel_id=1, source_target_pairs={{0,2},{2,4},{3,1},{4,6},{5,3},{6,8},{7,5},{8,10},{9,7},{10,12},{11... | collective-permute-start | bytes 983048 | tf_op jit(solution)/shard_map/ppermute | solution.py:383
  50.1 13.0 %collective-permute-start.12 = (bf16[16,32,320]{2,1,0:T(8,128)(2,1)S(1)}, bf16[16,32,320]{2,1,0:T(8,128)(2,1)S(1)}, u32[]{:S(2)}, u32[]{:S(2)}) collective-permute-start(bf16[16,32,320]{2,1,0:T(8,128)(2,1)S(1)} %bitcast.43), channel_id=1, source_target_pairs={{1,3},{2,0},{3,5},{4,2},{5,7},{6,4},{7,9},{8,6},{9,11},{10,8},{11,... | collective-permute-start | bytes 983048 | tf_op jit(solution)/shard_map/ppermute | solution.py:383
  54.7 9.7 %collective-permute-start.11 = (bf16[16,32,320]{2,1,0:T(8,128)(2,1)S(1)}, bf16[16,32,320]{2,1,0:T(8,128)(2,1)S(1)}, u32[]{:S(2)}, u32[]{:S(2)}) collective-permute-start(bf16[16,32,320]{2,1,0:T(8,128)(2,1)S(1)} %bitcast.42), channel_id=1, source_target_pairs={{0,2},{2,4},{3,1},{4,6},{5,3},{6,8},{7,5},{8,10},{9,7},{10,12},{11... | collective-permute-start | bytes 983048 | tf_op jit(solution)/shard_map/ppermute | solution.py:383
  71.8 3.6 %collective-permute-start.13 = (bf16[2,5,320,240]{3,2,1,0:T(8,128)(2,1)S(1)}, bf16[2,5,320,240]{3,2,1,0:T(8,128)(2,1)S(1)}, u32[]{:S(2)}, u32[]{:S(2)}) collective-permute-start(bf16[2,5,320,240]{3,2,1,0:T(8,128)(2,1)S(1)} %get-tuple-element.80), channel_id=1, source_target_pairs={{0,32},{32,0},{64,96},{96,64},{1,33},{33,1},{65,97},{97,65},{2,34}... | collective-permute-start | bytes 4608008 | tf_op jit(solution)/shard_map/ppermute | solution.py:383
  78.0 52.1 %all-to-all-start = ((bf16[64,100,128]{2,1,0:T(8,128)(2,1)}), bf16[64,100,128]{2,1,0:T(8,128)(2,1)S(1)}, u32[]{:S(2)}, u32[]{:S(2)}) async-start(bf16[64,100,128]{2,1,0:T(8,128)(2,1)} %shard_map.77), calls=%async_computation | async-start | bytes 3407872 | tf_op jit(solution)/shard_map/all_to_all | solution.py:468
  94.7 33.6 %collective-permute-start.6 = (bf16[2560,128]{1,0:T(8,128)(2,1)S(1)}, bf16[2560,128]{1,0:T(8,128)(2,1)S(1)}, u32[]{:S(2)}, u32[]{:S(2)}) collective-permute-start(bf16[2560,128]{1,0:T(8,128)(2,1)S(1)} %get-tuple-element.59), channel_id=1, source_target_pairs={{0,1},{1,0},{2,3},{3,2},{4,5},{5,4},{6,7},{7,6},{8,9},{9,8},{10,11... | collective-permute-start | bytes 1966088 | tf_op jit(solution)/shard_map/ppermute | solution.py:383

commit v9 on v8

--- a/solution.py
+++ b/solution.py
@@ -222,7 +222,7 @@
     for q in range(4):
         while done < q + 3:
             v = states[done][...].astype(F32)
-            acts[done] = (v * sigmoid(v)).astype(BF)
+            acts[done] = (v * (0.5 + 0.5 * jnp.tanh(0.5 * v))).astype(BF)
             done += 1
         term = three_taps([acts.at[q + k] for k in range(3)], vw, layer, wk)
         yield (states[q + 1][...].astype(F32) + term).astype(BF)
@@ -291,7 +291,7 @@
             blocks[b, layer] = side(*[v[:, b * WIDTH : (b + 1) * WIDTH] for v in values])
 
 
-def back_zero(at, left, back, right, s0, s1, s2, s3, vw, wk, own_sides, sides2, sides3, passing, kept, sent, flip):
+def back_zero(at, left, back, right, s0, s1, s2, s3, vw, wk, own_sides, sides2, sides3, passing, sent, flip):
     core = at[1]
     six = [left] + [back.at[q] for q in range(4)] + [right]
     column = lax.broadcasted_iota(jnp.int32, (1, PX), 1) % COLS
@@ -303,16 +303,23 @@
         flip[q, pl.ds(0, C), :] = ahead.astype(BF)
         flip[q, pl.ds(C, C), :] = turned
         flip[q, pl.ds(2 * C, C), :] = behind.astype(BF)
-    sides = (own_sides.at[0], own_sides.at[1], sides2, sides3)
+    spatial_blocks(flip, (own_sides.at[0], own_sides.at[1], sides2, sides3), passing, sent, 1 - core)
+
+
+def keep_blocks(at, flip, own_sides, sides2, sides3, passing, kept):
+    spatial_blocks(flip, (own_sides.at[0], own_sides.at[1], sides2, sides3), passing, kept, at[1])
+
+
+def spatial_blocks(flip, sides, passing, out, core):
     for half in range(2):
-        for out, b in ((kept, 2 * half + core), (sent, 2 * half + 1 - core)):
-            total = jnp.zeros((3 * C, 3 * WIDTH), F32)
-            for q in range(4):
-                total = total + dot(flip[q], sides[q][b])
-            for j in range(3):
-                out[half, j] = total[j * C : (j + 1) * C].astype(BF)
-            for layer in range(2):
-                out[half, 3 + layer] = passing[b, layer]
+        b = 2 * half + core
+        total = jnp.zeros((3 * C, 3 * WIDTH), F32)
+        for q in range(4):
+            total = total + dot(flip[q], sides[q][b])
+        for j in range(3):
+            out[half, j] = total[j * C : (j + 1) * C].astype(BF)
+        for layer in range(2):
+            out[half, 3 + layer] = passing[b, layer]
 
 
 def pack(at, kept, got, out, wide, rows):
@@ -445,12 +452,14 @@
         flops=16 * flops,
     )
     shares = (2, 5, C, 3 * WIDTH)
-    kept, sent = run(
+    sent, flip = run(
         back_zero,
-        [shares] * 2,
+        [shares, (4, 3 * C, PX)],
         (at, back_left, back1, back_right, s0, s1, s2, s3, vb, vbk, own_sides, sides2, sides3, temporal_blocks),
-        [(4, 3 * C, PX)],
-        flops=32 * flops,
+        flops=20 * flops,
+    )
+    (kept,) = run(
+        keep_blocks, [shares], (at, flip, own_sides, sides2, sides3, temporal_blocks), flops=12 * flops
     )
     got = send(sent, cores, "clip")
     (out,) = run(place, [(2, FULL, C)], (at, own, returned), [two], 4, 1000, far_outs=True)

time: 133 us -> 131 us (0.985)
  waiting for transfers between devices: 49.6 us -> 46.9 us
    ppermute x14, waiting for transfers between devices: 49.6 us -> 46.9 us  [send(): return lax.ppermute(value, axis, perm).reshape(shape)]
    pallas_call x12 -> x13, Pallas kernels: 35.6 us -> 36.3 us  [run(): pl.pallas_call(kernel, out_shape=[jax.ShapeDtypeStruct(s, kind) for s in...]
  transfers between devices with their start and end apart: 15 -> 15, of which waited for: 7 -> 7; matrix products, arithmetic and copies ran while one was open for 0% -> 0% of each run, Pallas kernels for 18% -> 20%
where the time goes in v9:
time: 131 us; the launch traced here: 130 us
  waiting for transfers between devices  46.9 us (36%)
  starting transfers between devices  41.5 us (32%)
  Pallas kernels  36.3 us (28%)
  local copies, waits for them, and re-layouts  4.1 us (3%)
    ppermute x14, waiting for transfers between devices, send(): return lax.ppermute(value, axis, perm).reshape(shape)  46.9 us
    pallas_call x13, Pallas kernels, run(): pl.pallas_call(kernel, out_shape=[jax.ShapeDtypeStruct(s, kind) for s in...  36.3 us
    ppermute x14, starting transfers between devices, send(): return lax.ppermute(value, axis, perm).reshape(shape)  24.9 us
    all_to_all x1, starting transfers between devices, step(): lax.all_to_all(packs, ('frame', 'clip'), split_axis=0, concat_axis=0, axi...  16.6 us
    unnamed x10, local copies, waits for them, and re-layouts  3.04 us
  transfers between devices with their start and end apart: 15, of which 7 were waited for; matrix products, arithmetic and copies ran while one was open for 0% of the time, Pallas kernels for 20%

profile of v9, /device:TPU:8, one launch (start us, length us, event | category | flops | bytes accessed | tf_op | source)
XLA Modules:
  0.0 129.7 jit_solution(11950298795205586492)
XLA Ops:
  0.7 1.1 constant_dynamic-slice_fusion
  1.7 0.4 collective-permute-start
  2.1 0.1 pad_add_fusion.at
  2.2 1.6 %copy-done = bf16[3,3,320,320]{3,2,1,0:T(8,128)(2,1)S(1)} copy-done((bf16[3,3,320,320]{3,2,1,0:T(8,128)(2,1)S(1)}, bf16[3,3,320,320]{3,2,1,0:T(8,128)(2,1)}, u32[]{:S(2)}) %copy-start) | copy-done | bytes 1843224
  3.8 1.4 %copy-done.2 = bf16[1,2,32,32,320]{4,3,2,1,0:T(8,128)(2,1)S(1)} copy-done((bf16[1,2,32,32,320]{4,3,2,1,0:T(8,128)(2,1)S(1)}, bf16[1,2,32,32,320]{4,3,2,1,0:T(8,128)(2,1)}, u32[]{:S(2)}) %copy-start.2) | copy-done | bytes 1310744
  5.2 3.3 %shard_map.67 = (bf16[512,320]{1,0:T(8,128)(2,1)S(1)}, bf16[512,320]{1,0:T(8,128)(2,1)S(1)}, bf16[2,4,512,240]{3,2,1,0:T(8,128)(2,1)S(1)}, bf16[1360,128]{1,0:T(...) custom-call(s32[2]{0:T(128)S(1)} %pad_add_fusion.at, ...), custom_call_target="tpu_custom_call" | custom-call | flops 838860800 | bytes 6787080 | tf_op jit(solution)/shard_map/pallas_call | solution.py:81
  8.5 1.8 %collective-permute-start.2 = (bf16[1360,128]{1,0:T(8,128)(2,1)S(1)}, bf16[1360,128]{1,0:T(8,128)(2,1)S(1)}, u32[]{:S(2)}, u32[]{:S(2)}) collective-permute-start(bf16[1360,128]{1,0:T(8,128)(2,1)S(1)} %get-tuple-element.49), channel_id=1, source_target_pairs={{0,1},{1,0},{2,3},{3,2},{4,5},{5,4},{6,7},{7,6},{8,9},{9,8},{10,11... | collective-permute-start | bytes 1044488 | tf_op jit(solution)/shard_map/ppermute | solution.py:390
  10.3 4.0 %collective-permute-done = bf16[17,32,320]{2,1,0:T(8,128)(2,1)S(1)} collective-permute-done((bf16[17,32,320]{2,1,0:T(8,128)(2,1)S(1)}, bf16[17,32,320]{2,1,0:T(8,128)(2,1)S(1)}, u32[]{:S(2)}, u32[]{:S(2)}) %collective-permute-start) | collective-permute-done | bytes 348192 | tf_op jit(solution)/shard_map/ppermute | solution.py:390
  14.3 0.0 copy-done.1
  14.3 1.9 %shard_map.68 = (bf16[512,320]{1,0:T(8,128)(2,1)S(1)}, bf16[4,512,240]{2,1,0:T(8,128)(2,1)S(1)}) custom-call(s32[2]{0:T(128)S(1)} %pad_add_fusion.at, bf16[544,320]{1,0:T(8,128)(2,1)S(1)} %bitcast.32, bf16[9,320,320]{2,1,0:T(8,128)(2,1)S(1)} %bitcast.24, bf16[3,256,192]{2,1,0:T(8,128)(2,1)S(1)} %get-tuple-element.43.wn, ...), custom_call_target="tpu_custom_call" | custom-call | flops 419430400 | bytes 4165640 | tf_op jit(solution)/shard_map/pallas_call | solution.py:81
  16.3 1.2 shard_map.70
  17.5 3.2 %collective-permute-done.2.x = bf16[1360,128]{1,0:T(8,128)(2,1)S(1)} collective-permute-done((bf16[1360,128]{1,0:T(8,128)(2,1)S(1)}, bf16[1360,128]{1,0:T(8,128)(2,1)S(1)}, u32[]{:S(2)}, u32[]{:S(2)}) %collective-permute-start.2) | collective-permute-done | bytes 348192 | tf_op jit(solution)/shard_map/ppermute | solution.py:390
  20.6 0.3 collective-permute-start.7
  20.9 3.6 %collective-permute-start.3 = (bf16[16,32,320]{2,1,0:T(8,128)(2,1)S(1)}, bf16[16,32,320]{2,1,0:T(8,128)(2,1)S(1)}, u32[]{:S(2)}, u32[]{:S(2)}) collective-permute-start(bf16[16,32,320]{2,1,0:T(8,128)(2,1)S(1)} %bitcast.28), channel_id=1, source_target_pairs={{1,3},{2,0},{3,5},{4,2},{5,7},{6,4},{7,9},{8,6},{9,11},{10,8},{11,... | collective-permute-start | bytes 983048 | tf_op jit(solution)/shard_map/ppermute | solution.py:390
  24.5 1.3 collective-permute-start.1
  25.8 4.6 %collective-permute-start.10 = (bf16[16,32,320]{2,1,0:T(8,128)(2,1)S(1)}, bf16[16,32,320]{2,1,0:T(8,128)(2,1)S(1)}, u32[]{:S(2)}, u32[]{:S(2)}) collective-permute-start(bf16[16,32,320]{2,1,0:T(8,128)(2,1)S(1)} %bitcast.30), channel_id=1, source_target_pairs={{1,3},{2,0},{3,5},{4,2},{5,7},{6,4},{7,9},{8,6},{9,11},{10,8},{11,... | collective-permute-start | bytes 983048 | tf_op jit(solution)/shard_map/ppermute | solution.py:390
  30.4 0.0 collective-permute-done.7.folded3
  30.4 0.1 collective-permute-start.9
  30.5 1.3 collective-permute-start.8
  31.8 2.0 %shard_map.69 = (bf16[512,320]{1,0:T(8,128)(2,1)S(1)}, bf16[4,512,240]{2,1,0:T(8,128)(2,1)S(1)}) custom-call(s32[2]{0:T(128)S(1)} %pad_add_fusion.at, bf16[1360,128]{1,0:T(8,128)(2,1)S(1)} %collective-permute-done.2.x, bf16[9,320,320]{2,1,0:T(8,128)(2,1)S(1)} %bitcast.25, bf16[3,256,192]{2,1,0:T(8,128)(2,1)S(1)} %get-tuple-element.43.wn, ...), custom_call_target="tpu_custom_call" | custom-call | flops 419430400 | bytes 4165640 | tf_op jit(solution)/shard_map/pallas_call | solution.py:81
  33.8 0.2 collective-permute-done.3
  34.0 4.4 %collective-permute-done.1 = bf16[16,32,320]{2,1,0:T(8,128)(2,1)S(1)} collective-permute-done((bf16[16,32,320]{2,1,0:T(8,128)(2,1)S(1)}, bf16[16,32,320]{2,1,0:T(8,128)(2,1)S(1)}, u32[]{:S(2)}, u32[]{:S(2)}) %collective-permute-start.1) | collective-permute-done | bytes 327712 | tf_op jit(solution)/shard_map/ppermute | solution.py:390
  38.4 3.1 %shard_map.71 = (bf16[6,512,320]{2,1,0:T(8,128)(2,1)S(1)}, bf16[4,512,320]{2,1,0:T(8,128)(2,1)S(1)}, bf16[512,320]{1,0:T(8,128)(2,1)S(1)}, bf16[512,320]{1,0:T(8,128)(2,1)S(1)}) custom-call(s32[2]{0:T(128)S(1)} %pad_add_fusion.at, bf16[512,320]{1,0:T(8,128)(2,1)S(1)} %bitcast.39, bf16[512,320]{1,0:T(8,128)(2,1)S(1)} %get-tuple-element.47.s0, ...), custom_call_target="tpu_custom_call" | custom-call | flops 838860800 | bytes 7372808 | tf_op jit(solution)/shard_map/pallas_call | solution.py:81
  41.5 3.4 %collective-permute-start.5 = (bf16[16,32,320]{2,1,0:T(8,128)(2,1)S(1)}, bf16[16,32,320]{2,1,0:T(8,128)(2,1)S(1)}, u32[]{:S(2)}, u32[]{:S(2)}) collective-permute-start(bf16[16,32,320]{2,1,0:T(8,128)(2,1)S(1)} %bitcast.41), channel_id=1, source_target_pairs={{1,3},{2,0},{3,5},{4,2},{5,7},{6,4},{7,9},{8,6},{9,11},{10,8},{11,... | collective-permute-start | bytes 983048 | tf_op jit(solution)/shard_map/ppermute | solution.py:390
  44.9 1.5 %collective-permute-start.4 = (bf16[16,32,320]{2,1,0:T(8,128)(2,1)S(1)}, bf16[16,32,320]{2,1,0:T(8,128)(2,1)S(1)}, u32[]{:S(2)}, u32[]{:S(2)}) collective-permute-start(bf16[16,32,320]{2,1,0:T(8,128)(2,1)S(1)} %bitcast.40), channel_id=1, source_target_pairs={{0,2},{2,4},{3,1},{4,6},{5,3},{6,8},{7,5},{8,10},{9,7},{10,12},{11... | collective-permute-start | bytes 983048 | tf_op jit(solution)/shard_map/ppermute | solution.py:390
  46.4 0.0 collective-permute-done.10
  46.4 0.0 collective-permute-done.9.folded2
  46.4 0.0 collective-permute-done.8.folded
  46.4 3.5 %shard_map.74 = (bf16[4,512,320]{2,1,0:T(8,128)(2,1)S(1)}, bf16[512,320]{1,0:T(8,128)(2,1)S(1)}, bf16[512,320]{1,0:T(8,128)(2,1)S(1)}, bf16[512,320]{1,0:T(8,128)(2,1)S(1)}, bf16[512,320]{1,0:T(8,128)(2,1)S(1)}) custom-call(s32[2]{0:T(128)S(1)} %pad_add_fusion.at, bf16[1280,128]{1,0:T(8,128)(2,1)S(1)} %collective-permute-done.8.folded, ...), custom_call_target="tpu_custom_call" | custom-call | flops 838860800 | bytes 7372808 | tf_op jit(solution)/shard_map/pallas_call | solution.py:81
  49.9 4.6 %collective-permute-start.12 = (bf16[16,32,320]{2,1,0:T(8,128)(2,1)S(1)}, bf16[16,32,320]{2,1,0:T(8,128)(2,1)S(1)}, u32[]{:S(2)}, u32[]{:S(2)}) collective-permute-start(bf16[16,32,320]{2,1,0:T(8,128)(2,1)S(1)} %bitcast.43), channel_id=1, source_target_pairs={{1,3},{2,0},{3,5},{4,2},{5,7},{6,4},{7,9},{8,6},{9,11},{10,8},{11,... | collective-permute-start | bytes 983048 | tf_op jit(solution)/shard_map/ppermute | solution.py:390
  54.5 1.3 collective-permute-start.11
  55.8 0.0 collective-permute-done.5
  55.8 0.0 collective-permute-done.4
  55.8 3.2 %shard_map.72 = (bf16[6,512,320]{2,1,0:T(8,128)(2,1)S(1)}, bf16[2,512,320]{2,1,0:T(8,128)(2,1)S(1)}, bf16[2560,128]{1,0:T(8,128)(2,1)S(1)}) custom-call(s32[2]{0:T(128)S(1)} %pad_add_fusion.at, bf16[512,320]{1,0:T(8,128)(2,1)S(1)} %bitcast.37, bf16[4,512,320]{2,1,0:T(8,128)(2,1)S(1)} %get-tuple-element.56.state, bf16[512,320]{1,0:T(8,128)(2,1)S(1)} %bitcast.36, ...), custom_call_target="tpu_custom_call" | custom-call | flops 838860800 | bytes 6717448 | tf_op jit(solution)/shard_map/pallas_call | solution.py:81
  59.0 3.8 %shard_map.75.passing = bf16[4,2,320,240]{3,2,1,0:T(8,128)(2,1)S(1)} custom-call(s32[2]{0:T(128)S(1)} %pad_add_fusion.at, bf16[512,320]{1,0:T(8,128)(2,1)S(1)} %get-tuple-element.66.cot0, bf16[512,320]{1,0:T(8,128)(2,1)S(1)} %get-tuple-element.63.cot1, bf16[512,320]{1,0:T(8,128)(2,1)S(1)} %get-tuple-element.75.c2, ...), custom_call_target="tpu_custom_call" | custom-call | flops 1677721600 | bytes 7782408 | tf_op jit(solution)/shard_map/pallas_call | solution.py:81
  62.8 0.0 collective-permute-done.12
  62.8 1.4 %collective-permute-done.11 = bf16[16,32,320]{2,1,0:T(8,128)(2,1)S(1)} collective-permute-done((bf16[16,32,320]{2,1,0:T(8,128)(2,1)S(1)}, bf16[16,32,320]{2,1,0:T(8,128)(2,1)S(1)}, u32[]{:S(2)}, u32[]{:S(2)}) %collective-permute-start.11) | collective-permute-done | bytes 327712 | tf_op jit(solution)/shard_map/ppermute | solution.py:390
  64.2 5.6 %shard_map.76 = (bf16[2,5,320,240]{3,2,1,0:T(8,128)(2,1)S(1)}, bf16[4,960,512]{2,1,0:T(8,128)(2,1)S(1)}) custom-call(s32[2]{0:T(128)S(1)} %pad_add_fusion.at, bf16[512,320]{1,0:T(8,128)(2,1)S(1)} %bitcast.34, bf16[4,512,320]{2,1,0:T(8,128)(2,1)S(1)} %get-tuple-element.70.back, bf16[512,320]{1,0:T(8,128)(2,1)S(1)} %bitcast.33, ...), custom_call_target="tpu_custom_call" | custom-call | flops 2097152000 | bytes 15380488 | tf_op jit(solution)/shard_map/pallas_call | solution.py:81
  69.8 0.3 collective-permute-start.13
  70.1 2.8 %shard_map.77.kept = bf16[2,5,320,240]{3,2,1,0:T(8,128)(2,1)S(1)} custom-call(s32[2]{0:T(128)S(1)} %pad_add_fusion.at, bf16[4,960,512]{2,1,0:T(8,128)(2,1)S(1)} %get-tuple-element.79.flip, bf16[2,4,512,240]{3,2,1,0:T(8,128)(2,1)S(1)} %get-tuple-element.72.own_sides, bf16[4,512,240]{2,1,0:T(8,128)(2,1)S(1)} %get-tuple-element.73.sides2, ...), custom_call_target="tpu_custom_call" | custom-call | flops 1258291200 | bytes 10629128 | tf_op jit(solution)/shard_map/pallas_call | solution.py:81
  72.9 0.7 collective-permute-done.13.got
  73.6 2.7 %shard_map.78 = bf16[64,100,128]{2,1,0:T(8,128)(2,1)} custom-call(s32[2]{0:T(128)S(1)} %pad_add_fusion.at, bf16[2,5,320,240]{3,2,1,0:T(8,128)(2,1)S(1)} %shard_map.77.kept, bf16[2,5,320,240]{3,2,1,0:T(8,128)(2,1)S(1)} %collective-permute-done.13.got), custom_call_target="tpu_custom_call" | custom-call | flops 1000 | bytes 4710408 | tf_op jit(solution)/shard_map/pallas_call | solution.py:81
  76.2 16.6 %all-to-all-start = ((bf16[64,100,128]{2,1,0:T(8,128)(2,1)}), bf16[64,100,128]{2,1,0:T(8,128)(2,1)S(1)}, u32[]{:S(2)}, u32[]{:S(2)}) async-start(bf16[64,100,128]{2,1,0:T(8,128)(2,1)} %shard_map.78), calls=%async_computation | async-start | bytes 3407872 | tf_op jit(solution)/shard_map/all_to_all | solution.py:477
  92.9 0.5 collective-permute-start.6
  93.4 33.1 %collective-permute-done.6.got = bf16[2560,128]{1,0:T(8,128)(2,1)S(1)} collective-permute-done((bf16[2560,128]{1,0:T(8,128)(2,1)S(1)}, bf16[2560,128]{1,0:T(8,128)(2,1)S(1)}, u32[]{:S(2)}, u32[]{:S(2)}) %collective-permute-start.6) | collective-permute-done | bytes 655392 | tf_op jit(solution)/shard_map/ppermute | solution.py:390
  126.5 1.7 %shard_map.73 = bf16[2,1024,320]{2,1,0:T(8,128)(2,1)} custom-call(s32[2]{0:T(128)S(1)} %pad_add_fusion.at, bf16[2,512,320]{2,1,0:T(8,128)(2,1)S(1)} %get-tuple-element.58.own, bf16[2560,128]{1,0:T(8,128)(2,1)S(1)} %collective-permute-done.6.got), custom_call_target="tpu_custom_call" | custom-call | flops 1000 | bytes 2621448 | tf_op jit(solution)/shard_map/pallas_call | solution.py:81
  128.2 0.0 all-to-all-done.parts
  128.2 1.5 %shard_map.79 = (f32[10,3,3,80]{3,2,1,0:T(4,128)}, f32[10,3,2,80]{3,2,1,0:T(2,128)}) custom-call(s32[2]{0:T(128)S(1)} %pad_add_fusion.at, bf16[64,100,128]{2,1,0:T(8,128)(2,1)S(1)} %all-to-all-done.parts), custom_call_target="tpu_custom_call" | custom-call | flops 1000 | bytes 1662408 | tf_op jit(solution)/shard_map/pallas_call | solution.py:81
  (7 shorter events, 0.0 us)
Async XLA Ops:
  1.7 12.6 %collective-permute-start = (bf16[17,32,320]{2,1,0:T(8,128)(2,1)S(1)}, bf16[17,32,320]{2,1,0:T(8,128)(2,1)S(1)}, u32[]{:S(2)}, u32[]{:S(2)}) collective-permute-start(bf16[17,32,320]{2,1,0:T(8,128)(2,1)S(1)} %bitcast.45), channel_id=1, source_target_pairs={{0,1},{1,0},{2,3},{3,2},{4,5},{5,4},{6,7},{7,6},{8,9},{9,8},{10,11... | collective-permute-start | bytes 1044488 | tf_op jit(solution)/shard_map/ppermute | solution.py:390
  2.2 1.6 %copy-start = (bf16[3,3,320,320]{3,2,1,0:T(8,128)(2,1)S(1)}, bf16[3,3,320,320]{3,2,1,0:T(8,128)(2,1)}, u32[]{:S(2)}) copy-start(bf16[3,3,320,320]{3,2,1,0:T(8,128)(2,1)} %param.6) | copy-start | bytes 5529604
  3.8 1.4 %copy-start.2 = (bf16[1,2,32,32,320]{4,3,2,1,0:T(8,128)(2,1)S(1)}, bf16[1,2,32,32,320]{4,3,2,1,0:T(8,128)(2,1)}, u32[]{:S(2)}) copy-start(bf16[1,2,32,32,320]{4,3,2,1,0:T(8,128)(2,1)} %param.4) | copy-start | bytes 3932164
  5.2 9.1 %copy-start.1 = (bf16[3,3,320,320]{3,2,1,0:T(8,128)(2,1)S(1)}, bf16[3,3,320,320]{3,2,1,0:T(8,128)(2,1)}, u32[]{:S(2)}) copy-start(bf16[3,3,320,320]{3,2,1,0:T(8,128)(2,1)} %param.6) | copy-start | bytes 5529604
  8.5 12.1 %collective-permute-start.2 = (bf16[1360,128]{1,0:T(8,128)(2,1)S(1)}, bf16[1360,128]{1,0:T(8,128)(2,1)S(1)}, u32[]{:S(2)}, u32[]{:S(2)}) collective-permute-start(bf16[1360,128]{1,0:T(8,128)(2,1)S(1)} %get-tuple-element.49), channel_id=1, source_target_pairs={{0,1},{1,0},{2,3},{3,2},{4,5},{5,4},{6,7},{7,6},{8,9},{9,8},{10,11... | collective-permute-start | bytes 1044488 | tf_op jit(solution)/shard_map/ppermute | solution.py:390
  14.3 1.9 %copy-start.3 = (bf16[1,2,32,32,320]{4,3,2,1,0:T(8,128)(2,1)S(1)}, bf16[1,2,32,32,320]{4,3,2,1,0:T(8,128)(2,1)}, u32[]{:S(2)}) copy-start(bf16[1,2,32,32,320]{4,3,2,1,0:T(8,128)(2,1)} %param.5) | copy-start | bytes 3932164
  14.3 1.9 %copy-start.4 = (bf16[2,3,320,320]{3,2,1,0:T(8,128)(2,1)S(1)}, bf16[2,3,320,320]{3,2,1,0:T(8,128)(2,1)}, u32[]{:S(2)}) copy-start(bf16[2,3,320,320]{3,2,1,0:T(8,128)(2,1)} %tw) | copy-start | bytes 3686404
  20.6 9.7 %collective-permute-start.7 = (bf16[1280,128]{1,0:T(8,128)(2,1)S(1)}, bf16[1280,128]{1,0:T(8,128)(2,1)S(1)}, u32[]{:S(2)}, u32[]{:S(2)}) collective-permute-start(bf16[1280,128]{1,0:T(8,128)(2,1)S(1)} %get-tuple-element.61), channel_id=1, source_target_pairs={{0,1},{1,0},{2,3},{3,2},{4,5},{5,4},{6,7},{7,6},{8,9},{9,8},{10,11... | collective-permute-start | bytes 983048 | tf_op jit(solution)/shard_map/ppermute | solution.py:390
  20.9 13.0 %collective-permute-start.3 = (bf16[16,32,320]{2,1,0:T(8,128)(2,1)S(1)}, bf16[16,32,320]{2,1,0:T(8,128)(2,1)S(1)}, u32[]{:S(2)}, u32[]{:S(2)}) collective-permute-start(bf16[16,32,320]{2,1,0:T(8,128)(2,1)S(1)} %bitcast.28), channel_id=1, source_target_pairs={{1,3},{2,0},{3,5},{4,2},{5,7},{6,4},{7,9},{8,6},{9,11},{10,8},{11,... | collective-permute-start | bytes 983048 | tf_op jit(solution)/shard_map/ppermute | solution.py:390
  24.5 13.9 %collective-permute-start.1 = (bf16[16,32,320]{2,1,0:T(8,128)(2,1)S(1)}, bf16[16,32,320]{2,1,0:T(8,128)(2,1)S(1)}, u32[]{:S(2)}, u32[]{:S(2)}) collective-permute-start(bf16[16,32,320]{2,1,0:T(8,128)(2,1)S(1)} %bitcast.29), channel_id=1, source_target_pairs={{0,2},{2,4},{3,1},{4,6},{5,3},{6,8},{7,5},{8,10},{9,7},{10,12},{11... | collective-permute-start | bytes 983048 | tf_op jit(solution)/shard_map/ppermute | solution.py:390
  25.8 20.6 %collective-permute-start.10 = (bf16[16,32,320]{2,1,0:T(8,128)(2,1)S(1)}, bf16[16,32,320]{2,1,0:T(8,128)(2,1)S(1)}, u32[]{:S(2)}, u32[]{:S(2)}) collective-permute-start(bf16[16,32,320]{2,1,0:T(8,128)(2,1)S(1)} %bitcast.30), channel_id=1, source_target_pairs={{1,3},{2,0},{3,5},{4,2},{5,7},{6,4},{7,9},{8,6},{9,11},{10,8},{11,... | collective-permute-start | bytes 983048 | tf_op jit(solution)/shard_map/ppermute | solution.py:390
  30.4 16.0 %collective-permute-start.9 = (bf16[1280,128]{1,0:T(8,128)(2,1)S(1)}, bf16[1280,128]{1,0:T(8,128)(2,1)S(1)}, u32[]{:S(2)}, u32[]{:S(2)}) collective-permute-start(bf16[1280,128]{1,0:T(8,128)(2,1)S(1)} %get-tuple-element.65), channel_id=1, source_target_pairs={{0,1},{1,0},{2,3},{3,2},{4,5},{5,4},{6,7},{7,6},{8,9},{9,8},{10,11... | collective-permute-start | bytes 983048 | tf_op jit(solution)/shard_map/ppermute | solution.py:390
  30.5 15.9 %collective-permute-start.8 = (bf16[1280,128]{1,0:T(8,128)(2,1)S(1)}, bf16[1280,128]{1,0:T(8,128)(2,1)S(1)}, u32[]{:S(2)}, u32[]{:S(2)}) collective-permute-start(bf16[1280,128]{1,0:T(8,128)(2,1)S(1)} %collective-permute-done.7.folded3), channel_id=1, source_target_pairs={{0,2},{2,4},{3,1},{4,6},{5,3},{6,8},{7,5},{8,10},{9,7},{10,12},{11... | collective-permute-start | bytes 983048 | tf_op jit(solution)/shard_map/ppermute | solution.py:390
  41.5 14.3 %collective-permute-start.5 = (bf16[16,32,320]{2,1,0:T(8,128)(2,1)S(1)}, bf16[16,32,320]{2,1,0:T(8,128)(2,1)S(1)}, u32[]{:S(2)}, u32[]{:S(2)}) collective-permute-start(bf16[16,32,320]{2,1,0:T(8,128)(2,1)S(1)} %bitcast.41), channel_id=1, source_target_pairs={{1,3},{2,0},{3,5},{4,2},{5,7},{6,4},{7,9},{8,6},{9,11},{10,8},{11,... | collective-permute-start | bytes 983048 | tf_op jit(solution)/shard_map/ppermute | solution.py:390
  44.9 10.9 %collective-permute-start.4 = (bf16[16,32,320]{2,1,0:T(8,128)(2,1)S(1)}, bf16[16,32,320]{2,1,0:T(8,128)(2,1)S(1)}, u32[]{:S(2)}, u32[]{:S(2)}) collective-permute-start(bf16[16,32,320]{2,1,0:T(8,128)(2,1)S(1)} %bitcast.40), channel_id=1, source_target_pairs={{0,2},{2,4},{3,1},{4,6},{5,3},{6,8},{7,5},{8,10},{9,7},{10,12},{11... | collective-permute-start | bytes 983048 | tf_op jit(solution)/shard_map/ppermute | solution.py:390
  49.9 12.9 %collective-permute-start.12 = (bf16[16,32,320]{2,1,0:T(8,128)(2,1)S(1)}, bf16[16,32,320]{2,1,0:T(8,128)(2,1)S(1)}, u32[]{:S(2)}, u32[]{:S(2)}) collective-permute-start(bf16[16,32,320]{2,1,0:T(8,128)(2,1)S(1)} %bitcast.43), channel_id=1, source_target_pairs={{1,3},{2,0},{3,5},{4,2},{5,7},{6,4},{7,9},{8,6},{9,11},{10,8},{11,... | collective-permute-start | bytes 983048 | tf_op jit(solution)/shard_map/ppermute | solution.py:390
  54.5 9.7 %collective-permute-start.11 = (bf16[16,32,320]{2,1,0:T(8,128)(2,1)S(1)}, bf16[16,32,320]{2,1,0:T(8,128)(2,1)S(1)}, u32[]{:S(2)}, u32[]{:S(2)}) collective-permute-start(bf16[16,32,320]{2,1,0:T(8,128)(2,1)S(1)} %bitcast.42), channel_id=1, source_target_pairs={{0,2},{2,4},{3,1},{4,6},{5,3},{6,8},{7,5},{8,10},{9,7},{10,12},{11... | collective-permute-start | bytes 983048 | tf_op jit(solution)/shard_map/ppermute | solution.py:390
  69.8 3.8 %collective-permute-start.13 = (bf16[2,5,320,240]{3,2,1,0:T(8,128)(2,1)S(1)}, bf16[2,5,320,240]{3,2,1,0:T(8,128)(2,1)S(1)}, u32[]{:S(2)}, u32[]{:S(2)}) collective-permute-start(bf16[2,5,320,240]{3,2,1,0:T(8,128)(2,1)S(1)} %get-tuple-element.80), channel_id=1, source_target_pairs={{0,32},{32,0},{64,96},{96,64},{1,33},{33,1},{65,97},{97,65},{2,34}... | collective-permute-start | bytes 4608008 | tf_op jit(solution)/shard_map/ppermute | solution.py:390
  76.2 52.0 %all-to-all-start = ((bf16[64,100,128]{2,1,0:T(8,128)(2,1)}), bf16[64,100,128]{2,1,0:T(8,128)(2,1)S(1)}, u32[]{:S(2)}, u32[]{:S(2)}) async-start(bf16[64,100,128]{2,1,0:T(8,128)(2,1)} %shard_map.78), calls=%async_computation | async-start | bytes 3407872 | tf_op jit(solution)/shard_map/all_to_all | solution.py:477
  92.9 33.6 %collective-permute-start.6 = (bf16[2560,128]{1,0:T(8,128)(2,1)S(1)}, bf16[2560,128]{1,0:T(8,128)(2,1)S(1)}, u32[]{:S(2)}, u32[]{:S(2)}) collective-permute-start(bf16[2560,128]{1,0:T(8,128)(2,1)S(1)} %get-tuple-element.59), channel_id=1, source_target_pairs={{0,1},{1,0},{2,3},{3,2},{4,5},{5,4},{6,7},{7,6},{8,9},{9,8},{10,11... | collective-permute-start | bytes 1966088 | tf_op jit(solution)/shard_map/ppermute | solution.py:390
